TPU v7x, 32 devices: a whole 2x2x4 slice. The times are simulated.
32 devices in a mesh: lat: 4 (over y, x), lon: 2 (over core), fsdp: 4 (over z).
Axes of the slice: x: 2, y: 2, z: 4, core: 2. Of those that a mesh axis runs over, the one named last changes fastest.
Arguments:
- latent: bfloat16 [4, 2, 24, 24, 512], P('fsdp', None, 'lat', 'lon'), may hold values from -6 to 6
- norm_gain: float32 [2, 512], replicated, may hold values from 0.1 to 1.9
- qkv_weight: bfloat16 [2, 512, 1536], P(None, 'fsdp'), may hold values from -0.25 to 0.25
- out_weight: bfloat16 [2, 512, 512], P(None, 'fsdp'), may hold values from -0.25 to 0.25
- rel_bias: float32 [2, 759, 16], replicated, may hold values from -4 to 304, as said below
- bias_index: int32 [144, 144], replicated, may hold values from 0 to 758
- region_ids: int32 [2, 24, 24], P(None, 'lat', 'lon'), may hold values from 0 to 3
Outputs:
- mixed: bfloat16 [4, 2, 24, 24, 512], P('fsdp', None, 'lat', 'lon')
Inputs may be any that keep to these rules, and one draw needn't show every extreme that they name: `rel_bias`: in the hidden draw.
All inputs are finite; a program needn't handle non-finite values.
Results may differ from a plain program's by a relative error of at most 0.012.
Values may be sent and summed in bfloat16 or wider, within the bound.
No kernel may reach another device: no remote copies, remote signals or barrier semaphores. Data moves between devices by JAX's collectives and lax.ppermute only.
A program may use at most 64 MiB of HBM per device.

v0:
```python
import jax
import jax.numpy as jnp
from jax import lax
from jax.sharding import PartitionSpec as P

D = 512
HEADS = 16
HEAD_DIM = 32
WZ = 2
WH = 6
WW = 12
WIN = 144


def passed_along(block, axis, distance):
    devices = range(lax.axis_size(axis))
    route = [((i - distance) % len(devices), i) for i in devices]
    return lax.ppermute(block, axis, route)


def layer_norm(hidden, gain_row):
    values = hidden.astype(jnp.float32)
    centre = jnp.mean(values, axis=-1, keepdims=True)
    shifted = values - centre
    variance = jnp.mean(shifted * shifted, axis=-1, keepdims=True)
    return (shifted * lax.rsqrt(variance + 1e-05) * gain_row).astype(jnp.bfloat16)


def bias_table(rel_bias, bias_index, block_index):
    return jnp.take(jnp.transpose(rel_bias[block_index]), bias_index, axis=1)


def split_tile(field_tile):
    sample_count, level_count, row_count, col_count, feature_width = field_tile.shape
    pieces = field_tile.reshape(
        sample_count, level_count // WZ, WZ, row_count // WH, WH, col_count // WW, WW, feature_width
    )
    pieces = jnp.transpose(pieces, (0, 1, 3, 5, 2, 4, 6, 7))
    return pieces.reshape(-1, WIN, feature_width)


def merge_tile(windows, tile_shape):
    sample_count, level_count, row_count, col_count, feature_width = tile_shape
    pieces = windows.reshape(
        sample_count, level_count // WZ, row_count // WH, col_count // WW, WZ, WH, WW, feature_width
    )
    pieces = jnp.transpose(pieces, (0, 1, 4, 2, 5, 3, 6, 7))
    return pieces.reshape(tile_shape)


def attend(normed, weight, bias_heads, region_tags):
    packed = jnp.dot(normed.reshape(-1, D), weight, preferred_element_type=jnp.float32).astype(
        jnp.bfloat16
    )
    packed = split_tile(packed.reshape(normed.shape[:-1] + (3 * D,)))
    packed = packed.reshape(-1, WIN, 3, HEADS, HEAD_DIM)
    scores = jnp.einsum(
        "gqhd,gkhd->ghqk", packed[:, :, 0], packed[:, :, 1], preferred_element_type=jnp.float32
    )
    scores = scores * HEAD_DIM ** (-0.5) + bias_heads[None]
    if region_tags is not None:
        window_tags = split_tile(region_tags[..., None])[..., 0]
        allowed = window_tags[:, :, None] == window_tags[:, None, :]
        blocked = jnp.where(allowed, jnp.float32(0.0), -jnp.inf)
        scores = scores + blocked[:, None]
    row_peak = jnp.max(scores, axis=-1, keepdims=True)
    exponent = jnp.exp(scores - row_peak)
    row_total = jnp.sum(exponent, axis=-1, keepdims=True)
    attn_probs = (exponent / row_total).astype(jnp.bfloat16)
    mixed_out = jnp.einsum(
        "ghqk,gkhd->gqhd", attn_probs, packed[:, :, 2], preferred_element_type=jnp.float32
    )
    return merge_tile(mixed_out.astype(jnp.bfloat16).reshape(-1, WIN, D), normed.shape)


def local(latent, norm_gain, qkv_weight, out_weight, rel_bias, bias_index, region_ids):
    half_rows = WH // 2
    half_cols = WW // 2
    row_count = latent.shape[2]
    col_count = latent.shape[3]
    gathered_qkv, gathered_out = (
        lax.all_gather(qkv_weight, "fsdp", axis=1, tiled=True),
        lax.all_gather(out_weight, "fsdp", axis=1, tiled=True),
    )

    def fetch_weights(block_index):
        return (gathered_qkv[block_index], gathered_out[block_index])

    first_qkv, first_out = fetch_weights(0)
    normed = layer_norm(latent, norm_gain[0])
    mixed_out = attend(normed, first_qkv, bias_table(rel_bias, bias_index, 0), None)
    projected = jnp.dot(mixed_out.reshape(-1, D), first_out, preferred_element_type=jnp.float32)
    middle = (latent.astype(jnp.float32) + projected.reshape(latent.shape)).astype(jnp.bfloat16)
    second_qkv, second_out = fetch_weights(1)
    normed = jnp.roll(layer_norm(middle, norm_gain[1]), -1, axis=1)
    east_strip = passed_along(normed[:, :, :, :half_cols], "lon", -1)
    widened = jnp.concatenate([normed[:, :, :, half_cols:], east_strip], axis=3)
    north_strip = passed_along(widened[:, :, :half_rows], "lat", -1)
    rolled = jnp.concatenate([widened[:, :, half_rows:], north_strip], axis=2)
    level_pos = lax.broadcasted_iota(jnp.int32, region_ids.shape, 0)
    row_pos = (
        lax.broadcasted_iota(jnp.int32, region_ids.shape, 1) + lax.axis_index("lat") * row_count
    )
    region_tags = region_ids * 4 + (level_pos == region_ids.shape[0] - 1).astype(jnp.int32) * 2
    region_tags = region_tags + (row_pos >= row_count * lax.axis_size("lat") - half_rows).astype(
        jnp.int32
    )
    region_tags = region_tags[None]
    mixed_out = attend(rolled, second_qkv, bias_table(rel_bias, bias_index, 1), region_tags)
    south_strip = passed_along(mixed_out[:, :, row_count - half_rows :], "lat", 1)
    widened = jnp.concatenate([south_strip, mixed_out[:, :, : row_count - half_rows]], axis=2)
    west_strip = passed_along(widened[:, :, :, col_count - half_cols :], "lon", 1)
    mixed_out = jnp.concatenate([west_strip, widened[:, :, :, : col_count - half_cols]], axis=3)
    mixed_out = jnp.roll(mixed_out, 1, axis=1)
    projected = jnp.dot(mixed_out.reshape(-1, D), second_out, preferred_element_type=jnp.float32)
    return (middle.astype(jnp.float32) + projected.reshape(latent.shape)).astype(jnp.bfloat16)


def solution(mesh):
    return jax.shard_map(
        local,
        mesh=mesh,
        in_specs=(
            P("fsdp", None, "lat", "lon", None),
            P(),
            P(None, "fsdp", None),
            P(None, "fsdp", None),
            P(),
            P(),
            P(None, "lat", "lon"),
        ),
        out_specs=P("fsdp", None, "lat", "lon", None),
        check_vma=False,
    )
```

profile of v0, /device:TPU:0, one launch (start us, length us, event | category | flops | bytes accessed | tf_op | source)
XLA Modules:
  0.0 186.9 jit_solution(10951183909749663442)
XLA Ops:
  6.5 0.7 all-gather.3.cloned.1.call-update
  7.3 0.7 all-gather.5.cloned.1.call-update
  8.0 1.0 convert_reduce_fusion
  9.0 1.1 fusion.12
  10.2 0.8 fusion.28
  10.9 1.1 fusion.14
  12.1 0.9 compare_select_fusion
  13.3 38.7 %gather_fusion = f32[20736,16]{1,0:T(8,128)} fusion(f32[16,759]{0,1:T(8,128)S(1)} %bitcast.95, s32[21504]{0:T(1024)S(1)} %pad_clamp_fusion), kind=kCustom, calls=%fused_computation.clone | custom fusion | bytes 2737152 | tf_op jit(solution)/shard_map/jit(_take)/gather | solution.py:30
  52.0 11.7 %copy.30 = f32[144,144,16]{0,1,2:T(8,128)S(1)} copy(f32[144,144,16]{2,1,0:T(8,128)} %bitcast.97) | data formatting | bytes 2654208 | tf_op jit(solution)/shard_map/jit(_take)/gather | solution.py:30
  63.9 11.2 %all-gather.3.cloned.1.call-done = bf16[2,512,1536]{2,1,0:T(8,128)(2,1)} async-done(((bf16[2,128,1536]{2,1,0:T(8,128)(2,1)}), bf16[2,512,1536]{2,1,0:T(8,128)(2,1)}) %all-gather.3.cloned.1.call-update) | async-done | bytes 3145744 | tf_op jit(solution)/shard_map/all_gather | solution.py:82
  75.1 2.6 %convolution_convert_fusion.1 = bf16[144,1536]{1,0:T(8,128)(2,1)} fusion(bf16[144,512]{1,0:T(8,128)(2,1)S(1)} %reshape.193, bf16[2,512,1536]{2,1,0:T(8,128)(2,1)} %all-gather.3.cloned.1.call-done), kind=kOutput, calls=%fused_computation.5 | convolution fusion | flops 226713600 | bytes 2162688 | tf_op jit(solution)/shard_map/dot_general | solution.py:52
  77.7 1.3 copy.26
  79.0 0.5 bitcast_add_fusion.1
  79.5 1.4 copy-done.1
  81.5 3.3 %fusion.8 = bf16[1,144,16,32]{1,3,2,0:T(8,128)(2,1)S(1)} fusion(f32[16,144]{1,0:T(8,128)S(1)} %fusion.29, bf16[1,144,3,16,32]{1,4,3,2,0:T(8,128)(2,1)S(1)} %bitcast.101, f32[16,144,144]{1,2,0:T(8,128)} %copy-done.1), kind=kOutput, calls=%fused_computation.24 | convolution fusion | flops 22305168 | bytes 5144576 | tf_op jit(solution)/shard_map/ghqk,gkhd->gqhd/dot_general | solution.py:70
  85.2 0.5 reshape.197
  85.8 17.6 %all-gather.5.cloned.1.call-done = bf16[2,512,512]{2,1,0:T(8,128)(2,1)} async-done(((bf16[2,128,512]{2,1,0:T(8,128)(2,1)}), bf16[2,512,512]{2,1,0:T(8,128)(2,1)}) %all-gather.5.cloned.1.call-update) | async-done | bytes 1048592 | tf_op jit(solution)/shard_map/all_gather | solution.py:83
  103.3 1.4 fusion.30
  105.4 1.1 collective-permute-done
  106.6 2.6 %collective-permute-start.1 = (bf16[1,2,3,12,512]{4,3,2,1,0:T(8,128)(2,1)S(1)}, bf16[1,2,3,12,512]{4,3,2,1,0:T(8,128)(2,1)S(1)}, u32[]{:S(2)}, u32[]{:S(2)}) collective-permute-start(bf16[1,2,3,12,512]{4,3,2,1,0:T(8,128)(2,1)S(1)} %get-tuple-element.11), channel_id=1, source_target_pairs={{8,0},{16,8},{24,16},{0,24},{9,1},{17,9},{25,17},{1,25},{10,2},{18... | collective-permute-start | bytes 221192 | tf_op jit(solution)/shard_map/ppermute | solution.py:18
  109.2 0.7 compare_select_fusion.1
  110.1 38.7 %gather_fusion.1 = f32[20736,16]{1,0:T(8,128)} fusion(f32[16,759]{0,1:T(8,128)S(1)} %bitcast.94, s32[21504]{0:T(1024)S(1)} %pad_clamp_fusion), kind=kCustom, calls=%fused_computation.1.clone | custom fusion | bytes 2737152 | tf_op jit(solution)/shard_map/jit(_take)/gather | solution.py:30
  148.8 11.7 %copy.37 = f32[144,144,16]{0,1,2:T(8,128)S(1)} copy(f32[144,144,16]{2,1,0:T(8,128)} %bitcast.96) | data formatting | bytes 2654208 | tf_op jit(solution)/shard_map/jit(_take)/gather | solution.py:30
  160.5 2.6 %convolution_convert_fusion = bf16[144,1536]{1,0:T(8,128)(2,1)} fusion(bf16[144,512]{1,0:T(8,128)(2,1)S(1)} %reshape.198, bf16[2,512,1536]{2,1,0:T(8,128)(2,1)} %all-gather.3.cloned.1.call-done), kind=kOutput, calls=%fused_computation.4 | convolution fusion | flops 226713600 | bytes 2162688 | tf_op jit(solution)/shard_map/dot_general | solution.py:52
  163.1 1.3 copy.33
  164.4 1.5 fusion.2
  165.9 1.4 copy-done
  167.8 3.0 %fusion.9 = bf16[1,144,16,32]{1,3,2,0:T(8,128)(2,1)S(1)} fusion(f32[16,144]{1,0:T(8,128)S(1)} %fusion.31, bf16[1,144,3,16,32]{1,4,3,2,0:T(8,128)(2,1)S(1)} %bitcast.99, f32[16,144,144]{1,2,0:T(8,128)} %copy-done), kind=kOutput, calls=%fused_computation.25 | convolution fusion | flops 22305168 | bytes 5144576 | tf_op jit(solution)/shard_map/ghqk,gkhd->gqhd/dot_general | solution.py:70
  171.3 0.5 reshape_transpose_reshape_reshape.3
  172.0 5.5 %collective-permute-done.2 = bf16[1,2,3,12,512]{4,3,2,1,0:T(8,128)(2,1)S(1)} collective-permute-done((bf16[1,2,3,12,512]{4,3,2,1,0:T(8,128)(2,1)S(1)}, bf16[1,2,3,12,512]{4,3,2,1,0:T(8,128)(2,1)S(1)}, u32[]{:S(2)}, u32[]{:S(2)}) %collective-permute-start.2) | collective-permute-done | bytes 73760 | tf_op jit(solution)/shard_map/ppermute | solution.py:18
  177.6 1.3 collective-permute-done.3
  179.3 0.8 copy.41
  (53 shorter events, 4.0 us)
Async XLA Ops:
  6.5 6.6 %copy-start.6 = (f32[2,759,16]{1,2,0:T(8,128)S(1)}, f32[2,759,16]{1,2,0:T(8,128)}, u32[]{:S(2)}) copy-start(f32[2,759,16]{1,2,0:T(8,128)} %param.13) | copy-start | bytes 291460
  6.5 68.6 %all-gather.3.cloned.1.call-start = ((), (), s32[]{:S(2)}) async-start(), calls=%async_computation | async-start | bytes 3932160 | tf_op jit(solution)/shard_map/all_gather | solution.py:82
  7.3 96.1 %all-gather.5.cloned.1.call-start = ((), (), s32[]{:S(2)}) async-start(), calls=%async_computation.1 | async-start | bytes 1310720 | tf_op jit(solution)/shard_map/all_gather | solution.py:83
  52.0 11.7 %copy-start.4 = (s32[144,144]{1,0:T(8,128)S(1)}, s32[144,144]{1,0:T(8,128)}, u32[]{:S(2)}) copy-start(s32[144,144]{1,0:T(8,128)} %param.14) | copy-start | bytes 248836
  63.9 15.6 %copy-start.5 = (pred[144,144]{0,1:T(8,128)(4,1)}, pred[144,144]{0,1:T(8,128)(4,1)S(1)}, u32[]{:S(2)}) copy-start(pred[144,144]{0,1:T(8,128)(4,1)S(1)} %copy.27) | copy-start | bytes 62212
  79.5 1.4 copy-start.1
  81.4 21.9 %copy-start.2 = (bf16[1,2,6,12,512]{4,1,3,2,0:T(2,128)(2,1)S(1)}, bf16[1,2,6,12,512]{4,1,3,2,0:T(2,128)(2,1)}, u32[]{:S(2)}) copy-start(bf16[1,2,6,12,512]{4,1,3,2,0:T(2,128)(2,1)} %param.9) | copy-start | bytes 442372
  84.7 20.5 %copy-start.7 = (s32[2,6,12]{2,0,1:T(2,128)S(1)}, s32[2,6,12]{2,0,1:T(2,128)}, u32[]{:S(2)}) copy-start(s32[2,6,12]{2,0,1:T(2,128)} %param.15) | copy-start | bytes 1732
  105.1 1.4 collective-permute-start
  106.6 53.8 %collective-permute-start.1 = (bf16[1,2,3,12,512]{4,3,2,1,0:T(8,128)(2,1)S(1)}, bf16[1,2,3,12,512]{4,3,2,1,0:T(8,128)(2,1)S(1)}, u32[]{:S(2)}, u32[]{:S(2)}) collective-permute-start(bf16[1,2,3,12,512]{4,3,2,1,0:T(8,128)(2,1)S(1)} %get-tuple-element.11), channel_id=1, source_target_pairs={{8,0},{16,8},{24,16},{0,24},{9,1},{17,9},{25,17},{1,25},{10,2},{18... | collective-permute-start | bytes 221192 | tf_op jit(solution)/shard_map/ppermute | solution.py:18
  165.9 1.4 copy-start
  170.8 8.2 %copy-start.3 = (bf16[2,512,512]{2,1,0:T(8,128)(2,1)S(1)}, bf16[2,512,512]{2,1,0:T(8,128)(2,1)}, u32[]{:S(2)}) copy-start(bf16[2,512,512]{2,1,0:T(8,128)(2,1)} %all-gather.5.cloned.1.call-done) | copy-start | bytes 3145732
  171.9 5.6 %collective-permute-start.2 = (bf16[1,2,3,12,512]{4,3,2,1,0:T(8,128)(2,1)S(1)}, bf16[1,2,3,12,512]{4,3,2,1,0:T(8,128)(2,1)S(1)}, u32[]{:S(2)}, u32[]{:S(2)}) collective-permute-start(bf16[1,2,3,12,512]{4,3,2,1,0:T(8,128)(2,1)S(1)} %get-tuple-element.8), channel_id=1, source_target_pairs={{24,0},{0,8},{8,16},{16,24},{25,1},{1,9},{9,17},{17,25},{26,2},{2,... | collective-permute-start | bytes 221192 | tf_op jit(solution)/shard_map/ppermute | solution.py:18
  177.5 1.4 collective-permute-start.3
Sparse Core Ops, SparseCore 0:
  8.9 66.1 all-gather.2
  76.7 26.6 all-gather.4
where the time goes:
time: 187 us
  local copies, waits for them, and re-layouts  110 us (59%)
  waiting for transfers between devices  38 us (20%)
  matrix products  15.2 us (8%)
  between operations  13.8 us (7%)
  other arithmetic  6.58 us (4%)
  starting transfers between devices  2.85 us (2%)
    gather x4, local copies, waits for them, and re-layouts, bias_table(): return jnp.take(jnp.transpose(rel_bias[block_index]), bias_index, axis=1)  101 us
    all_gather x1, waiting for transfers between devices, local(): lax.all_gather(out_weight, 'fsdp', axis=1, tiled=True)  17.6 us
    all_gather x1, waiting for transfers between devices, local(): lax.all_gather(qkv_weight, 'fsdp', axis=1, tiled=True)  11.2 us
    ppermute x4, waiting for transfers between devices, passed_along(): return lax.ppermute(block, axis, route)  7.9 us
    dot_general x2, matrix products, attend(): jnp.einsum('ghqk,gkhd->gqhd', attn_probs, packed[:, :, 2], preferred_elem...  6.29 us
    dot_general x2, matrix products, attend(): jnp.dot(normed.reshape(-1, D), weight, preferred_element_type=jnp.float32)  5.17 us
  transfers between devices with their start and end apart: 6, of which 5 were waited for; matrix products, arithmetic and copies ran while one was open for 62% of the time, Pallas kernels for 0%

commit v1 on v0

--- a/solution.py
+++ b/solution.py
@@ -1,6 +1,11 @@
+import functools
+
 import jax
 import jax.numpy as jnp
+import numpy as np
 from jax import lax
+from jax.experimental import pallas as pl
+from jax.experimental.pallas import tpu as pltpu
 from jax.sharding import PartitionSpec as P
 
 D = 512
@@ -10,6 +15,11 @@
 WH = 6
 WW = 12
 WIN = 144
+BIAS_ROWS = 759
+HALF = WIN // 2
+LOG2E = 1.4426950408889634
+SCALE2 = HEAD_DIM ** (-0.5) * LOG2E
+NEG = -1e30
 
 
 def passed_along(block, axis, distance):
@@ -73,7 +83,7 @@
     return merge_tile(mixed_out.astype(jnp.bfloat16).reshape(-1, WIN, D), normed.shape)
 
 
-def local(latent, norm_gain, qkv_weight, out_weight, rel_bias, bias_index, region_ids):
+def any_mesh(latent, norm_gain, qkv_weight, out_weight, rel_bias, bias_index, region_ids):
     half_rows = WH // 2
     half_cols = WW // 2
     row_count = latent.shape[2]
@@ -116,7 +126,413 @@
     return (middle.astype(jnp.float32) + projected.reshape(latent.shape)).astype(jnp.bfloat16)
 
 
+PAIR = 2
+MY_HEADS = HEADS // PAIR
+MINE = MY_HEADS * HEAD_DIM
+QKV = 3 * MINE
+COLS = QKV + D // PAIR
+TALL = 3 * WIN
+KEEP0 = 64
+KEEP1 = TALL - 64
+KEPT = KEEP1 - KEEP0
+PART = WIN - KEEP0
+REGION_ROWS = 8
+GROUP = 128 // HEAD_DIM
+F32 = jnp.float32
+BF16 = jnp.bfloat16
+
+
+def window_sources():
+    src = np.zeros((2, 2, WH, WW, WZ), np.int32)
+    for a in range(2):
+        for v in range(2):
+            for dh in range(WH):
+                for dw in range(WW):
+                    for dz in range(WZ):
+                        row = dh + (WH // 2 if a else -(WH // 2))
+                        col = (WW // 2 + WW * v + dw) % (2 * WW)
+                        level = (dz + 1) % WZ
+                        t = (row + WH) * WW * WZ + (col % WW) * WZ + level
+                        src[a, v, dh, dw, dz] = (col // WW) * KEPT + t - KEEP0
+    return src.reshape(-1, 1)
+
+
+def tile_sources():
+    src = np.zeros((2, WH, WW, WZ), np.int32)
+    for l in range(2):
+        for row in range(WH):
+            for cw in range(WW):
+                for level in range(WZ):
+                    a = 0 if row < WH // 2 else 1
+                    dh = (row + WH // 2) % WH
+                    col = (WW * l + cw - WW // 2) % (2 * WW)
+                    dz = (level - 1) % WZ
+                    t = dh * WW * WZ + (col % WW) * WZ + dz - (0 if a else KEEP0)
+                    src[l, row, cw, level] = (a * 2 + col // WW) * PART + t
+    return src.reshape(-1, 1)
+
+
+def one_hot(sources, width):
+    lanes = lax.broadcasted_iota(jnp.int32, (sources.shape[0], width), 1)
+    return jnp.where(lanes == sources, 1.0, 0.0).astype(BF16)
+
+
+def nt_dot(a, b):
+    return lax.dot_general(a, b, (((1,), (1,)), ((), ())), preferred_element_type=F32)
+
+
+def nn_dot(a, b):
+    return jnp.dot(a, b, preferred_element_type=F32)
+
+
+def norm_rows(values, gain_row):
+    centre = jnp.mean(values, axis=-1, keepdims=True)
+    shifted = values - centre
+    variance = jnp.mean(shifted * shifted, axis=-1, keepdims=True)
+    return (shifted * lax.rsqrt(variance + 1e-05) * gain_row).astype(BF16)
+
+
+def bias_kernel(table_ref, index_ref, first_ref, second_ref, table, index):
+    me = lax.axis_index("lon")
+    for b in range(2):
+        heads = table_ref[b, pl.ds(pl.multiple_of(MY_HEADS * me, MY_HEADS), MY_HEADS), :]
+        table[b, :, 0:BIAS_ROWS] = heads * LOG2E
+    to = lax.broadcasted_iota(jnp.int32, (WIN, WIN), 0)
+    frm = lax.broadcasted_iota(jnp.int32, (WIN, WIN), 1)
+    move = jnp.where((to & 1) * HALF + (to >> 1) == frm, 1.0, 0.0).astype(BF16)
+
+    def moved(a):
+        a = nn_dot(move, a.astype(F32).astype(BF16)).astype(BF16)
+        return nt_dot(a, move).astype(jnp.int32)
+
+    whole = index_ref[...]
+    index[:, 0:WIN] = moved(whole >> 8) * 256 + moved(whole & 255)
+    outs = (first_ref, second_ref)
+    chunks = (BIAS_ROWS + 127) // 128
+
+    def step(g, carry):
+        rows = pl.ds(pl.multiple_of(g * 8, 8), 8)
+        for lo, hi in ((0, 128), (128, WIN)):
+            at = index[rows, lo : lo + 128]
+            low = at & 127
+            chunk = at >> 7
+            masks = [chunk == k for k in range(chunks)]
+            for b in range(2):
+                for h in range(MY_HEADS):
+                    acc = None
+                    for k in range(chunks):
+                        row = jnp.broadcast_to(
+                            table[b, h : h + 1, 128 * k : 128 * k + 128], (8, 128)
+                        )
+                        got = jnp.take_along_axis(row, low, axis=1, mode="promise_in_bounds")
+                        acc = got if acc is None else jnp.where(masks[k], got, acc)
+                    outs[b][h, rows, lo:hi] = acc[:, : hi - lo]
+        return carry
+
+    lax.fori_loop(0, WIN // 8, step, 0)
+
+
+def bias_call(table, index):
+    out = jax.ShapeDtypeStruct((MY_HEADS, WIN, WIN), F32)
+    return pl.pallas_call(
+        bias_kernel,
+        out_shape=(out, out),
+        scratch_shapes=[
+            pltpu.VMEM((2, MY_HEADS, (BIAS_ROWS + 127) // 128 * 128), F32),
+            pltpu.VMEM((WIN, 256), jnp.int32),
+        ],
+        cost_estimate=pl.CostEstimate(flops=10**9, bytes_accessed=2 * 10**6, transcendentals=0),
+        name="bias",
+    )(table, index)
+
+
+def enter_kernel(mine_ref, other_ref, gain_ref, x_ref, n_ref, row_ref, col_ref):
+    me = lax.axis_index("lon")
+    n_lat = lax.axis_size("lat")
+    lat = lax.axis_index("lat")
+    for k in range(3):
+        for ref, l in ((mine_ref, me), (other_ref, 1 - me)):
+            tokens = ref[k, 0:WIN, :]
+            x_ref[l, WIN * k : WIN * (k + 1), :] = tokens
+            n_ref[l, WIN * k : WIN * (k + 1), :] = norm_rows(tokens.astype(F32), gain_ref[0:1, :])
+    lanes = lax.broadcasted_iota(jnp.int32, (1, WIN), 1)
+    level = lanes & 1
+    dh = lanes // (WW * WZ)
+    rows = []
+    for a in range(2):
+        window = (lat + n_lat - 1 + a) % n_lat
+        late = window * WH + dh >= n_lat * WH - WH // 2
+        extra = jnp.where(level == WZ - 1, 2.0, 0.0) + jnp.where(late, 1.0, 0.0)
+        mine = mine_ref[a, WIN : WIN + REGION_ROWS, 0:WIN].astype(F32)[0:1]
+        other = other_ref[a, WIN : WIN + REGION_ROWS, 0:WIN].astype(F32)[0:1]
+        west = jnp.where(me == 0, mine, other)
+        east = jnp.where(me == 0, other, mine)
+        rows += [4.0 * west + extra, 4.0 * east + extra]
+    tags = jnp.concatenate(rows + rows, axis=0)
+    row_ref[...] = tags
+    to = lax.broadcasted_iota(jnp.int32, (WIN, WIN), 0)
+    frm = lax.broadcasted_iota(jnp.int32, (WIN, WIN), 1)
+    col_ref[...] = nt_dot(jnp.where(to == frm, 1.0, 0.0).astype(BF16), tags.astype(BF16))
+
+
+def enter_call(mine, other, gain):
+    return pl.pallas_call(
+        enter_kernel,
+        out_shape=(
+            jax.ShapeDtypeStruct((PAIR, TALL, D), BF16),
+            jax.ShapeDtypeStruct((PAIR, TALL, D), BF16),
+            jax.ShapeDtypeStruct((8, WIN), F32),
+            jax.ShapeDtypeStruct((WIN, 8), F32),
+        ),
+        cost_estimate=pl.CostEstimate(flops=10**8, bytes_accessed=2 * 10**6, transcendentals=0),
+        name="enter",
+    )(mine, other, gain)
+
+
+def join_kernel(n_fsdp, n_lat, own_ref, *refs):
+    far, near = refs[: n_fsdp - 1], refs[n_fsdp - 1 : n_fsdp + n_lat - 2]
+    qkv_ref, out_ref = refs[-2:]
+    z = lax.axis_index("fsdp")
+    lat = lax.axis_index("lat")
+    depth = own_ref.shape[0]
+    part = depth // n_lat
+
+    def put(first, size, piece):
+        rows = pl.ds(pl.multiple_of(first, part), size)
+        qkv_ref[rows, :] = piece[:, 0:QKV]
+        out_ref[rows, :] = piece[:, QKV:COLS]
+
+    put(z * depth, depth, own_ref[...])
+    for k in range(1, n_fsdp):
+        base = ((z + n_fsdp - k) % n_fsdp) * depth
+        put(base + lat * part, part, far[k - 1][...])
+        for j in range(1, n_lat):
+            giver = (lat + n_lat - j) % n_lat
+            put(base + giver * part, part, near[j - 1][part * (k - 1) : part * k, :])
+
+
+def join_call(own, far, near):
+    n_fsdp, n_lat = len(far) + 1, len(near) + 1
+    rows = own.shape[0] * n_fsdp
+    return pl.pallas_call(
+        functools.partial(join_kernel, n_fsdp, n_lat),
+        out_shape=(
+            jax.ShapeDtypeStruct((rows, QKV), BF16),
+            jax.ShapeDtypeStruct((rows, D // PAIR), BF16),
+        ),
+        cost_estimate=pl.CostEstimate(flops=10**6, bytes_accessed=2 * 10**6, transcendentals=0),
+        name="join",
+    )(own, *far, *near)
+
+
+def window_attend(q, k, v, bias_at, allowed, put):
+    n = q.shape[0]
+    lanes = lax.broadcasted_iota(jnp.int32, (n, 128), 1)
+    owns = [(lanes >= HEAD_DIM * j) & (lanes < HEAD_DIM * (j + 1)) for j in range(GROUP)]
+    ones = jnp.ones((WIN, 128), BF16)
+    for g in range(MINE // 128):
+        cols = slice(128 * g, 128 * (g + 1))
+        q_g = q[:, cols]
+        k_g = k[:, cols]
+        v_g = jnp.concatenate([v[:, cols], ones], axis=1)
+        q_all = jnp.concatenate([jnp.where(o, q_g, jnp.zeros_like(q_g)) for o in owns], axis=0)
+        scores = nt_dot(q_all, k_g)
+        probs = []
+        for j in range(GROUP):
+            s = scores[n * j : n * (j + 1)] * SCALE2 + bias_at(GROUP * g + j)
+            if allowed is not None:
+                s = jnp.where(allowed, s, NEG)
+            peak = jnp.max(s, axis=-1, keepdims=True)
+            probs.append(jnp.exp2(s - peak).astype(BF16))
+        mixed = nn_dot(jnp.concatenate(probs, axis=0), v_g)
+        acc = None
+        for j in range(GROUP):
+            m = mixed[n * j : n * (j + 1)]
+            value = m[:, 0:128] / m[:, 128:256]
+            acc = value if acc is None else jnp.where(owns[j], value, acc)
+        put(128 * g, acc.astype(BF16))
+
+
+def project(n, w_ref, q_s, k_s, v_s):
+    both = nn_dot(n, w_ref[...]).astype(BF16)
+    q_s[...] = both[:, 0:MINE]
+    k_s[...] = both[:, MINE : 2 * MINE]
+    v_s[...] = both[:, 2 * MINE : 3 * MINE]
+
+
+def first_kernel(n_ref, w_ref, bias_ref, o_ref, q_s, k_s, v_s):
+    project(n_ref[...].reshape(PAIR * TALL, D), w_ref, q_s, k_s, v_s)
+    for l in range(PAIR):
+        for part, (q0, q1, o0) in enumerate(
+            ((KEEP0, WIN, 0), (0, WIN, PART), (0, PART, PART + WIN))
+        ):
+            t = TALL * l + WIN * part
+
+            def put(col, value, l=l, o0=o0, q0=q0, q1=q1):
+                o_ref[l, o0 : o0 + q1 - q0, col : col + 128] = value
+
+            window_attend(
+                q_s[t + q0 : t + q1, :],
+                k_s[t : t + WIN, :],
+                v_s[t : t + WIN, :],
+                lambda h, q0=q0, q1=q1: bias_ref[h, q0:q1, :],
+                None,
+                put,
+            )
+
+
+def first_call(normed, weight, bias):
+    scratch = pltpu.VMEM((PAIR * TALL, MINE), BF16)
+    return pl.pallas_call(
+        first_kernel,
+        out_shape=jax.ShapeDtypeStruct((PAIR, KEPT, MINE), BF16),
+        scratch_shapes=[scratch, scratch, scratch],
+        cost_estimate=pl.CostEstimate(flops=2 * 10**9, bytes_accessed=4 * 10**6, transcendentals=10**6),
+        name="first",
+    )(normed, weight, bias)
+
+
+def pair_columns(me, ref, mine, other):
+    width = mine.shape[-1]
+    ref[:, pl.ds(pl.multiple_of(width * me, width), width)] = mine
+    ref[:, pl.ds(pl.multiple_of(width * (1 - me), width), width)] = other
+
+
+def second_kernel(
+    mine_ref, other_ref, wo_mine_ref, wo_other_ref, x_ref, gain_ref, src_ref, w_ref, bias_ref,
+    row_ref, col_ref, back_ref, mid_ref, keep_ref, send_ref, o_s, wo_s, m_s, n_s, q_s, k_s, v_s, a_s, t_s,
+):
+    me = lax.axis_index("lon")
+    tokens = PAIR * KEPT
+    pair_columns(me, o_s, mine_ref[...].reshape(tokens, MINE), other_ref[...].reshape(tokens, MINE))
+    pair_columns(me, wo_s, wo_mine_ref[...], wo_other_ref[...])
+    for l in range(PAIR):
+        rows = slice(KEPT * l, KEPT * (l + 1))
+        value = x_ref[l, KEEP0:KEEP1, :].astype(F32) + nn_dot(o_s[rows, :], wo_s[...])
+        value = value.astype(BF16)
+        m_s[l] = value
+        n_s[rows, :] = norm_rows(value.astype(F32), gain_ref[1:2, :])
+    mid_ref[...] = m_s[me, PART : PART + WIN, :]
+    windows = nn_dot(one_hot(src_ref[...], tokens), n_s[...]).astype(BF16)
+    project(windows, w_ref, q_s, k_s, v_s)
+    for w in range(4):
+        q0, q1 = (KEEP0, WIN) if w < 2 else (0, PART)
+        t = WIN * w
+        allowed = col_ref[q0:q1, w : w + 1] == row_ref[w : w + 1, :]
+
+        def put(col, value, w=w):
+            a_s[PART * w : PART * (w + 1), col : col + 128] = value
+
+        window_attend(
+            q_s[t + q0 : t + q1, :],
+            k_s[t : t + WIN, :],
+            v_s[t : t + WIN, :],
+            lambda h, q0=q0, q1=q1: bias_ref[h, q0:q1, :],
+            allowed,
+            put,
+        )
+    tiles = nn_dot(one_hot(back_ref[...], 4 * PART), a_s[...]).astype(BF16)
+    t_s[0] = tiles[0:WIN]
+    t_s[1] = tiles[WIN : 2 * WIN]
+    keep_ref[...] = t_s[me]
+    send_ref[...] = t_s[1 - me]
+
+
+def second_call(mine, other, wo_mine, wo_other, x, gain, weight, bias, row, col):
+    tokens = PAIR * KEPT
+    qkv = pltpu.VMEM((4 * WIN, MINE), BF16)
+    return pl.pallas_call(
+        second_kernel,
+        out_shape=(
+            jax.ShapeDtypeStruct((WIN, D), BF16),
+            jax.ShapeDtypeStruct((WIN, MINE), BF16),
+            jax.ShapeDtypeStruct((WIN, MINE), BF16),
+        ),
+        scratch_shapes=[
+            pltpu.VMEM((tokens, D), BF16),
+            pltpu.VMEM((D, D), BF16),
+            pltpu.VMEM((PAIR, KEPT, D), BF16),
+            pltpu.VMEM((tokens, D), BF16),
+            qkv,
+            qkv,
+            qkv,
+            pltpu.VMEM((4 * PART, MINE), BF16),
+            pltpu.VMEM((PAIR, WIN, MINE), BF16),
+        ],
+        cost_estimate=pl.CostEstimate(flops=2 * 10**9, bytes_accessed=4 * 10**6, transcendentals=10**6),
+        name="second",
+    )(
+        mine, other, wo_mine, wo_other, x, gain, jnp.asarray(window_sources()), weight, bias,
+        row, col, jnp.asarray(tile_sources()),
+    )
+
+
+def last_kernel(mid_ref, keep_ref, got_ref, wo_mine_ref, wo_other_ref, out_ref, o_s, wo_s):
+    me = lax.axis_index("lon")
+    pair_columns(me, o_s, keep_ref[...], got_ref[...])
+    pair_columns(me, wo_s, wo_mine_ref[...], wo_other_ref[...])
+    value = mid_ref[...].astype(F32) + nn_dot(o_s[...], wo_s[...])
+    out_ref[...] = value.astype(BF16)
+
+
+def last_call(mid, keep, got, wo_mine, wo_other):
+    return pl.pallas_call(
+        last_kernel,
+        out_shape=jax.ShapeDtypeStruct((WIN, D), BF16),
+        scratch_shapes=[pltpu.VMEM((WIN, D), BF16), pltpu.VMEM((D, D), BF16)],
+        cost_estimate=pl.CostEstimate(flops=10**8, bytes_accessed=10**6, transcendentals=0),
+        name="last",
+    )(mid, keep, got, wo_mine, wo_other)
+
+
+def paired(latent, norm_gain, qkv_weight, out_weight, rel_bias, bias_index, region_ids):
+    me = lax.axis_index("lon")
+    lat = lax.axis_index("lat")
+    n_fsdp, n_lat = lax.axis_size("fsdp"), lax.axis_size("lat")
+    depth = qkv_weight.shape[1]
+    part = depth // n_lat
+
+    def mine_of(w, groups):
+        w = w.reshape(2, depth, groups, PAIR, w.shape[2] // groups // PAIR)
+        return lax.dynamic_index_in_dim(w, me, 3, keepdims=False).reshape(2, depth, -1)
+
+    own = jnp.concatenate([mine_of(qkv_weight, 3), mine_of(out_weight, 1)], axis=2)
+    slices = lax.dynamic_slice_in_dim(own, lat * part, part, 1)
+
+    swap = functools.partial(passed_along, axis="lon", distance=1)
+    far = [[passed_along(slices[b], "fsdp", k) for k in range(1, n_fsdp)] for b in range(2)]
+
+    tokens = jnp.transpose(latent[0], (1, 2, 0, 3)).reshape(WIN, D)
+    regions = jnp.transpose(region_ids, (1, 2, 0)).reshape(1, WIN).astype(BF16)
+    tile = jnp.concatenate(
+        [tokens, jnp.pad(regions, ((0, REGION_ROWS - 1), (0, D - WIN)))], axis=0
+    )
+    tall = jnp.stack([passed_along(tile, "lat", 1), tile, passed_along(tile, "lat", -1)])
+    x, normed, tag_row, tag_col = enter_call(tall, swap(tall), norm_gain)
+    bias = bias_call(jnp.transpose(rel_bias, (0, 2, 1)), bias_index)
+
+    weights = []
+    for b in range(2):
+        given = jnp.concatenate(far[b], axis=0)
+        near = [passed_along(given, "lat", j) for j in range(1, n_lat)]
+        weights.append(join_call(own[b], far[b], near))
+    (w0, wo0), (w1, wo1) = weights
+    o0 = first_call(normed, w0, bias[0])
+    mid, keep, send = second_call(
+        o0, swap(o0), wo0, swap(wo0), x, norm_gain, w1, bias[1], tag_row, tag_col
+    )
+    out = last_call(mid, keep, swap(send), wo1, swap(wo1))
+    return jnp.transpose(out.reshape(WH, WW, WZ, D), (2, 0, 1, 3))[None]
+
+
 def solution(mesh):
+    def local(latent, norm_gain, qkv_weight, out_weight, *rest):
+        one_window = latent.shape[:4] == (1, WZ, WH, WW)
+        even = qkv_weight.shape[1] % (16 * mesh.shape["lat"]) == 0
+        pays = mesh.shape["lon"] == PAIR and one_window and even
+        program = paired if pays else any_mesh
+        return program(latent, norm_gain, qkv_weight, out_weight, *rest)
+
     return jax.shard_map(
         local,
         mesh=mesh,

time: 187 us -> 78.5 us (0.42)
  local copies, waits for them, and re-layouts: 110 us -> 8.54 us
  Pallas kernels: 0 us -> 29.2 us
  waiting for transfers between devices: 38 us -> 15.5 us
  starting transfers between devices: 2.85 us -> 22 us
  matrix products: 15.2 us -> 0 us
  between operations: 13.8 us -> 0.3 us
  other arithmetic: 6.58 us -> 1.73 us
    gather x4 -> x0, local copies, waits for them, and re-layouts: 101 us -> none  [bias_table(): return jnp.take(jnp.transpose(rel_bias[block_index]), bias_index, axis=1)]
    pallas_call x0 -> x7, Pallas kernels: none -> 29.2 us  [the longest x1 7.67 us: bias_call(): pl.pallas_call(bias_kernel, out_shape=(out, out), scratch_shapes=[pltpu.V...]
    all_gather x2 -> x0, waiting for transfers between devices: 28.7 us -> none  [the longest x1 17.6 us: local(): lax.all_gather(out_weight, 'fsdp', axis=1, tiled=True)]
    ppermute x4 -> x19, starting transfers between devices: 2.8 us -> 22 us  [passed_along(): return lax.ppermute(block, axis, route)]
    dot_general x8 -> x0, matrix products: 15.2 us -> none  [the longest x2 6.29 us: attend(): jnp.einsum('ghqk,gkhd->gqhd', attn_probs, packed[:, :, 2], preferred_elem...]
    ppermute x4 -> x19, waiting for transfers between devices: 7.9 us -> 15.5 us  [passed_along(): return lax.ppermute(block, axis, route)]
    convert_element_type x5 -> x2, local copies, waits for them, and re-layouts: 4.33 us -> 0.29 us  [paired(): regions = jnp.transpose(region_ids, (1, 2, 0)).reshape(1, WIN).astype(BF16)]
    reshape x2 -> x4, local copies, waits for them, and re-layouts: 0.07 us -> 3.8 us  [the longest x1 1.63 us: paired(): return jnp.transpose(out.reshape(WH, WW, WZ, D), (2, 0, 1, 3))[None]]
  transfers between devices with their start and end apart: 6 -> 19, of which waited for: 5 -> 6; matrix products, arithmetic and copies ran while one was open for 62% -> 4% of each run, Pallas kernels for 0% -> 35%
where the time goes in v1:
time: 78.5 us; the launch traced here: 77.3 us
  Pallas kernels  29.2 us (37%)
  starting transfers between devices  22 us (28%)
  waiting for transfers between devices  15.5 us (20%)
  local copies, waits for them, and re-layouts  8.54 us (11%)
  other arithmetic  1.73 us (2%)
    ppermute x19, starting transfers between devices, passed_along(): return lax.ppermute(block, axis, route)  22 us
    ppermute x19, waiting for transfers between devices, passed_along(): return lax.ppermute(block, axis, route)  15.5 us
    pallas_call x1, Pallas kernels, bias_call(): pl.pallas_call(bias_kernel, out_shape=(out, out), scratch_shapes=[pltpu.V...  7.67 us
    pallas_call x1, Pallas kernels, second_call(): pl.pallas_call(second_kernel, out_shape=(jax.ShapeDtypeStruct((WIN, D), B...  6.34 us
    pallas_call x1, Pallas kernels, first_call(): pl.pallas_call(first_kernel, out_shape=jax.ShapeDtypeStruct((PAIR, KEPT,...  5.66 us
    pallas_call x2, Pallas kernels, join_call(): pl.pallas_call(functools.partial(join_kernel, n_fsdp, n_lat), out_shape=(...  4.62 us
    unnamed x44, local copies, waits for them, and re-layouts  4.12 us
    pallas_call x1, Pallas kernels, enter_call(): pl.pallas_call(enter_kernel, out_shape=(jax.ShapeDtypeStruct((PAIR, TALL,...  2.75 us
  transfers between devices with their start and end apart: 19, of which 6 were waited for; matrix products, arithmetic and copies ran while one was open for 4% of the time, Pallas kernels for 35%

profile of v1, /device:TPU:0, one launch (start us, length us, event | category | flops | bytes accessed | tf_op | source)
XLA Modules:
  0.0 77.3 jit_solution(8109959393452002410)
XLA Ops:
  0.0 0.8 convert_bitcast_fusion
  1.1 1.0 %reshape.34 = bf16[144,512]{1,0:T(8,128)(2,1)S(1)} reshape(bf16[6,12,2,512]{3,2,1,0:T(2,128)(2,1)} %bitcast.32) | data formatting | bytes 294912 | tf_op jit(solution)/shard_map/reshape | solution.py:505
  2.1 4.0 %collective-permute-start.1 = (bf16[152,512]{1,0:T(8,128)(2,1)S(1)}, bf16[152,512]{1,0:T(8,128)(2,1)S(1)}, u32[]{:S(2)}, u32[]{:S(2)}) collective-permute-start(bf16[152,512]{1,0:T(8,128)(2,1)S(1)} %get-tuple-element.34), channel_id=1, source_target_pairs={{8,0},{16,8},{24,16},{0,24},{9,1},{17,9},{25,17},{1,25},{10,2},{18... | collective-permute-start | bytes 466952 | tf_op jit(solution)/shard_map/ppermute | solution.py:28
  6.0 1.0 %reshape.37 = bf16[2,128,1,2,256]{4,3,1,0,2:T(2,128)(2,1)S(1)} reshape(bf16[2,128,512]{2,1,0:T(8,128)(2,1)} %param.12) | data formatting | bytes 524288 | tf_op jit(solution)/shard_map/reshape | solution.py:496
  8.0 1.6 %collective-permute-start.3 = (bf16[32,1024]{1,0:T(8,128)(2,1)S(1)}, bf16[32,1024]{1,0:T(8,128)(2,1)S(1)}, u32[]{:S(2)}, u32[]{:S(2)}) collective-permute-start(bf16[32,1024]{1,0:T(8,128)(2,1)S(1)} %get-tuple-element.36), channel_id=1, source_target_pairs={{3,0},{0,1},{1,2},{2,3},{7,4},{4,5},{5,6},{6,7},{11,8},{8,9},{9,10... | collective-permute-start | bytes 196616 | tf_op jit(solution)/shard_map/ppermute | solution.py:28
  9.7 2.6 %collective-permute-start.4 = (bf16[32,1024]{1,0:T(8,128)(2,1)S(1)}, bf16[32,1024]{1,0:T(8,128)(2,1)S(1)}, u32[]{:S(2)}, u32[]{:S(2)}) collective-permute-start(bf16[32,1024]{1,0:T(8,128)(2,1)S(1)} %get-tuple-element.36), channel_id=1, source_target_pairs={{2,0},{3,1},{0,2},{1,3},{6,4},{7,5},{4,6},{5,7},{10,8},{11,9},{8,1... | collective-permute-start | bytes 196616 | tf_op jit(solution)/shard_map/ppermute | solution.py:28
  12.3 1.3 %collective-permute-start.5 = (bf16[32,1024]{1,0:T(8,128)(2,1)S(1)}, bf16[32,1024]{1,0:T(8,128)(2,1)S(1)}, u32[]{:S(2)}, u32[]{:S(2)}) collective-permute-start(bf16[32,1024]{1,0:T(8,128)(2,1)S(1)} %get-tuple-element.36), channel_id=1, source_target_pairs={{1,0},{2,1},{3,2},{0,3},{5,4},{6,5},{7,6},{4,7},{9,8},{10,9},{11,1... | collective-permute-start | bytes 196616 | tf_op jit(solution)/shard_map/ppermute | solution.py:28
  13.6 7.7 %bias.1 = (f32[8,144,144]{2,1,0:T(8,128)}, f32[8,144,144]{2,1,0:T(8,128)}) custom-call(f32[2,16,759]{2,1,0:T(8,128)} %bitcast.33, s32[144,144]{1,0:T(8,128)} %index_ref.1), custom_call_target="tpu_custom_call" | custom-call | flops 1000000000 | bytes 2000000 | tf_op jit(solution)/shard_map/bias/pallas_call | solution.py:237
  21.3 0.9 %fusion.3 = (bf16[128,1024]{1,0:T(8,128)(2,1)}, bf16[128,1024]{1,0:T(8,128)(2,1)}) fusion(bf16[2,128,256]{2,1,0:T(8,128)(2,1)S(1)} %bitcast.29, bf16[2,128,768]{2,1,0:T(8,128)(2,1)S(1)} %copy.19), kind=kLoop, calls=%fused_computation.10 | loop fusion | flops 1048576 | bytes 1048576 | tf_op jit(solution)/shard_map/squeeze | solution.py:518
  22.2 0.7 collective-permute-start.11
  23.4 2.0 %collective-permute-start.6 = (bf16[96,1024]{1,0:T(8,128)(2,1)S(1)}, bf16[96,1024]{1,0:T(8,128)(2,1)S(1)}, u32[]{:S(2)}, u32[]{:S(2)}) collective-permute-start(bf16[96,1024]{1,0:T(8,128)(2,1)S(1)} %constant_dynamic-update-slice_fusion), channel_id=1, source_target_pairs={{24,0},{0,8},{8,16},{16,24},{25,1},{1,9},{9,17},{17,25},{26,2},{2,... | collective-permute-start | bytes 589832 | tf_op jit(solution)/shard_map/ppermute | solution.py:28
  25.4 1.5 %collective-permute-start.7 = (bf16[96,1024]{1,0:T(8,128)(2,1)S(1)}, bf16[96,1024]{1,0:T(8,128)(2,1)S(1)}, u32[]{:S(2)}, u32[]{:S(2)}) collective-permute-start(bf16[96,1024]{1,0:T(8,128)(2,1)S(1)} %constant_dynamic-update-slice_fusion), channel_id=1, source_target_pairs={{16,0},{24,8},{0,16},{8,24},{17,1},{25,9},{1,17},{9,25},{18,2},{26... | collective-permute-start | bytes 589832 | tf_op jit(solution)/shard_map/ppermute | solution.py:28
  27.0 1.4 %collective-permute-done.11.refs_0_ = bf16[32,1024]{1,0:T(8,128)(2,1)S(1)} collective-permute-done((bf16[32,1024]{1,0:T(8,128)(2,1)S(1)}, bf16[32,1024]{1,0:T(8,128)(2,1)S(1)}, u32[]{:S(2)}, u32[]{:S(2)}) %collective-permute-start.11) | collective-permute-done | bytes 65568 | tf_op jit(solution)/shard_map/ppermute | solution.py:28
  28.3 2.9 %collective-permute-start.8 = (bf16[96,1024]{1,0:T(8,128)(2,1)S(1)}, bf16[96,1024]{1,0:T(8,128)(2,1)S(1)}, u32[]{:S(2)}, u32[]{:S(2)}) collective-permute-start(bf16[96,1024]{1,0:T(8,128)(2,1)S(1)} %constant_dynamic-update-slice_fusion), channel_id=1, source_target_pairs={{8,0},{16,8},{24,16},{0,24},{9,1},{17,9},{25,17},{1,25},{10,2},{18... | collective-permute-start | bytes 589832 | tf_op jit(solution)/shard_map/ppermute | solution.py:28
  31.3 0.8 %collective-permute-done.6.refs_3_ = bf16[96,1024]{1,0:T(8,128)(2,1)S(1)} collective-permute-done((bf16[96,1024]{1,0:T(8,128)(2,1)S(1)}, bf16[96,1024]{1,0:T(8,128)(2,1)S(1)}, u32[]{:S(2)}, u32[]{:S(2)}) %collective-permute-start.6) | collective-permute-done | bytes 196640 | tf_op jit(solution)/shard_map/ppermute | solution.py:28
  32.2 4.0 %collective-permute-done.7.refs_4_ = bf16[96,1024]{1,0:T(8,128)(2,1)S(1)} collective-permute-done((bf16[96,1024]{1,0:T(8,128)(2,1)S(1)}, bf16[96,1024]{1,0:T(8,128)(2,1)S(1)}, u32[]{:S(2)}, u32[]{:S(2)}) %collective-permute-start.7) | collective-permute-done | bytes 196640 | tf_op jit(solution)/shard_map/ppermute | solution.py:28
  36.9 2.3 %join.2 = (bf16[512,768]{1,0:T(8,128)(2,1)}, bf16[512,256]{1,0:T(8,128)(2,1)}) custom-call(bf16[128,1024]{1,0:T(8,128)(2,1)} %get-tuple-element.32.own_ref, bf16[32,1024]{1,0:T(8,128)(2,1)} %copy-done.5, bf16[32,1024]{1,0:T(8,128)(2,1)} %copy-done.6, bf16[32,1024]{1,0:T(8,128)(2,1)} %copy-done.7, bf16[96,1024]{1,0:T(8,128)(2,1)} %copy-done.10, ...), custom_call_target="tpu_custom_call" | custom-call | flops 1000000 | bytes 2000000 | tf_op jit(solution)/shard_map/join/pallas_call | solution.py:317
  39.3 0.8 %copy-done.2 = bf16[3,152,512]{2,1,0:T(8,128)(2,1)} copy-done((bf16[3,152,512]{2,1,0:T(8,128)(2,1)}, bf16[3,152,512]{2,1,0:T(8,128)(2,1)S(1)}, u32[]{:S(2)}) %copy-start.2) | copy-done | bytes 466968
  40.1 2.7 %enter.1 = (bf16[2,432,512]{2,1,0:T(8,128)(2,1)}, bf16[2,432,512]{2,1,0:T(8,128)(2,1)}, f32[8,144]{1,0:T(8,128)}, f32[144,8]{1,0:T(8,128)}) custom-call(bf16[3,152,512]{2,1,0:T(8,128)(2,1)} %copy-done, bf16[3,152,512]{2,1,0:T(8,128)(2,1)} %copy-done.2, f32[2,512]{1,0:T(2,128)} %gain_ref.3), custom_call_target="tpu_custom_call" | custom-call | flops 100000000 | bytes 2000000 | tf_op jit(solution)/shard_map/enter/pallas_call | solution.py:279
  42.8 5.7 %first.1.mine_ref = bf16[2,304,256]{2,1,0:T(8,128)(2,1)} custom-call(bf16[2,432,512]{2,1,0:T(8,128)(2,1)} %get-tuple-element.18.n_ref, bf16[512,768]{1,0:T(8,128)(2,1)} %get-tuple-element.19.w_ref, f32[8,144,144]{2,1,0:T(8,128)} %get-tuple-element.20.bias_ref), custom_call_target="tpu_custom_call" | custom-call | flops 2000000000 | bytes 4000000 | tf_op jit(solution)/shard_map/first/pallas_call | solution.py:386
  49.0 1.7 %collective-permute-start.14 = (bf16[96,1024]{1,0:T(8,128)(2,1)S(1)}, bf16[96,1024]{1,0:T(8,128)(2,1)S(1)}, u32[]{:S(2)}, u32[]{:S(2)}) collective-permute-start(bf16[96,1024]{1,0:T(8,128)(2,1)S(1)} %constant_dynamic-update-slice_fusion.3), channel_id=1, source_target_pairs={{24,0},{0,8},{8,16},{16,24},{25,1},{1,9},{9,17},{17,25},{26,2},{2,... | collective-permute-start | bytes 589832 | tf_op jit(solution)/shard_map/ppermute | solution.py:28
  50.7 0.7 collective-permute-start.15
  51.4 1.4 %collective-permute-start.16 = (bf16[96,1024]{1,0:T(8,128)(2,1)S(1)}, bf16[96,1024]{1,0:T(8,128)(2,1)S(1)}, u32[]{:S(2)}, u32[]{:S(2)}) collective-permute-start(bf16[96,1024]{1,0:T(8,128)(2,1)S(1)} %constant_dynamic-update-slice_fusion.3), channel_id=1, source_target_pairs={{8,0},{16,8},{24,16},{0,24},{9,1},{17,9},{25,17},{1,25},{10,2},{18... | collective-permute-start | bytes 589832 | tf_op jit(solution)/shard_map/ppermute | solution.py:28
  52.8 5.0 %collective-permute-done.14.refs_3_ = bf16[96,1024]{1,0:T(8,128)(2,1)S(1)} collective-permute-done((bf16[96,1024]{1,0:T(8,128)(2,1)S(1)}, bf16[96,1024]{1,0:T(8,128)(2,1)S(1)}, u32[]{:S(2)}, u32[]{:S(2)}) %collective-permute-start.14) | collective-permute-done | bytes 196640 | tf_op jit(solution)/shard_map/ppermute | solution.py:28
  57.7 3.2 %collective-permute-done.15.refs_4_ = bf16[96,1024]{1,0:T(8,128)(2,1)S(1)} collective-permute-done((bf16[96,1024]{1,0:T(8,128)(2,1)S(1)}, bf16[96,1024]{1,0:T(8,128)(2,1)S(1)}, u32[]{:S(2)}, u32[]{:S(2)}) %collective-permute-start.15) | collective-permute-done | bytes 196640 | tf_op jit(solution)/shard_map/ppermute | solution.py:28
  61.0 0.7 copy-done.14
  61.7 2.3 %join.3 = (bf16[512,768]{1,0:T(8,128)(2,1)}, bf16[512,256]{1,0:T(8,128)(2,1)}) custom-call(bf16[128,1024]{1,0:T(8,128)(2,1)} %get-tuple-element.31.own_ref, bf16[32,1024]{1,0:T(8,128)(2,1)} %copy-done.3, bf16[32,1024]{1,0:T(8,128)(2,1)} %copy-done.4, bf16[32,1024]{1,0:T(8,128)(2,1)} %copy-done.8, bf16[96,1024]{1,0:T(8,128)(2,1)} %copy-done.13, ...), custom_call_target="tpu_custom_call" | custom-call | flops 1000000 | bytes 2000000 | tf_op jit(solution)/shard_map/join/pallas_call | solution.py:317
  64.1 0.7 copy-done.18
  64.9 6.3 %second.1 = (bf16[144,512]{1,0:T(8,128)(2,1)}, bf16[144,256]{1,0:T(8,128)(2,1)}, bf16[144,256]{1,0:T(8,128)(2,1)}) custom-call(bf16[2,304,256]{2,1,0:T(8,128)(2,1)} %first.1.mine_ref, bf16[2,304,256]{2,1,0:T(8,128)(2,1)} %copy-done.17, bf16[512,256]{1,0:T(8,128)(2,1)} %get-tuple-element.21.wo_mine_ref, bf16[512,256]{1,0:T(8,128)(2,1)} %copy-done.18, ...), custom_call_target="tpu_custom_call" | custom-call | flops 2000000000 | bytes 4000000 | tf_op jit(solution)/shard_map/second/pallas_call | solution.py:444
  71.8 1.1 %collective-permute-done.17.got_ref = bf16[144,256]{1,0:T(8,128)(2,1)S(1)} collective-permute-done((bf16[144,256]{1,0:T(8,128)(2,1)}, bf16[144,256]{1,0:T(8,128)(2,1)S(1)}, u32[]{:S(2)}, u32[]{:S(2)}) %collective-permute-start.17) | collective-permute-done | bytes 73760 | tf_op jit(solution)/shard_map/ppermute | solution.py:28
  73.5 2.2 %last.1 = bf16[144,512]{1,0:T(8,128)(2,1)} custom-call(bf16[144,512]{1,0:T(8,128)(2,1)} %get-tuple-element.27.mid_ref, bf16[144,256]{1,0:T(8,128)(2,1)} %get-tuple-element.28.keep_ref, bf16[144,256]{1,0:T(8,128)(2,1)} %copy-done.16, bf16[512,256]{1,0:T(8,128)(2,1)} %get-tuple-element.30.wo_mine_ref, bf16[512,256]{1,0:T(8,128)(2,1)} %copy-done.9), custom_call_target="tpu_custom_call" | custom-call | flops 100000000 | bytes 1000000 | tf_op jit(solution)/shard_map/last/pallas_call | solution.py:479
  75.7 1.6 %reshape.39 = bf16[6,12,2,512]{3,2,1,0:T(2,128)(2,1)} reshape(bf16[144,512]{1,0:T(8,128)(2,1)} %last.1) | data formatting | bytes 294912 | tf_op jit(solution)/shard_map/reshape | solution.py:525
  (73 shorter events, 4.4 us)
Async XLA Ops:
  0.0 7.4 %copy-start.1 = (bf16[2,128,1536]{2,1,0:T(8,128)(2,1)S(1)}, bf16[2,128,1536]{2,1,0:T(8,128)(2,1)}, u32[]{:S(2)}) copy-start(bf16[2,128,1536]{2,1,0:T(8,128)(2,1)} %param.11) | copy-start | bytes 2359300
  2.1 20.1 %collective-permute-start.1 = (bf16[152,512]{1,0:T(8,128)(2,1)S(1)}, bf16[152,512]{1,0:T(8,128)(2,1)S(1)}, u32[]{:S(2)}, u32[]{:S(2)}) collective-permute-start(bf16[152,512]{1,0:T(8,128)(2,1)S(1)} %get-tuple-element.34), channel_id=1, source_target_pairs={{8,0},{16,8},{24,16},{0,24},{9,1},{17,9},{25,17},{1,25},{10,2},{18... | collective-permute-start | bytes 466952 | tf_op jit(solution)/shard_map/ppermute | solution.py:28
  6.0 16.8 %collective-permute-start = (bf16[152,512]{1,0:T(8,128)(2,1)S(1)}, bf16[152,512]{1,0:T(8,128)(2,1)S(1)}, u32[]{:S(2)}, u32[]{:S(2)}) collective-permute-start(bf16[152,512]{1,0:T(8,128)(2,1)S(1)} %get-tuple-element.34), channel_id=1, source_target_pairs={{24,0},{0,8},{8,16},{16,24},{25,1},{1,9},{9,17},{17,25},{26,2},{2,... | collective-permute-start | bytes 466952 | tf_op jit(solution)/shard_map/ppermute | solution.py:28
  8.0 15.2 %collective-permute-start.3 = (bf16[32,1024]{1,0:T(8,128)(2,1)S(1)}, bf16[32,1024]{1,0:T(8,128)(2,1)S(1)}, u32[]{:S(2)}, u32[]{:S(2)}) collective-permute-start(bf16[32,1024]{1,0:T(8,128)(2,1)S(1)} %get-tuple-element.36), channel_id=1, source_target_pairs={{3,0},{0,1},{1,2},{2,3},{7,4},{4,5},{5,6},{6,7},{11,8},{8,9},{9,10... | collective-permute-start | bytes 196616 | tf_op jit(solution)/shard_map/ppermute | solution.py:28
  9.7 13.7 %collective-permute-start.4 = (bf16[32,1024]{1,0:T(8,128)(2,1)S(1)}, bf16[32,1024]{1,0:T(8,128)(2,1)S(1)}, u32[]{:S(2)}, u32[]{:S(2)}) collective-permute-start(bf16[32,1024]{1,0:T(8,128)(2,1)S(1)} %get-tuple-element.36), channel_id=1, source_target_pairs={{2,0},{3,1},{0,2},{1,3},{6,4},{7,5},{4,6},{5,7},{10,8},{11,9},{8,1... | collective-permute-start | bytes 196616 | tf_op jit(solution)/shard_map/ppermute | solution.py:28
  12.3 11.1 %collective-permute-start.5 = (bf16[32,1024]{1,0:T(8,128)(2,1)S(1)}, bf16[32,1024]{1,0:T(8,128)(2,1)S(1)}, u32[]{:S(2)}, u32[]{:S(2)}) collective-permute-start(bf16[32,1024]{1,0:T(8,128)(2,1)S(1)} %get-tuple-element.36), channel_id=1, source_target_pairs={{1,0},{2,1},{3,2},{0,3},{5,4},{6,5},{7,6},{4,7},{9,8},{10,9},{11,1... | collective-permute-start | bytes 196616 | tf_op jit(solution)/shard_map/ppermute | solution.py:28
  22.2 6.2 %collective-permute-start.11 = (bf16[32,1024]{1,0:T(8,128)(2,1)S(1)}, bf16[32,1024]{1,0:T(8,128)(2,1)S(1)}, u32[]{:S(2)}, u32[]{:S(2)}) collective-permute-start(bf16[32,1024]{1,0:T(8,128)(2,1)S(1)} %get-tuple-element.35), channel_id=1, source_target_pairs={{3,0},{0,1},{1,2},{2,3},{7,4},{4,5},{5,6},{6,7},{11,8},{8,9},{9,10... | collective-permute-start | bytes 196616 | tf_op jit(solution)/shard_map/ppermute | solution.py:28
  22.8 8.4 %collective-permute-start.12 = (bf16[32,1024]{1,0:T(8,128)(2,1)S(1)}, bf16[32,1024]{1,0:T(8,128)(2,1)S(1)}, u32[]{:S(2)}, u32[]{:S(2)}) collective-permute-start(bf16[32,1024]{1,0:T(8,128)(2,1)S(1)} %get-tuple-element.35), channel_id=1, source_target_pairs={{2,0},{3,1},{0,2},{1,3},{6,4},{7,5},{4,6},{5,7},{10,8},{11,9},{8,1... | collective-permute-start | bytes 196616 | tf_op jit(solution)/shard_map/ppermute | solution.py:28
  23.2 16.1 %copy-start = (bf16[3,152,512]{2,1,0:T(8,128)(2,1)}, bf16[3,152,512]{2,1,0:T(8,128)(2,1)S(1)}, u32[]{:S(2)}) copy-start(bf16[3,152,512]{2,1,0:T(8,128)(2,1)S(1)} %pad_maximum_fusion.mine_ref) | copy-start | bytes 1400836
  23.2 12.9 %copy-start.5 = (bf16[32,1024]{1,0:T(8,128)(2,1)}, bf16[32,1024]{1,0:T(8,128)(2,1)S(1)}, u32[]{:S(2)}) copy-start(bf16[32,1024]{1,0:T(8,128)(2,1)S(1)} %collective-permute-done.3.refs_0_) | copy-start | bytes 196612
  23.3 16.0 %collective-permute-start.2 = (bf16[3,152,512]{2,1,0:T(8,128)(2,1)S(1)}, bf16[3,152,512]{2,1,0:T(8,128)(2,1)S(1)}, u32[]{:S(2)}, u32[]{:S(2)}) collective-permute-start(bf16[3,152,512]{2,1,0:T(8,128)(2,1)S(1)} %pad_maximum_fusion.mine_ref), channel_id=1, source_target_pairs={{4,0},{0,4},{5,1},{1,5},{6,2},{2,6},{7,3},{3,7},{12,8},{8,12},{13,... | collective-permute-start | bytes 1400840 | tf_op jit(solution)/shard_map/ppermute | solution.py:28
  23.4 12.8 %copy-start.6 = (bf16[32,1024]{1,0:T(8,128)(2,1)}, bf16[32,1024]{1,0:T(8,128)(2,1)S(1)}, u32[]{:S(2)}) copy-start(bf16[32,1024]{1,0:T(8,128)(2,1)S(1)} %collective-permute-done.4.refs_1_) | copy-start | bytes 196612
  23.4 12.8 %copy-start.7 = (bf16[32,1024]{1,0:T(8,128)(2,1)}, bf16[32,1024]{1,0:T(8,128)(2,1)S(1)}, u32[]{:S(2)}) copy-start(bf16[32,1024]{1,0:T(8,128)(2,1)S(1)} %collective-permute-done.5.refs_2_) | copy-start | bytes 196612
  23.4 8.8 %collective-permute-start.6 = (bf16[96,1024]{1,0:T(8,128)(2,1)S(1)}, bf16[96,1024]{1,0:T(8,128)(2,1)S(1)}, u32[]{:S(2)}, u32[]{:S(2)}) collective-permute-start(bf16[96,1024]{1,0:T(8,128)(2,1)S(1)} %constant_dynamic-update-slice_fusion), channel_id=1, source_target_pairs={{24,0},{0,8},{8,16},{16,24},{25,1},{1,9},{9,17},{17,25},{26,2},{2,... | collective-permute-start | bytes 589832 | tf_op jit(solution)/shard_map/ppermute | solution.py:28
  25.4 10.7 %collective-permute-start.7 = (bf16[96,1024]{1,0:T(8,128)(2,1)S(1)}, bf16[96,1024]{1,0:T(8,128)(2,1)S(1)}, u32[]{:S(2)}, u32[]{:S(2)}) collective-permute-start(bf16[96,1024]{1,0:T(8,128)(2,1)S(1)} %constant_dynamic-update-slice_fusion), channel_id=1, source_target_pairs={{16,0},{24,8},{0,16},{8,24},{17,1},{25,9},{1,17},{9,25},{18,2},{26... | collective-permute-start | bytes 589832 | tf_op jit(solution)/shard_map/ppermute | solution.py:28
  28.3 20.2 %copy-start.3 = (bf16[32,1024]{1,0:T(8,128)(2,1)}, bf16[32,1024]{1,0:T(8,128)(2,1)S(1)}, u32[]{:S(2)}) copy-start(bf16[32,1024]{1,0:T(8,128)(2,1)S(1)} %collective-permute-done.11.refs_0_) | copy-start | bytes 196612
  28.3 7.8 %collective-permute-start.8 = (bf16[96,1024]{1,0:T(8,128)(2,1)S(1)}, bf16[96,1024]{1,0:T(8,128)(2,1)S(1)}, u32[]{:S(2)}, u32[]{:S(2)}) collective-permute-start(bf16[96,1024]{1,0:T(8,128)(2,1)S(1)} %constant_dynamic-update-slice_fusion), channel_id=1, source_target_pairs={{8,0},{16,8},{24,16},{0,24},{9,1},{17,9},{25,17},{1,25},{10,2},{18... | collective-permute-start | bytes 589832 | tf_op jit(solution)/shard_map/ppermute | solution.py:28
  31.3 17.2 %copy-start.4 = (bf16[32,1024]{1,0:T(8,128)(2,1)}, bf16[32,1024]{1,0:T(8,128)(2,1)S(1)}, u32[]{:S(2)}) copy-start(bf16[32,1024]{1,0:T(8,128)(2,1)S(1)} %collective-permute-done.12.refs_1_) | copy-start | bytes 196612
  31.3 17.7 %collective-permute-start.13 = (bf16[32,1024]{1,0:T(8,128)(2,1)S(1)}, bf16[32,1024]{1,0:T(8,128)(2,1)S(1)}, u32[]{:S(2)}, u32[]{:S(2)}) collective-permute-start(bf16[32,1024]{1,0:T(8,128)(2,1)S(1)} %get-tuple-element.35), channel_id=1, source_target_pairs={{1,0},{2,1},{3,2},{0,3},{5,4},{6,5},{7,6},{4,7},{9,8},{10,9},{11,1... | collective-permute-start | bytes 196616 | tf_op jit(solution)/shard_map/ppermute | solution.py:28
  32.2 4.0 %copy-start.10 = (bf16[96,1024]{1,0:T(8,128)(2,1)}, bf16[96,1024]{1,0:T(8,128)(2,1)S(1)}, u32[]{:S(2)}) copy-start(bf16[96,1024]{1,0:T(8,128)(2,1)S(1)} %collective-permute-done.6.refs_3_) | copy-start | bytes 589828
  39.2 24.8 %collective-permute-start.10 = (bf16[512,256]{1,0:T(8,128)(2,1)}, bf16[512,256]{1,0:T(8,128)(2,1)S(1)}, u32[]{:S(2)}, u32[]{:S(2)}) collective-permute-start(bf16[512,256]{1,0:T(8,128)(2,1)} %get-tuple-element.21.wo_mine_ref), channel_id=1, source_target_pairs={{4,0},{0,4},{5,1},{1,5},{6,2},{2,6},{7,3},{3,7},{12,8},{8,12},{13,... | collective-permute-start | bytes 786440 | tf_op jit(solution)/shard_map/ppermute | solution.py:28
  39.3 0.8 %copy-start.2 = (bf16[3,152,512]{2,1,0:T(8,128)(2,1)}, bf16[3,152,512]{2,1,0:T(8,128)(2,1)S(1)}, u32[]{:S(2)}) copy-start(bf16[3,152,512]{2,1,0:T(8,128)(2,1)S(1)} %collective-permute-done.2.other_ref) | copy-start | bytes 1400836
  48.5 15.6 %collective-permute-start.9 = (bf16[2,304,256]{2,1,0:T(8,128)(2,1)}, bf16[2,304,256]{2,1,0:T(8,128)(2,1)S(1)}, u32[]{:S(2)}, u32[]{:S(2)}) collective-permute-start(bf16[2,304,256]{2,1,0:T(8,128)(2,1)} %first.1.mine_ref), channel_id=1, source_target_pairs={{4,0},{0,4},{5,1},{1,5},{6,2},{2,6},{7,3},{3,7},{12,8},{8,12},{13,... | collective-permute-start | bytes 933896 | tf_op jit(solution)/shard_map/ppermute | solution.py:28
  49.0 12.0 %copy-start.8 = (bf16[32,1024]{1,0:T(8,128)(2,1)}, bf16[32,1024]{1,0:T(8,128)(2,1)S(1)}, u32[]{:S(2)}) copy-start(bf16[32,1024]{1,0:T(8,128)(2,1)S(1)} %collective-permute-done.13.refs_2_) | copy-start | bytes 196612
  49.0 8.8 %collective-permute-start.14 = (bf16[96,1024]{1,0:T(8,128)(2,1)S(1)}, bf16[96,1024]{1,0:T(8,128)(2,1)S(1)}, u32[]{:S(2)}, u32[]{:S(2)}) collective-permute-start(bf16[96,1024]{1,0:T(8,128)(2,1)S(1)} %constant_dynamic-update-slice_fusion.3), channel_id=1, source_target_pairs={{24,0},{0,8},{8,16},{16,24},{25,1},{1,9},{9,17},{17,25},{26,2},{2,... | collective-permute-start | bytes 589832 | tf_op jit(solution)/shard_map/ppermute | solution.py:28
  50.7 10.3 %collective-permute-start.15 = (bf16[96,1024]{1,0:T(8,128)(2,1)S(1)}, bf16[96,1024]{1,0:T(8,128)(2,1)S(1)}, u32[]{:S(2)}, u32[]{:S(2)}) collective-permute-start(bf16[96,1024]{1,0:T(8,128)(2,1)S(1)} %constant_dynamic-update-slice_fusion.3), channel_id=1, source_target_pairs={{16,0},{24,8},{0,16},{8,24},{17,1},{25,9},{1,17},{9,25},{18,2},{26... | collective-permute-start | bytes 589832 | tf_op jit(solution)/shard_map/ppermute | solution.py:28
  51.4 9.6 %collective-permute-start.16 = (bf16[96,1024]{1,0:T(8,128)(2,1)S(1)}, bf16[96,1024]{1,0:T(8,128)(2,1)S(1)}, u32[]{:S(2)}, u32[]{:S(2)}) collective-permute-start(bf16[96,1024]{1,0:T(8,128)(2,1)S(1)} %constant_dynamic-update-slice_fusion.3), channel_id=1, source_target_pairs={{8,0},{16,8},{24,16},{0,24},{9,1},{17,9},{25,17},{1,25},{10,2},{18... | collective-permute-start | bytes 589832 | tf_op jit(solution)/shard_map/ppermute | solution.py:28
  57.7 3.3 %copy-start.13 = (bf16[96,1024]{1,0:T(8,128)(2,1)}, bf16[96,1024]{1,0:T(8,128)(2,1)S(1)}, u32[]{:S(2)}) copy-start(bf16[96,1024]{1,0:T(8,128)(2,1)S(1)} %collective-permute-done.14.refs_3_) | copy-start | bytes 589828
  64.1 7.7 %collective-permute-start.18 = (bf16[512,256]{1,0:T(8,128)(2,1)}, bf16[512,256]{1,0:T(8,128)(2,1)S(1)}, u32[]{:S(2)}, u32[]{:S(2)}) collective-permute-start(bf16[512,256]{1,0:T(8,128)(2,1)} %get-tuple-element.30.wo_mine_ref), channel_id=1, source_target_pairs={{4,0},{0,4},{5,1},{1,5},{6,2},{2,6},{7,3},{3,7},{12,8},{8,12},{13,... | collective-permute-start | bytes 786440 | tf_op jit(solution)/shard_map/ppermute | solution.py:28
  64.1 0.8 %copy-start.17 = (bf16[2,304,256]{2,1,0:T(8,128)(2,1)}, bf16[2,304,256]{2,1,0:T(8,128)(2,1)S(1)}, u32[]{:S(2)}) copy-start(bf16[2,304,256]{2,1,0:T(8,128)(2,1)S(1)} %collective-permute-done.9.other_ref) | copy-start | bytes 933892
  71.2 1.6 %collective-permute-start.17 = (bf16[144,256]{1,0:T(8,128)(2,1)}, bf16[144,256]{1,0:T(8,128)(2,1)S(1)}, u32[]{:S(2)}, u32[]{:S(2)}) collective-permute-start(bf16[144,256]{1,0:T(8,128)(2,1)} %get-tuple-element.29), channel_id=1, source_target_pairs={{4,0},{0,4},{5,1},{1,5},{6,2},{2,6},{7,3},{3,7},{12,8},{8,12},{13,... | collective-permute-start | bytes 221192 | tf_op jit(solution)/shard_map/ppermute | solution.py:28
  71.7 1.1 %copy-start.9 = (bf16[512,256]{1,0:T(8,128)(2,1)}, bf16[512,256]{1,0:T(8,128)(2,1)S(1)}, u32[]{:S(2)}) copy-start(bf16[512,256]{1,0:T(8,128)(2,1)S(1)} %collective-permute-done.18.wo_other_ref) | copy-start | bytes 786436
  (6 other events, 4.2 us)

commit v2 on v1

--- a/solution.py
+++ b/solution.py
@@ -7,6 +7,7 @@
 from jax.experimental import pallas as pl
 from jax.experimental.pallas import tpu as pltpu
 from jax.sharding import PartitionSpec as P
+
 
 D = 512
 HEADS = 16
@@ -130,7 +131,8 @@
 MY_HEADS = HEADS // PAIR
 MINE = MY_HEADS * HEAD_DIM
 QKV = 3 * MINE
-COLS = QKV + D // PAIR
+OUT = D // PAIR
+REST = OUT + QKV + OUT
 TALL = 3 * WIN
 KEEP0 = 64
 KEEP1 = TALL - 64
@@ -140,6 +142,21 @@
 GROUP = 128 // HEAD_DIM
 F32 = jnp.float32
 BF16 = jnp.bfloat16
+
+
+def vmem(mib):
+    return pltpu.CompilerParams(vmem_limit_bytes=mib * 2**20)
+
+
+def partner(index, step, size):
+    if size & (size - 1) == 0:
+        return index ^ step
+    return (index + size - step) % size
+
+
+def heard_from(block, axis, step):
+    size = lax.axis_size(axis)
+    return lax.ppermute(block, axis, [(partner(i, step, size), i) for i in range(size)])
 
 
 def window_sources():
@@ -241,9 +258,120 @@
             pltpu.VMEM((2, MY_HEADS, (BIAS_ROWS + 127) // 128 * 128), F32),
             pltpu.VMEM((WIN, 256), jnp.int32),
         ],
+        compiler_params=vmem(8),
         cost_estimate=pl.CostEstimate(flops=10**9, bytes_accessed=2 * 10**6, transcendentals=0),
         name="bias",
     )(table, index)
+
+
+def tile_kernel(latent_ref, region_ref, tile_ref):
+    tile_ref[0:WIN, :] = latent_ref[...].reshape(WIN, D)
+    col = lax.broadcasted_iota(jnp.int32, (WW, WIN), 0)
+    token = lax.broadcasted_iota(jnp.int32, (WW, WIN), 1)
+    spread = jnp.where(token % (WW * WZ) // WZ == col, 1.0, 0.0).astype(BF16)
+    level = lax.broadcasted_iota(jnp.int32, (WZ, WIN), 0)
+    token = lax.broadcasted_iota(jnp.int32, (WZ, WIN), 1)
+    total = jnp.zeros((WZ, WIN), F32)
+    for dh in range(WH):
+        here = (token // (WW * WZ) == dh) & (token % WZ == level)
+        total += jnp.where(here, nn_dot(region_ref[dh].astype(F32).astype(BF16), spread), 0.0)
+    regions = jnp.sum(total, axis=0, keepdims=True)
+    tile_ref[WIN : WIN + REGION_ROWS, 0:WIN] = jnp.broadcast_to(regions, (REGION_ROWS, WIN)).astype(BF16)
+    tile_ref[WIN : WIN + REGION_ROWS, WIN:D] = jnp.zeros((REGION_ROWS, D - WIN), BF16)
+
+
+def tile_call(latent, regions):
+    return pl.pallas_call(
+        tile_kernel,
+        out_shape=jax.ShapeDtypeStruct((WIN + REGION_ROWS, D), BF16),
+        compiler_params=vmem(4),
+        cost_estimate=pl.CostEstimate(flops=10**6, bytes_accessed=3 * 10**5, transcendentals=0),
+        name="tile",
+    )(latent, regions)
+
+
+def fetch(copies):
+    for copy in copies:
+        copy.start()
+    for copy in copies:
+        copy.wait()
+
+
+def first_columns(qkv_ref, rows, me, dst, sems):
+    return [
+        pltpu.make_async_copy(
+            qkv_ref.at[0, rows, pl.ds(pl.multiple_of(D * k + MINE * me, MINE), MINE)],
+            dst.at[:, pl.ds(MINE * k, MINE)],
+            sems.at[k],
+        )
+        for k in range(3)
+    ]
+
+
+def rest_columns(qkv_ref, out_ref, rows, me, dst, sems):
+    mine = pl.ds(pl.multiple_of(MINE * me, MINE), MINE)
+    outs = [
+        pltpu.make_async_copy(out_ref.at[b, rows, mine], dst.at[:, pl.ds(at, OUT)], sems.at[b])
+        for b, at in ((0, 0), (1, OUT + QKV))
+    ]
+    return outs + [
+        pltpu.make_async_copy(
+            qkv_ref.at[1, rows, pl.ds(pl.multiple_of(D * k + MINE * me, MINE), MINE)],
+            dst.at[:, pl.ds(OUT + MINE * k, MINE)],
+            sems.at[2 + k],
+        )
+        for k in range(3)
+    ]
+
+
+def cut_first_kernel(qkv_ref, part_ref, sems):
+    part = part_ref.shape[0]
+    rows = pl.ds(pl.multiple_of(lax.axis_index("lat") * part, part), part)
+    fetch(first_columns(qkv_ref, rows, lax.axis_index("lon"), part_ref, sems))
+
+
+def cut_rest_kernel(qkv_ref, out_ref, part_ref, own0_ref, own1_ref, sems):
+    part, depth = part_ref.shape[0], own0_ref.shape[0]
+    me = lax.axis_index("lon")
+    rows = pl.ds(pl.multiple_of(lax.axis_index("lat") * part, part), part)
+    every = pl.ds(0, depth)
+    fetch(
+        rest_columns(qkv_ref, out_ref, rows, me, part_ref, sems.at[0])
+        + rest_columns(qkv_ref, out_ref, every, me, own1_ref, sems.at[1])
+        + first_columns(qkv_ref, every, me, own0_ref, sems.at[2])
+    )
+
+
+ANYWHERE = pl.BlockSpec(memory_space=pl.ANY)
+
+
+def cut_first_call(qkv, part):
+    return pl.pallas_call(
+        cut_first_kernel,
+        out_shape=jax.ShapeDtypeStruct((part, QKV), BF16),
+        in_specs=[ANYWHERE],
+        scratch_shapes=[pltpu.SemaphoreType.DMA((3,))],
+        compiler_params=vmem(4),
+        cost_estimate=pl.CostEstimate(flops=0, bytes_accessed=10**5, transcendentals=0),
+        name="cut_first",
+    )(qkv)
+
+
+def cut_rest_call(qkv, out, part):
+    depth = qkv.shape[1]
+    return pl.pallas_call(
+        cut_rest_kernel,
+        out_shape=(
+            jax.ShapeDtypeStruct((part, REST), BF16),
+            jax.ShapeDtypeStruct((depth, QKV), BF16),
+            jax.ShapeDtypeStruct((depth, REST), BF16),
+        ),
+        in_specs=[ANYWHERE, ANYWHERE],
+        scratch_shapes=[pltpu.SemaphoreType.DMA((3, 5))],
+        compiler_params=vmem(4),
+        cost_estimate=pl.CostEstimate(flops=0, bytes_accessed=10**6, transcendentals=0),
+        name="cut_rest",
+    )(qkv, out)
 
 
 def enter_kernel(mine_ref, other_ref, gain_ref, x_ref, n_ref, row_ref, col_ref):
@@ -284,42 +412,46 @@
             jax.ShapeDtypeStruct((8, WIN), F32),
             jax.ShapeDtypeStruct((WIN, 8), F32),
         ),
+        compiler_params=vmem(16),
         cost_estimate=pl.CostEstimate(flops=10**8, bytes_accessed=2 * 10**6, transcendentals=0),
         name="enter",
     )(mine, other, gain)
 
 
-def join_kernel(n_fsdp, n_lat, own_ref, *refs):
-    far, near = refs[: n_fsdp - 1], refs[n_fsdp - 1 : n_fsdp + n_lat - 2]
-    qkv_ref, out_ref = refs[-2:]
-    z = lax.axis_index("fsdp")
-    lat = lax.axis_index("lat")
-    depth = own_ref.shape[0]
+def place(put, own, far, near):
+    n_fsdp, n_lat = len(far) + 1, len(near) + 1
+    z, lat = lax.axis_index("fsdp"), lax.axis_index("lat")
+    depth = own.shape[0]
     part = depth // n_lat
+    put(pl.multiple_of(z * depth, depth), depth, own[...])
+    for k in range(1, n_fsdp):
+        base = partner(z, k, n_fsdp) * depth
+        put(pl.multiple_of(base + lat * part, part), part, far[k - 1][...])
+        for j in range(1, n_lat):
+            row = pl.multiple_of(base + partner(lat, j, n_lat) * part, part)
+            put(row, part, near[j - 1][part * (k - 1) : part * k, :])
+
+
+def join_kernel(n_far, n_near, own, *refs):
+    far, near = refs[:n_far], refs[n_far : n_far + n_near]
+    wo0_ref, qkv_ref, wo1_ref = refs[n_far + n_near :]
 
     def put(first, size, piece):
-        rows = pl.ds(pl.multiple_of(first, part), size)
-        qkv_ref[rows, :] = piece[:, 0:QKV]
-        out_ref[rows, :] = piece[:, QKV:COLS]
-
-    put(z * depth, depth, own_ref[...])
-    for k in range(1, n_fsdp):
-        base = ((z + n_fsdp - k) % n_fsdp) * depth
-        put(base + lat * part, part, far[k - 1][...])
-        for j in range(1, n_lat):
-            giver = (lat + n_lat - j) % n_lat
-            put(base + giver * part, part, near[j - 1][part * (k - 1) : part * k, :])
+        rows = pl.ds(first, size)
+        wo0_ref[rows, :] = piece[:, 0:OUT]
+        qkv_ref[rows, :] = piece[:, OUT : OUT + QKV]
+        wo1_ref[rows, :] = piece[:, OUT + QKV : REST]
+
+    place(put, own, far, near)
 
 
 def join_call(own, far, near):
-    n_fsdp, n_lat = len(far) + 1, len(near) + 1
-    rows = own.shape[0] * n_fsdp
-    return pl.pallas_call(
-        functools.partial(join_kernel, n_fsdp, n_lat),
-        out_shape=(
-            jax.ShapeDtypeStruct((rows, QKV), BF16),
-            jax.ShapeDtypeStruct((rows, D // PAIR), BF16),
-        ),
+    rows = own.shape[0] * (len(far) + 1)
+    half = jax.ShapeDtypeStruct((rows, OUT), BF16)
+    return pl.pallas_call(
+        functools.partial(join_kernel, len(far), len(near)),
+        out_shape=(half, jax.ShapeDtypeStruct((rows, QKV), BF16), half),
+        compiler_params=vmem(8),
         cost_estimate=pl.CostEstimate(flops=10**6, bytes_accessed=2 * 10**6, transcendentals=0),
         name="join",
     )(own, *far, *near)
@@ -360,8 +492,15 @@
     v_s[...] = both[:, 2 * MINE : 3 * MINE]
 
 
-def first_kernel(n_ref, w_ref, bias_ref, o_ref, q_s, k_s, v_s):
-    project(n_ref[...].reshape(PAIR * TALL, D), w_ref, q_s, k_s, v_s)
+def first_kernel(n_far, n_near, n_ref, bias_ref, own, *refs):
+    far, near = refs[:n_far], refs[n_far : n_far + n_near]
+    o_ref, w_s, q_s, k_s, v_s = refs[n_far + n_near :]
+
+    def join(first, size, piece):
+        w_s[pl.ds(first, size), :] = piece
+
+    place(join, own, far, near)
+    project(n_ref[...].reshape(PAIR * TALL, D), w_s, q_s, k_s, v_s)
     for l in range(PAIR):
         for part, (q0, q1, o0) in enumerate(
             ((KEEP0, WIN, 0), (0, WIN, PART), (0, PART, PART + WIN))
@@ -381,15 +520,16 @@
             )
 
 
-def first_call(normed, weight, bias):
+def first_call(normed, bias, own, far, near):
     scratch = pltpu.VMEM((PAIR * TALL, MINE), BF16)
     return pl.pallas_call(
-        first_kernel,
+        functools.partial(first_kernel, len(far), len(near)),
         out_shape=jax.ShapeDtypeStruct((PAIR, KEPT, MINE), BF16),
-        scratch_shapes=[scratch, scratch, scratch],
+        scratch_shapes=[pltpu.VMEM((D, QKV), BF16), scratch, scratch, scratch],
+        compiler_params=vmem(24),
         cost_estimate=pl.CostEstimate(flops=2 * 10**9, bytes_accessed=4 * 10**6, transcendentals=10**6),
         name="first",
-    )(normed, weight, bias)
+    )(normed, bias, own, *far, *near)
 
 
 def pair_columns(me, ref, mine, other):
@@ -459,6 +599,7 @@
             pltpu.VMEM((4 * PART, MINE), BF16),
             pltpu.VMEM((PAIR, WIN, MINE), BF16),
         ],
+        compiler_params=vmem(24),
         cost_estimate=pl.CostEstimate(flops=2 * 10**9, bytes_accessed=4 * 10**6, transcendentals=10**6),
         name="second",
     )(
@@ -472,52 +613,49 @@
     pair_columns(me, o_s, keep_ref[...], got_ref[...])
     pair_columns(me, wo_s, wo_mine_ref[...], wo_other_ref[...])
     value = mid_ref[...].astype(F32) + nn_dot(o_s[...], wo_s[...])
-    out_ref[...] = value.astype(BF16)
+    out_ref[...] = value.reshape(WIN // WZ, WZ, D).astype(BF16)
 
 
 def last_call(mid, keep, got, wo_mine, wo_other):
     return pl.pallas_call(
         last_kernel,
-        out_shape=jax.ShapeDtypeStruct((WIN, D), BF16),
+        out_shape=jax.ShapeDtypeStruct((WIN // WZ, WZ, D), BF16),
         scratch_shapes=[pltpu.VMEM((WIN, D), BF16), pltpu.VMEM((D, D), BF16)],
+        compiler_params=vmem(8),
         cost_estimate=pl.CostEstimate(flops=10**8, bytes_accessed=10**6, transcendentals=0),
         name="last",
     )(mid, keep, got, wo_mine, wo_other)
 
 
 def paired(latent, norm_gain, qkv_weight, out_weight, rel_bias, bias_index, region_ids):
-    me = lax.axis_index("lon")
-    lat = lax.axis_index("lat")
-    n_fsdp, n_lat = lax.axis_size("fsdp"), lax.axis_size("lat")
-    depth = qkv_weight.shape[1]
-    part = depth // n_lat
-
-    def mine_of(w, groups):
-        w = w.reshape(2, depth, groups, PAIR, w.shape[2] // groups // PAIR)
-        return lax.dynamic_index_in_dim(w, me, 3, keepdims=False).reshape(2, depth, -1)
-
-    own = jnp.concatenate([mine_of(qkv_weight, 3), mine_of(out_weight, 1)], axis=2)
-    slices = lax.dynamic_slice_in_dim(own, lat * part, part, 1)
-
-    swap = functools.partial(passed_along, axis="lon", distance=1)
-    far = [[passed_along(slices[b], "fsdp", k) for k in range(1, n_fsdp)] for b in range(2)]
-
-    tokens = jnp.transpose(latent[0], (1, 2, 0, 3)).reshape(WIN, D)
-    regions = jnp.transpose(region_ids, (1, 2, 0)).reshape(1, WIN).astype(BF16)
-    tile = jnp.concatenate(
-        [tokens, jnp.pad(regions, ((0, REGION_ROWS - 1), (0, D - WIN)))], axis=0
-    )
-    tall = jnp.stack([passed_along(tile, "lat", 1), tile, passed_along(tile, "lat", -1)])
+    n_lat = lax.axis_size("lat")
+    part = qkv_weight.shape[1] // n_lat
+
+    def swap(block):
+        return passed_along(block, "lon", 1)
+
+    def spread(block, axis):
+        got = []
+        for k in range(1, lax.axis_size(axis)):
+            got.append(heard_from(block, axis, k))
+        return got
+
+    far0 = spread(cut_first_call(qkv_weight, part), "fsdp")
+    tile = tile_call(
+        jnp.transpose(latent[0], (1, 2, 0, 3)).reshape(WIN // WZ, WZ, D),
+        jnp.transpose(region_ids, (1, 0, 2)),
+    )
+    before = passed_along(tile, "lat", 1)
+    after = passed_along(tile, "lat", -1)
+    cut, own0, own1 = cut_rest_call(qkv_weight, out_weight, part)
+    far1 = spread(cut, "fsdp")
+    near0 = spread(jnp.concatenate(far0, axis=0), "lat")
+    near1 = spread(jnp.concatenate(far1, axis=0), "lat")
+    tall = jnp.stack([before, tile, after])
     x, normed, tag_row, tag_col = enter_call(tall, swap(tall), norm_gain)
     bias = bias_call(jnp.transpose(rel_bias, (0, 2, 1)), bias_index)
-
-    weights = []
-    for b in range(2):
-        given = jnp.concatenate(far[b], axis=0)
-        near = [passed_along(given, "lat", j) for j in range(1, n_lat)]
-        weights.append(join_call(own[b], far[b], near))
-    (w0, wo0), (w1, wo1) = weights
-    o0 = first_call(normed, w0, bias[0])
+    o0 = first_call(normed, bias[0], own0, far0, near0)
+    wo0, w1, wo1 = join_call(own1, far1, near1)
     mid, keep, send = second_call(
         o0, swap(o0), wo0, swap(wo0), x, norm_gain, w1, bias[1], tag_row, tag_col
     )
@@ -526,11 +664,12 @@
 
 
 def solution(mesh):
+    pair = mesh.shape["lon"] == PAIR
+
     def local(latent, norm_gain, qkv_weight, out_weight, *rest):
         one_window = latent.shape[:4] == (1, WZ, WH, WW)
         even = qkv_weight.shape[1] % (16 * mesh.shape["lat"]) == 0
-        pays = mesh.shape["lon"] == PAIR and one_window and even
-        program = paired if pays else any_mesh
+        program = paired if pair and one_window and even else any_mesh
         return program(latent, norm_gain, qkv_weight, out_weight, *rest)
 
     return jax.shard_map(

time: 78.5 us -> 51 us (0.65); the launches traced: 77.3 us -> 50.8 us
  Pallas kernels: 29.2 us -> 14.4 us
  waiting for transfers between devices: 15.5 us -> 9.68 us
  local copies, waits for them, and re-layouts: 8.54 us -> 2.84 us
  starting transfers between devices: 22 us -> 23.7 us
  other arithmetic: 1.73 us -> 0.05 us
    ppermute x0 -> x12, starting transfers between devices: none -> 18.8 us  [heard_from(): lax.ppermute(block, axis, [(partner(i, step, size), i) for i in range(siz...]
    ppermute x19 -> x7, starting transfers between devices: 22 us -> 4.89 us  [passed_along(): return lax.ppermute(block, axis, route)]
    ppermute x19 -> x7, waiting for transfers between devices: 15.5 us -> 2.16 us  [passed_along(): return lax.ppermute(block, axis, route)]
    pallas_call x4 -> x6, Pallas kernels: 12.4 us -> 4.84 us  [the longest x1 3.2 us: first_call(): pl.pallas_call(functools.partial(first_kernel, len(far), len(near)), out_...]
    ppermute x0 -> x12, waiting for transfers between devices: none -> 7.52 us  [heard_from(): lax.ppermute(block, axis, [(partner(i, step, size), i) for i in range(siz...]
    reshape x4 -> x0, local copies, waits for them, and re-layouts: 3.8 us -> none  [the longest x1 1.63 us: paired(): return jnp.transpose(out.reshape(WH, WW, WZ, D), (2, 0, 1, 3))[None]]
    pallas_call x1, Pallas kernels: 6.34 us -> 3.5 us  [second_call(): pl.pallas_call(second_kernel, out_shape=(jax.ShapeDtypeStruct((WIN, D), B...]
    pallas_call x1, Pallas kernels: 7.67 us -> 5.37 us  [bias_call(): pl.pallas_call(bias_kernel, out_shape=(out, out), scratch_shapes=[pltpu.V...]
  transfers between devices with their start and end apart: 19 -> 19, of which waited for: 6 -> 7; matrix products, arithmetic and copies ran while one was open for 4% -> 0% of each run, Pallas kernels for 35% -> 26%
where the time goes in v2:
time: 51 us; the launch traced here: 50.8 us
  starting transfers between devices  23.7 us (46%)
  Pallas kernels  14.4 us (28%)
  waiting for transfers between devices  9.68 us (19%)
  local copies, waits for them, and re-layouts  2.84 us (6%)
    ppermute x12, starting transfers between devices, heard_from(): lax.ppermute(block, axis, [(partner(i, step, size), i) for i in range(siz...  18.8 us
    ppermute x12, waiting for transfers between devices, heard_from(): lax.ppermute(block, axis, [(partner(i, step, size), i) for i in range(siz...  7.52 us
    pallas_call x1, Pallas kernels, bias_call(): pl.pallas_call(bias_kernel, out_shape=(out, out), scratch_shapes=[pltpu.V...  5.37 us
    ppermute x7, starting transfers between devices, passed_along(): return lax.ppermute(block, axis, route)  4.89 us
    pallas_call x1, Pallas kernels, second_call(): pl.pallas_call(second_kernel, out_shape=(jax.ShapeDtypeStruct((WIN, D), B...  3.5 us
    pallas_call x1, Pallas kernels, first_call(): pl.pallas_call(functools.partial(first_kernel, len(far), len(near)), out_...  3.2 us
    unnamed x22, local copies, waits for them, and re-layouts  2.83 us
    ppermute x7, waiting for transfers between devices, passed_along(): return lax.ppermute(block, axis, route)  2.16 us
  transfers between devices with their start and end apart: 19, of which 7 were waited for; matrix products, arithmetic and copies ran while one was open for 0% of the time, Pallas kernels for 26%

profile of v2, /device:TPU:0, one launch (start us, length us, event | category | flops | bytes accessed | tf_op | source)
XLA Modules:
  0.0 50.8 jit_solution(536837588998154648)
XLA Ops:
  0.0 1.0 %copy-done.2 = bf16[1,2,6,12,512]{4,1,3,2,0:T(2,128)(2,1)S(1)} copy-done((bf16[1,2,6,12,512]{4,1,3,2,0:T(2,128)(2,1)S(1)}, bf16[1,2,6,12,512]{4,1,3,2,0:T(2,128)(2,1)}, u32[]{:S(2)}) %copy-start.2) | copy-done | bytes 147480
  1.0 0.7 %copy-done.3 = s32[2,6,12]{2,0,1:T(2,128)S(1)} copy-done((s32[2,6,12]{2,0,1:T(2,128)S(1)}, s32[2,6,12]{2,0,1:T(2,128)}, u32[]{:S(2)}) %copy-start.3) | copy-done | bytes 600
  1.6 0.2 tile.1
  1.8 4.0 %collective-permute-start.1 = (bf16[152,512]{1,0:T(8,128)(2,1)S(1)}, bf16[152,512]{1,0:T(8,128)(2,1)S(1)}, u32[]{:S(2)}, u32[]{:S(2)}) collective-permute-start(bf16[152,512]{1,0:T(8,128)(2,1)S(1)} %tile.1), channel_id=1, source_target_pairs={{8,0},{16,8},{24,16},{0,24},{9,1},{17,9},{25,17},{1,25},{10,2},{18... | collective-permute-start | bytes 466952 | tf_op jit(solution)/shard_map/ppermute | solution.py:29
  5.8 1.1 %copy-done = bf16[2,128,1536]{2,1,0:T(8,128)(2,1)S(1)} copy-done((bf16[2,128,1536]{2,1,0:T(8,128)(2,1)S(1)}, bf16[2,128,1536]{2,1,0:T(8,128)(2,1)}, u32[]{:S(2)}) %copy-start) | copy-done | bytes 786456
  7.0 1.6 %collective-permute-start.3 = (bf16[32,768]{1,0:T(8,128)(2,1)S(1)}, bf16[32,768]{1,0:T(8,128)(2,1)S(1)}, u32[]{:S(2)}, u32[]{:S(2)}) collective-permute-start(bf16[32,768]{1,0:T(8,128)(2,1)S(1)} %cut_first.1), channel_id=1, source_target_pairs={{1,0},{0,1},{3,2},{2,3},{5,4},{4,5},{7,6},{6,7},{9,8},{8,9},{11,10... | collective-permute-start | bytes 147464 | tf_op jit(solution)/shard_map/ppermute | solution.py:159
  8.6 2.6 %collective-permute-start.4 = (bf16[32,768]{1,0:T(8,128)(2,1)S(1)}, bf16[32,768]{1,0:T(8,128)(2,1)S(1)}, u32[]{:S(2)}, u32[]{:S(2)}) collective-permute-start(bf16[32,768]{1,0:T(8,128)(2,1)S(1)} %cut_first.1), channel_id=1, source_target_pairs={{2,0},{3,1},{0,2},{1,3},{6,4},{7,5},{4,6},{5,7},{10,8},{11,9},{8,1... | collective-permute-start | bytes 147464 | tf_op jit(solution)/shard_map/ppermute | solution.py:159
  11.2 0.2 collective-permute-start.5
  11.4 0.2 cut_rest.1
  11.7 5.4 %bias.1 = (f32[8,144,144]{2,1,0:T(8,128)S(1)}, f32[8,144,144]{2,1,0:T(8,128)S(1)}) custom-call(f32[2,16,759]{2,1,0:T(8,128)S(1)} %bitcast.18, s32[144,144]{1,0:T(8,128)S(1)} %copy-done.5), custom_call_target="tpu_custom_call" | custom-call | flops 1000000000 | bytes 2000000 | tf_op jit(solution)/shard_map/bias/pallas_call | solution.py:254
  17.1 0.7 %collective-permute-start.10 = (bf16[32,1280]{1,0:T(8,128)(2,1)S(1)}, bf16[32,1280]{1,0:T(8,128)(2,1)S(1)}, u32[]{:S(2)}, u32[]{:S(2)}) collective-permute-start(bf16[32,1280]{1,0:T(8,128)(2,1)S(1)} %get-tuple-element.24), channel_id=1, source_target_pairs={{1,0},{0,1},{3,2},{2,3},{5,4},{4,5},{7,6},{6,7},{9,8},{8,9},{11,10... | collective-permute-start | bytes 245768 | tf_op jit(solution)/shard_map/ppermute | solution.py:159
  17.8 3.5 %collective-permute-start.11 = (bf16[32,1280]{1,0:T(8,128)(2,1)S(1)}, bf16[32,1280]{1,0:T(8,128)(2,1)S(1)}, u32[]{:S(2)}, u32[]{:S(2)}) collective-permute-start(bf16[32,1280]{1,0:T(8,128)(2,1)S(1)} %get-tuple-element.24), channel_id=1, source_target_pairs={{2,0},{3,1},{0,2},{1,3},{6,4},{7,5},{4,6},{5,7},{10,8},{11,9},{8,1... | collective-permute-start | bytes 245768 | tf_op jit(solution)/shard_map/ppermute | solution.py:159
  21.4 0.3 collective-permute-start.12
  21.7 2.0 %collective-permute-start.6 = (bf16[96,768]{1,0:T(8,128)(2,1)S(1)}, bf16[96,768]{1,0:T(8,128)(2,1)S(1)}, u32[]{:S(2)}, u32[]{:S(2)}) collective-permute-start(bf16[96,768]{1,0:T(8,128)(2,1)S(1)} %constant_dynamic-update-slice_fusion), channel_id=1, source_target_pairs={{8,0},{0,8},{24,16},{16,24},{9,1},{1,9},{25,17},{17,25},{10,2},{2,... | collective-permute-start | bytes 442376 | tf_op jit(solution)/shard_map/ppermute | solution.py:159
  23.7 1.5 %collective-permute-start.7 = (bf16[96,768]{1,0:T(8,128)(2,1)S(1)}, bf16[96,768]{1,0:T(8,128)(2,1)S(1)}, u32[]{:S(2)}, u32[]{:S(2)}) collective-permute-start(bf16[96,768]{1,0:T(8,128)(2,1)S(1)} %constant_dynamic-update-slice_fusion), channel_id=1, source_target_pairs={{16,0},{24,8},{0,16},{8,24},{17,1},{25,9},{1,17},{9,25},{18,2},{26... | collective-permute-start | bytes 442376 | tf_op jit(solution)/shard_map/ppermute | solution.py:159
  25.4 0.5 %collective-permute-done.11.refs_1_ = bf16[32,1280]{1,0:T(8,128)(2,1)S(1)} collective-permute-done((bf16[32,1280]{1,0:T(8,128)(2,1)S(1)}, bf16[32,1280]{1,0:T(8,128)(2,1)S(1)}, u32[]{:S(2)}, u32[]{:S(2)}) %collective-permute-start.11) | collective-permute-done | bytes 81952 | tf_op jit(solution)/shard_map/ppermute | solution.py:159
  25.9 2.6 %collective-permute-start.8 = (bf16[96,768]{1,0:T(8,128)(2,1)S(1)}, bf16[96,768]{1,0:T(8,128)(2,1)S(1)}, u32[]{:S(2)}, u32[]{:S(2)}) collective-permute-start(bf16[96,768]{1,0:T(8,128)(2,1)S(1)} %constant_dynamic-update-slice_fusion), channel_id=1, source_target_pairs={{24,0},{16,8},{8,16},{0,24},{25,1},{17,9},{9,17},{1,25},{26,2},{18... | collective-permute-start | bytes 442376 | tf_op jit(solution)/shard_map/ppermute | solution.py:159
  28.6 1.1 %collective-permute-start.13 = (bf16[96,1280]{1,0:T(8,128)(2,1)S(1)}, bf16[96,1280]{1,0:T(8,128)(2,1)S(1)}, u32[]{:S(2)}, u32[]{:S(2)}) collective-permute-start(bf16[96,1280]{1,0:T(8,128)(2,1)S(1)} %constant_dynamic-update-slice_fusion.3), channel_id=1, source_target_pairs={{8,0},{0,8},{24,16},{16,24},{9,1},{1,9},{25,17},{17,25},{10,2},{2,... | collective-permute-start | bytes 737288 | tf_op jit(solution)/shard_map/ppermute | solution.py:159
  29.7 1.5 %collective-permute-start.14 = (bf16[96,1280]{1,0:T(8,128)(2,1)S(1)}, bf16[96,1280]{1,0:T(8,128)(2,1)S(1)}, u32[]{:S(2)}, u32[]{:S(2)}) collective-permute-start(bf16[96,1280]{1,0:T(8,128)(2,1)S(1)} %constant_dynamic-update-slice_fusion.3), channel_id=1, source_target_pairs={{16,0},{24,8},{0,16},{8,24},{17,1},{25,9},{1,17},{9,25},{18,2},{26... | collective-permute-start | bytes 737288 | tf_op jit(solution)/shard_map/ppermute | solution.py:159
  31.2 1.0 %collective-permute-start.15 = (bf16[96,1280]{1,0:T(8,128)(2,1)S(1)}, bf16[96,1280]{1,0:T(8,128)(2,1)S(1)}, u32[]{:S(2)}, u32[]{:S(2)}) collective-permute-start(bf16[96,1280]{1,0:T(8,128)(2,1)S(1)} %constant_dynamic-update-slice_fusion.3), channel_id=1, source_target_pairs={{24,0},{16,8},{8,16},{0,24},{25,1},{17,9},{9,17},{1,25},{26,2},{18... | collective-permute-start | bytes 737288 | tf_op jit(solution)/shard_map/ppermute | solution.py:159
  32.2 0.7 %enter.1 = (bf16[2,432,512]{2,1,0:T(8,128)(2,1)S(1)}, bf16[2,432,512]{2,1,0:T(8,128)(2,1)S(1)}, f32[8,144]{1,0:T(8,128)S(1)}, f32[144,8]{1,0:T(8,128)S(1)}) custom-call(bf16[3,152,512]{2,1,0:T(8,128)(2,1)S(1)} %pad_maximum_fusion.mine_ref, bf16[3,152,512]{2,1,0:T(8,128)(2,1)S(1)} %collective-permute-done.2.other_ref, f32[2,512]{1,0:T(2,128)S(1)} %copy-done.4), custom_call_target="tpu_custom_call" | custom-call | flops 100000000 | bytes 2000000 | tf_op jit(solution)/shard_map/enter/pallas_call | solution.py:407
  32.9 0.7 %collective-permute-done.8.refs_5_ = bf16[96,768]{1,0:T(8,128)(2,1)S(1)} collective-permute-done((bf16[96,768]{1,0:T(8,128)(2,1)S(1)}, bf16[96,768]{1,0:T(8,128)(2,1)S(1)}, u32[]{:S(2)}, u32[]{:S(2)}) %collective-permute-start.8) | collective-permute-done | bytes 147488 | tf_op jit(solution)/shard_map/ppermute | solution.py:159
  33.6 3.2 %first.1.mine_ref = bf16[2,304,256]{2,1,0:T(8,128)(2,1)S(1)} custom-call(bf16[2,432,512]{2,1,0:T(8,128)(2,1)S(1)} %get-tuple-element.20.n_ref, f32[8,144,144]{2,1,0:T(8,128)S(1)} %get-tuple-element.21.bias_ref, bf16[128,768]{1,0:T(8,128)(2,1)S(1)} %get-tuple-element.22.own, bf16[32,768]{1,0:T(8,128)(2,1)S(1)} %collective-permute-done.3.refs_0_, ...), custom_call_target="tpu_custom_call" | custom-call | flops 2000000000 | bytes 4000000 | tf_op jit(solution)/shard_map/first/pallas_call | solution.py:525
  36.9 1.3 %collective-permute-done.13.refs_3_ = bf16[96,1280]{1,0:T(8,128)(2,1)S(1)} collective-permute-done((bf16[96,1280]{1,0:T(8,128)(2,1)S(1)}, bf16[96,1280]{1,0:T(8,128)(2,1)S(1)}, u32[]{:S(2)}, u32[]{:S(2)}) %collective-permute-start.13) | collective-permute-done | bytes 245792 | tf_op jit(solution)/shard_map/ppermute | solution.py:159
  38.2 3.4 %collective-permute-done.14.refs_4_ = bf16[96,1280]{1,0:T(8,128)(2,1)S(1)} collective-permute-done((bf16[96,1280]{1,0:T(8,128)(2,1)S(1)}, bf16[96,1280]{1,0:T(8,128)(2,1)S(1)}, u32[]{:S(2)}, u32[]{:S(2)}) %collective-permute-start.14) | collective-permute-done | bytes 245792 | tf_op jit(solution)/shard_map/ppermute | solution.py:159
  41.6 1.5 %collective-permute-done.15.refs_5_ = bf16[96,1280]{1,0:T(8,128)(2,1)S(1)} collective-permute-done((bf16[96,1280]{1,0:T(8,128)(2,1)S(1)}, bf16[96,1280]{1,0:T(8,128)(2,1)S(1)}, u32[]{:S(2)}, u32[]{:S(2)}) %collective-permute-start.15) | collective-permute-done | bytes 245792 | tf_op jit(solution)/shard_map/ppermute | solution.py:159
  43.3 0.5 collective-permute-start.18
  43.8 1.0 %collective-permute-done.16.wo_other_ref = bf16[512,256]{1,0:T(8,128)(2,1)S(1)} collective-permute-done((bf16[512,256]{1,0:T(8,128)(2,1)S(1)}, bf16[512,256]{1,0:T(8,128)(2,1)S(1)}, u32[]{:S(2)}, u32[]{:S(2)}) %collective-permute-start.16) | collective-permute-done | bytes 262176 | tf_op jit(solution)/shard_map/ppermute | solution.py:29
  44.9 3.5 %second.1 = (bf16[144,512]{1,0:T(8,128)(2,1)S(1)}, bf16[144,256]{1,0:T(8,128)(2,1)S(1)}, bf16[144,256]{1,0:T(8,128)(2,1)S(1)}) custom-call(bf16[2,304,256]{2,1,0:T(8,128)(2,1)S(1)} %first.1.mine_ref, bf16[2,304,256]{2,1,0:T(8,128)(2,1)S(1)} %collective-permute-done.9.other_ref, bf16[512,256]{1,0:T(8,128)(2,1)S(1)} %get-tuple-element.25.wo_mine_ref, ...), custom_call_target="tpu_custom_call" | custom-call | flops 2000000000 | bytes 4000000 | tf_op jit(solution)/shard_map/second/pallas_call | solution.py:584
  48.4 0.2 collective-permute-start.17
  48.6 1.1 %collective-permute-done.17.got_ref = bf16[144,256]{1,0:T(8,128)(2,1)S(1)} collective-permute-done((bf16[144,256]{1,0:T(8,128)(2,1)S(1)}, bf16[144,256]{1,0:T(8,128)(2,1)S(1)}, u32[]{:S(2)}, u32[]{:S(2)}) %collective-permute-start.17) | collective-permute-done | bytes 73760 | tf_op jit(solution)/shard_map/ppermute | solution.py:29
  49.7 1.1 %last.1 = bf16[72,2,512]{2,1,0:T(2,128)(2,1)} custom-call(bf16[144,512]{1,0:T(8,128)(2,1)S(1)} %get-tuple-element.31.mid_ref, bf16[144,256]{1,0:T(8,128)(2,1)S(1)} %get-tuple-element.32.keep_ref, bf16[144,256]{1,0:T(8,128)(2,1)S(1)} %collective-permute-done.17.got_ref, bf16[512,256]{1,0:T(8,128)(2,1)S(1)} %get-tuple-element.34.wo_mine_ref, ...), custom_call_target="tpu_custom_call" | custom-call | flops 100000000 | bytes 1000000 | tf_op jit(solution)/shard_map/last/pallas_call | solution.py:620
  (40 shorter events, 0.5 us)
Async XLA Ops:
  0.0 11.4 %copy-start.1 = (bf16[2,128,512]{2,1,0:T(8,128)(2,1)S(1)}, bf16[2,128,512]{2,1,0:T(8,128)(2,1)}, u32[]{:S(2)}) copy-start(bf16[2,128,512]{2,1,0:T(8,128)(2,1)} %out_ref.1) | copy-start | bytes 786436
  0.0 1.0 %copy-start.2 = (bf16[1,2,6,12,512]{4,1,3,2,0:T(2,128)(2,1)S(1)}, bf16[1,2,6,12,512]{4,1,3,2,0:T(2,128)(2,1)}, u32[]{:S(2)}) copy-start(bf16[1,2,6,12,512]{4,1,3,2,0:T(2,128)(2,1)} %param.9) | copy-start | bytes 442372
  1.0 0.7 %copy-start.3 = (s32[2,6,12]{2,0,1:T(2,128)S(1)}, s32[2,6,12]{2,0,1:T(2,128)}, u32[]{:S(2)}) copy-start(s32[2,6,12]{2,0,1:T(2,128)} %param.15) | copy-start | bytes 1732
  1.8 19.9 %collective-permute-start.1 = (bf16[152,512]{1,0:T(8,128)(2,1)S(1)}, bf16[152,512]{1,0:T(8,128)(2,1)S(1)}, u32[]{:S(2)}, u32[]{:S(2)}) collective-permute-start(bf16[152,512]{1,0:T(8,128)(2,1)S(1)} %tile.1), channel_id=1, source_target_pairs={{8,0},{16,8},{24,16},{0,24},{9,1},{17,9},{25,17},{1,25},{10,2},{18... | collective-permute-start | bytes 466952 | tf_op jit(solution)/shard_map/ppermute | solution.py:29
  5.8 17.9 %collective-permute-start = (bf16[152,512]{1,0:T(8,128)(2,1)S(1)}, bf16[152,512]{1,0:T(8,128)(2,1)S(1)}, u32[]{:S(2)}, u32[]{:S(2)}) collective-permute-start(bf16[152,512]{1,0:T(8,128)(2,1)S(1)} %tile.1), channel_id=1, source_target_pairs={{24,0},{0,8},{8,16},{16,24},{25,1},{1,9},{9,17},{17,25},{26,2},{2,... | collective-permute-start | bytes 466952 | tf_op jit(solution)/shard_map/ppermute | solution.py:29
  5.8 1.1 %copy-start = (bf16[2,128,1536]{2,1,0:T(8,128)(2,1)S(1)}, bf16[2,128,1536]{2,1,0:T(8,128)(2,1)}, u32[]{:S(2)}) copy-start(bf16[2,128,1536]{2,1,0:T(8,128)(2,1)} %qkv_ref.3) | copy-start | bytes 2359300
  6.9 4.7 %copy-start.5 = (s32[144,144]{1,0:T(8,128)S(1)}, s32[144,144]{1,0:T(8,128)}, u32[]{:S(2)}) copy-start(s32[144,144]{1,0:T(8,128)} %index_ref.1) | copy-start | bytes 248836
  6.9 4.8 %copy-start.6 = (f32[2,759,16]{1,2,0:T(8,128)S(1)}, f32[2,759,16]{1,2,0:T(8,128)}, u32[]{:S(2)}) copy-start(f32[2,759,16]{1,2,0:T(8,128)} %param.13) | copy-start | bytes 291460
  7.0 10.1 %collective-permute-start.3 = (bf16[32,768]{1,0:T(8,128)(2,1)S(1)}, bf16[32,768]{1,0:T(8,128)(2,1)S(1)}, u32[]{:S(2)}, u32[]{:S(2)}) collective-permute-start(bf16[32,768]{1,0:T(8,128)(2,1)S(1)} %cut_first.1), channel_id=1, source_target_pairs={{1,0},{0,1},{3,2},{2,3},{5,4},{4,5},{7,6},{6,7},{9,8},{8,9},{11,10... | collective-permute-start | bytes 147464 | tf_op jit(solution)/shard_map/ppermute | solution.py:159
  8.6 9.2 %collective-permute-start.4 = (bf16[32,768]{1,0:T(8,128)(2,1)S(1)}, bf16[32,768]{1,0:T(8,128)(2,1)S(1)}, u32[]{:S(2)}, u32[]{:S(2)}) collective-permute-start(bf16[32,768]{1,0:T(8,128)(2,1)S(1)} %cut_first.1), channel_id=1, source_target_pairs={{2,0},{3,1},{0,2},{1,3},{6,4},{7,5},{4,6},{5,7},{10,8},{11,9},{8,1... | collective-permute-start | bytes 147464 | tf_op jit(solution)/shard_map/ppermute | solution.py:159
  11.2 10.2 %collective-permute-start.5 = (bf16[32,768]{1,0:T(8,128)(2,1)S(1)}, bf16[32,768]{1,0:T(8,128)(2,1)S(1)}, u32[]{:S(2)}, u32[]{:S(2)}) collective-permute-start(bf16[32,768]{1,0:T(8,128)(2,1)S(1)} %cut_first.1), channel_id=1, source_target_pairs={{3,0},{2,1},{1,2},{0,3},{7,4},{6,5},{5,6},{4,7},{11,8},{10,9},{9,1... | collective-permute-start | bytes 147464 | tf_op jit(solution)/shard_map/ppermute | solution.py:159
  17.1 15.1 %copy-start.4 = (f32[2,512]{1,0:T(2,128)S(1)}, f32[2,512]{1,0:T(2,128)}, u32[]{:S(2)}) copy-start(f32[2,512]{1,0:T(2,128)} %gain_ref.3) | copy-start | bytes 12292
  17.1 8.2 %collective-permute-start.10 = (bf16[32,1280]{1,0:T(8,128)(2,1)S(1)}, bf16[32,1280]{1,0:T(8,128)(2,1)S(1)}, u32[]{:S(2)}, u32[]{:S(2)}) collective-permute-start(bf16[32,1280]{1,0:T(8,128)(2,1)S(1)} %get-tuple-element.24), channel_id=1, source_target_pairs={{1,0},{0,1},{3,2},{2,3},{5,4},{4,5},{7,6},{6,7},{9,8},{8,9},{11,10... | collective-permute-start | bytes 245768 | tf_op jit(solution)/shard_map/ppermute | solution.py:159
  17.8 8.1 %collective-permute-start.11 = (bf16[32,1280]{1,0:T(8,128)(2,1)S(1)}, bf16[32,1280]{1,0:T(8,128)(2,1)S(1)}, u32[]{:S(2)}, u32[]{:S(2)}) collective-permute-start(bf16[32,1280]{1,0:T(8,128)(2,1)S(1)} %get-tuple-element.24), channel_id=1, source_target_pairs={{2,0},{3,1},{0,2},{1,3},{6,4},{7,5},{4,6},{5,7},{10,8},{11,9},{8,1... | collective-permute-start | bytes 245768 | tf_op jit(solution)/shard_map/ppermute | solution.py:159
  21.4 7.2 %collective-permute-start.12 = (bf16[32,1280]{1,0:T(8,128)(2,1)S(1)}, bf16[32,1280]{1,0:T(8,128)(2,1)S(1)}, u32[]{:S(2)}, u32[]{:S(2)}) collective-permute-start(bf16[32,1280]{1,0:T(8,128)(2,1)S(1)} %get-tuple-element.24), channel_id=1, source_target_pairs={{3,0},{2,1},{1,2},{0,3},{7,4},{6,5},{5,6},{4,7},{11,8},{10,9},{9,1... | collective-permute-start | bytes 245768 | tf_op jit(solution)/shard_map/ppermute | solution.py:159
  21.7 8.0 %collective-permute-start.6 = (bf16[96,768]{1,0:T(8,128)(2,1)S(1)}, bf16[96,768]{1,0:T(8,128)(2,1)S(1)}, u32[]{:S(2)}, u32[]{:S(2)}) collective-permute-start(bf16[96,768]{1,0:T(8,128)(2,1)S(1)} %constant_dynamic-update-slice_fusion), channel_id=1, source_target_pairs={{8,0},{0,8},{24,16},{16,24},{9,1},{1,9},{25,17},{17,25},{10,2},{2,... | collective-permute-start | bytes 442376 | tf_op jit(solution)/shard_map/ppermute | solution.py:159
  23.7 9.2 %collective-permute-start.7 = (bf16[96,768]{1,0:T(8,128)(2,1)S(1)}, bf16[96,768]{1,0:T(8,128)(2,1)S(1)}, u32[]{:S(2)}, u32[]{:S(2)}) collective-permute-start(bf16[96,768]{1,0:T(8,128)(2,1)S(1)} %constant_dynamic-update-slice_fusion), channel_id=1, source_target_pairs={{16,0},{24,8},{0,16},{8,24},{17,1},{25,9},{1,17},{9,25},{18,2},{26... | collective-permute-start | bytes 442376 | tf_op jit(solution)/shard_map/ppermute | solution.py:159
  25.3 5.9 %collective-permute-start.2 = (bf16[3,152,512]{2,1,0:T(8,128)(2,1)S(1)}, bf16[3,152,512]{2,1,0:T(8,128)(2,1)S(1)}, u32[]{:S(2)}, u32[]{:S(2)}) collective-permute-start(bf16[3,152,512]{2,1,0:T(8,128)(2,1)S(1)} %pad_maximum_fusion.mine_ref), channel_id=1, source_target_pairs={{4,0},{0,4},{5,1},{1,5},{6,2},{2,6},{7,3},{3,7},{12,8},{8,12},{13,... | collective-permute-start | bytes 1400840 | tf_op jit(solution)/shard_map/ppermute | solution.py:29
  25.9 7.6 %collective-permute-start.8 = (bf16[96,768]{1,0:T(8,128)(2,1)S(1)}, bf16[96,768]{1,0:T(8,128)(2,1)S(1)}, u32[]{:S(2)}, u32[]{:S(2)}) collective-permute-start(bf16[96,768]{1,0:T(8,128)(2,1)S(1)} %constant_dynamic-update-slice_fusion), channel_id=1, source_target_pairs={{24,0},{16,8},{8,16},{0,24},{25,1},{17,9},{9,17},{1,25},{26,2},{18... | collective-permute-start | bytes 442376 | tf_op jit(solution)/shard_map/ppermute | solution.py:159
  28.6 9.6 %collective-permute-start.13 = (bf16[96,1280]{1,0:T(8,128)(2,1)S(1)}, bf16[96,1280]{1,0:T(8,128)(2,1)S(1)}, u32[]{:S(2)}, u32[]{:S(2)}) collective-permute-start(bf16[96,1280]{1,0:T(8,128)(2,1)S(1)} %constant_dynamic-update-slice_fusion.3), channel_id=1, source_target_pairs={{8,0},{0,8},{24,16},{16,24},{9,1},{1,9},{25,17},{17,25},{10,2},{2,... | collective-permute-start | bytes 737288 | tf_op jit(solution)/shard_map/ppermute | solution.py:159
  29.7 12.0 %collective-permute-start.14 = (bf16[96,1280]{1,0:T(8,128)(2,1)S(1)}, bf16[96,1280]{1,0:T(8,128)(2,1)S(1)}, u32[]{:S(2)}, u32[]{:S(2)}) collective-permute-start(bf16[96,1280]{1,0:T(8,128)(2,1)S(1)} %constant_dynamic-update-slice_fusion.3), channel_id=1, source_target_pairs={{16,0},{24,8},{0,16},{8,24},{17,1},{25,9},{1,17},{9,25},{18,2},{26... | collective-permute-start | bytes 737288 | tf_op jit(solution)/shard_map/ppermute | solution.py:159
  31.2 12.0 %collective-permute-start.15 = (bf16[96,1280]{1,0:T(8,128)(2,1)S(1)}, bf16[96,1280]{1,0:T(8,128)(2,1)S(1)}, u32[]{:S(2)}, u32[]{:S(2)}) collective-permute-start(bf16[96,1280]{1,0:T(8,128)(2,1)S(1)} %constant_dynamic-update-slice_fusion.3), channel_id=1, source_target_pairs={{24,0},{16,8},{8,16},{0,24},{25,1},{17,9},{9,17},{1,25},{26,2},{18... | collective-permute-start | bytes 737288 | tf_op jit(solution)/shard_map/ppermute | solution.py:159
  36.8 8.1 %copy-start.7 = (s32[576,1]{1,0:T(8,128)S(1)}, s32[576,1]{1,0:T(8,128)}, u32[]{:S(2)}) copy-start(s32[576,1]{1,0:T(8,128)} %constant.4.clone.src_ref) | copy-start | bytes 6916
  36.8 8.1 %copy-start.8 = (s32[288,1]{1,0:T(8,128)S(1)}, s32[288,1]{1,0:T(8,128)}, u32[]{:S(2)}) copy-start(s32[288,1]{1,0:T(8,128)} %constant.5.clone.back_ref) | copy-start | bytes 3460
  36.8 8.1 %collective-permute-start.9 = (bf16[2,304,256]{2,1,0:T(8,128)(2,1)S(1)}, bf16[2,304,256]{2,1,0:T(8,128)(2,1)S(1)}, u32[]{:S(2)}, u32[]{:S(2)}) collective-permute-start(bf16[2,304,256]{2,1,0:T(8,128)(2,1)S(1)} %first.1.mine_ref), channel_id=1, source_target_pairs={{4,0},{0,4},{5,1},{1,5},{6,2},{2,6},{7,3},{3,7},{12,8},{8,12},{13,... | collective-permute-start | bytes 933896 | tf_op jit(solution)/shard_map/ppermute | solution.py:29
  43.3 1.6 %collective-permute-start.16 = (bf16[512,256]{1,0:T(8,128)(2,1)S(1)}, bf16[512,256]{1,0:T(8,128)(2,1)S(1)}, u32[]{:S(2)}, u32[]{:S(2)}) collective-permute-start(bf16[512,256]{1,0:T(8,128)(2,1)S(1)} %get-tuple-element.25.wo_mine_ref), channel_id=1, source_target_pairs={{4,0},{0,4},{5,1},{1,5},{6,2},{2,6},{7,3},{3,7},{12,8},{8,12},{13,... | collective-permute-start | bytes 786440 | tf_op jit(solution)/shard_map/ppermute | solution.py:29
  43.3 5.2 %collective-permute-start.18 = (bf16[512,256]{1,0:T(8,128)(2,1)S(1)}, bf16[512,256]{1,0:T(8,128)(2,1)S(1)}, u32[]{:S(2)}, u32[]{:S(2)}) collective-permute-start(bf16[512,256]{1,0:T(8,128)(2,1)S(1)} %get-tuple-element.34.wo_mine_ref), channel_id=1, source_target_pairs={{4,0},{0,4},{5,1},{1,5},{6,2},{2,6},{7,3},{3,7},{12,8},{8,12},{13,... | collective-permute-start | bytes 786440 | tf_op jit(solution)/shard_map/ppermute | solution.py:29
  48.4 1.3 %collective-permute-start.17 = (bf16[144,256]{1,0:T(8,128)(2,1)S(1)}, bf16[144,256]{1,0:T(8,128)(2,1)S(1)}, u32[]{:S(2)}, u32[]{:S(2)}) collective-permute-start(bf16[144,256]{1,0:T(8,128)(2,1)S(1)} %get-tuple-element.33), channel_id=1, source_target_pairs={{4,0},{0,4},{5,1},{1,5},{6,2},{2,6},{7,3},{3,7},{12,8},{8,12},{13,... | collective-permute-start | bytes 221192 | tf_op jit(solution)/shard_map/ppermute | solution.py:29

commit v3 on v1

--- a/solution.py
+++ b/solution.py
@@ -7,6 +7,7 @@
 from jax.experimental import pallas as pl
 from jax.experimental.pallas import tpu as pltpu
 from jax.sharding import PartitionSpec as P
+
 
 D = 512
 HEADS = 16
@@ -130,7 +131,8 @@
 MY_HEADS = HEADS // PAIR
 MINE = MY_HEADS * HEAD_DIM
 QKV = 3 * MINE
-COLS = QKV + D // PAIR
+OUT = D // PAIR
+COLS = QKV + OUT
 TALL = 3 * WIN
 KEEP0 = 64
 KEEP1 = TALL - 64
@@ -140,6 +142,21 @@
 GROUP = 128 // HEAD_DIM
 F32 = jnp.float32
 BF16 = jnp.bfloat16
+
+
+def vmem(mib):
+    return pltpu.CompilerParams(vmem_limit_bytes=mib * 2**20)
+
+
+def partner(index, step, size):
+    if size & (size - 1) == 0:
+        return index ^ step
+    return (index + size - step) % size
+
+
+def heard_from(block, axis, step):
+    size = lax.axis_size(axis)
+    return lax.ppermute(block, axis, [(partner(i, step, size), i) for i in range(size)])
 
 
 def window_sources():
@@ -192,11 +209,10 @@
     return (shifted * lax.rsqrt(variance + 1e-05) * gain_row).astype(BF16)
 
 
-def bias_kernel(table_ref, index_ref, first_ref, second_ref, table, index):
+def bias_kernel(b, table_ref, index_ref, bias_ref, table, index):
     me = lax.axis_index("lon")
-    for b in range(2):
-        heads = table_ref[b, pl.ds(pl.multiple_of(MY_HEADS * me, MY_HEADS), MY_HEADS), :]
-        table[b, :, 0:BIAS_ROWS] = heads * LOG2E
+    heads = table_ref[b, pl.ds(pl.multiple_of(MY_HEADS * me, MY_HEADS), MY_HEADS), :]
+    table[:, 0:BIAS_ROWS] = heads * LOG2E
     to = lax.broadcasted_iota(jnp.int32, (WIN, WIN), 0)
     frm = lax.broadcasted_iota(jnp.int32, (WIN, WIN), 1)
     move = jnp.where((to & 1) * HALF + (to >> 1) == frm, 1.0, 0.0).astype(BF16)
@@ -207,7 +223,7 @@
 
     whole = index_ref[...]
     index[:, 0:WIN] = moved(whole >> 8) * 256 + moved(whole & 255)
-    outs = (first_ref, second_ref)
+    index[:, WIN:256] = jnp.zeros((WIN, 256 - WIN), jnp.int32)
     chunks = (BIAS_ROWS + 127) // 128
 
     def step(g, carry):
@@ -217,33 +233,129 @@
             low = at & 127
             chunk = at >> 7
             masks = [chunk == k for k in range(chunks)]
-            for b in range(2):
-                for h in range(MY_HEADS):
-                    acc = None
-                    for k in range(chunks):
-                        row = jnp.broadcast_to(
-                            table[b, h : h + 1, 128 * k : 128 * k + 128], (8, 128)
-                        )
-                        got = jnp.take_along_axis(row, low, axis=1, mode="promise_in_bounds")
-                        acc = got if acc is None else jnp.where(masks[k], got, acc)
-                    outs[b][h, rows, lo:hi] = acc[:, : hi - lo]
+            for h in range(MY_HEADS):
+                acc = None
+                for k in range(chunks):
+                    row = jnp.broadcast_to(table[h : h + 1, 128 * k : 128 * k + 128], (8, 128))
+                    got = jnp.take_along_axis(row, low, axis=1, mode="promise_in_bounds")
+                    acc = got if acc is None else jnp.where(masks[k], got, acc)
+                bias_ref[h, rows, lo:hi] = acc[:, : hi - lo]
         return carry
 
     lax.fori_loop(0, WIN // 8, step, 0)
 
 
-def bias_call(table, index):
-    out = jax.ShapeDtypeStruct((MY_HEADS, WIN, WIN), F32)
-    return pl.pallas_call(
-        bias_kernel,
-        out_shape=(out, out),
+def bias_call(b, table, index):
+    return pl.pallas_call(
+        functools.partial(bias_kernel, b),
+        out_shape=jax.ShapeDtypeStruct((MY_HEADS, WIN, WIN), F32),
         scratch_shapes=[
-            pltpu.VMEM((2, MY_HEADS, (BIAS_ROWS + 127) // 128 * 128), F32),
+            pltpu.VMEM((MY_HEADS, (BIAS_ROWS + 127) // 128 * 128), F32),
             pltpu.VMEM((WIN, 256), jnp.int32),
         ],
-        cost_estimate=pl.CostEstimate(flops=10**9, bytes_accessed=2 * 10**6, transcendentals=0),
-        name="bias",
+        compiler_params=vmem(8),
+        cost_estimate=pl.CostEstimate(flops=10**9, bytes_accessed=10**6, transcendentals=0),
     )(table, index)
+
+
+def columns(qkv_ref, out_ref, b, rows, me, dst, at, sems):
+    mine = pl.ds(pl.multiple_of(MINE * me, MINE), MINE)
+    sources = [
+        qkv_ref.at[b, rows, pl.ds(pl.multiple_of(D * k + MINE * me, MINE), MINE)] for k in range(3)
+    ]
+    sources += [out_ref.at[b, rows, mine]]
+    to = pl.ds(at, rows.size)
+    return [
+        pltpu.make_async_copy(source, dst.at[to, pl.ds(MINE * k, MINE)], sems.at[k])
+        for k, source in enumerate(sources)
+    ]
+
+
+def open_kernel(
+    wide, latent_ref, region_ref, qkv_ref, out_ref, part0_ref, part1_ref, tile_ref,
+    latent, regions, sems, own_sems,
+):
+    part = part0_ref.shape[0]
+    me, lat = lax.axis_index("lon"), lax.axis_index("lat")
+
+    def cut(b, dst, step, at, n):
+        rows = pl.ds(pl.multiple_of((lat ^ step) * part, part), part)
+        return columns(qkv_ref, out_ref, b, rows, me, dst, at, sems.at[n])
+
+    copies = cut(0, part0_ref, 0, 0, 0)
+    for i, step in enumerate(wide):
+        copies += cut(1, part1_ref, step, part * i, 1 + i)
+    inputs = [
+        pltpu.make_async_copy(latent_ref, latent, own_sems.at[0]),
+        pltpu.make_async_copy(region_ref, regions, own_sems.at[1]),
+    ]
+    for copy in copies + inputs:
+        copy.start()
+    for copy in inputs:
+        copy.wait()
+    tile_ref[0:WIN, :] = latent[...].reshape(WIN, D)
+    col = lax.broadcasted_iota(jnp.int32, (WW, WIN), 0)
+    token = lax.broadcasted_iota(jnp.int32, (WW, WIN), 1)
+    spread = jnp.where(token % (WW * WZ) // WZ == col, 1.0, 0.0).astype(BF16)
+    level = lax.broadcasted_iota(jnp.int32, (WZ, WIN), 0)
+    token = lax.broadcasted_iota(jnp.int32, (WZ, WIN), 1)
+    total = jnp.zeros((WZ, WIN), F32)
+    for dh in range(WH):
+        here = (token // (WW * WZ) == dh) & (token % WZ == level)
+        total += jnp.where(here, nn_dot(regions[dh].astype(F32).astype(BF16), spread), 0.0)
+    row = jnp.sum(total, axis=0, keepdims=True)
+    tile_ref[WIN : WIN + REGION_ROWS, 0:WIN] = jnp.broadcast_to(row, (REGION_ROWS, WIN)).astype(BF16)
+    tile_ref[WIN : WIN + REGION_ROWS, WIN:D] = jnp.zeros((REGION_ROWS, D - WIN), BF16)
+    for copy in copies:
+        copy.wait()
+
+
+STAY = pl.BlockSpec(memory_space=pltpu.HBM)
+
+
+def open_call(latent, regions, qkv, out, part, wide):
+    return pl.pallas_call(
+        functools.partial(open_kernel, wide),
+        out_shape=(
+            jax.ShapeDtypeStruct((part, COLS), BF16),
+            jax.ShapeDtypeStruct((part * len(wide), COLS), BF16),
+            jax.ShapeDtypeStruct((WIN + REGION_ROWS, D), BF16),
+        ),
+        in_specs=[STAY] * 4,
+        scratch_shapes=[
+            pltpu.VMEM(latent.shape, BF16),
+            pltpu.VMEM(regions.shape, jnp.int32),
+            pltpu.SemaphoreType.DMA((1 + len(wide), 4)),
+            pltpu.SemaphoreType.DMA((2,)),
+        ],
+        compiler_params=pltpu.CompilerParams(vmem_limit_bytes=67043328-400*1024),
+        cost_estimate=pl.CostEstimate(flops=10**6, bytes_accessed=10**6, transcendentals=0),
+        name="open",
+    )(latent, regions, qkv, out)
+
+
+def own_kernel(qkv_ref, out_ref, own0_ref, own1_ref, sems):
+    me = lax.axis_index("lon")
+    copies = []
+    for b, ref in enumerate((own0_ref, own1_ref)):
+        copies += columns(qkv_ref, out_ref, b, pl.ds(0, ref.shape[0]), me, ref, 0, sems.at[b])
+    for copy in copies:
+        copy.start()
+    for copy in copies:
+        copy.wait()
+
+
+def own_call(qkv, out):
+    own = jax.ShapeDtypeStruct((qkv.shape[1], COLS), BF16)
+    return pl.pallas_call(
+        own_kernel,
+        out_shape=(own, own),
+        in_specs=[STAY] * 2,
+        scratch_shapes=[pltpu.SemaphoreType.DMA((2, 4))],
+        compiler_params=pltpu.CompilerParams(vmem_limit_bytes=67043328-2**20*6),
+        cost_estimate=pl.CostEstimate(flops=0, bytes_accessed=10**6, transcendentals=0),
+        name="own",
+    )(qkv, out)
 
 
 def enter_kernel(mine_ref, other_ref, gain_ref, x_ref, n_ref, row_ref, col_ref):
@@ -284,44 +396,44 @@
             jax.ShapeDtypeStruct((8, WIN), F32),
             jax.ShapeDtypeStruct((WIN, 8), F32),
         ),
+        compiler_params=vmem(16),
         cost_estimate=pl.CostEstimate(flops=10**8, bytes_accessed=2 * 10**6, transcendentals=0),
         name="enter",
     )(mine, other, gain)
 
 
-def join_kernel(n_fsdp, n_lat, own_ref, *refs):
-    far, near = refs[: n_fsdp - 1], refs[n_fsdp - 1 : n_fsdp + n_lat - 2]
+def join_kernel(n_fsdp, n_lat, steps, wide, own_ref, *refs):
+    far, near = refs[: n_fsdp - 1], refs[n_fsdp - 1 : n_fsdp - 1 + len(steps)]
     qkv_ref, out_ref = refs[-2:]
-    z = lax.axis_index("fsdp")
-    lat = lax.axis_index("lat")
+    z, lat = lax.axis_index("fsdp"), lax.axis_index("lat")
     depth = own_ref.shape[0]
     part = depth // n_lat
 
     def put(first, size, piece):
-        rows = pl.ds(pl.multiple_of(first, part), size)
+        rows = pl.ds(pl.multiple_of(first, size), size)
         qkv_ref[rows, :] = piece[:, 0:QKV]
         out_ref[rows, :] = piece[:, QKV:COLS]
 
     put(z * depth, depth, own_ref[...])
     for k in range(1, n_fsdp):
-        base = ((z + n_fsdp - k) % n_fsdp) * depth
-        put(base + lat * part, part, far[k - 1][...])
-        for j in range(1, n_lat):
-            giver = (lat + n_lat - j) % n_lat
-            put(base + giver * part, part, near[j - 1][part * (k - 1) : part * k, :])
-
-
-def join_call(own, far, near):
-    n_fsdp, n_lat = len(far) + 1, len(near) + 1
-    rows = own.shape[0] * n_fsdp
-    return pl.pallas_call(
-        functools.partial(join_kernel, n_fsdp, n_lat),
+        base = partner(z, k, n_fsdp) * depth
+        for i, step in enumerate(wide):
+            put(base + (lat ^ step) * part, part, far[k - 1][part * i : part * (i + 1), :])
+        for j, step in enumerate(steps):
+            row = base + partner(lat, step, n_lat) * part
+            put(row, part, near[j][part * (k - 1) : part * k, :])
+
+
+def join_call(n_lat, steps, wide, own, far, near):
+    rows = own.shape[0] * (len(far) + 1)
+    return pl.pallas_call(
+        functools.partial(join_kernel, len(far) + 1, n_lat, steps, wide),
         out_shape=(
             jax.ShapeDtypeStruct((rows, QKV), BF16),
-            jax.ShapeDtypeStruct((rows, D // PAIR), BF16),
+            jax.ShapeDtypeStruct((rows, OUT), BF16),
         ),
+        compiler_params=vmem(8),
         cost_estimate=pl.CostEstimate(flops=10**6, bytes_accessed=2 * 10**6, transcendentals=0),
-        name="join",
     )(own, *far, *near)
 
 
@@ -387,6 +499,7 @@
         first_kernel,
         out_shape=jax.ShapeDtypeStruct((PAIR, KEPT, MINE), BF16),
         scratch_shapes=[scratch, scratch, scratch],
+        compiler_params=vmem(24),
         cost_estimate=pl.CostEstimate(flops=2 * 10**9, bytes_accessed=4 * 10**6, transcendentals=10**6),
         name="first",
     )(normed, weight, bias)
@@ -459,6 +572,7 @@
             pltpu.VMEM((4 * PART, MINE), BF16),
             pltpu.VMEM((PAIR, WIN, MINE), BF16),
         ],
+        compiler_params=vmem(24),
         cost_estimate=pl.CostEstimate(flops=2 * 10**9, bytes_accessed=4 * 10**6, transcendentals=10**6),
         name="second",
     )(
@@ -472,65 +586,77 @@
     pair_columns(me, o_s, keep_ref[...], got_ref[...])
     pair_columns(me, wo_s, wo_mine_ref[...], wo_other_ref[...])
     value = mid_ref[...].astype(F32) + nn_dot(o_s[...], wo_s[...])
-    out_ref[...] = value.astype(BF16)
+    out_ref[...] = value.reshape(WIN // WZ, WZ, D).astype(BF16)
 
 
 def last_call(mid, keep, got, wo_mine, wo_other):
     return pl.pallas_call(
         last_kernel,
-        out_shape=jax.ShapeDtypeStruct((WIN, D), BF16),
+        out_shape=jax.ShapeDtypeStruct((WIN // WZ, WZ, D), BF16),
         scratch_shapes=[pltpu.VMEM((WIN, D), BF16), pltpu.VMEM((D, D), BF16)],
+        compiler_params=vmem(8),
         cost_estimate=pl.CostEstimate(flops=10**8, bytes_accessed=10**6, transcendentals=0),
         name="last",
     )(mid, keep, got, wo_mine, wo_other)
 
 
+def sharing(n_lat):
+    every = tuple(range(1, n_lat))
+    if n_lat == 4:
+        return (((0,), every), ((0, 3), (1, 2)))
+    return (((0,), every), ((0,), every))
+
+
 def paired(latent, norm_gain, qkv_weight, out_weight, rel_bias, bias_index, region_ids):
-    me = lax.axis_index("lon")
-    lat = lax.axis_index("lat")
     n_fsdp, n_lat = lax.axis_size("fsdp"), lax.axis_size("lat")
-    depth = qkv_weight.shape[1]
-    part = depth // n_lat
-
-    def mine_of(w, groups):
-        w = w.reshape(2, depth, groups, PAIR, w.shape[2] // groups // PAIR)
-        return lax.dynamic_index_in_dim(w, me, 3, keepdims=False).reshape(2, depth, -1)
-
-    own = jnp.concatenate([mine_of(qkv_weight, 3), mine_of(out_weight, 1)], axis=2)
-    slices = lax.dynamic_slice_in_dim(own, lat * part, part, 1)
-
-    swap = functools.partial(passed_along, axis="lon", distance=1)
-    far = [[passed_along(slices[b], "fsdp", k) for k in range(1, n_fsdp)] for b in range(2)]
-
-    tokens = jnp.transpose(latent[0], (1, 2, 0, 3)).reshape(WIN, D)
-    regions = jnp.transpose(region_ids, (1, 2, 0)).reshape(1, WIN).astype(BF16)
-    tile = jnp.concatenate(
-        [tokens, jnp.pad(regions, ((0, REGION_ROWS - 1), (0, D - WIN)))], axis=0
-    )
-    tall = jnp.stack([passed_along(tile, "lat", 1), tile, passed_along(tile, "lat", -1)])
+    part = qkv_weight.shape[1] // n_lat
+    plan = sharing(n_lat)
+
+    def swap(block):
+        return passed_along(block, "lon", 1)
+
+    def spread(block, axis, steps):
+        got = []
+        for k in steps:
+            got.append(heard_from(block, axis, k))
+        return got
+
+    part0, part1, tile = open_call(
+        jnp.transpose(latent[0], (1, 2, 0, 3)).reshape(WIN // WZ, WZ, D),
+        jnp.transpose(region_ids, (1, 0, 2)),
+        qkv_weight,
+        out_weight,
+        part,
+        plan[1][0],
+    )
+    far0 = spread(part0, "fsdp", range(1, n_fsdp))
+    before = passed_along(tile, "lat", 1)
+    after = passed_along(tile, "lat", -1)
+    far1 = spread(part1, "fsdp", range(1, n_fsdp))
+    near0 = spread(jnp.concatenate(far0, axis=0), "lat", plan[0][1])
+    near1 = spread(jnp.concatenate([f[:part] for f in far1], axis=0), "lat", plan[1][1])
+    own0, own1 = own_call(qkv_weight, out_weight)
+    tall = jnp.stack([before, tile, after])
     x, normed, tag_row, tag_col = enter_call(tall, swap(tall), norm_gain)
-    bias = bias_call(jnp.transpose(rel_bias, (0, 2, 1)), bias_index)
-
-    weights = []
-    for b in range(2):
-        given = jnp.concatenate(far[b], axis=0)
-        near = [passed_along(given, "lat", j) for j in range(1, n_lat)]
-        weights.append(join_call(own[b], far[b], near))
-    (w0, wo0), (w1, wo1) = weights
-    o0 = first_call(normed, w0, bias[0])
+    table = jnp.transpose(rel_bias, (0, 2, 1))
+    w0, wo0 = join_call(n_lat, plan[0][1], plan[0][0], own0, far0, near0)
+    o0 = first_call(normed, w0, bias_call(0, table, bias_index))
+    w1, wo1 = join_call(n_lat, plan[1][1], plan[1][0], own1, far1, near1)
     mid, keep, send = second_call(
-        o0, swap(o0), wo0, swap(wo0), x, norm_gain, w1, bias[1], tag_row, tag_col
+        o0, swap(o0), wo0, swap(wo0), x, norm_gain, w1,
+        bias_call(1, table, bias_index), tag_row, tag_col,
     )
     out = last_call(mid, keep, swap(send), wo1, swap(wo1))
     return jnp.transpose(out.reshape(WH, WW, WZ, D), (2, 0, 1, 3))[None]
 
 
 def solution(mesh):
+    pair = mesh.shape["lon"] == PAIR
+
     def local(latent, norm_gain, qkv_weight, out_weight, *rest):
         one_window = latent.shape[:4] == (1, WZ, WH, WW)
         even = qkv_weight.shape[1] % (16 * mesh.shape["lat"]) == 0
-        pays = mesh.shape["lon"] == PAIR and one_window and even
-        program = paired if pays else any_mesh
+        program = paired if pair and one_window and even else any_mesh
         return program(latent, norm_gain, qkv_weight, out_weight, *rest)
 
     return jax.shard_map(

time: 78.5 us -> 54.6 us (0.70); the launches traced: 77.3 us -> 54.3 us
  Pallas kernels: 29.2 us -> 19.7 us
  local copies, waits for them, and re-layouts: 8.54 us -> 0.59 us
  waiting for transfers between devices: 15.5 us -> 9.94 us
    ppermute x0 -> x11, starting transfers between devices: none -> 17.9 us  [heard_from(): lax.ppermute(block, axis, [(partner(i, step, size), i) for i in range(siz...]
    ppermute x19 -> x7, starting transfers between devices: 22 us -> 4.83 us  [passed_along(): return lax.ppermute(block, axis, route)]
    ppermute x19 -> x7, waiting for transfers between devices: 15.5 us -> 2.04 us  [passed_along(): return lax.ppermute(block, axis, route)]
    ppermute x0 -> x11, waiting for transfers between devices: none -> 7.9 us  [heard_from(): lax.ppermute(block, axis, [(partner(i, step, size), i) for i in range(siz...]
    reshape x4 -> x0, local copies, waits for them, and re-layouts: 3.8 us -> none  [the longest x1 1.63 us: paired(): return jnp.transpose(out.reshape(WH, WW, WZ, D), (2, 0, 1, 3))[None]]
    unnamed x44 -> x26, local copies, waits for them, and re-layouts: 4.12 us -> 0.57 us
    pallas_call x1, Pallas kernels: 6.34 us -> 3.49 us  [second_call(): pl.pallas_call(second_kernel, out_shape=(jax.ShapeDtypeStruct((WIN, D), B...]
    pallas_call x1, Pallas kernels: 5.66 us -> 3.14 us  [first_call(): pl.pallas_call(first_kernel, out_shape=jax.ShapeDtypeStruct((PAIR, KEPT,...]
  transfers between devices with their start and end apart: 19 -> 18, of which waited for: 6 -> 6; matrix products, arithmetic and copies ran while one was open for 4% -> 2% of each run, Pallas kernels for 35% -> 23%
where the time goes in v3:
time: 54.6 us; the launch traced here: 54.3 us
  starting transfers between devices  22.7 us (42%)
  Pallas kernels  19.7 us (36%)
  waiting for transfers between devices  9.94 us (18%)
  other arithmetic  1.02 us (2%)
  local copies, waits for them, and re-layouts  0.59 us (1%)
    ppermute x11, starting transfers between devices, heard_from(): lax.ppermute(block, axis, [(partner(i, step, size), i) for i in range(siz...  17.9 us
    ppermute x11, waiting for transfers between devices, heard_from(): lax.ppermute(block, axis, [(partner(i, step, size), i) for i in range(siz...  7.9 us
    pallas_call x2, Pallas kernels, bias_call(): pl.pallas_call(functools.partial(bias_kernel, b), out_shape=jax.ShapeDtyp...  7.09 us
    ppermute x7, starting transfers between devices, passed_along(): return lax.ppermute(block, axis, route)  4.83 us
    pallas_call x1, Pallas kernels, second_call(): pl.pallas_call(second_kernel, out_shape=(jax.ShapeDtypeStruct((WIN, D), B...  3.49 us
    pallas_call x1, Pallas kernels, first_call(): pl.pallas_call(first_kernel, out_shape=jax.ShapeDtypeStruct((PAIR, KEPT,...  3.14 us
    pallas_call x1, Pallas kernels, open_call(): pl.pallas_call(functools.partial(open_kernel, wide), out_shape=(jax.Shape...  2.09 us
    ppermute x7, waiting for transfers between devices, passed_along(): return lax.ppermute(block, axis, route)  2.04 us
  transfers between devices with their start and end apart: 18, of which 6 were waited for; matrix products, arithmetic and copies ran while one was open for 2% of the time, Pallas kernels for 23%

profile of v3, /device:TPU:0, one launch (start us, length us, event | category | flops | bytes accessed | tf_op | source)
XLA Modules:
  0.0 54.3 jit_solution(7725739342376515419)
XLA Ops:
  0.0 2.1 %open.1 = (bf16[32,1024]{1,0:T(8,128)(2,1)}, bf16[64,1024]{1,0:T(8,128)(2,1)}, bf16[152,512]{1,0:T(8,128)(2,1)}) custom-call(bf16[72,2,512]{2,1,0:T(2,128)(2,1)} %bitcast.20, s32[6,2,12]{2,1,0:T(2,128)} %bitcast.21, bf16[2,128,1536]{2,1,0:T(8,128)(2,1)} %qkv_ref.3, bf16[2,128,512]{2,1,0:T(8,128)(2,1)} %out_ref.3), custom_call_target="tpu_custom_call" | custom-call | flops 1000000 | bytes 1000000 | tf_op jit(solution)/shard_map/open/pallas_call | solution.py:317
  2.1 3.0 %collective-permute-start = (bf16[152,512]{1,0:T(8,128)(2,1)}, bf16[152,512]{1,0:T(8,128)(2,1)S(1)}, u32[]{:S(2)}, u32[]{:S(2)}) collective-permute-start(bf16[152,512]{1,0:T(8,128)(2,1)} %get-tuple-element.21), channel_id=1, source_target_pairs={{24,0},{0,8},{8,16},{16,24},{25,1},{1,9},{9,17},{17,25},{26,2},{2,... | collective-permute-start | bytes 466952 | tf_op jit(solution)/shard_map/ppermute | solution.py:29
  5.1 1.0 %collective-permute-start.1 = (bf16[152,512]{1,0:T(8,128)(2,1)}, bf16[152,512]{1,0:T(8,128)(2,1)S(1)}, u32[]{:S(2)}, u32[]{:S(2)}) collective-permute-start(bf16[152,512]{1,0:T(8,128)(2,1)} %get-tuple-element.21), channel_id=1, source_target_pairs={{8,0},{16,8},{24,16},{0,24},{9,1},{17,9},{25,17},{1,25},{10,2},{18... | collective-permute-start | bytes 466952 | tf_op jit(solution)/shard_map/ppermute | solution.py:29
  6.2 2.0 %collective-permute-start.3 = (bf16[32,1024]{1,0:T(8,128)(2,1)}, bf16[32,1024]{1,0:T(8,128)(2,1)S(1)}, u32[]{:S(2)}, u32[]{:S(2)}) collective-permute-start(bf16[32,1024]{1,0:T(8,128)(2,1)} %get-tuple-element.24), channel_id=1, source_target_pairs={{1,0},{0,1},{3,2},{2,3},{5,4},{4,5},{7,6},{6,7},{9,8},{8,9},{11,10... | collective-permute-start | bytes 196616 | tf_op jit(solution)/shard_map/ppermute | solution.py:159
  8.1 2.6 %collective-permute-start.4 = (bf16[32,1024]{1,0:T(8,128)(2,1)}, bf16[32,1024]{1,0:T(8,128)(2,1)S(1)}, u32[]{:S(2)}, u32[]{:S(2)}) collective-permute-start(bf16[32,1024]{1,0:T(8,128)(2,1)} %get-tuple-element.24), channel_id=1, source_target_pairs={{2,0},{3,1},{0,2},{1,3},{6,4},{7,5},{4,6},{5,7},{10,8},{11,9},{8,1... | collective-permute-start | bytes 196616 | tf_op jit(solution)/shard_map/ppermute | solution.py:159
  10.7 0.4 collective-permute-done
  11.2 2.0 %collective-permute-start.11 = (bf16[64,1024]{1,0:T(8,128)(2,1)}, bf16[64,1024]{1,0:T(8,128)(2,1)S(1)}, u32[]{:S(2)}, u32[]{:S(2)}) collective-permute-start(bf16[64,1024]{1,0:T(8,128)(2,1)} %get-tuple-element.29), channel_id=1, source_target_pairs={{1,0},{0,1},{3,2},{2,3},{5,4},{4,5},{7,6},{6,7},{9,8},{8,9},{11,10... | collective-permute-start | bytes 393224 | tf_op jit(solution)/shard_map/ppermute | solution.py:159
  13.2 0.7 %collective-permute-done.1 = bf16[152,512]{1,0:T(8,128)(2,1)S(1)} collective-permute-done((bf16[152,512]{1,0:T(8,128)(2,1)}, bf16[152,512]{1,0:T(8,128)(2,1)S(1)}, u32[]{:S(2)}, u32[]{:S(2)}) %collective-permute-start.1) | collective-permute-done | bytes 155680 | tf_op jit(solution)/shard_map/ppermute | solution.py:29
  13.9 2.6 %collective-permute-start.12 = (bf16[64,1024]{1,0:T(8,128)(2,1)}, bf16[64,1024]{1,0:T(8,128)(2,1)S(1)}, u32[]{:S(2)}, u32[]{:S(2)}) collective-permute-start(bf16[64,1024]{1,0:T(8,128)(2,1)} %get-tuple-element.29), channel_id=1, source_target_pairs={{2,0},{3,1},{0,2},{1,3},{6,4},{7,5},{4,6},{5,7},{10,8},{11,9},{8,1... | collective-permute-start | bytes 393224 | tf_op jit(solution)/shard_map/ppermute | solution.py:159
  16.5 1.0 %pad_maximum_fusion.mine_ref = bf16[3,152,512]{2,1,0:T(8,128)(2,1)S(1)} fusion(bf16[1,152,512]{2,1,0:T(8,128)(2,1)S(1)} %bitcast.19, bf16[1,152,512]{2,1,0:T(8,128)(2,1)} %bitcast.17, bf16[1,152,512]{2,1,0:T(8,128)(2,1)S(1)} %bitcast.18), kind=kLoop, calls=%fused_computation | loop fusion | flops 466944 | bytes 933888 | tf_op jit(solution)/shard_map/stack | solution.py:639
  17.5 0.1 collective-permute-start.2
  17.7 1.6 %collective-permute-start.6 = (bf16[96,1024]{1,0:T(8,128)(2,1)S(1)}, bf16[96,1024]{1,0:T(8,128)(2,1)S(1)}, u32[]{:S(2)}, u32[]{:S(2)}) collective-permute-start(bf16[96,1024]{1,0:T(8,128)(2,1)S(1)} %constant_dynamic-update-slice_fusion), channel_id=1, source_target_pairs={{8,0},{0,8},{24,16},{16,24},{9,1},{1,9},{25,17},{17,25},{10,2},{2,... | collective-permute-start | bytes 589832 | tf_op jit(solution)/shard_map/ppermute | solution.py:159
  19.2 0.5 collective-permute-start.7
  19.7 1.5 %collective-permute-start.8 = (bf16[96,1024]{1,0:T(8,128)(2,1)S(1)}, bf16[96,1024]{1,0:T(8,128)(2,1)S(1)}, u32[]{:S(2)}, u32[]{:S(2)}) collective-permute-start(bf16[96,1024]{1,0:T(8,128)(2,1)S(1)} %constant_dynamic-update-slice_fusion), channel_id=1, source_target_pairs={{24,0},{16,8},{8,16},{0,24},{25,1},{17,9},{9,17},{1,25},{26,2},{18... | collective-permute-start | bytes 589832 | tf_op jit(solution)/shard_map/ppermute | solution.py:159
  21.2 1.4 %collective-permute-done.12.refs_1_ = bf16[64,1024]{1,0:T(8,128)(2,1)S(1)} collective-permute-done((bf16[64,1024]{1,0:T(8,128)(2,1)}, bf16[64,1024]{1,0:T(8,128)(2,1)S(1)}, u32[]{:S(2)}, u32[]{:S(2)}) %collective-permute-start.12) | collective-permute-done | bytes 131104 | tf_op jit(solution)/shard_map/ppermute | solution.py:159
  22.7 3.1 %collective-permute-start.13 = (bf16[64,1024]{1,0:T(8,128)(2,1)S(1)}, bf16[64,1024]{1,0:T(8,128)(2,1)S(1)}, u32[]{:S(2)}, u32[]{:S(2)}) collective-permute-start(bf16[64,1024]{1,0:T(8,128)(2,1)S(1)} %copy-done.11), channel_id=1, source_target_pairs={{3,0},{2,1},{1,2},{0,3},{7,4},{6,5},{5,6},{4,7},{11,8},{10,9},{9,1... | collective-permute-start | bytes 393224 | tf_op jit(solution)/shard_map/ppermute | solution.py:159
  25.8 1.9 %own.1 = (bf16[128,1024]{1,0:T(8,128)(2,1)}, bf16[128,1024]{1,0:T(8,128)(2,1)}) custom-call(bf16[2,128,1536]{2,1,0:T(8,128)(2,1)} %qkv_ref.3, bf16[2,128,512]{2,1,0:T(8,128)(2,1)} %out_ref.3), custom_call_target="tpu_custom_call" | custom-call | bytes 1000000 | tf_op jit(solution)/shard_map/own/pallas_call | solution.py:350
  27.7 3.5 %shard_map.92.bias_ref = f32[8,144,144]{2,1,0:T(8,128)S(1)} custom-call(f32[2,16,759]{2,1,0:T(8,128)S(1)} %bitcast.15, s32[144,144]{1,0:T(8,128)S(1)} %copy-done.7), custom_call_target="tpu_custom_call" | custom-call | flops 1000000000 | bytes 1000000 | tf_op jit(solution)/shard_map/pallas_call | solution.py:249
  31.4 0.1 shard_map.91
  31.5 0.5 copy-done.6
  32.0 0.7 %enter.1 = (bf16[2,432,512]{2,1,0:T(8,128)(2,1)S(1)}, bf16[2,432,512]{2,1,0:T(8,128)(2,1)S(1)}, f32[8,144]{1,0:T(8,128)S(1)}, f32[144,8]{1,0:T(8,128)S(1)}) custom-call(bf16[3,152,512]{2,1,0:T(8,128)(2,1)S(1)} %pad_maximum_fusion.mine_ref, bf16[3,152,512]{2,1,0:T(8,128)(2,1)S(1)} %collective-permute-done.2.other_ref, f32[2,512]{1,0:T(2,128)S(1)} %copy-done.6), custom_call_target="tpu_custom_call" | custom-call | flops 100000000 | bytes 2000000 | tf_op jit(solution)/shard_map/enter/pallas_call | solution.py:391
  32.7 3.1 %first.1.mine_ref = bf16[2,304,256]{2,1,0:T(8,128)(2,1)S(1)} custom-call(bf16[2,432,512]{2,1,0:T(8,128)(2,1)S(1)} %get-tuple-element.22.n_ref, bf16[512,768]{1,0:T(8,128)(2,1)S(1)} %get-tuple-element.25.w_ref, f32[8,144,144]{2,1,0:T(8,128)S(1)} %shard_map.92.bias_ref), custom_call_target="tpu_custom_call" | custom-call | flops 2000000000 | bytes 4000000 | tf_op jit(solution)/shard_map/first/pallas_call | solution.py:498
  36.0 1.5 %collective-permute-start.14 = (bf16[96,1024]{1,0:T(8,128)(2,1)S(1)}, bf16[96,1024]{1,0:T(8,128)(2,1)S(1)}, u32[]{:S(2)}, u32[]{:S(2)}) collective-permute-start(bf16[96,1024]{1,0:T(8,128)(2,1)S(1)} %pad_maximum_fusion.1), channel_id=1, source_target_pairs={{8,0},{0,8},{24,16},{16,24},{9,1},{1,9},{25,17},{17,25},{10,2},{2,... | collective-permute-start | bytes 589832 | tf_op jit(solution)/shard_map/ppermute | solution.py:159
  37.5 0.6 %collective-permute-start.15 = (bf16[96,1024]{1,0:T(8,128)(2,1)S(1)}, bf16[96,1024]{1,0:T(8,128)(2,1)S(1)}, u32[]{:S(2)}, u32[]{:S(2)}) collective-permute-start(bf16[96,1024]{1,0:T(8,128)(2,1)S(1)} %pad_maximum_fusion.1), channel_id=1, source_target_pairs={{16,0},{24,8},{0,16},{8,24},{17,1},{25,9},{1,17},{9,25},{18,2},{26... | collective-permute-start | bytes 589832 | tf_op jit(solution)/shard_map/ppermute | solution.py:159
  38.0 5.3 %collective-permute-done.14.refs_3_ = bf16[96,1024]{1,0:T(8,128)(2,1)S(1)} collective-permute-done((bf16[96,1024]{1,0:T(8,128)(2,1)S(1)}, bf16[96,1024]{1,0:T(8,128)(2,1)S(1)}, u32[]{:S(2)}, u32[]{:S(2)}) %collective-permute-start.14) | collective-permute-done | bytes 196640 | tf_op jit(solution)/shard_map/ppermute | solution.py:159
  43.3 1.1 %collective-permute-done.15.refs_4_ = bf16[96,1024]{1,0:T(8,128)(2,1)S(1)} collective-permute-done((bf16[96,1024]{1,0:T(8,128)(2,1)S(1)}, bf16[96,1024]{1,0:T(8,128)(2,1)S(1)}, u32[]{:S(2)}, u32[]{:S(2)}) %collective-permute-start.15) | collective-permute-done | bytes 196640 | tf_op jit(solution)/shard_map/ppermute | solution.py:159
  44.5 0.1 shard_map.93
  44.7 3.5 %shard_map.94.bias_ref = f32[8,144,144]{2,1,0:T(8,128)S(1)} custom-call(f32[2,16,759]{2,1,0:T(8,128)S(1)} %bitcast.16, s32[144,144]{1,0:T(8,128)S(1)} %copy-done.7), custom_call_target="tpu_custom_call" | custom-call | flops 1000000000 | bytes 1000000 | tf_op jit(solution)/shard_map/pallas_call | solution.py:249
  48.3 3.5 %second.1 = (bf16[144,512]{1,0:T(8,128)(2,1)S(1)}, bf16[144,256]{1,0:T(8,128)(2,1)S(1)}, bf16[144,256]{1,0:T(8,128)(2,1)S(1)}) custom-call(bf16[2,304,256]{2,1,0:T(8,128)(2,1)S(1)} %first.1.mine_ref, bf16[2,304,256]{2,1,0:T(8,128)(2,1)S(1)} %collective-permute-done.9.other_ref, bf16[512,256]{1,0:T(8,128)(2,1)S(1)} %get-tuple-element.26.wo_mine_ref, ...), custom_call_target="tpu_custom_call" | custom-call | flops 2000000000 | bytes 4000000 | tf_op jit(solution)/shard_map/second/pallas_call | solution.py:557
  51.8 0.6 %collective-permute-start.16 = (bf16[144,256]{1,0:T(8,128)(2,1)S(1)}, bf16[144,256]{1,0:T(8,128)(2,1)S(1)}, u32[]{:S(2)}, u32[]{:S(2)}) collective-permute-start(bf16[144,256]{1,0:T(8,128)(2,1)S(1)} %get-tuple-element.35), channel_id=1, source_target_pairs={{4,0},{0,4},{5,1},{1,5},{6,2},{2,6},{7,3},{3,7},{12,8},{8,12},{13,... | collective-permute-start | bytes 221192 | tf_op jit(solution)/shard_map/ppermute | solution.py:29
  52.3 0.9 %collective-permute-done.16.got_ref = bf16[144,256]{1,0:T(8,128)(2,1)S(1)} collective-permute-done((bf16[144,256]{1,0:T(8,128)(2,1)S(1)}, bf16[144,256]{1,0:T(8,128)(2,1)S(1)}, u32[]{:S(2)}, u32[]{:S(2)}) %collective-permute-start.16) | collective-permute-done | bytes 73760 | tf_op jit(solution)/shard_map/ppermute | solution.py:29
  53.2 1.1 %last.1 = bf16[72,2,512]{2,1,0:T(2,128)(2,1)} custom-call(bf16[144,512]{1,0:T(8,128)(2,1)S(1)} %get-tuple-element.33.mid_ref, bf16[144,256]{1,0:T(8,128)(2,1)S(1)} %get-tuple-element.34.keep_ref, bf16[144,256]{1,0:T(8,128)(2,1)S(1)} %collective-permute-done.16.got_ref, bf16[512,256]{1,0:T(8,128)(2,1)S(1)} %get-tuple-element.36.wo_mine_ref, ...), custom_call_target="tpu_custom_call" | custom-call | flops 100000000 | bytes 1000000 | tf_op jit(solution)/shard_map/last/pallas_call | solution.py:593
  (48 shorter events, 0.3 us)
Async XLA Ops:
  2.1 20.6 %copy-start.11 = (bf16[64,1024]{1,0:T(8,128)(2,1)S(1)}, bf16[64,1024]{1,0:T(8,128)(2,1)}, u32[]{:S(2)}) copy-start(bf16[64,1024]{1,0:T(8,128)(2,1)} %get-tuple-element.29) | copy-start | bytes 393220
  2.1 9.1 %collective-permute-start = (bf16[152,512]{1,0:T(8,128)(2,1)}, bf16[152,512]{1,0:T(8,128)(2,1)S(1)}, u32[]{:S(2)}, u32[]{:S(2)}) collective-permute-start(bf16[152,512]{1,0:T(8,128)(2,1)} %get-tuple-element.21), channel_id=1, source_target_pairs={{24,0},{0,8},{8,16},{16,24},{25,1},{1,9},{9,17},{17,25},{26,2},{2,... | collective-permute-start | bytes 466952 | tf_op jit(solution)/shard_map/ppermute | solution.py:29
  5.1 8.8 %collective-permute-start.1 = (bf16[152,512]{1,0:T(8,128)(2,1)}, bf16[152,512]{1,0:T(8,128)(2,1)S(1)}, u32[]{:S(2)}, u32[]{:S(2)}) collective-permute-start(bf16[152,512]{1,0:T(8,128)(2,1)} %get-tuple-element.21), channel_id=1, source_target_pairs={{8,0},{16,8},{24,16},{0,24},{9,1},{17,9},{25,17},{1,25},{10,2},{18... | collective-permute-start | bytes 466952 | tf_op jit(solution)/shard_map/ppermute | solution.py:29
  6.2 11.4 %collective-permute-start.3 = (bf16[32,1024]{1,0:T(8,128)(2,1)}, bf16[32,1024]{1,0:T(8,128)(2,1)S(1)}, u32[]{:S(2)}, u32[]{:S(2)}) collective-permute-start(bf16[32,1024]{1,0:T(8,128)(2,1)} %get-tuple-element.24), channel_id=1, source_target_pairs={{1,0},{0,1},{3,2},{2,3},{5,4},{4,5},{7,6},{6,7},{9,8},{8,9},{11,10... | collective-permute-start | bytes 196616 | tf_op jit(solution)/shard_map/ppermute | solution.py:159
  8.1 9.5 %collective-permute-start.4 = (bf16[32,1024]{1,0:T(8,128)(2,1)}, bf16[32,1024]{1,0:T(8,128)(2,1)S(1)}, u32[]{:S(2)}, u32[]{:S(2)}) collective-permute-start(bf16[32,1024]{1,0:T(8,128)(2,1)} %get-tuple-element.24), channel_id=1, source_target_pairs={{2,0},{3,1},{0,2},{1,3},{6,4},{7,5},{4,6},{5,7},{10,8},{11,9},{8,1... | collective-permute-start | bytes 196616 | tf_op jit(solution)/shard_map/ppermute | solution.py:159
  10.7 6.9 %collective-permute-start.5 = (bf16[32,1024]{1,0:T(8,128)(2,1)}, bf16[32,1024]{1,0:T(8,128)(2,1)S(1)}, u32[]{:S(2)}, u32[]{:S(2)}) collective-permute-start(bf16[32,1024]{1,0:T(8,128)(2,1)} %get-tuple-element.24), channel_id=1, source_target_pairs={{3,0},{2,1},{1,2},{0,3},{7,4},{6,5},{5,6},{4,7},{11,8},{10,9},{9,1... | collective-permute-start | bytes 196616 | tf_op jit(solution)/shard_map/ppermute | solution.py:159
  11.2 8.6 %collective-permute-start.11 = (bf16[64,1024]{1,0:T(8,128)(2,1)}, bf16[64,1024]{1,0:T(8,128)(2,1)S(1)}, u32[]{:S(2)}, u32[]{:S(2)}) collective-permute-start(bf16[64,1024]{1,0:T(8,128)(2,1)} %get-tuple-element.29), channel_id=1, source_target_pairs={{1,0},{0,1},{3,2},{2,3},{5,4},{4,5},{7,6},{6,7},{9,8},{8,9},{11,10... | collective-permute-start | bytes 393224 | tf_op jit(solution)/shard_map/ppermute | solution.py:159
  13.9 8.8 %collective-permute-start.12 = (bf16[64,1024]{1,0:T(8,128)(2,1)}, bf16[64,1024]{1,0:T(8,128)(2,1)S(1)}, u32[]{:S(2)}, u32[]{:S(2)}) collective-permute-start(bf16[64,1024]{1,0:T(8,128)(2,1)} %get-tuple-element.29), channel_id=1, source_target_pairs={{2,0},{3,1},{0,2},{1,3},{6,4},{7,5},{4,6},{5,7},{10,8},{11,9},{8,1... | collective-permute-start | bytes 393224 | tf_op jit(solution)/shard_map/ppermute | solution.py:159
  16.5 11.2 %copy-start.7 = (s32[144,144]{1,0:T(8,128)S(1)}, s32[144,144]{1,0:T(8,128)}, u32[]{:S(2)}) copy-start(s32[144,144]{1,0:T(8,128)} %index_ref.3) | copy-start | bytes 248836
  16.5 11.2 %copy-start.8 = (f32[2,759,16]{1,2,0:T(8,128)S(1)}, f32[2,759,16]{1,2,0:T(8,128)}, u32[]{:S(2)}) copy-start(f32[2,759,16]{1,2,0:T(8,128)} %param.13) | copy-start | bytes 291460
  17.5 13.9 %collective-permute-start.2 = (bf16[3,152,512]{2,1,0:T(8,128)(2,1)S(1)}, bf16[3,152,512]{2,1,0:T(8,128)(2,1)S(1)}, u32[]{:S(2)}, u32[]{:S(2)}) collective-permute-start(bf16[3,152,512]{2,1,0:T(8,128)(2,1)S(1)} %pad_maximum_fusion.mine_ref), channel_id=1, source_target_pairs={{4,0},{0,4},{5,1},{1,5},{6,2},{2,6},{7,3},{3,7},{12,8},{8,12},{13,... | collective-permute-start | bytes 1400840 | tf_op jit(solution)/shard_map/ppermute | solution.py:29
  17.7 13.7 %collective-permute-start.6 = (bf16[96,1024]{1,0:T(8,128)(2,1)S(1)}, bf16[96,1024]{1,0:T(8,128)(2,1)S(1)}, u32[]{:S(2)}, u32[]{:S(2)}) collective-permute-start(bf16[96,1024]{1,0:T(8,128)(2,1)S(1)} %constant_dynamic-update-slice_fusion), channel_id=1, source_target_pairs={{8,0},{0,8},{24,16},{16,24},{9,1},{1,9},{25,17},{17,25},{10,2},{2,... | collective-permute-start | bytes 589832 | tf_op jit(solution)/shard_map/ppermute | solution.py:159
  19.2 12.1 %collective-permute-start.7 = (bf16[96,1024]{1,0:T(8,128)(2,1)S(1)}, bf16[96,1024]{1,0:T(8,128)(2,1)S(1)}, u32[]{:S(2)}, u32[]{:S(2)}) collective-permute-start(bf16[96,1024]{1,0:T(8,128)(2,1)S(1)} %constant_dynamic-update-slice_fusion), channel_id=1, source_target_pairs={{16,0},{24,8},{0,16},{8,24},{17,1},{25,9},{1,17},{9,25},{18,2},{26... | collective-permute-start | bytes 589832 | tf_op jit(solution)/shard_map/ppermute | solution.py:159
  19.7 11.5 %copy-start = (bf16[64,1024]{1,0:T(8,128)(2,1)}, bf16[64,1024]{1,0:T(8,128)(2,1)S(1)}, u32[]{:S(2)}) copy-start(bf16[64,1024]{1,0:T(8,128)(2,1)S(1)} %collective-permute-done.11.refs_0_) | copy-start | bytes 393220
  19.7 11.6 %collective-permute-start.8 = (bf16[96,1024]{1,0:T(8,128)(2,1)S(1)}, bf16[96,1024]{1,0:T(8,128)(2,1)S(1)}, u32[]{:S(2)}, u32[]{:S(2)}) collective-permute-start(bf16[96,1024]{1,0:T(8,128)(2,1)S(1)} %constant_dynamic-update-slice_fusion), channel_id=1, source_target_pairs={{24,0},{16,8},{8,16},{0,24},{25,1},{17,9},{9,17},{1,25},{26,2},{18... | collective-permute-start | bytes 589832 | tf_op jit(solution)/shard_map/ppermute | solution.py:159
  22.7 8.6 %copy-start.2 = (bf16[64,1024]{1,0:T(8,128)(2,1)}, bf16[64,1024]{1,0:T(8,128)(2,1)S(1)}, u32[]{:S(2)}) copy-start(bf16[64,1024]{1,0:T(8,128)(2,1)S(1)} %collective-permute-done.12.refs_1_) | copy-start | bytes 393220
  22.7 8.6 %collective-permute-start.13 = (bf16[64,1024]{1,0:T(8,128)(2,1)S(1)}, bf16[64,1024]{1,0:T(8,128)(2,1)S(1)}, u32[]{:S(2)}, u32[]{:S(2)}) collective-permute-start(bf16[64,1024]{1,0:T(8,128)(2,1)S(1)} %copy-done.11), channel_id=1, source_target_pairs={{3,0},{2,1},{1,2},{0,3},{7,4},{6,5},{5,6},{4,7},{11,8},{10,9},{9,1... | collective-permute-start | bytes 393224 | tf_op jit(solution)/shard_map/ppermute | solution.py:159
  27.7 3.6 %copy-start.5 = (bf16[128,1024]{1,0:T(8,128)(2,1)S(1)}, bf16[128,1024]{1,0:T(8,128)(2,1)}, u32[]{:S(2)}) copy-start(bf16[128,1024]{1,0:T(8,128)(2,1)} %get-tuple-element.23.own_ref) | copy-start | bytes 786436
  31.3 0.7 %copy-start.6 = (f32[2,512]{1,0:T(2,128)S(1)}, f32[2,512]{1,0:T(2,128)}, u32[]{:S(2)}) copy-start(f32[2,512]{1,0:T(2,128)} %gain_ref.3) | copy-start | bytes 12292
  32.7 3.3 %slice-start = ((bf16[64,1024]{1,0:T(8,128)(2,1)}), bf16[32,1024]{1,0:T(8,128)(2,1)S(1)}, s32[]{:S(2)}) async-start(bf16[64,1024]{1,0:T(8,128)(2,1)} %copy-done), calls=%async_computation | async-start | bytes 131072 | tf_op jit(solution)/shard_map/slice | solution.py:637
  32.7 3.3 %slice-start.1 = ((bf16[64,1024]{1,0:T(8,128)(2,1)}), bf16[32,1024]{1,0:T(8,128)(2,1)S(1)}, s32[]{:S(2)}) async-start(bf16[64,1024]{1,0:T(8,128)(2,1)} %copy-done.2), calls=%async_computation.1 | async-start | bytes 131072 | tf_op jit(solution)/shard_map/slice | solution.py:637
  32.7 11.8 %copy-start.1 = (bf16[64,1024]{1,0:T(8,128)(2,1)S(1)}, bf16[64,1024]{1,0:T(8,128)(2,1)}, u32[]{:S(2)}) copy-start(bf16[64,1024]{1,0:T(8,128)(2,1)} %copy-done) | copy-start | bytes 393220
  32.7 11.8 %copy-start.3 = (bf16[64,1024]{1,0:T(8,128)(2,1)S(1)}, bf16[64,1024]{1,0:T(8,128)(2,1)}, u32[]{:S(2)}) copy-start(bf16[64,1024]{1,0:T(8,128)(2,1)} %copy-done.2) | copy-start | bytes 393220
  32.7 11.8 %copy-start.4 = (bf16[128,1024]{1,0:T(8,128)(2,1)S(1)}, bf16[128,1024]{1,0:T(8,128)(2,1)}, u32[]{:S(2)}) copy-start(bf16[128,1024]{1,0:T(8,128)(2,1)} %get-tuple-element.28.own_ref) | copy-start | bytes 786436
  35.9 12.4 %collective-permute-start.9 = (bf16[2,304,256]{2,1,0:T(8,128)(2,1)S(1)}, bf16[2,304,256]{2,1,0:T(8,128)(2,1)S(1)}, u32[]{:S(2)}, u32[]{:S(2)}) collective-permute-start(bf16[2,304,256]{2,1,0:T(8,128)(2,1)S(1)} %first.1.mine_ref), channel_id=1, source_target_pairs={{4,0},{0,4},{5,1},{1,5},{6,2},{2,6},{7,3},{3,7},{12,8},{8,12},{13,... | collective-permute-start | bytes 933896 | tf_op jit(solution)/shard_map/ppermute | solution.py:29
  36.0 7.3 %collective-permute-start.14 = (bf16[96,1024]{1,0:T(8,128)(2,1)S(1)}, bf16[96,1024]{1,0:T(8,128)(2,1)S(1)}, u32[]{:S(2)}, u32[]{:S(2)}) collective-permute-start(bf16[96,1024]{1,0:T(8,128)(2,1)S(1)} %pad_maximum_fusion.1), channel_id=1, source_target_pairs={{8,0},{0,8},{24,16},{16,24},{9,1},{1,9},{25,17},{17,25},{10,2},{2,... | collective-permute-start | bytes 589832 | tf_op jit(solution)/shard_map/ppermute | solution.py:159
  37.5 7.0 %collective-permute-start.15 = (bf16[96,1024]{1,0:T(8,128)(2,1)S(1)}, bf16[96,1024]{1,0:T(8,128)(2,1)S(1)}, u32[]{:S(2)}, u32[]{:S(2)}) collective-permute-start(bf16[96,1024]{1,0:T(8,128)(2,1)S(1)} %pad_maximum_fusion.1), channel_id=1, source_target_pairs={{16,0},{24,8},{0,16},{8,24},{17,1},{25,9},{1,17},{9,25},{18,2},{26... | collective-permute-start | bytes 589832 | tf_op jit(solution)/shard_map/ppermute | solution.py:159
  38.0 10.2 %collective-permute-start.10 = (bf16[512,256]{1,0:T(8,128)(2,1)S(1)}, bf16[512,256]{1,0:T(8,128)(2,1)S(1)}, u32[]{:S(2)}, u32[]{:S(2)}) collective-permute-start(bf16[512,256]{1,0:T(8,128)(2,1)S(1)} %get-tuple-element.26.wo_mine_ref), channel_id=1, source_target_pairs={{4,0},{0,4},{5,1},{1,5},{6,2},{2,6},{7,3},{3,7},{12,8},{8,12},{13,... | collective-permute-start | bytes 786440 | tf_op jit(solution)/shard_map/ppermute | solution.py:29
  44.6 3.7 %copy-start.9 = (s32[576,1]{1,0:T(8,128)S(1)}, s32[576,1]{1,0:T(8,128)}, u32[]{:S(2)}) copy-start(s32[576,1]{1,0:T(8,128)} %constant.4.clone.src_ref) | copy-start | bytes 6916
  44.6 3.7 %copy-start.10 = (s32[288,1]{1,0:T(8,128)S(1)}, s32[288,1]{1,0:T(8,128)}, u32[]{:S(2)}) copy-start(s32[288,1]{1,0:T(8,128)} %constant.5.clone.back_ref) | copy-start | bytes 3460
  44.6 7.7 %collective-permute-start.17 = (bf16[512,256]{1,0:T(8,128)(2,1)S(1)}, bf16[512,256]{1,0:T(8,128)(2,1)S(1)}, u32[]{:S(2)}, u32[]{:S(2)}) collective-permute-start(bf16[512,256]{1,0:T(8,128)(2,1)S(1)} %get-tuple-element.36.wo_mine_ref), channel_id=1, source_target_pairs={{4,0},{0,4},{5,1},{1,5},{6,2},{2,6},{7,3},{3,7},{12,8},{8,12},{13,... | collective-permute-start | bytes 786440 | tf_op jit(solution)/shard_map/ppermute | solution.py:29
  51.8 1.5 %collective-permute-start.16 = (bf16[144,256]{1,0:T(8,128)(2,1)S(1)}, bf16[144,256]{1,0:T(8,128)(2,1)S(1)}, u32[]{:S(2)}, u32[]{:S(2)}) collective-permute-start(bf16[144,256]{1,0:T(8,128)(2,1)S(1)} %get-tuple-element.35), channel_id=1, source_target_pairs={{4,0},{0,4},{5,1},{1,5},{6,2},{2,6},{7,3},{3,7},{12,8},{8,12},{13,... | collective-permute-start | bytes 221192 | tf_op jit(solution)/shard_map/ppermute | solution.py:29

commit v4 on v3

--- a/solution.py
+++ b/solution.py
@@ -209,50 +209,73 @@
     return (shifted * lax.rsqrt(variance + 1e-05) * gain_row).astype(BF16)
 
 
-def bias_kernel(b, table_ref, index_ref, bias_ref, table, index):
+def gather_heads(b, table_ref, index, table, bias_ref):
     me = lax.axis_index("lon")
     heads = table_ref[b, pl.ds(pl.multiple_of(MY_HEADS * me, MY_HEADS), MY_HEADS), :]
     table[:, 0:BIAS_ROWS] = heads * LOG2E
+    chunks = (BIAS_ROWS + 127) // 128
+
+    def look_up(at, put):
+        low = at & 127
+        chunk = at >> 7
+        masks = [chunk == k for k in range(chunks)]
+        for h in range(MY_HEADS):
+            acc = None
+            for k in range(chunks):
+                row = jnp.broadcast_to(table[h : h + 1, 128 * k : 128 * k + 128], (8, 128))
+                got = jnp.take_along_axis(row, low, axis=1, mode="promise_in_bounds")
+                acc = got if acc is None else jnp.where(masks[k], got, acc)
+            put(h, acc)
+
+    def step(g, carry):
+        rows = pl.ds(pl.multiple_of(g * 8, 8), 8)
+
+        def put(h, value):
+            bias_ref[h, rows, 0:128] = value
+
+        look_up(index[rows, 0:128], put)
+        return carry
+
+    lax.fori_loop(0, WIN // 8, step, 0)
+    rest = WIN - 128
+    each = 128 // rest
+    groups = WIN // 8
+    for first in range(0, groups, each):
+        here = range(first, min(first + each, groups))
+        pieces = [index[8 * g : 8 * g + 8, 128:WIN] for g in here]
+        pieces += [jnp.zeros((8, rest), jnp.int32)] * (each - len(pieces))
+
+        def put(h, value, here=here):
+            for r, g in enumerate(here):
+                bias_ref[h, 8 * g : 8 * g + 8, 128:WIN] = value[:, rest * r : rest * (r + 1)]
+
+        look_up(jnp.concatenate(pieces, axis=1), put)
+
+
+def bias0_kernel(table_ref, index_ref, bias_ref, moved_ref, table):
     to = lax.broadcasted_iota(jnp.int32, (WIN, WIN), 0)
     frm = lax.broadcasted_iota(jnp.int32, (WIN, WIN), 1)
     move = jnp.where((to & 1) * HALF + (to >> 1) == frm, 1.0, 0.0).astype(BF16)
-
-    def moved(a):
-        a = nn_dot(move, a.astype(F32).astype(BF16)).astype(BF16)
-        return nt_dot(a, move).astype(jnp.int32)
-
     whole = index_ref[...]
-    index[:, 0:WIN] = moved(whole >> 8) * 256 + moved(whole & 255)
-    index[:, WIN:256] = jnp.zeros((WIN, 256 - WIN), jnp.int32)
-    chunks = (BIAS_ROWS + 127) // 128
-
-    def step(g, carry):
-        rows = pl.ds(pl.multiple_of(g * 8, 8), 8)
-        for lo, hi in ((0, 128), (128, WIN)):
-            at = index[rows, lo : lo + 128]
-            low = at & 127
-            chunk = at >> 7
-            masks = [chunk == k for k in range(chunks)]
-            for h in range(MY_HEADS):
-                acc = None
-                for k in range(chunks):
-                    row = jnp.broadcast_to(table[h : h + 1, 128 * k : 128 * k + 128], (8, 128))
-                    got = jnp.take_along_axis(row, low, axis=1, mode="promise_in_bounds")
-                    acc = got if acc is None else jnp.where(masks[k], got, acc)
-                bias_ref[h, rows, lo:hi] = acc[:, : hi - lo]
-        return carry
-
-    lax.fori_loop(0, WIN // 8, step, 0)
+    parts = jnp.concatenate([whole >> 8, whole & 255], axis=0).astype(F32).astype(BF16)
+    parts = nt_dot(parts, move).astype(BF16)
+    moved_ref[...] = (
+        nn_dot(move, parts[0:WIN]) * 256.0 + nn_dot(move, parts[WIN : 2 * WIN])
+    ).astype(jnp.int32)
+    gather_heads(0, table_ref, moved_ref, table, bias_ref)
+
+
+def bias1_kernel(table_ref, index_ref, bias_ref, table):
+    gather_heads(1, table_ref, index_ref, table, bias_ref)
 
 
 def bias_call(b, table, index):
-    return pl.pallas_call(
-        functools.partial(bias_kernel, b),
-        out_shape=jax.ShapeDtypeStruct((MY_HEADS, WIN, WIN), F32),
-        scratch_shapes=[
-            pltpu.VMEM((MY_HEADS, (BIAS_ROWS + 127) // 128 * 128), F32),
-            pltpu.VMEM((WIN, 256), jnp.int32),
-        ],
+    bias = jax.ShapeDtypeStruct((MY_HEADS, WIN, WIN), F32)
+    moved = jax.ShapeDtypeStruct((WIN, WIN), jnp.int32)
+    return pl.pallas_call(
+        bias1_kernel if b else bias0_kernel,
+        out_shape=bias if b else (bias, moved),
+        scratch_shapes=[pltpu.VMEM((MY_HEADS, (BIAS_ROWS + 127) // 128 * 128), F32)],
         compiler_params=vmem(8),
         cost_estimate=pl.CostEstimate(flops=10**9, bytes_accessed=10**6, transcendentals=0),
     )(table, index)
@@ -334,28 +357,20 @@
     )(latent, regions, qkv, out)
 
 
-def own_kernel(qkv_ref, out_ref, own0_ref, own1_ref, sems):
-    me = lax.axis_index("lon")
-    copies = []
-    for b, ref in enumerate((own0_ref, own1_ref)):
-        copies += columns(qkv_ref, out_ref, b, pl.ds(0, ref.shape[0]), me, ref, 0, sems.at[b])
-    for copy in copies:
-        copy.start()
-    for copy in copies:
-        copy.wait()
-
-
-def own_call(qkv, out):
-    own = jax.ShapeDtypeStruct((qkv.shape[1], COLS), BF16)
-    return pl.pallas_call(
-        own_kernel,
-        out_shape=(own, own),
-        in_specs=[STAY] * 2,
-        scratch_shapes=[pltpu.SemaphoreType.DMA((2, 4))],
-        compiler_params=pltpu.CompilerParams(vmem_limit_bytes=67043328-2**20*6),
+def stack_kernel(before_ref, tile_ref, after_ref, tall_ref):
+    tall_ref[0] = before_ref[...]
+    tall_ref[1] = tile_ref[...]
+    tall_ref[2] = after_ref[...]
+
+
+def stack_call(before, tile, after):
+    return pl.pallas_call(
+        stack_kernel,
+        out_shape=jax.ShapeDtypeStruct((3,) + tile.shape, BF16),
+        compiler_params=vmem(4),
         cost_estimate=pl.CostEstimate(flops=0, bytes_accessed=10**6, transcendentals=0),
-        name="own",
-    )(qkv, out)
+        name="stack",
+    )(before, tile, after)
 
 
 def enter_kernel(mine_ref, other_ref, gain_ref, x_ref, n_ref, row_ref, col_ref):
@@ -402,19 +417,24 @@
     )(mine, other, gain)
 
 
-def join_kernel(n_fsdp, n_lat, steps, wide, own_ref, *refs):
+def join_kernel(b, n_fsdp, n_lat, steps, wide, own_qkv_ref, own_out_ref, *refs):
     far, near = refs[: n_fsdp - 1], refs[n_fsdp - 1 : n_fsdp - 1 + len(steps)]
     qkv_ref, out_ref = refs[-2:]
     z, lat = lax.axis_index("fsdp"), lax.axis_index("lat")
-    depth = own_ref.shape[0]
+    depth = own_qkv_ref.shape[1]
     part = depth // n_lat
+    me = lax.axis_index("lon")
 
     def put(first, size, piece):
         rows = pl.ds(pl.multiple_of(first, size), size)
         qkv_ref[rows, :] = piece[:, 0:QKV]
         out_ref[rows, :] = piece[:, QKV:COLS]
 
-    put(z * depth, depth, own_ref[...])
+    own = pl.ds(pl.multiple_of(z * depth, depth), depth)
+    for k in range(3):
+        mine = pl.ds(pl.multiple_of(D * k + MINE * me, MINE), MINE)
+        qkv_ref[own, MINE * k : MINE * (k + 1)] = own_qkv_ref[b, :, mine]
+    out_ref[own, :] = own_out_ref[b, :, pl.ds(pl.multiple_of(OUT * me, OUT), OUT)]
     for k in range(1, n_fsdp):
         base = partner(z, k, n_fsdp) * depth
         for i, step in enumerate(wide):
@@ -424,17 +444,17 @@
             put(row, part, near[j][part * (k - 1) : part * k, :])
 
 
-def join_call(n_lat, steps, wide, own, far, near):
-    rows = own.shape[0] * (len(far) + 1)
-    return pl.pallas_call(
-        functools.partial(join_kernel, len(far) + 1, n_lat, steps, wide),
+def join_call(b, n_lat, steps, wide, qkv, out, far, near):
+    rows = qkv.shape[1] * (len(far) + 1)
+    return pl.pallas_call(
+        functools.partial(join_kernel, b, len(far) + 1, n_lat, steps, wide),
         out_shape=(
             jax.ShapeDtypeStruct((rows, QKV), BF16),
             jax.ShapeDtypeStruct((rows, OUT), BF16),
         ),
         compiler_params=vmem(8),
         cost_estimate=pl.CostEstimate(flops=10**6, bytes_accessed=2 * 10**6, transcendentals=0),
-    )(own, *far, *near)
+    )(qkv, out, *far, *near)
 
 
 def window_attend(q, k, v, bias_at, allowed, put):
@@ -472,7 +492,8 @@
     v_s[...] = both[:, 2 * MINE : 3 * MINE]
 
 
-def first_kernel(n_ref, w_ref, bias_ref, o_ref, q_s, k_s, v_s):
+def first_kernel(n_ref, w_ref, bias_ref, wo_ref, o_ref, q_s, k_s, v_s):
+    o_ref[PAIR * KEPT :, :] = wo_ref[...]
     project(n_ref[...].reshape(PAIR * TALL, D), w_ref, q_s, k_s, v_s)
     for l in range(PAIR):
         for part, (q0, q1, o0) in enumerate(
@@ -481,7 +502,7 @@
             t = TALL * l + WIN * part
 
             def put(col, value, l=l, o0=o0, q0=q0, q1=q1):
-                o_ref[l, o0 : o0 + q1 - q0, col : col + 128] = value
+                o_ref[KEPT * l + o0 : KEPT * l + o0 + q1 - q0, col : col + 128] = value
 
             window_attend(
                 q_s[t + q0 : t + q1, :],
@@ -493,16 +514,16 @@
             )
 
 
-def first_call(normed, weight, bias):
+def first_call(normed, weight, bias, wo):
     scratch = pltpu.VMEM((PAIR * TALL, MINE), BF16)
     return pl.pallas_call(
         first_kernel,
-        out_shape=jax.ShapeDtypeStruct((PAIR, KEPT, MINE), BF16),
+        out_shape=jax.ShapeDtypeStruct((PAIR * KEPT + D, MINE), BF16),
         scratch_shapes=[scratch, scratch, scratch],
         compiler_params=vmem(24),
         cost_estimate=pl.CostEstimate(flops=2 * 10**9, bytes_accessed=4 * 10**6, transcendentals=10**6),
         name="first",
-    )(normed, weight, bias)
+    )(normed, weight, bias, wo)
 
 
 def pair_columns(me, ref, mine, other):
@@ -512,13 +533,13 @@
 
 
 def second_kernel(
-    mine_ref, other_ref, wo_mine_ref, wo_other_ref, x_ref, gain_ref, src_ref, w_ref, bias_ref,
+    mine_ref, other_ref, x_ref, gain_ref, src_ref, w_ref, bias_ref,
     row_ref, col_ref, back_ref, mid_ref, keep_ref, send_ref, o_s, wo_s, m_s, n_s, q_s, k_s, v_s, a_s, t_s,
 ):
     me = lax.axis_index("lon")
     tokens = PAIR * KEPT
-    pair_columns(me, o_s, mine_ref[...].reshape(tokens, MINE), other_ref[...].reshape(tokens, MINE))
-    pair_columns(me, wo_s, wo_mine_ref[...], wo_other_ref[...])
+    pair_columns(me, o_s, mine_ref[0:tokens, :], other_ref[0:tokens, :])
+    pair_columns(me, wo_s, mine_ref[tokens:, :], other_ref[tokens:, :])
     for l in range(PAIR):
         rows = slice(KEPT * l, KEPT * (l + 1))
         value = x_ref[l, KEEP0:KEEP1, :].astype(F32) + nn_dot(o_s[rows, :], wo_s[...])
@@ -551,7 +572,7 @@
     send_ref[...] = t_s[1 - me]
 
 
-def second_call(mine, other, wo_mine, wo_other, x, gain, weight, bias, row, col):
+def second_call(mine, other, x, gain, weight, bias, row, col):
     tokens = PAIR * KEPT
     qkv = pltpu.VMEM((4 * WIN, MINE), BF16)
     return pl.pallas_call(
@@ -576,28 +597,43 @@
         cost_estimate=pl.CostEstimate(flops=2 * 10**9, bytes_accessed=4 * 10**6, transcendentals=10**6),
         name="second",
     )(
-        mine, other, wo_mine, wo_other, x, gain, jnp.asarray(window_sources()), weight, bias,
+        mine, other, x, gain, jnp.asarray(window_sources()), weight, bias,
         row, col, jnp.asarray(tile_sources()),
     )
 
 
-def last_kernel(mid_ref, keep_ref, got_ref, wo_mine_ref, wo_other_ref, out_ref, o_s, wo_s):
+def most_kernel(mid_ref, keep_ref, wo_mine_ref, wo_other_ref, sum_ref, rows_ref, wo_s):
     me = lax.axis_index("lon")
-    pair_columns(me, o_s, keep_ref[...], got_ref[...])
     pair_columns(me, wo_s, wo_mine_ref[...], wo_other_ref[...])
-    value = mid_ref[...].astype(F32) + nn_dot(o_s[...], wo_s[...])
+    mine = pl.ds(pl.multiple_of(MINE * me, MINE), MINE)
+    rows_ref[...] = wo_s[pl.ds(pl.multiple_of(MINE * (1 - me), MINE), MINE), :]
+    sum_ref[...] = mid_ref[...].astype(F32) + nn_dot(keep_ref[...], wo_s[mine, :])
+
+
+def most_call(mid, keep, wo_mine, wo_other):
+    return pl.pallas_call(
+        most_kernel,
+        out_shape=(jax.ShapeDtypeStruct((WIN, D), F32), jax.ShapeDtypeStruct((MINE, D), BF16)),
+        scratch_shapes=[pltpu.VMEM((D, D), BF16)],
+        compiler_params=vmem(8),
+        cost_estimate=pl.CostEstimate(flops=10**8, bytes_accessed=10**6, transcendentals=0),
+        name="most",
+    )(mid, keep, wo_mine, wo_other)
+
+
+def last_kernel(sum_ref, rows_ref, got_ref, out_ref):
+    value = sum_ref[...] + nn_dot(got_ref[...], rows_ref[...])
     out_ref[...] = value.reshape(WIN // WZ, WZ, D).astype(BF16)
 
 
-def last_call(mid, keep, got, wo_mine, wo_other):
+def last_call(total, rows, got):
     return pl.pallas_call(
         last_kernel,
         out_shape=jax.ShapeDtypeStruct((WIN // WZ, WZ, D), BF16),
-        scratch_shapes=[pltpu.VMEM((WIN, D), BF16), pltpu.VMEM((D, D), BF16)],
         compiler_params=vmem(8),
         cost_estimate=pl.CostEstimate(flops=10**8, bytes_accessed=10**6, transcendentals=0),
         name="last",
-    )(mid, keep, got, wo_mine, wo_other)
+    )(total, rows, got)
 
 
 def sharing(n_lat):
@@ -635,18 +671,18 @@
     far1 = spread(part1, "fsdp", range(1, n_fsdp))
     near0 = spread(jnp.concatenate(far0, axis=0), "lat", plan[0][1])
     near1 = spread(jnp.concatenate([f[:part] for f in far1], axis=0), "lat", plan[1][1])
-    own0, own1 = own_call(qkv_weight, out_weight)
-    tall = jnp.stack([before, tile, after])
+    tall = stack_call(before, tile, after)
     x, normed, tag_row, tag_col = enter_call(tall, swap(tall), norm_gain)
     table = jnp.transpose(rel_bias, (0, 2, 1))
-    w0, wo0 = join_call(n_lat, plan[0][1], plan[0][0], own0, far0, near0)
-    o0 = first_call(normed, w0, bias_call(0, table, bias_index))
-    w1, wo1 = join_call(n_lat, plan[1][1], plan[1][0], own1, far1, near1)
-    mid, keep, send = second_call(
-        o0, swap(o0), wo0, swap(wo0), x, norm_gain, w1,
-        bias_call(1, table, bias_index), tag_row, tag_col,
-    )
-    out = last_call(mid, keep, swap(send), wo1, swap(wo1))
+    params = (qkv_weight, out_weight)
+    w0, wo0 = join_call(0, n_lat, plan[0][1], plan[0][0], *params, far0, near0)
+    bias0, index = bias_call(0, table, bias_index)
+    o0 = first_call(normed, w0, bias0, wo0)
+    w1, wo1 = join_call(1, n_lat, plan[1][1], plan[1][0], *params, far1, near1)
+    bias1 = bias_call(1, table, index)
+    mid, keep, send = second_call(o0, swap(o0), x, norm_gain, w1, bias1, tag_row, tag_col)
+    total, rows = most_call(mid, keep, wo1, swap(wo1))
+    out = last_call(total, rows, swap(send))
     return jnp.transpose(out.reshape(WH, WW, WZ, D), (2, 0, 1, 3))[None]
 
 

time: 54.6 us -> 62.5 us (1.14)
  waiting for transfers between devices: 9.94 us -> 24 us
  starting transfers between devices: 22.7 us -> 19.1 us
  Pallas kernels: 19.7 us -> 17.9 us
  other arithmetic: 1.02 us -> 0.02 us
    ppermute x11, waiting for transfers between devices: 7.9 us -> 20.2 us  [heard_from(): lax.ppermute(block, axis, [(partner(i, step, size), i) for i in range(siz...]
    ppermute x11, starting transfers between devices: 17.9 us -> 14.3 us  [heard_from(): lax.ppermute(block, axis, [(partner(i, step, size), i) for i in range(siz...]
    ppermute x7 -> x6, waiting for transfers between devices: 2.04 us -> 3.8 us  [passed_along(): return lax.ppermute(block, axis, route)]
    pallas_call x6 -> x7, Pallas kernels: 12.3 us -> 10.7 us  [the longest x2 7.02 us: bias_call(): pl.pallas_call(bias1_kernel if b else bias0_kernel, out_shape=bias if b e...]
    another operation x1 -> x0, other arithmetic: 1.01 us -> none  [paired(): tall = jnp.stack([before, tile, after])]
    ppermute x7 -> x6, starting transfers between devices: 4.83 us -> 4.8 us  [passed_along(): return lax.ppermute(block, axis, route)]
  transfers between devices with their start and end apart: 18 -> 17, of which waited for: 6 -> 11; matrix products, arithmetic and copies ran while one was open for 2% -> 0% of each run, Pallas kernels for 23% -> 18%
where the time goes in v4:
time: 62.5 us; the launch traced here: 62.2 us
  waiting for transfers between devices  24 us (38%)
  starting transfers between devices  19.1 us (31%)
  Pallas kernels  17.9 us (29%)
  local copies, waits for them, and re-layouts  0.98 us (2%)
    ppermute x11, waiting for transfers between devices, heard_from(): lax.ppermute(block, axis, [(partner(i, step, size), i) for i in range(siz...  20.2 us
    ppermute x11, starting transfers between devices, heard_from(): lax.ppermute(block, axis, [(partner(i, step, size), i) for i in range(siz...  14.3 us
    pallas_call x2, Pallas kernels, bias_call(): pl.pallas_call(bias1_kernel if b else bias0_kernel, out_shape=bias if b e...  7.02 us
    ppermute x6, starting transfers between devices, passed_along(): return lax.ppermute(block, axis, route)  4.8 us
    ppermute x6, waiting for transfers between devices, passed_along(): return lax.ppermute(block, axis, route)  3.8 us
    pallas_call x1, Pallas kernels, second_call(): pl.pallas_call(second_kernel, out_shape=(jax.ShapeDtypeStruct((WIN, D), B...  3.49 us
    pallas_call x1, Pallas kernels, first_call(): pl.pallas_call(first_kernel, out_shape=jax.ShapeDtypeStruct((PAIR * KEPT...  3.15 us
    pallas_call x1, Pallas kernels, open_call(): pl.pallas_call(functools.partial(open_kernel, wide), out_shape=(jax.Shape...  2.12 us
  transfers between devices with their start and end apart: 17, of which 11 were waited for; matrix products, arithmetic and copies ran while one was open for 0% of the time, Pallas kernels for 18%

profile of v4, /device:TPU:0, one launch (start us, length us, event | category | flops | bytes accessed | tf_op | source)
XLA Modules:
  0.0 62.2 jit_solution(17631026655015725397)
XLA Ops:
  0.0 2.1 %open.1 = (bf16[32,1024]{1,0:T(8,128)(2,1)}, bf16[64,1024]{1,0:T(8,128)(2,1)}, bf16[152,512]{1,0:T(8,128)(2,1)}) custom-call(bf16[72,2,512]{2,1,0:T(2,128)(2,1)} %bitcast.14, s32[6,2,12]{2,1,0:T(2,128)} %bitcast.15, bf16[2,128,1536]{2,1,0:T(8,128)(2,1)} %own_qkv_ref.3, bf16[2,128,512]{2,1,0:T(8,128)(2,1)} %own_out_ref.3), custom_call_target="tpu_custom_call" | custom-call | flops 1000000 | bytes 1000000 | tf_op jit(solution)/shard_map/open/pallas_call | solution.py:340
  2.1 3.0 %collective-permute-start = (bf16[152,512]{1,0:T(8,128)(2,1)}, bf16[152,512]{1,0:T(8,128)(2,1)S(1)}, u32[]{:S(2)}, u32[]{:S(2)}) collective-permute-start(bf16[152,512]{1,0:T(8,128)(2,1)} %get-tuple-element.23.tile_ref), channel_id=1, source_target_pairs={{24,0},{0,8},{8,16},{16,24},{25,1},{1,9},{9,17},{17,25},{26,2},{2,... | collective-permute-start | bytes 466952 | tf_op jit(solution)/shard_map/ppermute | solution.py:29
  5.2 1.0 %collective-permute-start.1 = (bf16[152,512]{1,0:T(8,128)(2,1)}, bf16[152,512]{1,0:T(8,128)(2,1)S(1)}, u32[]{:S(2)}, u32[]{:S(2)}) collective-permute-start(bf16[152,512]{1,0:T(8,128)(2,1)} %get-tuple-element.23.tile_ref), channel_id=1, source_target_pairs={{8,0},{16,8},{24,16},{0,24},{9,1},{17,9},{25,17},{1,25},{10,2},{18... | collective-permute-start | bytes 466952 | tf_op jit(solution)/shard_map/ppermute | solution.py:29
  6.2 2.0 %collective-permute-start.3 = (bf16[32,1024]{1,0:T(8,128)(2,1)}, bf16[32,1024]{1,0:T(8,128)(2,1)S(1)}, u32[]{:S(2)}, u32[]{:S(2)}) collective-permute-start(bf16[32,1024]{1,0:T(8,128)(2,1)} %get-tuple-element.25), channel_id=1, source_target_pairs={{1,0},{0,1},{3,2},{2,3},{5,4},{4,5},{7,6},{6,7},{9,8},{8,9},{11,10... | collective-permute-start | bytes 196616 | tf_op jit(solution)/shard_map/ppermute | solution.py:159
  8.2 2.6 %collective-permute-start.4 = (bf16[32,1024]{1,0:T(8,128)(2,1)}, bf16[32,1024]{1,0:T(8,128)(2,1)S(1)}, u32[]{:S(2)}, u32[]{:S(2)}) collective-permute-start(bf16[32,1024]{1,0:T(8,128)(2,1)} %get-tuple-element.25), channel_id=1, source_target_pairs={{2,0},{3,1},{0,2},{1,3},{6,4},{7,5},{4,6},{5,7},{10,8},{11,9},{8,1... | collective-permute-start | bytes 196616 | tf_op jit(solution)/shard_map/ppermute | solution.py:159
  10.8 0.4 collective-permute-done.before_ref
  11.2 2.7 %collective-permute-done.1.after_ref = bf16[152,512]{1,0:T(8,128)(2,1)S(1)} collective-permute-done((bf16[152,512]{1,0:T(8,128)(2,1)}, bf16[152,512]{1,0:T(8,128)(2,1)S(1)}, u32[]{:S(2)}, u32[]{:S(2)}) %collective-permute-start.1) | collective-permute-done | bytes 155680 | tf_op jit(solution)/shard_map/ppermute | solution.py:29
  13.9 0.9 %copy-done.2 = bf16[152,512]{1,0:T(8,128)(2,1)S(1)} copy-done((bf16[152,512]{1,0:T(8,128)(2,1)S(1)}, bf16[152,512]{1,0:T(8,128)(2,1)}, u32[]{:S(2)}) %copy-start.2) | copy-done | bytes 155672
  15.1 1.9 %collective-permute-done.5.refs_2_ = bf16[32,1024]{1,0:T(8,128)(2,1)S(1)} collective-permute-done((bf16[32,1024]{1,0:T(8,128)(2,1)}, bf16[32,1024]{1,0:T(8,128)(2,1)S(1)}, u32[]{:S(2)}, u32[]{:S(2)}) %collective-permute-start.5) | collective-permute-done | bytes 65568 | tf_op jit(solution)/shard_map/ppermute | solution.py:159
  17.0 0.6 collective-permute-start.6
  17.6 1.5 %collective-permute-start.7 = (bf16[96,1024]{1,0:T(8,128)(2,1)S(1)}, bf16[96,1024]{1,0:T(8,128)(2,1)S(1)}, u32[]{:S(2)}, u32[]{:S(2)}) collective-permute-start(bf16[96,1024]{1,0:T(8,128)(2,1)S(1)} %constant_dynamic-update-slice_fusion), channel_id=1, source_target_pairs={{16,0},{24,8},{0,16},{8,24},{17,1},{25,9},{1,17},{9,25},{18,2},{26... | collective-permute-start | bytes 589832 | tf_op jit(solution)/shard_map/ppermute | solution.py:159
  19.2 1.4 %collective-permute-start.8 = (bf16[96,1024]{1,0:T(8,128)(2,1)S(1)}, bf16[96,1024]{1,0:T(8,128)(2,1)S(1)}, u32[]{:S(2)}, u32[]{:S(2)}) collective-permute-start(bf16[96,1024]{1,0:T(8,128)(2,1)S(1)} %constant_dynamic-update-slice_fusion), channel_id=1, source_target_pairs={{24,0},{16,8},{8,16},{0,24},{25,1},{17,9},{9,17},{1,25},{26,2},{18... | collective-permute-start | bytes 589832 | tf_op jit(solution)/shard_map/ppermute | solution.py:159
  20.5 3.7 %shard_map.92 = (f32[8,144,144]{2,1,0:T(8,128)S(1)}, s32[144,144]{1,0:T(8,128)S(1)}) custom-call(f32[2,16,759]{2,1,0:T(8,128)S(1)} %bitcast.12, s32[144,144]{1,0:T(8,128)S(1)} %copy-done.4), custom_call_target="tpu_custom_call" | custom-call | flops 1000000000 | bytes 1000000 | tf_op jit(solution)/shard_map/pallas_call | solution.py:275
  24.3 0.5 collective-permute-done.6.refs_3_
  24.8 3.0 %collective-permute-done.7.refs_4_ = bf16[96,1024]{1,0:T(8,128)(2,1)S(1)} collective-permute-done((bf16[96,1024]{1,0:T(8,128)(2,1)S(1)}, bf16[96,1024]{1,0:T(8,128)(2,1)S(1)}, u32[]{:S(2)}, u32[]{:S(2)}) %collective-permute-start.7) | collective-permute-done | bytes 196640 | tf_op jit(solution)/shard_map/ppermute | solution.py:159
  28.0 0.7 %enter.1 = (bf16[2,432,512]{2,1,0:T(8,128)(2,1)S(1)}, bf16[2,432,512]{2,1,0:T(8,128)(2,1)S(1)}, f32[8,144]{1,0:T(8,128)S(1)}, f32[144,8]{1,0:T(8,128)S(1)}) custom-call(bf16[3,152,512]{2,1,0:T(8,128)(2,1)S(1)} %stack.1.mine_ref, bf16[3,152,512]{2,1,0:T(8,128)(2,1)S(1)} %collective-permute-done.2.other_ref, f32[2,512]{1,0:T(2,128)S(1)} %copy-done.3), custom_call_target="tpu_custom_call" | custom-call | flops 100000000 | bytes 2000000 | tf_op jit(solution)/shard_map/enter/pallas_call | solution.py:406
  28.7 3.1 %first.1.mine_ref = bf16[1120,256]{1,0:T(8,128)(2,1)S(1)} custom-call(bf16[2,432,512]{2,1,0:T(8,128)(2,1)S(1)} %get-tuple-element.24.n_ref, bf16[512,768]{1,0:T(8,128)(2,1)S(1)} %get-tuple-element.26.w_ref, f32[8,144,144]{2,1,0:T(8,128)S(1)} %get-tuple-element.27.bias_ref, bf16[512,256]{1,0:T(8,128)(2,1)S(1)} %get-tuple-element.28.wo_ref), custom_call_target="tpu_custom_call" | custom-call | flops 2000000000 | bytes 4000000 | tf_op jit(solution)/shard_map/first/pallas_call | solution.py:519
  31.9 1.6 %collective-permute-start.10 = (bf16[64,1024]{1,0:T(8,128)(2,1)S(1)}, bf16[64,1024]{1,0:T(8,128)(2,1)S(1)}, u32[]{:S(2)}, u32[]{:S(2)}) collective-permute-start(bf16[64,1024]{1,0:T(8,128)(2,1)S(1)} %copy-done.8), channel_id=1, source_target_pairs={{1,0},{0,1},{3,2},{2,3},{5,4},{4,5},{7,6},{6,7},{9,8},{8,9},{11,10... | collective-permute-start | bytes 393224 | tf_op jit(solution)/shard_map/ppermute | solution.py:159
  33.6 2.6 %collective-permute-start.11 = (bf16[64,1024]{1,0:T(8,128)(2,1)S(1)}, bf16[64,1024]{1,0:T(8,128)(2,1)S(1)}, u32[]{:S(2)}, u32[]{:S(2)}) collective-permute-start(bf16[64,1024]{1,0:T(8,128)(2,1)S(1)} %copy-done.8), channel_id=1, source_target_pairs={{2,0},{3,1},{0,2},{1,3},{6,4},{7,5},{4,6},{5,7},{10,8},{11,9},{8,1... | collective-permute-start | bytes 393224 | tf_op jit(solution)/shard_map/ppermute | solution.py:159
  36.1 0.2 collective-permute-start.12
  36.4 3.6 %collective-permute-done.10.refs_0_ = bf16[64,1024]{1,0:T(8,128)(2,1)S(1)} collective-permute-done((bf16[64,1024]{1,0:T(8,128)(2,1)S(1)}, bf16[64,1024]{1,0:T(8,128)(2,1)S(1)}, u32[]{:S(2)}, u32[]{:S(2)}) %collective-permute-start.10) | collective-permute-done | bytes 131104 | tf_op jit(solution)/shard_map/ppermute | solution.py:159
  40.0 6.5 %collective-permute-done.11.refs_1_ = bf16[64,1024]{1,0:T(8,128)(2,1)S(1)} collective-permute-done((bf16[64,1024]{1,0:T(8,128)(2,1)S(1)}, bf16[64,1024]{1,0:T(8,128)(2,1)S(1)}, u32[]{:S(2)}, u32[]{:S(2)}) %collective-permute-start.11) | collective-permute-done | bytes 131104 | tf_op jit(solution)/shard_map/ppermute | solution.py:159
  46.5 0.6 collective-permute-start.13
  47.1 1.2 %collective-permute-start.14 = (bf16[96,1024]{1,0:T(8,128)(2,1)S(1)}, bf16[96,1024]{1,0:T(8,128)(2,1)S(1)}, u32[]{:S(2)}, u32[]{:S(2)}) collective-permute-start(bf16[96,1024]{1,0:T(8,128)(2,1)S(1)} %pad_maximum_fusion), channel_id=1, source_target_pairs={{16,0},{24,8},{0,16},{8,24},{17,1},{25,9},{1,17},{9,25},{18,2},{26... | collective-permute-start | bytes 589832 | tf_op jit(solution)/shard_map/ppermute | solution.py:159
  48.3 4.0 %collective-permute-done.13.refs_3_ = bf16[96,1024]{1,0:T(8,128)(2,1)S(1)} collective-permute-done((bf16[96,1024]{1,0:T(8,128)(2,1)S(1)}, bf16[96,1024]{1,0:T(8,128)(2,1)S(1)}, u32[]{:S(2)}, u32[]{:S(2)}) %collective-permute-start.13) | collective-permute-done | bytes 196640 | tf_op jit(solution)/shard_map/ppermute | solution.py:159
  52.3 0.5 collective-permute-done.14.refs_4_
  53.0 3.3 %shard_map.94.bias_ref = f32[8,144,144]{2,1,0:T(8,128)S(1)} custom-call(f32[2,16,759]{2,1,0:T(8,128)S(1)} %bitcast.13, s32[144,144]{1,0:T(8,128)S(1)} %get-tuple-element.32.index_ref), custom_call_target="tpu_custom_call" | custom-call | flops 1000000000 | bytes 1000000 | tf_op jit(solution)/shard_map/pallas_call | solution.py:275
  56.3 3.5 %second.1 = (bf16[144,512]{1,0:T(8,128)(2,1)S(1)}, bf16[144,256]{1,0:T(8,128)(2,1)S(1)}, bf16[144,256]{1,0:T(8,128)(2,1)S(1)}) custom-call(bf16[1120,256]{1,0:T(8,128)(2,1)S(1)} %first.1.mine_ref, bf16[1120,256]{1,0:T(8,128)(2,1)S(1)} %collective-permute-done.9.other_ref, bf16[2,432,512]{2,1,0:T(8,128)(2,1)S(1)} %get-tuple-element.29.x_ref, ...), custom_call_target="tpu_custom_call" | custom-call | flops 2000000000 | bytes 4000000 | tf_op jit(solution)/shard_map/second/pallas_call | solution.py:578
  59.8 0.5 collective-permute-start.16
  60.3 0.3 most.1
  60.6 0.6 %collective-permute-done.16.got_ref = bf16[144,256]{1,0:T(8,128)(2,1)S(1)} collective-permute-done((bf16[144,256]{1,0:T(8,128)(2,1)S(1)}, bf16[144,256]{1,0:T(8,128)(2,1)S(1)}, u32[]{:S(2)}, u32[]{:S(2)}) %collective-permute-start.16) | collective-permute-done | bytes 73760 | tf_op jit(solution)/shard_map/ppermute | solution.py:29
  61.3 1.0 %last.1 = bf16[72,2,512]{2,1,0:T(2,128)(2,1)} custom-call(f32[144,512]{1,0:T(8,128)S(1)} %get-tuple-element.38.sum_ref, bf16[256,512]{1,0:T(8,128)(2,1)S(1)} %get-tuple-element.39.rows_ref, bf16[144,256]{1,0:T(8,128)(2,1)S(1)} %collective-permute-done.16.got_ref), custom_call_target="tpu_custom_call" | custom-call | flops 100000000 | bytes 1000000 | tf_op jit(solution)/shard_map/last/pallas_call | solution.py:630
  (38 shorter events, 0.7 us)
Async XLA Ops:
  0.0 20.5 %copy-start.4 = (s32[144,144]{1,0:T(8,128)S(1)}, s32[144,144]{1,0:T(8,128)}, u32[]{:S(2)}) copy-start(s32[144,144]{1,0:T(8,128)} %index_ref.1) | copy-start | bytes 248836
  0.0 20.5 %copy-start.5 = (f32[2,759,16]{1,2,0:T(8,128)S(1)}, f32[2,759,16]{1,2,0:T(8,128)}, u32[]{:S(2)}) copy-start(f32[2,759,16]{1,2,0:T(8,128)} %param.13) | copy-start | bytes 291460
  2.1 9.1 %collective-permute-start = (bf16[152,512]{1,0:T(8,128)(2,1)}, bf16[152,512]{1,0:T(8,128)(2,1)S(1)}, u32[]{:S(2)}, u32[]{:S(2)}) collective-permute-start(bf16[152,512]{1,0:T(8,128)(2,1)} %get-tuple-element.23.tile_ref), channel_id=1, source_target_pairs={{24,0},{0,8},{8,16},{16,24},{25,1},{1,9},{9,17},{17,25},{26,2},{2,... | collective-permute-start | bytes 466952 | tf_op jit(solution)/shard_map/ppermute | solution.py:29
  5.2 8.8 %collective-permute-start.1 = (bf16[152,512]{1,0:T(8,128)(2,1)}, bf16[152,512]{1,0:T(8,128)(2,1)S(1)}, u32[]{:S(2)}, u32[]{:S(2)}) collective-permute-start(bf16[152,512]{1,0:T(8,128)(2,1)} %get-tuple-element.23.tile_ref), channel_id=1, source_target_pairs={{8,0},{16,8},{24,16},{0,24},{9,1},{17,9},{25,17},{1,25},{10,2},{18... | collective-permute-start | bytes 466952 | tf_op jit(solution)/shard_map/ppermute | solution.py:29
  6.2 8.8 %collective-permute-start.3 = (bf16[32,1024]{1,0:T(8,128)(2,1)}, bf16[32,1024]{1,0:T(8,128)(2,1)S(1)}, u32[]{:S(2)}, u32[]{:S(2)}) collective-permute-start(bf16[32,1024]{1,0:T(8,128)(2,1)} %get-tuple-element.25), channel_id=1, source_target_pairs={{1,0},{0,1},{3,2},{2,3},{5,4},{4,5},{7,6},{6,7},{9,8},{8,9},{11,10... | collective-permute-start | bytes 196616 | tf_op jit(solution)/shard_map/ppermute | solution.py:159
  8.2 6.9 %collective-permute-start.4 = (bf16[32,1024]{1,0:T(8,128)(2,1)}, bf16[32,1024]{1,0:T(8,128)(2,1)S(1)}, u32[]{:S(2)}, u32[]{:S(2)}) collective-permute-start(bf16[32,1024]{1,0:T(8,128)(2,1)} %get-tuple-element.25), channel_id=1, source_target_pairs={{2,0},{3,1},{0,2},{1,3},{6,4},{7,5},{4,6},{5,7},{10,8},{11,9},{8,1... | collective-permute-start | bytes 196616 | tf_op jit(solution)/shard_map/ppermute | solution.py:159
  10.8 6.3 %collective-permute-start.5 = (bf16[32,1024]{1,0:T(8,128)(2,1)}, bf16[32,1024]{1,0:T(8,128)(2,1)S(1)}, u32[]{:S(2)}, u32[]{:S(2)}) collective-permute-start(bf16[32,1024]{1,0:T(8,128)(2,1)} %get-tuple-element.25), channel_id=1, source_target_pairs={{3,0},{2,1},{1,2},{0,3},{7,4},{6,5},{5,6},{4,7},{11,8},{10,9},{9,1... | collective-permute-start | bytes 196616 | tf_op jit(solution)/shard_map/ppermute | solution.py:159
  13.9 0.9 %copy-start.2 = (bf16[152,512]{1,0:T(8,128)(2,1)S(1)}, bf16[152,512]{1,0:T(8,128)(2,1)}, u32[]{:S(2)}) copy-start(bf16[152,512]{1,0:T(8,128)(2,1)} %get-tuple-element.23.tile_ref) | copy-start | bytes 466948
  14.9 13.1 %collective-permute-start.2 = (bf16[3,152,512]{2,1,0:T(8,128)(2,1)S(1)}, bf16[3,152,512]{2,1,0:T(8,128)(2,1)S(1)}, u32[]{:S(2)}, u32[]{:S(2)}) collective-permute-start(bf16[3,152,512]{2,1,0:T(8,128)(2,1)S(1)} %stack.1.mine_ref), channel_id=1, source_target_pairs={{4,0},{0,4},{5,1},{1,5},{6,2},{2,6},{7,3},{3,7},{12,8},{8,12},{13,... | collective-permute-start | bytes 1400840 | tf_op jit(solution)/shard_map/ppermute | solution.py:29
  17.0 7.7 %collective-permute-start.6 = (bf16[96,1024]{1,0:T(8,128)(2,1)S(1)}, bf16[96,1024]{1,0:T(8,128)(2,1)S(1)}, u32[]{:S(2)}, u32[]{:S(2)}) collective-permute-start(bf16[96,1024]{1,0:T(8,128)(2,1)S(1)} %constant_dynamic-update-slice_fusion), channel_id=1, source_target_pairs={{8,0},{0,8},{24,16},{16,24},{9,1},{1,9},{25,17},{17,25},{10,2},{2,... | collective-permute-start | bytes 589832 | tf_op jit(solution)/shard_map/ppermute | solution.py:159
  17.6 10.2 %collective-permute-start.7 = (bf16[96,1024]{1,0:T(8,128)(2,1)S(1)}, bf16[96,1024]{1,0:T(8,128)(2,1)S(1)}, u32[]{:S(2)}, u32[]{:S(2)}) collective-permute-start(bf16[96,1024]{1,0:T(8,128)(2,1)S(1)} %constant_dynamic-update-slice_fusion), channel_id=1, source_target_pairs={{16,0},{24,8},{0,16},{8,24},{17,1},{25,9},{1,17},{9,25},{18,2},{26... | collective-permute-start | bytes 589832 | tf_op jit(solution)/shard_map/ppermute | solution.py:159
  19.2 8.7 %collective-permute-start.8 = (bf16[96,1024]{1,0:T(8,128)(2,1)S(1)}, bf16[96,1024]{1,0:T(8,128)(2,1)S(1)}, u32[]{:S(2)}, u32[]{:S(2)}) collective-permute-start(bf16[96,1024]{1,0:T(8,128)(2,1)S(1)} %constant_dynamic-update-slice_fusion), channel_id=1, source_target_pairs={{24,0},{16,8},{8,16},{0,24},{25,1},{17,9},{9,17},{1,25},{26,2},{18... | collective-permute-start | bytes 589832 | tf_op jit(solution)/shard_map/ppermute | solution.py:159
  20.5 7.3 %copy-start = (bf16[2,128,1536]{2,1,0:T(8,128)(2,1)S(1)}, bf16[2,128,1536]{2,1,0:T(8,128)(2,1)}, u32[]{:S(2)}) copy-start(bf16[2,128,1536]{2,1,0:T(8,128)(2,1)} %own_qkv_ref.3) | copy-start | bytes 2359300
  20.5 7.3 %copy-start.1 = (bf16[2,128,512]{2,1,0:T(8,128)(2,1)S(1)}, bf16[2,128,512]{2,1,0:T(8,128)(2,1)}, u32[]{:S(2)}) copy-start(bf16[2,128,512]{2,1,0:T(8,128)(2,1)} %own_out_ref.3) | copy-start | bytes 786436
  24.3 3.7 %copy-start.3 = (f32[2,512]{1,0:T(2,128)S(1)}, f32[2,512]{1,0:T(2,128)}, u32[]{:S(2)}) copy-start(f32[2,512]{1,0:T(2,128)} %gain_ref.3) | copy-start | bytes 12292
  28.7 3.2 %copy-start.8 = (bf16[64,1024]{1,0:T(8,128)(2,1)S(1)}, bf16[64,1024]{1,0:T(8,128)(2,1)}, u32[]{:S(2)}) copy-start(bf16[64,1024]{1,0:T(8,128)(2,1)} %get-tuple-element.30) | copy-start | bytes 393220
  31.8 24.5 %collective-permute-start.9 = (bf16[1120,256]{1,0:T(8,128)(2,1)S(1)}, bf16[1120,256]{1,0:T(8,128)(2,1)S(1)}, u32[]{:S(2)}, u32[]{:S(2)}) collective-permute-start(bf16[1120,256]{1,0:T(8,128)(2,1)S(1)} %first.1.mine_ref), channel_id=1, source_target_pairs={{4,0},{0,4},{5,1},{1,5},{6,2},{2,6},{7,3},{3,7},{12,8},{8,12},{13,... | collective-permute-start | bytes 1720328 | tf_op jit(solution)/shard_map/ppermute | solution.py:29
  31.9 8.1 %collective-permute-start.10 = (bf16[64,1024]{1,0:T(8,128)(2,1)S(1)}, bf16[64,1024]{1,0:T(8,128)(2,1)S(1)}, u32[]{:S(2)}, u32[]{:S(2)}) collective-permute-start(bf16[64,1024]{1,0:T(8,128)(2,1)S(1)} %copy-done.8), channel_id=1, source_target_pairs={{1,0},{0,1},{3,2},{2,3},{5,4},{4,5},{7,6},{6,7},{9,8},{8,9},{11,10... | collective-permute-start | bytes 393224 | tf_op jit(solution)/shard_map/ppermute | solution.py:159
  33.6 12.9 %collective-permute-start.11 = (bf16[64,1024]{1,0:T(8,128)(2,1)S(1)}, bf16[64,1024]{1,0:T(8,128)(2,1)S(1)}, u32[]{:S(2)}, u32[]{:S(2)}) collective-permute-start(bf16[64,1024]{1,0:T(8,128)(2,1)S(1)} %copy-done.8), channel_id=1, source_target_pairs={{2,0},{3,1},{0,2},{1,3},{6,4},{7,5},{4,6},{5,7},{10,8},{11,9},{8,1... | collective-permute-start | bytes 393224 | tf_op jit(solution)/shard_map/ppermute | solution.py:159
  36.1 10.4 %collective-permute-start.12 = (bf16[64,1024]{1,0:T(8,128)(2,1)S(1)}, bf16[64,1024]{1,0:T(8,128)(2,1)S(1)}, u32[]{:S(2)}, u32[]{:S(2)}) collective-permute-start(bf16[64,1024]{1,0:T(8,128)(2,1)S(1)} %copy-done.8), channel_id=1, source_target_pairs={{3,0},{2,1},{1,2},{0,3},{7,4},{6,5},{5,6},{4,7},{11,8},{10,9},{9,1... | collective-permute-start | bytes 393224 | tf_op jit(solution)/shard_map/ppermute | solution.py:159
  46.5 5.7 %collective-permute-start.13 = (bf16[96,1024]{1,0:T(8,128)(2,1)S(1)}, bf16[96,1024]{1,0:T(8,128)(2,1)S(1)}, u32[]{:S(2)}, u32[]{:S(2)}) collective-permute-start(bf16[96,1024]{1,0:T(8,128)(2,1)S(1)} %pad_maximum_fusion), channel_id=1, source_target_pairs={{8,0},{0,8},{24,16},{16,24},{9,1},{1,9},{25,17},{17,25},{10,2},{2,... | collective-permute-start | bytes 589832 | tf_op jit(solution)/shard_map/ppermute | solution.py:159
  47.1 5.7 %collective-permute-start.14 = (bf16[96,1024]{1,0:T(8,128)(2,1)S(1)}, bf16[96,1024]{1,0:T(8,128)(2,1)S(1)}, u32[]{:S(2)}, u32[]{:S(2)}) collective-permute-start(bf16[96,1024]{1,0:T(8,128)(2,1)S(1)} %pad_maximum_fusion), channel_id=1, source_target_pairs={{16,0},{24,8},{0,16},{8,24},{17,1},{25,9},{1,17},{9,25},{18,2},{26... | collective-permute-start | bytes 589832 | tf_op jit(solution)/shard_map/ppermute | solution.py:159
  52.9 7.5 %collective-permute-start.15 = (bf16[512,256]{1,0:T(8,128)(2,1)S(1)}, bf16[512,256]{1,0:T(8,128)(2,1)S(1)}, u32[]{:S(2)}, u32[]{:S(2)}) collective-permute-start(bf16[512,256]{1,0:T(8,128)(2,1)S(1)} %get-tuple-element.37.wo_mine_ref), channel_id=1, source_target_pairs={{4,0},{0,4},{5,1},{1,5},{6,2},{2,6},{7,3},{3,7},{12,8},{8,12},{13,... | collective-permute-start | bytes 786440 | tf_op jit(solution)/shard_map/ppermute | solution.py:29
  53.0 3.3 %copy-start.6 = (s32[576,1]{1,0:T(8,128)S(1)}, s32[576,1]{1,0:T(8,128)}, u32[]{:S(2)}) copy-start(s32[576,1]{1,0:T(8,128)} %constant.4.clone.src_ref) | copy-start | bytes 6916
  53.0 3.3 %copy-start.7 = (s32[288,1]{1,0:T(8,128)S(1)}, s32[288,1]{1,0:T(8,128)}, u32[]{:S(2)}) copy-start(s32[288,1]{1,0:T(8,128)} %constant.5.clone.back_ref) | copy-start | bytes 3460
  59.8 1.4 %collective-permute-start.16 = (bf16[144,256]{1,0:T(8,128)(2,1)S(1)}, bf16[144,256]{1,0:T(8,128)(2,1)S(1)}, u32[]{:S(2)}, u32[]{:S(2)}) collective-permute-start(bf16[144,256]{1,0:T(8,128)(2,1)S(1)} %get-tuple-element.40), channel_id=1, source_target_pairs={{4,0},{0,4},{5,1},{1,5},{6,2},{2,6},{7,3},{3,7},{12,8},{8,12},{13,... | collective-permute-start | bytes 221192 | tf_op jit(solution)/shard_map/ppermute | solution.py:29

commit v5 on v4

--- a/solution.py
+++ b/solution.py
@@ -236,7 +236,7 @@
         look_up(index[rows, 0:128], put)
         return carry
 
-    lax.fori_loop(0, WIN // 8, step, 0)
+    lax.fori_loop(0, WIN // 8, step, 0, unroll=9)
     rest = WIN - 128
     each = 128 // rest
     groups = WIN // 8
@@ -357,43 +357,35 @@
     )(latent, regions, qkv, out)
 
 
-def stack_kernel(before_ref, tile_ref, after_ref, tall_ref):
-    tall_ref[0] = before_ref[...]
-    tall_ref[1] = tile_ref[...]
-    tall_ref[2] = after_ref[...]
-
-
-def stack_call(before, tile, after):
-    return pl.pallas_call(
-        stack_kernel,
-        out_shape=jax.ShapeDtypeStruct((3,) + tile.shape, BF16),
-        compiler_params=vmem(4),
-        cost_estimate=pl.CostEstimate(flops=0, bytes_accessed=10**6, transcendentals=0),
-        name="stack",
-    )(before, tile, after)
-
-
-def enter_kernel(mine_ref, other_ref, gain_ref, x_ref, n_ref, row_ref, col_ref):
+def enter_kernel(mirrored, *refs):
+    mine, other = refs[0:3], refs[3:6]
+    gain_ref, x_ref, n_ref, row_ref, col_ref = refs[6:]
     me = lax.axis_index("lon")
     n_lat = lax.axis_size("lat")
     lat = lax.axis_index("lat")
-    for k in range(3):
-        for ref, l in ((mine_ref, me), (other_ref, 1 - me)):
-            tokens = ref[k, 0:WIN, :]
-            x_ref[l, WIN * k : WIN * (k + 1), :] = tokens
-            n_ref[l, WIN * k : WIN * (k + 1), :] = norm_rows(tokens.astype(F32), gain_ref[0:1, :])
+    odd = lat & 1 if mirrored else 1
+    places = (2 - 2 * odd, 1, 2 * odd)
+    for k, place in enumerate(places):
+        rows = pl.ds(pl.multiple_of(WIN * place, WIN), WIN)
+        for ref, l in ((mine[k], me), (other[k], 1 - me)):
+            tokens = ref[0:WIN, :]
+            x_ref[l, rows, :] = tokens
+            n_ref[l, rows, :] = norm_rows(tokens.astype(F32), gain_ref[0:1, :])
     lanes = lax.broadcasted_iota(jnp.int32, (1, WIN), 1)
     level = lanes & 1
     dh = lanes // (WW * WZ)
+
+    def regions(three):
+        found = [ref[WIN : WIN + REGION_ROWS, 0:WIN].astype(F32)[0:1] for ref in three]
+        return jnp.where(odd == 1, found[0], found[2]), found[1]
+
     rows = []
-    for a in range(2):
+    for a, (own, pair) in enumerate(zip(regions(mine), regions(other))):
         window = (lat + n_lat - 1 + a) % n_lat
         late = window * WH + dh >= n_lat * WH - WH // 2
         extra = jnp.where(level == WZ - 1, 2.0, 0.0) + jnp.where(late, 1.0, 0.0)
-        mine = mine_ref[a, WIN : WIN + REGION_ROWS, 0:WIN].astype(F32)[0:1]
-        other = other_ref[a, WIN : WIN + REGION_ROWS, 0:WIN].astype(F32)[0:1]
-        west = jnp.where(me == 0, mine, other)
-        east = jnp.where(me == 0, other, mine)
+        west = jnp.where(me == 0, own, pair)
+        east = jnp.where(me == 0, pair, own)
         rows += [4.0 * west + extra, 4.0 * east + extra]
     tags = jnp.concatenate(rows + rows, axis=0)
     row_ref[...] = tags
@@ -402,9 +394,9 @@
     col_ref[...] = nt_dot(jnp.where(to == frm, 1.0, 0.0).astype(BF16), tags.astype(BF16))
 
 
-def enter_call(mine, other, gain):
+def enter_call(mirrored, mine, other, gain):
     return pl.pallas_call(
-        enter_kernel,
+        functools.partial(enter_kernel, mirrored),
         out_shape=(
             jax.ShapeDtypeStruct((PAIR, TALL, D), BF16),
             jax.ShapeDtypeStruct((PAIR, TALL, D), BF16),
@@ -414,7 +406,7 @@
         compiler_params=vmem(16),
         cost_estimate=pl.CostEstimate(flops=10**8, bytes_accessed=2 * 10**6, transcendentals=0),
         name="enter",
-    )(mine, other, gain)
+    )(*mine, *other, gain)
 
 
 def join_kernel(b, n_fsdp, n_lat, steps, wide, own_qkv_ref, own_out_ref, *refs):
@@ -666,13 +658,15 @@
         plan[1][0],
     )
     far0 = spread(part0, "fsdp", range(1, n_fsdp))
-    before = passed_along(tile, "lat", 1)
-    after = passed_along(tile, "lat", -1)
+    mirrored = n_lat == 4
+    side = heard_from(tile, "lat", 1) if mirrored else passed_along(tile, "lat", 1)
+    cross = heard_from(side, "lat", 2) if mirrored else passed_along(tile, "lat", -1)
     far1 = spread(part1, "fsdp", range(1, n_fsdp))
     near0 = spread(jnp.concatenate(far0, axis=0), "lat", plan[0][1])
     near1 = spread(jnp.concatenate([f[:part] for f in far1], axis=0), "lat", plan[1][1])
-    tall = stack_call(before, tile, after)
-    x, normed, tag_row, tag_col = enter_call(tall, swap(tall), norm_gain)
+    three = (side, tile, cross)
+    pair = [swap(t) for t in three]
+    x, normed, tag_row, tag_col = enter_call(mirrored, three, pair, norm_gain)
     table = jnp.transpose(rel_bias, (0, 2, 1))
     params = (qkv_weight, out_weight)
     w0, wo0 = join_call(0, n_lat, plan[0][1], plan[0][0], *params, far0, near0)

time: 62.5 us -> 62 us (level)
  Pallas kernels: 17.9 us -> 15.6 us
  starting transfers between devices: 19.1 us -> 20.7 us
    ppermute x11 -> x13, starting transfers between devices: 14.3 us -> 19.5 us  [heard_from(): lax.ppermute(block, axis, [(partner(i, step, size), i) for i in range(siz...]
    ppermute x6, starting transfers between devices: 4.8 us -> 1.18 us  [passed_along(): return lax.ppermute(block, axis, route)]
    ppermute x11 -> x13, waiting for transfers between devices: 20.2 us -> 23.5 us  [heard_from(): lax.ppermute(block, axis, [(partner(i, step, size), i) for i in range(siz...]
    ppermute x6, waiting for transfers between devices: 3.8 us -> 0.64 us  [passed_along(): return lax.ppermute(block, axis, route)]
    pallas_call x2, Pallas kernels: 7.02 us -> 4.78 us  [bias_call(): pl.pallas_call(bias1_kernel if b else bias0_kernel, out_shape=bias if b e...]
  transfers between devices with their start and end apart: 17 -> 19, of which waited for: 11 -> 10; matrix products, arithmetic and copies ran while one was open for 0% -> 0% of each run, Pallas kernels for 18% -> 14%
where the time goes in v5:
time: 62 us; the launch traced here: 61.3 us
  waiting for transfers between devices  24.1 us (39%)
  starting transfers between devices  20.7 us (33%)
  Pallas kernels  15.6 us (25%)
  local copies, waits for them, and re-layouts  0.71 us (1%)
    ppermute x13, waiting for transfers between devices, heard_from(): lax.ppermute(block, axis, [(partner(i, step, size), i) for i in range(siz...  23.5 us
    ppermute x13, starting transfers between devices, heard_from(): lax.ppermute(block, axis, [(partner(i, step, size), i) for i in range(siz...  19.5 us
    pallas_call x2, Pallas kernels, bias_call(): pl.pallas_call(bias1_kernel if b else bias0_kernel, out_shape=bias if b e...  4.78 us
    pallas_call x1, Pallas kernels, second_call(): pl.pallas_call(second_kernel, out_shape=(jax.ShapeDtypeStruct((WIN, D), B...  3.49 us
    pallas_call x1, Pallas kernels, first_call(): pl.pallas_call(first_kernel, out_shape=jax.ShapeDtypeStruct((PAIR * KEPT...  3.14 us
    pallas_call x1, Pallas kernels, open_call(): pl.pallas_call(functools.partial(open_kernel, wide), out_shape=(jax.Shape...  2.11 us
  transfers between devices with their start and end apart: 19, of which 10 were waited for; matrix products, arithmetic and copies ran while one was open for 0% of the time, Pallas kernels for 14%

profile of v5, /device:TPU:0, one launch (start us, length us, event | category | flops | bytes accessed | tf_op | source)
XLA Modules:
  0.0 61.3 jit_solution(4351090005040488504)
XLA Ops:
  0.0 2.1 %open.1 = (bf16[32,1024]{1,0:T(8,128)(2,1)}, bf16[64,1024]{1,0:T(8,128)(2,1)}, bf16[152,512]{1,0:T(8,128)(2,1)}) custom-call(bf16[72,2,512]{2,1,0:T(2,128)(2,1)} %bitcast.14, s32[6,2,12]{2,1,0:T(2,128)} %bitcast.15, bf16[2,128,1536]{2,1,0:T(8,128)(2,1)} %own_qkv_ref.3, bf16[2,128,512]{2,1,0:T(8,128)(2,1)} %own_out_ref.3), custom_call_target="tpu_custom_call" | custom-call | flops 1000000 | bytes 1000000 | tf_op jit(solution)/shard_map/open/pallas_call | solution.py:340
  2.1 3.1 %collective-permute-start.5 = (bf16[32,1024]{1,0:T(8,128)(2,1)}, bf16[32,1024]{1,0:T(8,128)(2,1)S(1)}, u32[]{:S(2)}, u32[]{:S(2)}) collective-permute-start(bf16[32,1024]{1,0:T(8,128)(2,1)} %get-tuple-element.25), channel_id=1, source_target_pairs={{1,0},{0,1},{3,2},{2,3},{5,4},{4,5},{7,6},{6,7},{9,8},{8,9},{11,10... | collective-permute-start | bytes 196616 | tf_op jit(solution)/shard_map/ppermute | solution.py:159
  5.2 2.6 %collective-permute-start.6 = (bf16[32,1024]{1,0:T(8,128)(2,1)}, bf16[32,1024]{1,0:T(8,128)(2,1)S(1)}, u32[]{:S(2)}, u32[]{:S(2)}) collective-permute-start(bf16[32,1024]{1,0:T(8,128)(2,1)} %get-tuple-element.25), channel_id=1, source_target_pairs={{2,0},{3,1},{0,2},{1,3},{6,4},{7,5},{4,6},{5,7},{10,8},{11,9},{8,1... | collective-permute-start | bytes 196616 | tf_op jit(solution)/shard_map/ppermute | solution.py:159
  7.8 1.7 %collective-permute-start = (bf16[152,512]{1,0:T(8,128)(2,1)}, bf16[152,512]{1,0:T(8,128)(2,1)S(1)}, u32[]{:S(2)}, u32[]{:S(2)}) collective-permute-start(bf16[152,512]{1,0:T(8,128)(2,1)} %get-tuple-element.23.refs_1_), channel_id=1, source_target_pairs={{8,0},{0,8},{24,16},{16,24},{9,1},{1,9},{25,17},{17,25},{10,2},{2,... | collective-permute-start | bytes 466952 | tf_op jit(solution)/shard_map/ppermute | solution.py:159
  9.6 3.2 %collective-permute-done.6.refs_1_ = bf16[32,1024]{1,0:T(8,128)(2,1)S(1)} collective-permute-done((bf16[32,1024]{1,0:T(8,128)(2,1)}, bf16[32,1024]{1,0:T(8,128)(2,1)S(1)}, u32[]{:S(2)}, u32[]{:S(2)}) %collective-permute-start.6) | collective-permute-done | bytes 65568 | tf_op jit(solution)/shard_map/ppermute | solution.py:159
  12.7 1.4 %collective-permute-done.7.refs_2_ = bf16[32,1024]{1,0:T(8,128)(2,1)S(1)} collective-permute-done((bf16[32,1024]{1,0:T(8,128)(2,1)}, bf16[32,1024]{1,0:T(8,128)(2,1)S(1)}, u32[]{:S(2)}, u32[]{:S(2)}) %collective-permute-start.7) | collective-permute-done | bytes 65568 | tf_op jit(solution)/shard_map/ppermute | solution.py:159
  14.1 2.4 %collective-permute-start.10 = (bf16[96,1024]{1,0:T(8,128)(2,1)S(1)}, bf16[96,1024]{1,0:T(8,128)(2,1)S(1)}, u32[]{:S(2)}, u32[]{:S(2)}) collective-permute-start(bf16[96,1024]{1,0:T(8,128)(2,1)S(1)} %constant_dynamic-update-slice_fusion), channel_id=1, source_target_pairs={{24,0},{16,8},{8,16},{0,24},{25,1},{17,9},{9,17},{1,25},{26,2},{18... | collective-permute-start | bytes 589832 | tf_op jit(solution)/shard_map/ppermute | solution.py:159
  16.6 0.5 collective-permute-start.1
  17.1 0.5 collective-permute-start.8
  17.6 1.5 %collective-permute-start.9 = (bf16[96,1024]{1,0:T(8,128)(2,1)S(1)}, bf16[96,1024]{1,0:T(8,128)(2,1)S(1)}, u32[]{:S(2)}, u32[]{:S(2)}) collective-permute-start(bf16[96,1024]{1,0:T(8,128)(2,1)S(1)} %constant_dynamic-update-slice_fusion), channel_id=1, source_target_pairs={{16,0},{24,8},{0,16},{8,24},{17,1},{25,9},{1,17},{9,25},{18,2},{26... | collective-permute-start | bytes 589832 | tf_op jit(solution)/shard_map/ppermute | solution.py:159
  19.2 3.4 %collective-permute-done.10.refs_5_ = bf16[96,1024]{1,0:T(8,128)(2,1)S(1)} collective-permute-done((bf16[96,1024]{1,0:T(8,128)(2,1)S(1)}, bf16[96,1024]{1,0:T(8,128)(2,1)S(1)}, u32[]{:S(2)}, u32[]{:S(2)}) %collective-permute-start.10) | collective-permute-done | bytes 196640 | tf_op jit(solution)/shard_map/ppermute | solution.py:159
  22.6 2.2 %collective-permute-done.1.refs_2_ = bf16[152,512]{1,0:T(8,128)(2,1)S(1)} collective-permute-done((bf16[152,512]{1,0:T(8,128)(2,1)S(1)}, bf16[152,512]{1,0:T(8,128)(2,1)S(1)}, u32[]{:S(2)}, u32[]{:S(2)}) %collective-permute-start.1) | collective-permute-done | bytes 155680 | tf_op jit(solution)/shard_map/ppermute | solution.py:159
  24.9 2.6 %shard_map.92 = (f32[8,144,144]{2,1,0:T(8,128)S(1)}, s32[144,144]{1,0:T(8,128)S(1)}) custom-call(f32[2,16,759]{2,1,0:T(8,128)S(1)} %bitcast.12, s32[144,144]{1,0:T(8,128)S(1)} %copy-done.4), custom_call_target="tpu_custom_call" | custom-call | flops 1000000000 | bytes 1000000 | tf_op jit(solution)/shard_map/pallas_call | solution.py:275
  27.5 0.1 collective-permute-done.9.refs_4_
  27.7 0.6 %copy-done.2 = bf16[152,512]{1,0:T(8,128)(2,1)S(1)} copy-done((bf16[152,512]{1,0:T(8,128)(2,1)S(1)}, bf16[152,512]{1,0:T(8,128)(2,1)}, u32[]{:S(2)}) %copy-start.2) | copy-done | bytes 155672
  28.4 0.7 %enter.1 = (bf16[2,432,512]{2,1,0:T(8,128)(2,1)S(1)}, bf16[2,432,512]{2,1,0:T(8,128)(2,1)S(1)}, f32[8,144]{1,0:T(8,128)S(1)}, f32[144,8]{1,0:T(8,128)S(1)}) custom-call(bf16[152,512]{1,0:T(8,128)(2,1)S(1)} %collective-permute-done.refs_0_, bf16[152,512]{1,0:T(8,128)(2,1)S(1)} %copy-done.2, bf16[152,512]{1,0:T(8,128)(2,1)S(1)} %collective-permute-done.1.refs_2_, ...), custom_call_target="tpu_custom_call" | custom-call | flops 100000000 | bytes 2000000 | tf_op jit(solution)/shard_map/enter/pallas_call | solution.py:398
  29.1 3.1 %first.1.mine_ref = bf16[1120,256]{1,0:T(8,128)(2,1)S(1)} custom-call(bf16[2,432,512]{2,1,0:T(8,128)(2,1)S(1)} %get-tuple-element.24.n_ref, bf16[512,768]{1,0:T(8,128)(2,1)S(1)} %get-tuple-element.26.w_ref, f32[8,144,144]{2,1,0:T(8,128)S(1)} %get-tuple-element.27.bias_ref, bf16[512,256]{1,0:T(8,128)(2,1)S(1)} %get-tuple-element.28.wo_ref), custom_call_target="tpu_custom_call" | custom-call | flops 2000000000 | bytes 4000000 | tf_op jit(solution)/shard_map/first/pallas_call | solution.py:511
  32.2 0.6 collective-permute-start.11
  32.8 2.4 %collective-permute-start.13 = (bf16[64,1024]{1,0:T(8,128)(2,1)S(1)}, bf16[64,1024]{1,0:T(8,128)(2,1)S(1)}, u32[]{:S(2)}, u32[]{:S(2)}) collective-permute-start(bf16[64,1024]{1,0:T(8,128)(2,1)S(1)} %copy-done.8), channel_id=1, source_target_pairs={{2,0},{3,1},{0,2},{1,3},{6,4},{7,5},{4,6},{5,7},{10,8},{11,9},{8,1... | collective-permute-start | bytes 393224 | tf_op jit(solution)/shard_map/ppermute | solution.py:159
  35.2 2.0 %collective-permute-start.14 = (bf16[64,1024]{1,0:T(8,128)(2,1)S(1)}, bf16[64,1024]{1,0:T(8,128)(2,1)S(1)}, u32[]{:S(2)}, u32[]{:S(2)}) collective-permute-start(bf16[64,1024]{1,0:T(8,128)(2,1)S(1)} %copy-done.8), channel_id=1, source_target_pairs={{3,0},{2,1},{1,2},{0,3},{7,4},{6,5},{5,6},{4,7},{11,8},{10,9},{9,1... | collective-permute-start | bytes 393224 | tf_op jit(solution)/shard_map/ppermute | solution.py:159
  37.2 3.6 %collective-permute-done.12.refs_0_ = bf16[64,1024]{1,0:T(8,128)(2,1)S(1)} collective-permute-done((bf16[64,1024]{1,0:T(8,128)(2,1)S(1)}, bf16[64,1024]{1,0:T(8,128)(2,1)S(1)}, u32[]{:S(2)}, u32[]{:S(2)}) %collective-permute-start.12) | collective-permute-done | bytes 131104 | tf_op jit(solution)/shard_map/ppermute | solution.py:159
  40.8 5.0 %collective-permute-done.13.refs_1_ = bf16[64,1024]{1,0:T(8,128)(2,1)S(1)} collective-permute-done((bf16[64,1024]{1,0:T(8,128)(2,1)S(1)}, bf16[64,1024]{1,0:T(8,128)(2,1)S(1)}, u32[]{:S(2)}, u32[]{:S(2)}) %collective-permute-start.13) | collective-permute-done | bytes 131104 | tf_op jit(solution)/shard_map/ppermute | solution.py:159
  45.8 1.6 %collective-permute-start.15 = (bf16[96,1024]{1,0:T(8,128)(2,1)S(1)}, bf16[96,1024]{1,0:T(8,128)(2,1)S(1)}, u32[]{:S(2)}, u32[]{:S(2)}) collective-permute-start(bf16[96,1024]{1,0:T(8,128)(2,1)S(1)} %pad_maximum_fusion), channel_id=1, source_target_pairs={{8,0},{0,8},{24,16},{16,24},{9,1},{1,9},{25,17},{17,25},{10,2},{2,... | collective-permute-start | bytes 589832 | tf_op jit(solution)/shard_map/ppermute | solution.py:159
  47.3 1.1 %collective-permute-start.16 = (bf16[96,1024]{1,0:T(8,128)(2,1)S(1)}, bf16[96,1024]{1,0:T(8,128)(2,1)S(1)}, u32[]{:S(2)}, u32[]{:S(2)}) collective-permute-start(bf16[96,1024]{1,0:T(8,128)(2,1)S(1)} %pad_maximum_fusion), channel_id=1, source_target_pairs={{16,0},{24,8},{0,16},{8,24},{17,1},{25,9},{1,17},{9,25},{18,2},{26... | collective-permute-start | bytes 589832 | tf_op jit(solution)/shard_map/ppermute | solution.py:159
  48.5 3.0 %collective-permute-done.15.refs_3_ = bf16[96,1024]{1,0:T(8,128)(2,1)S(1)} collective-permute-done((bf16[96,1024]{1,0:T(8,128)(2,1)S(1)}, bf16[96,1024]{1,0:T(8,128)(2,1)S(1)}, u32[]{:S(2)}, u32[]{:S(2)}) %collective-permute-start.15) | collective-permute-done | bytes 196640 | tf_op jit(solution)/shard_map/ppermute | solution.py:159
  51.5 1.5 %collective-permute-done.16.refs_4_ = bf16[96,1024]{1,0:T(8,128)(2,1)S(1)} collective-permute-done((bf16[96,1024]{1,0:T(8,128)(2,1)S(1)}, bf16[96,1024]{1,0:T(8,128)(2,1)S(1)}, u32[]{:S(2)}, u32[]{:S(2)}) %collective-permute-start.16) | collective-permute-done | bytes 196640 | tf_op jit(solution)/shard_map/ppermute | solution.py:159
  53.2 2.2 %shard_map.94.bias_ref = f32[8,144,144]{2,1,0:T(8,128)S(1)} custom-call(f32[2,16,759]{2,1,0:T(8,128)S(1)} %bitcast.13, s32[144,144]{1,0:T(8,128)S(1)} %get-tuple-element.32.index_ref), custom_call_target="tpu_custom_call" | custom-call | flops 1000000000 | bytes 1000000 | tf_op jit(solution)/shard_map/pallas_call | solution.py:275
  55.4 3.5 %second.1 = (bf16[144,512]{1,0:T(8,128)(2,1)S(1)}, bf16[144,256]{1,0:T(8,128)(2,1)S(1)}, bf16[144,256]{1,0:T(8,128)(2,1)S(1)}) custom-call(bf16[1120,256]{1,0:T(8,128)(2,1)S(1)} %first.1.mine_ref, bf16[1120,256]{1,0:T(8,128)(2,1)S(1)} %collective-permute-done.11.other_ref, bf16[2,432,512]{2,1,0:T(8,128)(2,1)S(1)} %get-tuple-element.29.x_ref, ...), custom_call_target="tpu_custom_call" | custom-call | flops 2000000000 | bytes 4000000 | tf_op jit(solution)/shard_map/second/pallas_call | solution.py:570
  58.9 0.5 collective-permute-start.18
  59.5 0.3 most.1
  59.8 0.6 %collective-permute-done.18.got_ref = bf16[144,256]{1,0:T(8,128)(2,1)S(1)} collective-permute-done((bf16[144,256]{1,0:T(8,128)(2,1)S(1)}, bf16[144,256]{1,0:T(8,128)(2,1)S(1)}, u32[]{:S(2)}, u32[]{:S(2)}) %collective-permute-start.18) | collective-permute-done | bytes 73760 | tf_op jit(solution)/shard_map/ppermute | solution.py:29
  60.4 1.0 %last.1 = bf16[72,2,512]{2,1,0:T(2,128)(2,1)} custom-call(f32[144,512]{1,0:T(8,128)S(1)} %get-tuple-element.38.sum_ref, bf16[256,512]{1,0:T(8,128)(2,1)S(1)} %get-tuple-element.39.rows_ref, bf16[144,256]{1,0:T(8,128)(2,1)S(1)} %collective-permute-done.18.got_ref), custom_call_target="tpu_custom_call" | custom-call | flops 100000000 | bytes 1000000 | tf_op jit(solution)/shard_map/last/pallas_call | solution.py:622
  (41 shorter events, 0.4 us)
Async XLA Ops:
  0.0 24.8 %copy-start.5 = (f32[2,759,16]{1,2,0:T(8,128)S(1)}, f32[2,759,16]{1,2,0:T(8,128)}, u32[]{:S(2)}) copy-start(f32[2,759,16]{1,2,0:T(8,128)} %param.13) | copy-start | bytes 291460
  0.0 24.8 %copy-start.4 = (s32[144,144]{1,0:T(8,128)S(1)}, s32[144,144]{1,0:T(8,128)}, u32[]{:S(2)}) copy-start(s32[144,144]{1,0:T(8,128)} %index_ref.1) | copy-start | bytes 248836
  2.1 7.4 %collective-permute-start.5 = (bf16[32,1024]{1,0:T(8,128)(2,1)}, bf16[32,1024]{1,0:T(8,128)(2,1)S(1)}, u32[]{:S(2)}, u32[]{:S(2)}) collective-permute-start(bf16[32,1024]{1,0:T(8,128)(2,1)} %get-tuple-element.25), channel_id=1, source_target_pairs={{1,0},{0,1},{3,2},{2,3},{5,4},{4,5},{7,6},{6,7},{9,8},{8,9},{11,10... | collective-permute-start | bytes 196616 | tf_op jit(solution)/shard_map/ppermute | solution.py:159
  5.2 7.5 %collective-permute-start.6 = (bf16[32,1024]{1,0:T(8,128)(2,1)}, bf16[32,1024]{1,0:T(8,128)(2,1)S(1)}, u32[]{:S(2)}, u32[]{:S(2)}) collective-permute-start(bf16[32,1024]{1,0:T(8,128)(2,1)} %get-tuple-element.25), channel_id=1, source_target_pairs={{2,0},{3,1},{0,2},{1,3},{6,4},{7,5},{4,6},{5,7},{10,8},{11,9},{8,1... | collective-permute-start | bytes 196616 | tf_op jit(solution)/shard_map/ppermute | solution.py:159
  7.8 6.3 %collective-permute-start.7 = (bf16[32,1024]{1,0:T(8,128)(2,1)}, bf16[32,1024]{1,0:T(8,128)(2,1)S(1)}, u32[]{:S(2)}, u32[]{:S(2)}) collective-permute-start(bf16[32,1024]{1,0:T(8,128)(2,1)} %get-tuple-element.25), channel_id=1, source_target_pairs={{3,0},{2,1},{1,2},{0,3},{7,4},{6,5},{5,6},{4,7},{11,8},{10,9},{9,1... | collective-permute-start | bytes 196616 | tf_op jit(solution)/shard_map/ppermute | solution.py:159
  7.8 8.8 %collective-permute-start = (bf16[152,512]{1,0:T(8,128)(2,1)}, bf16[152,512]{1,0:T(8,128)(2,1)S(1)}, u32[]{:S(2)}, u32[]{:S(2)}) collective-permute-start(bf16[152,512]{1,0:T(8,128)(2,1)} %get-tuple-element.23.refs_1_), channel_id=1, source_target_pairs={{8,0},{0,8},{24,16},{16,24},{9,1},{1,9},{25,17},{17,25},{10,2},{2,... | collective-permute-start | bytes 466952 | tf_op jit(solution)/shard_map/ppermute | solution.py:159
  14.1 8.5 %collective-permute-start.10 = (bf16[96,1024]{1,0:T(8,128)(2,1)S(1)}, bf16[96,1024]{1,0:T(8,128)(2,1)S(1)}, u32[]{:S(2)}, u32[]{:S(2)}) collective-permute-start(bf16[96,1024]{1,0:T(8,128)(2,1)S(1)} %constant_dynamic-update-slice_fusion), channel_id=1, source_target_pairs={{24,0},{16,8},{8,16},{0,24},{25,1},{17,9},{9,17},{1,25},{26,2},{18... | collective-permute-start | bytes 589832 | tf_op jit(solution)/shard_map/ppermute | solution.py:159
  16.6 8.2 %collective-permute-start.1 = (bf16[152,512]{1,0:T(8,128)(2,1)S(1)}, bf16[152,512]{1,0:T(8,128)(2,1)S(1)}, u32[]{:S(2)}, u32[]{:S(2)}) collective-permute-start(bf16[152,512]{1,0:T(8,128)(2,1)S(1)} %collective-permute-done.refs_0_), channel_id=1, source_target_pairs={{16,0},{24,8},{0,16},{8,24},{17,1},{25,9},{1,17},{9,25},{18,2},{26... | collective-permute-start | bytes 466952 | tf_op jit(solution)/shard_map/ppermute | solution.py:159
  17.1 10.3 %collective-permute-start.8 = (bf16[96,1024]{1,0:T(8,128)(2,1)S(1)}, bf16[96,1024]{1,0:T(8,128)(2,1)S(1)}, u32[]{:S(2)}, u32[]{:S(2)}) collective-permute-start(bf16[96,1024]{1,0:T(8,128)(2,1)S(1)} %constant_dynamic-update-slice_fusion), channel_id=1, source_target_pairs={{8,0},{0,8},{24,16},{16,24},{9,1},{1,9},{25,17},{17,25},{10,2},{2,... | collective-permute-start | bytes 589832 | tf_op jit(solution)/shard_map/ppermute | solution.py:159
  17.6 10.0 %collective-permute-start.9 = (bf16[96,1024]{1,0:T(8,128)(2,1)S(1)}, bf16[96,1024]{1,0:T(8,128)(2,1)S(1)}, u32[]{:S(2)}, u32[]{:S(2)}) collective-permute-start(bf16[96,1024]{1,0:T(8,128)(2,1)S(1)} %constant_dynamic-update-slice_fusion), channel_id=1, source_target_pairs={{16,0},{24,8},{0,16},{8,24},{17,1},{25,9},{1,17},{9,25},{18,2},{26... | collective-permute-start | bytes 589832 | tf_op jit(solution)/shard_map/ppermute | solution.py:159
  19.2 8.5 %collective-permute-start.3 = (bf16[152,512]{1,0:T(8,128)(2,1)}, bf16[152,512]{1,0:T(8,128)(2,1)S(1)}, u32[]{:S(2)}, u32[]{:S(2)}) collective-permute-start(bf16[152,512]{1,0:T(8,128)(2,1)} %get-tuple-element.23.refs_1_), channel_id=1, source_target_pairs={{4,0},{0,4},{5,1},{1,5},{6,2},{2,6},{7,3},{3,7},{12,8},{8,12},{13,... | collective-permute-start | bytes 466952 | tf_op jit(solution)/shard_map/ppermute | solution.py:29
  22.6 5.1 %collective-permute-start.2 = (bf16[152,512]{1,0:T(8,128)(2,1)S(1)}, bf16[152,512]{1,0:T(8,128)(2,1)S(1)}, u32[]{:S(2)}, u32[]{:S(2)}) collective-permute-start(bf16[152,512]{1,0:T(8,128)(2,1)S(1)} %collective-permute-done.refs_0_), channel_id=1, source_target_pairs={{4,0},{0,4},{5,1},{1,5},{6,2},{2,6},{7,3},{3,7},{12,8},{8,12},{13,... | collective-permute-start | bytes 466952 | tf_op jit(solution)/shard_map/ppermute | solution.py:29
  24.8 2.9 %collective-permute-start.4 = (bf16[152,512]{1,0:T(8,128)(2,1)S(1)}, bf16[152,512]{1,0:T(8,128)(2,1)S(1)}, u32[]{:S(2)}, u32[]{:S(2)}) collective-permute-start(bf16[152,512]{1,0:T(8,128)(2,1)S(1)} %collective-permute-done.1.refs_2_), channel_id=1, source_target_pairs={{4,0},{0,4},{5,1},{1,5},{6,2},{2,6},{7,3},{3,7},{12,8},{8,12},{13,... | collective-permute-start | bytes 466952 | tf_op jit(solution)/shard_map/ppermute | solution.py:29
  24.8 2.8 %copy-start = (bf16[2,128,1536]{2,1,0:T(8,128)(2,1)S(1)}, bf16[2,128,1536]{2,1,0:T(8,128)(2,1)}, u32[]{:S(2)}) copy-start(bf16[2,128,1536]{2,1,0:T(8,128)(2,1)} %own_qkv_ref.3) | copy-start | bytes 2359300
  24.9 2.8 %copy-start.1 = (bf16[2,128,512]{2,1,0:T(8,128)(2,1)S(1)}, bf16[2,128,512]{2,1,0:T(8,128)(2,1)}, u32[]{:S(2)}) copy-start(bf16[2,128,512]{2,1,0:T(8,128)(2,1)} %own_out_ref.3) | copy-start | bytes 786436
  27.4 0.9 %copy-start.2 = (bf16[152,512]{1,0:T(8,128)(2,1)S(1)}, bf16[152,512]{1,0:T(8,128)(2,1)}, u32[]{:S(2)}) copy-start(bf16[152,512]{1,0:T(8,128)(2,1)} %get-tuple-element.23.refs_1_) | copy-start | bytes 466948
  27.4 0.9 %copy-start.3 = (f32[2,512]{1,0:T(2,128)S(1)}, f32[2,512]{1,0:T(2,128)}, u32[]{:S(2)}) copy-start(f32[2,512]{1,0:T(2,128)} %gain_ref.1) | copy-start | bytes 12292
  29.1 3.7 %copy-start.8 = (bf16[64,1024]{1,0:T(8,128)(2,1)S(1)}, bf16[64,1024]{1,0:T(8,128)(2,1)}, u32[]{:S(2)}) copy-start(bf16[64,1024]{1,0:T(8,128)(2,1)} %get-tuple-element.30) | copy-start | bytes 393220
  32.2 23.2 %collective-permute-start.11 = (bf16[1120,256]{1,0:T(8,128)(2,1)S(1)}, bf16[1120,256]{1,0:T(8,128)(2,1)S(1)}, u32[]{:S(2)}, u32[]{:S(2)}) collective-permute-start(bf16[1120,256]{1,0:T(8,128)(2,1)S(1)} %first.1.mine_ref), channel_id=1, source_target_pairs={{4,0},{0,4},{5,1},{1,5},{6,2},{2,6},{7,3},{3,7},{12,8},{8,12},{13,... | collective-permute-start | bytes 1720328 | tf_op jit(solution)/shard_map/ppermute | solution.py:29
  32.8 8.0 %collective-permute-start.12 = (bf16[64,1024]{1,0:T(8,128)(2,1)S(1)}, bf16[64,1024]{1,0:T(8,128)(2,1)S(1)}, u32[]{:S(2)}, u32[]{:S(2)}) collective-permute-start(bf16[64,1024]{1,0:T(8,128)(2,1)S(1)} %copy-done.8), channel_id=1, source_target_pairs={{1,0},{0,1},{3,2},{2,3},{5,4},{4,5},{7,6},{6,7},{9,8},{8,9},{11,10... | collective-permute-start | bytes 393224 | tf_op jit(solution)/shard_map/ppermute | solution.py:159
  32.8 12.9 %collective-permute-start.13 = (bf16[64,1024]{1,0:T(8,128)(2,1)S(1)}, bf16[64,1024]{1,0:T(8,128)(2,1)S(1)}, u32[]{:S(2)}, u32[]{:S(2)}) collective-permute-start(bf16[64,1024]{1,0:T(8,128)(2,1)S(1)} %copy-done.8), channel_id=1, source_target_pairs={{2,0},{3,1},{0,2},{1,3},{6,4},{7,5},{4,6},{5,7},{10,8},{11,9},{8,1... | collective-permute-start | bytes 393224 | tf_op jit(solution)/shard_map/ppermute | solution.py:159
  35.2 10.6 %collective-permute-start.14 = (bf16[64,1024]{1,0:T(8,128)(2,1)S(1)}, bf16[64,1024]{1,0:T(8,128)(2,1)S(1)}, u32[]{:S(2)}, u32[]{:S(2)}) collective-permute-start(bf16[64,1024]{1,0:T(8,128)(2,1)S(1)} %copy-done.8), channel_id=1, source_target_pairs={{3,0},{2,1},{1,2},{0,3},{7,4},{6,5},{5,6},{4,7},{11,8},{10,9},{9,1... | collective-permute-start | bytes 393224 | tf_op jit(solution)/shard_map/ppermute | solution.py:159
  45.8 5.7 %collective-permute-start.15 = (bf16[96,1024]{1,0:T(8,128)(2,1)S(1)}, bf16[96,1024]{1,0:T(8,128)(2,1)S(1)}, u32[]{:S(2)}, u32[]{:S(2)}) collective-permute-start(bf16[96,1024]{1,0:T(8,128)(2,1)S(1)} %pad_maximum_fusion), channel_id=1, source_target_pairs={{8,0},{0,8},{24,16},{16,24},{9,1},{1,9},{25,17},{17,25},{10,2},{2,... | collective-permute-start | bytes 589832 | tf_op jit(solution)/shard_map/ppermute | solution.py:159
  47.3 5.7 %collective-permute-start.16 = (bf16[96,1024]{1,0:T(8,128)(2,1)S(1)}, bf16[96,1024]{1,0:T(8,128)(2,1)S(1)}, u32[]{:S(2)}, u32[]{:S(2)}) collective-permute-start(bf16[96,1024]{1,0:T(8,128)(2,1)S(1)} %pad_maximum_fusion), channel_id=1, source_target_pairs={{16,0},{24,8},{0,16},{8,24},{17,1},{25,9},{1,17},{9,25},{18,2},{26... | collective-permute-start | bytes 589832 | tf_op jit(solution)/shard_map/ppermute | solution.py:159
  53.1 6.4 %collective-permute-start.17 = (bf16[512,256]{1,0:T(8,128)(2,1)S(1)}, bf16[512,256]{1,0:T(8,128)(2,1)S(1)}, u32[]{:S(2)}, u32[]{:S(2)}) collective-permute-start(bf16[512,256]{1,0:T(8,128)(2,1)S(1)} %get-tuple-element.37.wo_mine_ref), channel_id=1, source_target_pairs={{4,0},{0,4},{5,1},{1,5},{6,2},{2,6},{7,3},{3,7},{12,8},{8,12},{13,... | collective-permute-start | bytes 786440 | tf_op jit(solution)/shard_map/ppermute | solution.py:29
  53.2 2.2 %copy-start.6 = (s32[576,1]{1,0:T(8,128)S(1)}, s32[576,1]{1,0:T(8,128)}, u32[]{:S(2)}) copy-start(s32[576,1]{1,0:T(8,128)} %constant.4.clone.src_ref) | copy-start | bytes 6916
  53.2 2.2 %copy-start.7 = (s32[288,1]{1,0:T(8,128)S(1)}, s32[288,1]{1,0:T(8,128)}, u32[]{:S(2)}) copy-start(s32[288,1]{1,0:T(8,128)} %constant.5.clone.back_ref) | copy-start | bytes 3460
  58.9 1.5 %collective-permute-start.18 = (bf16[144,256]{1,0:T(8,128)(2,1)S(1)}, bf16[144,256]{1,0:T(8,128)(2,1)S(1)}, u32[]{:S(2)}, u32[]{:S(2)}) collective-permute-start(bf16[144,256]{1,0:T(8,128)(2,1)S(1)} %get-tuple-element.40), channel_id=1, source_target_pairs={{4,0},{0,4},{5,1},{1,5},{6,2},{2,6},{7,3},{3,7},{12,8},{8,12},{13,... | collective-permute-start | bytes 221192 | tf_op jit(solution)/shard_map/ppermute | solution.py:29

commit v6 on v5

--- a/solution.py
+++ b/solution.py
@@ -2,7 +2,6 @@
 
 import jax
 import jax.numpy as jnp
-import numpy as np
 from jax import lax
 from jax.experimental import pallas as pl
 from jax.experimental.pallas import tpu as pltpu
@@ -159,34 +158,30 @@
     return lax.ppermute(block, axis, [(partner(i, step, size), i) for i in range(size)])
 
 
+def as_column(lanes, size):
+    return jnp.transpose(lanes.astype(F32))[0:size, 0:1].astype(jnp.int32)
+
+
 def window_sources():
-    src = np.zeros((2, 2, WH, WW, WZ), np.int32)
-    for a in range(2):
-        for v in range(2):
-            for dh in range(WH):
-                for dw in range(WW):
-                    for dz in range(WZ):
-                        row = dh + (WH // 2 if a else -(WH // 2))
-                        col = (WW // 2 + WW * v + dw) % (2 * WW)
-                        level = (dz + 1) % WZ
-                        t = (row + WH) * WW * WZ + (col % WW) * WZ + level
-                        src[a, v, dh, dw, dz] = (col // WW) * KEPT + t - KEEP0
-    return src.reshape(-1, 1)
+    token = lax.broadcasted_iota(jnp.int32, (8, 5 * 128), 1)
+    a, v = token // (2 * WIN), token // WIN % 2
+    dh, dw, dz = token % WIN // (WW * WZ), token % (WW * WZ) // WZ, token % WZ
+    row = dh + WH * a - WH // 2
+    col = (WW // 2 + WW * v + dw) % (2 * WW)
+    level = (dz + 1) % WZ
+    return as_column(col // WW * KEPT + (row + WH) * WW * WZ + col % WW * WZ + level - KEEP0, 4 * WIN)
 
 
 def tile_sources():
-    src = np.zeros((2, WH, WW, WZ), np.int32)
-    for l in range(2):
-        for row in range(WH):
-            for cw in range(WW):
-                for level in range(WZ):
-                    a = 0 if row < WH // 2 else 1
-                    dh = (row + WH // 2) % WH
-                    col = (WW * l + cw - WW // 2) % (2 * WW)
-                    dz = (level - 1) % WZ
-                    t = dh * WW * WZ + (col % WW) * WZ + dz - (0 if a else KEEP0)
-                    src[l, row, cw, level] = (a * 2 + col // WW) * PART + t
-    return src.reshape(-1, 1)
+    token = lax.broadcasted_iota(jnp.int32, (8, 3 * 128), 1)
+    tile = token // WIN
+    row, cw, level = token % WIN // (WW * WZ), token % (WW * WZ) // WZ, token % WZ
+    a = row // (WH // 2)
+    dh = (row + WH // 2) % WH
+    col = (WW * tile + cw + 2 * WW - WW // 2) % (2 * WW)
+    dz = (level + WZ - 1) % WZ
+    found = (a * 2 + col // WW) * PART + dh * WW * WZ + col % WW * WZ + dz - KEEP0 * (1 - a)
+    return as_column(found, 2 * WIN)
 
 
 def one_hot(sources, width):
@@ -209,7 +204,7 @@
     return (shifted * lax.rsqrt(variance + 1e-05) * gain_row).astype(BF16)
 
 
-def gather_heads(b, table_ref, index, table, bias_ref):
+def gather_heads(b, start, table_ref, index, table, bias_ref):
     me = lax.axis_index("lon")
     heads = table_ref[b, pl.ds(pl.multiple_of(MY_HEADS * me, MY_HEADS), MY_HEADS), :]
     table[:, 0:BIAS_ROWS] = heads * LOG2E
@@ -219,10 +214,11 @@
         low = at & 127
         chunk = at >> 7
         masks = [chunk == k for k in range(chunks)]
-        for h in range(MY_HEADS):
+        for h in range(bias_ref.shape[0]):
             acc = None
+            at_h = slice(start + h, start + h + 1)
             for k in range(chunks):
-                row = jnp.broadcast_to(table[h : h + 1, 128 * k : 128 * k + 128], (8, 128))
+                row = jnp.broadcast_to(table[at_h, 128 * k : 128 * k + 128], (8, 128))
                 got = jnp.take_along_axis(row, low, axis=1, mode="promise_in_bounds")
                 acc = got if acc is None else jnp.where(masks[k], got, acc)
             put(h, acc)
@@ -262,19 +258,19 @@
     moved_ref[...] = (
         nn_dot(move, parts[0:WIN]) * 256.0 + nn_dot(move, parts[WIN : 2 * WIN])
     ).astype(jnp.int32)
-    gather_heads(0, table_ref, moved_ref, table, bias_ref)
-
-
-def bias1_kernel(table_ref, index_ref, bias_ref, table):
-    gather_heads(1, table_ref, index_ref, table, bias_ref)
-
-
-def bias_call(b, table, index):
-    bias = jax.ShapeDtypeStruct((MY_HEADS, WIN, WIN), F32)
+    gather_heads(0, 0, table_ref, moved_ref, table, bias_ref)
+
+
+def bias1_kernel(start, table_ref, index_ref, bias_ref, table):
+    gather_heads(1, start, table_ref, index_ref, table, bias_ref)
+
+
+def bias_call(kernel, heads, more, table, index):
+    bias = jax.ShapeDtypeStruct((heads, WIN, WIN), F32)
     moved = jax.ShapeDtypeStruct((WIN, WIN), jnp.int32)
     return pl.pallas_call(
-        bias1_kernel if b else bias0_kernel,
-        out_shape=bias if b else (bias, moved),
+        kernel,
+        out_shape=(bias, moved) if more else bias,
         scratch_shapes=[pltpu.VMEM((MY_HEADS, (BIAS_ROWS + 127) // 128 * 128), F32)],
         compiler_params=vmem(8),
         cost_estimate=pl.CostEstimate(flops=10**9, bytes_accessed=10**6, transcendentals=0),
@@ -463,25 +459,24 @@
         scores = nt_dot(q_all, k_g)
         probs = []
         for j in range(GROUP):
-            s = scores[n * j : n * (j + 1)] * SCALE2 + bias_at(GROUP * g + j)
+            s = scores[n * j : n * (j + 1)] + bias_at(GROUP * g + j)
             if allowed is not None:
                 s = jnp.where(allowed, s, NEG)
             peak = jnp.max(s, axis=-1, keepdims=True)
             probs.append(jnp.exp2(s - peak).astype(BF16))
         mixed = nn_dot(jnp.concatenate(probs, axis=0), v_g)
-        acc = None
-        for j in range(GROUP):
-            m = mixed[n * j : n * (j + 1)]
-            value = m[:, 0:128] / m[:, 128:256]
-            acc = value if acc is None else jnp.where(owns[j], value, acc)
-        put(128 * g, acc.astype(BF16))
+        value, total = mixed[0:n, 0:128], mixed[0:n, 128:256]
+        for j in range(1, GROUP):
+            value = jnp.where(owns[j], mixed[n * j : n * (j + 1), 0:128], value)
+            total = jnp.where(owns[j], mixed[n * j : n * (j + 1), 128:256], total)
+        put(128 * g, (value / total).astype(BF16))
 
 
 def project(n, w_ref, q_s, k_s, v_s):
-    both = nn_dot(n, w_ref[...]).astype(BF16)
-    q_s[...] = both[:, 0:MINE]
-    k_s[...] = both[:, MINE : 2 * MINE]
-    v_s[...] = both[:, 2 * MINE : 3 * MINE]
+    both = nn_dot(n, w_ref[...])
+    q_s[...] = (both[:, 0:MINE] * SCALE2).astype(BF16)
+    k_s[...] = both[:, MINE : 2 * MINE].astype(BF16)
+    v_s[...] = both[:, 2 * MINE : 3 * MINE].astype(BF16)
 
 
 def first_kernel(n_ref, w_ref, bias_ref, wo_ref, o_ref, q_s, k_s, v_s):
@@ -524,9 +519,8 @@
     ref[:, pl.ds(pl.multiple_of(width * (1 - me), width), width)] = other
 
 
-def second_kernel(
-    mine_ref, other_ref, x_ref, gain_ref, src_ref, w_ref, bias_ref,
-    row_ref, col_ref, back_ref, mid_ref, keep_ref, send_ref, o_s, wo_s, m_s, n_s, q_s, k_s, v_s, a_s, t_s,
+def middle_kernel(
+    mine_ref, other_ref, x_ref, gain_ref, mid_ref, win_ref, o_s, wo_s, m_s, n_s
 ):
     me = lax.axis_index("lon")
     tokens = PAIR * KEPT
@@ -539,46 +533,65 @@
         m_s[l] = value
         n_s[rows, :] = norm_rows(value.astype(F32), gain_ref[1:2, :])
     mid_ref[...] = m_s[me, PART : PART + WIN, :]
-    windows = nn_dot(one_hot(src_ref[...], tokens), n_s[...]).astype(BF16)
-    project(windows, w_ref, q_s, k_s, v_s)
-    for w in range(4):
-        q0, q1 = (KEEP0, WIN) if w < 2 else (0, PART)
-        t = WIN * w
-        allowed = col_ref[q0:q1, w : w + 1] == row_ref[w : w + 1, :]
-
-        def put(col, value, w=w):
-            a_s[PART * w : PART * (w + 1), col : col + 128] = value
-
-        window_attend(
-            q_s[t + q0 : t + q1, :],
-            k_s[t : t + WIN, :],
-            v_s[t : t + WIN, :],
-            lambda h, q0=q0, q1=q1: bias_ref[h, q0:q1, :],
-            allowed,
-            put,
-        )
-    tiles = nn_dot(one_hot(back_ref[...], 4 * PART), a_s[...]).astype(BF16)
-    t_s[0] = tiles[0:WIN]
-    t_s[1] = tiles[WIN : 2 * WIN]
-    keep_ref[...] = t_s[me]
-    send_ref[...] = t_s[1 - me]
-
-
-def second_call(mine, other, x, gain, weight, bias, row, col):
+    win_ref[...] = nn_dot(one_hot(window_sources(), tokens), n_s[...]).astype(BF16)
+
+
+def middle_call(mine, other, x, gain):
     tokens = PAIR * KEPT
-    qkv = pltpu.VMEM((4 * WIN, MINE), BF16)
-    return pl.pallas_call(
-        second_kernel,
+    return pl.pallas_call(
+        middle_kernel,
         out_shape=(
             jax.ShapeDtypeStruct((WIN, D), BF16),
-            jax.ShapeDtypeStruct((WIN, MINE), BF16),
-            jax.ShapeDtypeStruct((WIN, MINE), BF16),
+            jax.ShapeDtypeStruct((4 * WIN, D), BF16),
         ),
         scratch_shapes=[
             pltpu.VMEM((tokens, D), BF16),
             pltpu.VMEM((D, D), BF16),
             pltpu.VMEM((PAIR, KEPT, D), BF16),
             pltpu.VMEM((tokens, D), BF16),
+        ],
+        compiler_params=vmem(16),
+        cost_estimate=pl.CostEstimate(flops=10**9, bytes_accessed=3 * 10**6, transcendentals=0),
+        name="middle",
+    )(mine, other, x, gain)
+
+
+def second_kernel(
+    win_ref, w_ref, bias_a, bias_b, row_ref, col_ref, keep_ref, send_ref, q_s, k_s, v_s, a_s, t_s
+):
+    me = lax.axis_index("lon")
+    half = MY_HEADS // 2
+    project(win_ref[...], w_ref, q_s, k_s, v_s)
+    for w in range(4):
+        q0, q1 = (KEEP0, WIN) if w < 2 else (0, PART)
+        t = WIN * w
+        allowed = col_ref[q0:q1, w : w + 1] == row_ref[w : w + 1, :]
+
+        def put(col, value, w=w):
+            a_s[PART * w : PART * (w + 1), col : col + 128] = value
+
+        window_attend(
+            q_s[t + q0 : t + q1, :],
+            k_s[t : t + WIN, :],
+            v_s[t : t + WIN, :],
+            lambda h, q0=q0, q1=q1: (bias_a, bias_b)[h // half][h % half, q0:q1, :],
+            allowed,
+            put,
+        )
+    tiles = nn_dot(one_hot(tile_sources(), 4 * PART), a_s[...]).astype(BF16)
+    t_s[0] = tiles[0:WIN]
+    t_s[1] = tiles[WIN : 2 * WIN]
+    keep_ref[...] = t_s[me]
+    send_ref[...] = t_s[1 - me]
+
+
+def second_call(windows, weight, bias_a, bias_b, row, col):
+    qkv = pltpu.VMEM((4 * WIN, MINE), BF16)
+    half = jax.ShapeDtypeStruct((WIN, MINE), BF16)
+    return pl.pallas_call(
+        second_kernel,
+        out_shape=(half, half),
+        scratch_shapes=[
             qkv,
             qkv,
             qkv,
@@ -588,10 +601,7 @@
         compiler_params=vmem(24),
         cost_estimate=pl.CostEstimate(flops=2 * 10**9, bytes_accessed=4 * 10**6, transcendentals=10**6),
         name="second",
-    )(
-        mine, other, x, gain, jnp.asarray(window_sources()), weight, bias,
-        row, col, jnp.asarray(tile_sources()),
-    )
+    )(windows, weight, bias_a, bias_b, row, col)
 
 
 def most_kernel(mid_ref, keep_ref, wo_mine_ref, wo_other_ref, sum_ref, rows_ref, wo_s):
@@ -660,7 +670,7 @@
     far0 = spread(part0, "fsdp", range(1, n_fsdp))
     mirrored = n_lat == 4
     side = heard_from(tile, "lat", 1) if mirrored else passed_along(tile, "lat", 1)
-    cross = heard_from(side, "lat", 2) if mirrored else passed_along(tile, "lat", -1)
+    cross = heard_from(tile, "lat", 3) if mirrored else passed_along(tile, "lat", -1)
     far1 = spread(part1, "fsdp", range(1, n_fsdp))
     near0 = spread(jnp.concatenate(far0, axis=0), "lat", plan[0][1])
     near1 = spread(jnp.concatenate([f[:part] for f in far1], axis=0), "lat", plan[1][1])
@@ -670,11 +680,16 @@
     table = jnp.transpose(rel_bias, (0, 2, 1))
     params = (qkv_weight, out_weight)
     w0, wo0 = join_call(0, n_lat, plan[0][1], plan[0][0], *params, far0, near0)
-    bias0, index = bias_call(0, table, bias_index)
+    bias0, index = bias_call(bias0_kernel, MY_HEADS, True, table, bias_index)
     o0 = first_call(normed, w0, bias0, wo0)
     w1, wo1 = join_call(1, n_lat, plan[1][1], plan[1][0], *params, far1, near1)
-    bias1 = bias_call(1, table, index)
-    mid, keep, send = second_call(o0, swap(o0), x, norm_gain, w1, bias1, tag_row, tag_col)
+    half = MY_HEADS // 2
+    bias1 = [
+        bias_call(functools.partial(bias1_kernel, half * i), half, False, table, index)
+        for i in range(2)
+    ]
+    mid, windows = middle_call(o0, swap(o0), x, norm_gain)
+    keep, send = second_call(windows, w1, *bias1, tag_row, tag_col)
     total, rows = most_call(mid, keep, wo1, swap(wo1))
     out = last_call(total, rows, swap(send))
     return jnp.transpose(out.reshape(WH, WW, WZ, D), (2, 0, 1, 3))[None]

time: 62 us -> 65.1 us (1.050)
  waiting for transfers between devices: 24.1 us -> 26.4 us
    ppermute x13, waiting for transfers between devices: 23.5 us -> 25.8 us  [heard_from(): lax.ppermute(block, axis, [(partner(i, step, size), i) for i in range(siz...]
    pallas_call x3 -> x5, Pallas kernels: 8.27 us -> 8.42 us  [the longest x3 4.54 us: bias_call(): pl.pallas_call(kernel, out_shape=(bias, moved) if more else bias, scratch...]
  transfers between devices with their start and end apart: 19 -> 19, of which waited for: 10 -> 9; matrix products, arithmetic and copies ran while one was open for 0% -> 0% of each run, Pallas kernels for 14% -> 14%
where the time goes in v6:
time: 65.1 us; the launch traced here: 64.1 us
  waiting for transfers between devices  26.4 us (41%)
  starting transfers between devices  21 us (32%)
  Pallas kernels  15.8 us (24%)
  local copies, waits for them, and re-layouts  0.78 us (1%)
    ppermute x13, waiting for transfers between devices, heard_from(): lax.ppermute(block, axis, [(partner(i, step, size), i) for i in range(siz...  25.8 us
    ppermute x13, starting transfers between devices, heard_from(): lax.ppermute(block, axis, [(partner(i, step, size), i) for i in range(siz...  19.7 us
    pallas_call x3, Pallas kernels, bias_call(): pl.pallas_call(kernel, out_shape=(bias, moved) if more else bias, scratch...  4.54 us
    pallas_call x1, Pallas kernels, first_call(): pl.pallas_call(first_kernel, out_shape=jax.ShapeDtypeStruct((PAIR * KEPT...  3.13 us
    pallas_call x1, Pallas kernels, second_call(): pl.pallas_call(second_kernel, out_shape=(half, half), scratch_shapes=[qkv...  2.34 us
    pallas_call x1, Pallas kernels, open_call(): pl.pallas_call(functools.partial(open_kernel, wide), out_shape=(jax.Shape...  2.11 us
    pallas_call x1, Pallas kernels, middle_call(): pl.pallas_call(middle_kernel, out_shape=(jax.ShapeDtypeStruct((WIN, D), B...  1.54 us
  transfers between devices with their start and end apart: 19, of which 9 were waited for; matrix products, arithmetic and copies ran while one was open for 0% of the time, Pallas kernels for 14%

profile of v6, /device:TPU:0, one launch (start us, length us, event | category | flops | bytes accessed | tf_op | source)
XLA Modules:
  0.0 64.1 jit_solution(17950971723848819825)
XLA Ops:
  0.0 2.1 %open.1 = (bf16[32,1024]{1,0:T(8,128)(2,1)}, bf16[64,1024]{1,0:T(8,128)(2,1)}, bf16[152,512]{1,0:T(8,128)(2,1)}) custom-call(bf16[72,2,512]{2,1,0:T(2,128)(2,1)} %bitcast.15, s32[6,2,12]{2,1,0:T(2,128)} %bitcast.16, bf16[2,128,1536]{2,1,0:T(8,128)(2,1)} %own_qkv_ref.3, bf16[2,128,512]{2,1,0:T(8,128)(2,1)} %own_out_ref.3), custom_call_target="tpu_custom_call" | custom-call | flops 1000000 | bytes 1000000 | tf_op jit(solution)/shard_map/open/pallas_call | solution.py:336
  2.1 3.1 %collective-permute-start.5 = (bf16[32,1024]{1,0:T(8,128)(2,1)}, bf16[32,1024]{1,0:T(8,128)(2,1)S(1)}, u32[]{:S(2)}, u32[]{:S(2)}) collective-permute-start(bf16[32,1024]{1,0:T(8,128)(2,1)} %get-tuple-element.26), channel_id=1, source_target_pairs={{1,0},{0,1},{3,2},{2,3},{5,4},{4,5},{7,6},{6,7},{9,8},{8,9},{11,10... | collective-permute-start | bytes 196616 | tf_op jit(solution)/shard_map/ppermute | solution.py:158
  5.3 2.6 %collective-permute-start.6 = (bf16[32,1024]{1,0:T(8,128)(2,1)}, bf16[32,1024]{1,0:T(8,128)(2,1)S(1)}, u32[]{:S(2)}, u32[]{:S(2)}) collective-permute-start(bf16[32,1024]{1,0:T(8,128)(2,1)} %get-tuple-element.26), channel_id=1, source_target_pairs={{2,0},{3,1},{0,2},{1,3},{6,4},{7,5},{4,6},{5,7},{10,8},{11,9},{8,1... | collective-permute-start | bytes 196616 | tf_op jit(solution)/shard_map/ppermute | solution.py:158
  7.9 4.9 %collective-permute-done.6.refs_1_ = bf16[32,1024]{1,0:T(8,128)(2,1)S(1)} collective-permute-done((bf16[32,1024]{1,0:T(8,128)(2,1)}, bf16[32,1024]{1,0:T(8,128)(2,1)S(1)}, u32[]{:S(2)}, u32[]{:S(2)}) %collective-permute-start.6) | collective-permute-done | bytes 65568 | tf_op jit(solution)/shard_map/ppermute | solution.py:158
  12.7 1.4 %collective-permute-done.7.refs_2_ = bf16[32,1024]{1,0:T(8,128)(2,1)S(1)} collective-permute-done((bf16[32,1024]{1,0:T(8,128)(2,1)}, bf16[32,1024]{1,0:T(8,128)(2,1)S(1)}, u32[]{:S(2)}, u32[]{:S(2)}) %collective-permute-start.7) | collective-permute-done | bytes 65568 | tf_op jit(solution)/shard_map/ppermute | solution.py:158
  14.2 2.4 %collective-permute-start.10 = (bf16[96,1024]{1,0:T(8,128)(2,1)S(1)}, bf16[96,1024]{1,0:T(8,128)(2,1)S(1)}, u32[]{:S(2)}, u32[]{:S(2)}) collective-permute-start(bf16[96,1024]{1,0:T(8,128)(2,1)S(1)} %constant_dynamic-update-slice_fusion), channel_id=1, source_target_pairs={{24,0},{16,8},{8,16},{0,24},{25,1},{17,9},{9,17},{1,25},{26,2},{18... | collective-permute-start | bytes 589832 | tf_op jit(solution)/shard_map/ppermute | solution.py:158
  16.6 0.5 collective-permute-start
  17.1 1.4 %collective-permute-start.1 = (bf16[152,512]{1,0:T(8,128)(2,1)}, bf16[152,512]{1,0:T(8,128)(2,1)S(1)}, u32[]{:S(2)}, u32[]{:S(2)}) collective-permute-start(bf16[152,512]{1,0:T(8,128)(2,1)} %get-tuple-element.24.refs_1_), channel_id=1, source_target_pairs={{24,0},{16,8},{8,16},{0,24},{25,1},{17,9},{9,17},{1,25},{26,2},{18... | collective-permute-start | bytes 466952 | tf_op jit(solution)/shard_map/ppermute | solution.py:158
  18.6 0.5 collective-permute-start.8
  19.1 1.5 %collective-permute-start.9 = (bf16[96,1024]{1,0:T(8,128)(2,1)S(1)}, bf16[96,1024]{1,0:T(8,128)(2,1)S(1)}, u32[]{:S(2)}, u32[]{:S(2)}) collective-permute-start(bf16[96,1024]{1,0:T(8,128)(2,1)S(1)} %constant_dynamic-update-slice_fusion), channel_id=1, source_target_pairs={{16,0},{24,8},{0,16},{8,24},{17,1},{25,9},{1,17},{9,25},{18,2},{26... | collective-permute-start | bytes 589832 | tf_op jit(solution)/shard_map/ppermute | solution.py:158
  20.6 5.6 %collective-permute-done.refs_0_ = bf16[152,512]{1,0:T(8,128)(2,1)S(1)} collective-permute-done((bf16[152,512]{1,0:T(8,128)(2,1)}, bf16[152,512]{1,0:T(8,128)(2,1)S(1)}, u32[]{:S(2)}, u32[]{:S(2)}) %collective-permute-start) | collective-permute-done | bytes 155680 | tf_op jit(solution)/shard_map/ppermute | solution.py:158
  26.3 2.6 %collective-permute-done.1.refs_2_ = bf16[152,512]{1,0:T(8,128)(2,1)S(1)} collective-permute-done((bf16[152,512]{1,0:T(8,128)(2,1)}, bf16[152,512]{1,0:T(8,128)(2,1)S(1)}, u32[]{:S(2)}, u32[]{:S(2)}) %collective-permute-start.1) | collective-permute-done | bytes 155680 | tf_op jit(solution)/shard_map/ppermute | solution.py:158
  29.4 2.6 %shard_map.74 = (f32[8,144,144]{2,1,0:T(8,128)S(1)}, s32[144,144]{1,0:T(8,128)S(1)}) custom-call(f32[2,16,759]{2,1,0:T(8,128)S(1)} %bitcast.12, s32[144,144]{1,0:T(8,128)S(1)} %copy-done.4), custom_call_target="tpu_custom_call" | custom-call | flops 1000000000 | bytes 1000000 | tf_op jit(solution)/shard_map/pallas_call | solution.py:271
  32.2 0.7 %copy-done.2 = bf16[152,512]{1,0:T(8,128)(2,1)S(1)} copy-done((bf16[152,512]{1,0:T(8,128)(2,1)S(1)}, bf16[152,512]{1,0:T(8,128)(2,1)}, u32[]{:S(2)}) %copy-start.2) | copy-done | bytes 155672
  32.9 0.7 %enter.1 = (bf16[2,432,512]{2,1,0:T(8,128)(2,1)S(1)}, bf16[2,432,512]{2,1,0:T(8,128)(2,1)S(1)}, f32[8,144]{1,0:T(8,128)S(1)}, f32[144,8]{1,0:T(8,128)S(1)}) custom-call(bf16[152,512]{1,0:T(8,128)(2,1)S(1)} %collective-permute-done.refs_0_, bf16[152,512]{1,0:T(8,128)(2,1)S(1)} %copy-done.2, bf16[152,512]{1,0:T(8,128)(2,1)S(1)} %collective-permute-done.1.refs_2_, ...), custom_call_target="tpu_custom_call" | custom-call | flops 100000000 | bytes 2000000 | tf_op jit(solution)/shard_map/enter/pallas_call | solution.py:394
  33.6 3.1 %first.1.mine_ref = bf16[1120,256]{1,0:T(8,128)(2,1)S(1)} custom-call(bf16[2,432,512]{2,1,0:T(8,128)(2,1)S(1)} %get-tuple-element.25.n_ref, bf16[512,768]{1,0:T(8,128)(2,1)S(1)} %get-tuple-element.27.w_ref, f32[8,144,144]{2,1,0:T(8,128)S(1)} %get-tuple-element.28.bias_ref, bf16[512,256]{1,0:T(8,128)(2,1)S(1)} %get-tuple-element.29.wo_ref), custom_call_target="tpu_custom_call" | custom-call | flops 2000000000 | bytes 4000000 | tf_op jit(solution)/shard_map/first/pallas_call | solution.py:506
  36.8 0.6 collective-permute-start.12
  37.4 1.7 %collective-permute-start.13 = (bf16[64,1024]{1,0:T(8,128)(2,1)S(1)}, bf16[64,1024]{1,0:T(8,128)(2,1)S(1)}, u32[]{:S(2)}, u32[]{:S(2)}) collective-permute-start(bf16[64,1024]{1,0:T(8,128)(2,1)S(1)} %copy-done.6), channel_id=1, source_target_pairs={{2,0},{3,1},{0,2},{1,3},{6,4},{7,5},{4,6},{5,7},{10,8},{11,9},{8,1... | collective-permute-start | bytes 393224 | tf_op jit(solution)/shard_map/ppermute | solution.py:158
  39.1 2.2 %collective-permute-start.14 = (bf16[64,1024]{1,0:T(8,128)(2,1)S(1)}, bf16[64,1024]{1,0:T(8,128)(2,1)S(1)}, u32[]{:S(2)}, u32[]{:S(2)}) collective-permute-start(bf16[64,1024]{1,0:T(8,128)(2,1)S(1)} %copy-done.6), channel_id=1, source_target_pairs={{3,0},{2,1},{1,2},{0,3},{7,4},{6,5},{5,6},{4,7},{11,8},{10,9},{9,1... | collective-permute-start | bytes 393224 | tf_op jit(solution)/shard_map/ppermute | solution.py:158
  41.3 4.1 %collective-permute-done.12.refs_0_ = bf16[64,1024]{1,0:T(8,128)(2,1)S(1)} collective-permute-done((bf16[64,1024]{1,0:T(8,128)(2,1)S(1)}, bf16[64,1024]{1,0:T(8,128)(2,1)S(1)}, u32[]{:S(2)}, u32[]{:S(2)}) %collective-permute-start.12) | collective-permute-done | bytes 131104 | tf_op jit(solution)/shard_map/ppermute | solution.py:158
  45.4 5.0 %collective-permute-done.13.refs_1_ = bf16[64,1024]{1,0:T(8,128)(2,1)S(1)} collective-permute-done((bf16[64,1024]{1,0:T(8,128)(2,1)S(1)}, bf16[64,1024]{1,0:T(8,128)(2,1)S(1)}, u32[]{:S(2)}, u32[]{:S(2)}) %collective-permute-start.13) | collective-permute-done | bytes 131104 | tf_op jit(solution)/shard_map/ppermute | solution.py:158
  50.4 1.6 %collective-permute-start.15 = (bf16[96,1024]{1,0:T(8,128)(2,1)S(1)}, bf16[96,1024]{1,0:T(8,128)(2,1)S(1)}, u32[]{:S(2)}, u32[]{:S(2)}) collective-permute-start(bf16[96,1024]{1,0:T(8,128)(2,1)S(1)} %pad_maximum_fusion), channel_id=1, source_target_pairs={{8,0},{0,8},{24,16},{16,24},{9,1},{1,9},{25,17},{17,25},{10,2},{2,... | collective-permute-start | bytes 589832 | tf_op jit(solution)/shard_map/ppermute | solution.py:158
  51.9 1.5 %collective-permute-start.16 = (bf16[96,1024]{1,0:T(8,128)(2,1)S(1)}, bf16[96,1024]{1,0:T(8,128)(2,1)S(1)}, u32[]{:S(2)}, u32[]{:S(2)}) collective-permute-start(bf16[96,1024]{1,0:T(8,128)(2,1)S(1)} %pad_maximum_fusion), channel_id=1, source_target_pairs={{16,0},{24,8},{0,16},{8,24},{17,1},{25,9},{1,17},{9,25},{18,2},{26... | collective-permute-start | bytes 589832 | tf_op jit(solution)/shard_map/ppermute | solution.py:158
  53.5 1.0 %shard_map.76.bias_a = f32[4,144,144]{2,1,0:T(8,128)S(1)} custom-call(f32[2,16,759]{2,1,0:T(8,128)S(1)} %bitcast.13, s32[144,144]{1,0:T(8,128)S(1)} %get-tuple-element.35.index_ref), custom_call_target="tpu_custom_call" | custom-call | flops 1000000000 | bytes 1000000 | tf_op jit(solution)/shard_map/pallas_call | solution.py:271
  54.4 1.0 %shard_map.77.bias_b = f32[4,144,144]{2,1,0:T(8,128)S(1)} custom-call(f32[2,16,759]{2,1,0:T(8,128)S(1)} %bitcast.14, s32[144,144]{1,0:T(8,128)S(1)} %get-tuple-element.35.index_ref), custom_call_target="tpu_custom_call" | custom-call | flops 1000000000 | bytes 1000000 | tf_op jit(solution)/shard_map/pallas_call | solution.py:271
  55.4 0.9 %collective-permute-done.15.refs_3_ = bf16[96,1024]{1,0:T(8,128)(2,1)S(1)} collective-permute-done((bf16[96,1024]{1,0:T(8,128)(2,1)S(1)}, bf16[96,1024]{1,0:T(8,128)(2,1)S(1)}, u32[]{:S(2)}, u32[]{:S(2)}) %collective-permute-start.15) | collective-permute-done | bytes 196640 | tf_op jit(solution)/shard_map/ppermute | solution.py:158
  56.4 1.2 %collective-permute-done.16.refs_4_ = bf16[96,1024]{1,0:T(8,128)(2,1)S(1)} collective-permute-done((bf16[96,1024]{1,0:T(8,128)(2,1)S(1)}, bf16[96,1024]{1,0:T(8,128)(2,1)S(1)}, u32[]{:S(2)}, u32[]{:S(2)}) %collective-permute-start.16) | collective-permute-done | bytes 196640 | tf_op jit(solution)/shard_map/ppermute | solution.py:158
  57.8 1.5 %middle.1 = (bf16[144,512]{1,0:T(8,128)(2,1)S(1)}, bf16[576,512]{1,0:T(8,128)(2,1)S(1)}) custom-call(bf16[1120,256]{1,0:T(8,128)(2,1)S(1)} %first.1.mine_ref, bf16[1120,256]{1,0:T(8,128)(2,1)S(1)} %collective-permute-done.11.other_ref, bf16[2,432,512]{2,1,0:T(8,128)(2,1)S(1)} %get-tuple-element.30.x_ref, f32[2,512]{1,0:T(2,128)S(1)} %copy-done.3), custom_call_target="tpu_custom_call" | custom-call | flops 1000000000 | bytes 3000000 | tf_op jit(solution)/shard_map/middle/pallas_call | solution.py:541
  59.3 2.3 %second.1 = (bf16[144,256]{1,0:T(8,128)(2,1)S(1)}, bf16[144,256]{1,0:T(8,128)(2,1)S(1)}) custom-call(bf16[576,512]{1,0:T(8,128)(2,1)S(1)} %get-tuple-element.32.win_ref, bf16[512,768]{1,0:T(8,128)(2,1)S(1)} %get-tuple-element.34.w_ref, f32[4,144,144]{2,1,0:T(8,128)S(1)} %shard_map.76.bias_a, f32[4,144,144]{2,1,0:T(8,128)S(1)} %shard_map.77.bias_b, ...), custom_call_target="tpu_custom_call" | custom-call | flops 2000000000 | bytes 4000000 | tf_op jit(solution)/shard_map/second/pallas_call | solution.py:591
  61.7 0.6 collective-permute-start.18
  62.5 0.6 collective-permute-done.18.got_ref
  63.2 1.0 %last.1 = bf16[72,2,512]{2,1,0:T(2,128)(2,1)} custom-call(f32[144,512]{1,0:T(8,128)S(1)} %get-tuple-element.40.sum_ref, bf16[256,512]{1,0:T(8,128)(2,1)S(1)} %get-tuple-element.41.rows_ref, bf16[144,256]{1,0:T(8,128)(2,1)S(1)} %collective-permute-done.18.got_ref), custom_call_target="tpu_custom_call" | custom-call | flops 100000000 | bytes 1000000 | tf_op jit(solution)/shard_map/last/pallas_call | solution.py:632
  (39 shorter events, 1.2 us)
Async XLA Ops:
  0.0 29.4 %copy-start.5 = (f32[2,759,16]{1,2,0:T(8,128)S(1)}, f32[2,759,16]{1,2,0:T(8,128)}, u32[]{:S(2)}) copy-start(f32[2,759,16]{1,2,0:T(8,128)} %param.11) | copy-start | bytes 291460
  0.0 29.4 %copy-start.4 = (s32[144,144]{1,0:T(8,128)S(1)}, s32[144,144]{1,0:T(8,128)}, u32[]{:S(2)}) copy-start(s32[144,144]{1,0:T(8,128)} %index_ref.1) | copy-start | bytes 248836
  2.1 5.7 %collective-permute-start.5 = (bf16[32,1024]{1,0:T(8,128)(2,1)}, bf16[32,1024]{1,0:T(8,128)(2,1)S(1)}, u32[]{:S(2)}, u32[]{:S(2)}) collective-permute-start(bf16[32,1024]{1,0:T(8,128)(2,1)} %get-tuple-element.26), channel_id=1, source_target_pairs={{1,0},{0,1},{3,2},{2,3},{5,4},{4,5},{7,6},{6,7},{9,8},{8,9},{11,10... | collective-permute-start | bytes 196616 | tf_op jit(solution)/shard_map/ppermute | solution.py:158
  5.3 7.5 %collective-permute-start.6 = (bf16[32,1024]{1,0:T(8,128)(2,1)}, bf16[32,1024]{1,0:T(8,128)(2,1)S(1)}, u32[]{:S(2)}, u32[]{:S(2)}) collective-permute-start(bf16[32,1024]{1,0:T(8,128)(2,1)} %get-tuple-element.26), channel_id=1, source_target_pairs={{2,0},{3,1},{0,2},{1,3},{6,4},{7,5},{4,6},{5,7},{10,8},{11,9},{8,1... | collective-permute-start | bytes 196616 | tf_op jit(solution)/shard_map/ppermute | solution.py:158
  7.8 6.3 %collective-permute-start.7 = (bf16[32,1024]{1,0:T(8,128)(2,1)}, bf16[32,1024]{1,0:T(8,128)(2,1)S(1)}, u32[]{:S(2)}, u32[]{:S(2)}) collective-permute-start(bf16[32,1024]{1,0:T(8,128)(2,1)} %get-tuple-element.26), channel_id=1, source_target_pairs={{3,0},{2,1},{1,2},{0,3},{7,4},{6,5},{5,6},{4,7},{11,8},{10,9},{9,1... | collective-permute-start | bytes 196616 | tf_op jit(solution)/shard_map/ppermute | solution.py:158
  14.2 14.7 %collective-permute-start.10 = (bf16[96,1024]{1,0:T(8,128)(2,1)S(1)}, bf16[96,1024]{1,0:T(8,128)(2,1)S(1)}, u32[]{:S(2)}, u32[]{:S(2)}) collective-permute-start(bf16[96,1024]{1,0:T(8,128)(2,1)S(1)} %constant_dynamic-update-slice_fusion), channel_id=1, source_target_pairs={{24,0},{16,8},{8,16},{0,24},{25,1},{17,9},{9,17},{1,25},{26,2},{18... | collective-permute-start | bytes 589832 | tf_op jit(solution)/shard_map/ppermute | solution.py:158
  16.6 9.7 %collective-permute-start = (bf16[152,512]{1,0:T(8,128)(2,1)}, bf16[152,512]{1,0:T(8,128)(2,1)S(1)}, u32[]{:S(2)}, u32[]{:S(2)}) collective-permute-start(bf16[152,512]{1,0:T(8,128)(2,1)} %get-tuple-element.24.refs_1_), channel_id=1, source_target_pairs={{8,0},{0,8},{24,16},{16,24},{9,1},{1,9},{25,17},{17,25},{10,2},{2,... | collective-permute-start | bytes 466952 | tf_op jit(solution)/shard_map/ppermute | solution.py:158
  17.1 11.7 %collective-permute-start.1 = (bf16[152,512]{1,0:T(8,128)(2,1)}, bf16[152,512]{1,0:T(8,128)(2,1)S(1)}, u32[]{:S(2)}, u32[]{:S(2)}) collective-permute-start(bf16[152,512]{1,0:T(8,128)(2,1)} %get-tuple-element.24.refs_1_), channel_id=1, source_target_pairs={{24,0},{16,8},{8,16},{0,24},{25,1},{17,9},{9,17},{1,25},{26,2},{18... | collective-permute-start | bytes 466952 | tf_op jit(solution)/shard_map/ppermute | solution.py:158
  18.6 13.4 %collective-permute-start.8 = (bf16[96,1024]{1,0:T(8,128)(2,1)S(1)}, bf16[96,1024]{1,0:T(8,128)(2,1)S(1)}, u32[]{:S(2)}, u32[]{:S(2)}) collective-permute-start(bf16[96,1024]{1,0:T(8,128)(2,1)S(1)} %constant_dynamic-update-slice_fusion), channel_id=1, source_target_pairs={{8,0},{0,8},{24,16},{16,24},{9,1},{1,9},{25,17},{17,25},{10,2},{2,... | collective-permute-start | bytes 589832 | tf_op jit(solution)/shard_map/ppermute | solution.py:158
  19.1 12.9 %collective-permute-start.9 = (bf16[96,1024]{1,0:T(8,128)(2,1)S(1)}, bf16[96,1024]{1,0:T(8,128)(2,1)S(1)}, u32[]{:S(2)}, u32[]{:S(2)}) collective-permute-start(bf16[96,1024]{1,0:T(8,128)(2,1)S(1)} %constant_dynamic-update-slice_fusion), channel_id=1, source_target_pairs={{16,0},{24,8},{0,16},{8,24},{17,1},{25,9},{1,17},{9,25},{18,2},{26... | collective-permute-start | bytes 589832 | tf_op jit(solution)/shard_map/ppermute | solution.py:158
  26.3 5.9 %collective-permute-start.3 = (bf16[152,512]{1,0:T(8,128)(2,1)}, bf16[152,512]{1,0:T(8,128)(2,1)S(1)}, u32[]{:S(2)}, u32[]{:S(2)}) collective-permute-start(bf16[152,512]{1,0:T(8,128)(2,1)} %get-tuple-element.24.refs_1_), channel_id=1, source_target_pairs={{4,0},{0,4},{5,1},{1,5},{6,2},{2,6},{7,3},{3,7},{12,8},{8,12},{13,... | collective-permute-start | bytes 466952 | tf_op jit(solution)/shard_map/ppermute | solution.py:28
  28.9 3.3 %collective-permute-start.2 = (bf16[152,512]{1,0:T(8,128)(2,1)S(1)}, bf16[152,512]{1,0:T(8,128)(2,1)S(1)}, u32[]{:S(2)}, u32[]{:S(2)}) collective-permute-start(bf16[152,512]{1,0:T(8,128)(2,1)S(1)} %collective-permute-done.refs_0_), channel_id=1, source_target_pairs={{4,0},{0,4},{5,1},{1,5},{6,2},{2,6},{7,3},{3,7},{12,8},{8,12},{13,... | collective-permute-start | bytes 466952 | tf_op jit(solution)/shard_map/ppermute | solution.py:28
  28.9 3.3 %collective-permute-start.4 = (bf16[152,512]{1,0:T(8,128)(2,1)S(1)}, bf16[152,512]{1,0:T(8,128)(2,1)S(1)}, u32[]{:S(2)}, u32[]{:S(2)}) collective-permute-start(bf16[152,512]{1,0:T(8,128)(2,1)S(1)} %collective-permute-done.1.refs_2_), channel_id=1, source_target_pairs={{4,0},{0,4},{5,1},{1,5},{6,2},{2,6},{7,3},{3,7},{12,8},{8,12},{13,... | collective-permute-start | bytes 466952 | tf_op jit(solution)/shard_map/ppermute | solution.py:28
  29.4 2.6 %copy-start = (bf16[2,128,1536]{2,1,0:T(8,128)(2,1)S(1)}, bf16[2,128,1536]{2,1,0:T(8,128)(2,1)}, u32[]{:S(2)}) copy-start(bf16[2,128,1536]{2,1,0:T(8,128)(2,1)} %own_qkv_ref.3) | copy-start | bytes 2359300
  29.4 2.6 %copy-start.1 = (bf16[2,128,512]{2,1,0:T(8,128)(2,1)S(1)}, bf16[2,128,512]{2,1,0:T(8,128)(2,1)}, u32[]{:S(2)}) copy-start(bf16[2,128,512]{2,1,0:T(8,128)(2,1)} %own_out_ref.3) | copy-start | bytes 786436
  32.0 0.9 %copy-start.2 = (bf16[152,512]{1,0:T(8,128)(2,1)S(1)}, bf16[152,512]{1,0:T(8,128)(2,1)}, u32[]{:S(2)}) copy-start(bf16[152,512]{1,0:T(8,128)(2,1)} %get-tuple-element.24.refs_1_) | copy-start | bytes 466948
  32.0 0.9 %copy-start.3 = (f32[2,512]{1,0:T(2,128)S(1)}, f32[2,512]{1,0:T(2,128)}, u32[]{:S(2)}) copy-start(f32[2,512]{1,0:T(2,128)} %gain_ref.1) | copy-start | bytes 12292
  33.6 3.2 %copy-start.6 = (bf16[64,1024]{1,0:T(8,128)(2,1)S(1)}, bf16[64,1024]{1,0:T(8,128)(2,1)}, u32[]{:S(2)}) copy-start(bf16[64,1024]{1,0:T(8,128)(2,1)} %get-tuple-element.33) | copy-start | bytes 393220
  36.7 21.0 %collective-permute-start.11 = (bf16[1120,256]{1,0:T(8,128)(2,1)S(1)}, bf16[1120,256]{1,0:T(8,128)(2,1)S(1)}, u32[]{:S(2)}, u32[]{:S(2)}) collective-permute-start(bf16[1120,256]{1,0:T(8,128)(2,1)S(1)} %first.1.mine_ref), channel_id=1, source_target_pairs={{4,0},{0,4},{5,1},{1,5},{6,2},{2,6},{7,3},{3,7},{12,8},{8,12},{13,... | collective-permute-start | bytes 1720328 | tf_op jit(solution)/shard_map/ppermute | solution.py:28
  36.8 8.5 %collective-permute-start.12 = (bf16[64,1024]{1,0:T(8,128)(2,1)S(1)}, bf16[64,1024]{1,0:T(8,128)(2,1)S(1)}, u32[]{:S(2)}, u32[]{:S(2)}) collective-permute-start(bf16[64,1024]{1,0:T(8,128)(2,1)S(1)} %copy-done.6), channel_id=1, source_target_pairs={{1,0},{0,1},{3,2},{2,3},{5,4},{4,5},{7,6},{6,7},{9,8},{8,9},{11,10... | collective-permute-start | bytes 393224 | tf_op jit(solution)/shard_map/ppermute | solution.py:158
  37.4 12.9 %collective-permute-start.13 = (bf16[64,1024]{1,0:T(8,128)(2,1)S(1)}, bf16[64,1024]{1,0:T(8,128)(2,1)S(1)}, u32[]{:S(2)}, u32[]{:S(2)}) collective-permute-start(bf16[64,1024]{1,0:T(8,128)(2,1)S(1)} %copy-done.6), channel_id=1, source_target_pairs={{2,0},{3,1},{0,2},{1,3},{6,4},{7,5},{4,6},{5,7},{10,8},{11,9},{8,1... | collective-permute-start | bytes 393224 | tf_op jit(solution)/shard_map/ppermute | solution.py:158
  39.1 11.3 %collective-permute-start.14 = (bf16[64,1024]{1,0:T(8,128)(2,1)S(1)}, bf16[64,1024]{1,0:T(8,128)(2,1)S(1)}, u32[]{:S(2)}, u32[]{:S(2)}) collective-permute-start(bf16[64,1024]{1,0:T(8,128)(2,1)S(1)} %copy-done.6), channel_id=1, source_target_pairs={{3,0},{2,1},{1,2},{0,3},{7,4},{6,5},{5,6},{4,7},{11,8},{10,9},{9,1... | collective-permute-start | bytes 393224 | tf_op jit(solution)/shard_map/ppermute | solution.py:158
  50.4 6.0 %collective-permute-start.15 = (bf16[96,1024]{1,0:T(8,128)(2,1)S(1)}, bf16[96,1024]{1,0:T(8,128)(2,1)S(1)}, u32[]{:S(2)}, u32[]{:S(2)}) collective-permute-start(bf16[96,1024]{1,0:T(8,128)(2,1)S(1)} %pad_maximum_fusion), channel_id=1, source_target_pairs={{8,0},{0,8},{24,16},{16,24},{9,1},{1,9},{25,17},{17,25},{10,2},{2,... | collective-permute-start | bytes 589832 | tf_op jit(solution)/shard_map/ppermute | solution.py:158
  51.9 5.7 %collective-permute-start.16 = (bf16[96,1024]{1,0:T(8,128)(2,1)S(1)}, bf16[96,1024]{1,0:T(8,128)(2,1)S(1)}, u32[]{:S(2)}, u32[]{:S(2)}) collective-permute-start(bf16[96,1024]{1,0:T(8,128)(2,1)S(1)} %pad_maximum_fusion), channel_id=1, source_target_pairs={{16,0},{24,8},{0,16},{8,24},{17,1},{25,9},{1,17},{9,25},{18,2},{26... | collective-permute-start | bytes 589832 | tf_op jit(solution)/shard_map/ppermute | solution.py:158
  57.7 4.5 %collective-permute-start.17 = (bf16[512,256]{1,0:T(8,128)(2,1)S(1)}, bf16[512,256]{1,0:T(8,128)(2,1)S(1)}, u32[]{:S(2)}, u32[]{:S(2)}) collective-permute-start(bf16[512,256]{1,0:T(8,128)(2,1)S(1)} %get-tuple-element.39.wo_mine_ref), channel_id=1, source_target_pairs={{4,0},{0,4},{5,1},{1,5},{6,2},{2,6},{7,3},{3,7},{12,8},{8,12},{13,... | collective-permute-start | bytes 786440 | tf_op jit(solution)/shard_map/ppermute | solution.py:28
  61.7 1.5 %collective-permute-start.18 = (bf16[144,256]{1,0:T(8,128)(2,1)S(1)}, bf16[144,256]{1,0:T(8,128)(2,1)S(1)}, u32[]{:S(2)}, u32[]{:S(2)}) collective-permute-start(bf16[144,256]{1,0:T(8,128)(2,1)S(1)} %get-tuple-element.42), channel_id=1, source_target_pairs={{4,0},{0,4},{5,1},{1,5},{6,2},{2,6},{7,3},{3,7},{12,8},{8,12},{13,... | collective-permute-start | bytes 221192 | tf_op jit(solution)/shard_map/ppermute | solution.py:28

commit v7 on v6

--- a/solution.py
+++ b/solution.py
@@ -137,6 +137,9 @@
 KEEP1 = TALL - 64
 KEPT = KEEP1 - KEEP0
 PART = WIN - KEEP0
+MAIN = 128
+TAIL = WIN - MAIN
+LAG = 1
 REGION_ROWS = 8
 GROUP = 128 // HEAD_DIM
 F32 = jnp.float32
@@ -204,77 +207,93 @@
     return (shifted * lax.rsqrt(variance + 1e-05) * gain_row).astype(BF16)
 
 
-def gather_heads(b, start, table_ref, index, table, bias_ref):
+def look_up(table, at, heads, put):
+    chunks = (BIAS_ROWS + 127) // 128
+    low = at & 127
+    chunk = at >> 7
+    masks = [chunk == k for k in range(chunks)]
+    for h in heads:
+        acc = None
+        for k in range(chunks):
+            row = jnp.broadcast_to(table[h : h + 1, 128 * k : 128 * k + 128], (8, 128))
+            got = jnp.take_along_axis(row, low, axis=1, mode="promise_in_bounds")
+            acc = got if acc is None else jnp.where(masks[k], got, acc)
+        put(h, acc)
+
+
+def load_table(b, table_ref, table):
     me = lax.axis_index("lon")
     heads = table_ref[b, pl.ds(pl.multiple_of(MY_HEADS * me, MY_HEADS), MY_HEADS), :]
     table[:, 0:BIAS_ROWS] = heads * LOG2E
-    chunks = (BIAS_ROWS + 127) // 128
-
-    def look_up(at, put):
-        low = at & 127
-        chunk = at >> 7
-        masks = [chunk == k for k in range(chunks)]
-        for h in range(bias_ref.shape[0]):
-            acc = None
-            at_h = slice(start + h, start + h + 1)
-            for k in range(chunks):
-                row = jnp.broadcast_to(table[at_h, 128 * k : 128 * k + 128], (8, 128))
-                got = jnp.take_along_axis(row, low, axis=1, mode="promise_in_bounds")
-                acc = got if acc is None else jnp.where(masks[k], got, acc)
-            put(h, acc)
-
+
+
+def gather_main(start, index_ref, table, bias_ref):
     def step(g, carry):
         rows = pl.ds(pl.multiple_of(g * 8, 8), 8)
 
         def put(h, value):
-            bias_ref[h, rows, 0:128] = value
-
-        look_up(index[rows, 0:128], put)
+            bias_ref[h - start, rows, :] = value
+
+        look_up(table, index_ref[rows, 0:MAIN], range(start, start + bias_ref.shape[0]), put)
         return carry
 
     lax.fori_loop(0, WIN // 8, step, 0, unroll=9)
-    rest = WIN - 128
-    each = 128 // rest
-    groups = WIN // 8
-    for first in range(0, groups, each):
-        here = range(first, min(first + each, groups))
-        pieces = [index[8 * g : 8 * g + 8, 128:WIN] for g in here]
-        pieces += [jnp.zeros((8, rest), jnp.int32)] * (each - len(pieces))
-
-        def put(h, value, here=here):
-            for r, g in enumerate(here):
-                bias_ref[h, 8 * g : 8 * g + 8, 128:WIN] = value[:, rest * r : rest * (r + 1)]
-
-        look_up(jnp.concatenate(pieces, axis=1), put)
-
-
-def bias0_kernel(table_ref, index_ref, bias_ref, moved_ref, table):
+
+
+def gather_tail(flip_ref, table, tail_ref, flipped):
+    for t in range(0, TAIL, 8):
+        for lo in (0, 128):
+
+            def put(h, value, t=t, lo=lo):
+                flipped[TAIL * h + t : TAIL * h + t + 8, lo : lo + 128] = value
+
+            look_up(table, flip_ref[t : t + 8, lo : lo + 128], range(MY_HEADS), put)
+    tail_ref[...] = jnp.transpose(flipped[...])[0:WIN]
+
+
+def bias0_kernel(table_ref, index_ref, bias_ref, tail_ref, moved_ref, flip_ref, table, flipped):
     to = lax.broadcasted_iota(jnp.int32, (WIN, WIN), 0)
     frm = lax.broadcasted_iota(jnp.int32, (WIN, WIN), 1)
     move = jnp.where((to & 1) * HALF + (to >> 1) == frm, 1.0, 0.0).astype(BF16)
     whole = index_ref[...]
     parts = jnp.concatenate([whole >> 8, whole & 255], axis=0).astype(F32).astype(BF16)
     parts = nt_dot(parts, move).astype(BF16)
-    moved_ref[...] = (
-        nn_dot(move, parts[0:WIN]) * 256.0 + nn_dot(move, parts[WIN : 2 * WIN])
-    ).astype(jnp.int32)
-    gather_heads(0, 0, table_ref, moved_ref, table, bias_ref)
-
-
-def bias1_kernel(start, table_ref, index_ref, bias_ref, table):
-    gather_heads(1, start, table_ref, index_ref, table, bias_ref)
-
-
-def bias_call(kernel, heads, more, table, index):
-    bias = jax.ShapeDtypeStruct((heads, WIN, WIN), F32)
-    moved = jax.ShapeDtypeStruct((WIN, WIN), jnp.int32)
+    high, low = parts[0:WIN], parts[WIN : 2 * WIN]
+    moved = nn_dot(move, high) * 256.0 + nn_dot(move, low)
+    moved_ref[...] = moved.astype(jnp.int32)
+    flip_ref[:, WIN:256] = jnp.zeros((TAIL, 256 - WIN), jnp.int32)
+    flip_ref[:, 0:WIN] = jnp.transpose(moved[:, MAIN:WIN]).astype(jnp.int32)
+    load_table(0, table_ref, table)
+    gather_main(0, moved_ref, table, bias_ref)
+    gather_tail(flip_ref, table, tail_ref, flipped)
+
+
+def bias1_kernel(start, table_ref, index_ref, bias_ref, table, flipped):
+    load_table(1, table_ref, table)
+    gather_main(start, index_ref, table, bias_ref)
+
+
+def bias1_tail_kernel(start, table_ref, index_ref, flip_ref, bias_ref, tail_ref, table, flipped):
+    load_table(1, table_ref, table)
+    gather_main(start, index_ref, table, bias_ref)
+    gather_tail(flip_ref, table, tail_ref, flipped)
+
+
+def bias_call(kernel, heads, tail, first, *operands):
+    out = [jax.ShapeDtypeStruct((heads, WIN, MAIN), F32)]
+    out += [jax.ShapeDtypeStruct((WIN, MY_HEADS * TAIL), F32)] * tail
+    if first:
+        out += [jax.ShapeDtypeStruct((WIN, WIN), jnp.int32), jax.ShapeDtypeStruct((TAIL, 256), jnp.int32)]
     return pl.pallas_call(
         kernel,
-        out_shape=(bias, moved) if more else bias,
-        scratch_shapes=[pltpu.VMEM((MY_HEADS, (BIAS_ROWS + 127) // 128 * 128), F32)],
+        out_shape=out,
+        scratch_shapes=[
+            pltpu.VMEM((MY_HEADS, (BIAS_ROWS + 127) // 128 * 128), F32),
+            pltpu.VMEM((MY_HEADS * TAIL, 256), F32),
+        ],
         compiler_params=vmem(8),
         cost_estimate=pl.CostEstimate(flops=10**9, bytes_accessed=10**6, transcendentals=0),
-    )(table, index)
+    )(*operands)
 
 
 def columns(qkv_ref, out_ref, b, rows, me, dst, at, sems):
@@ -384,7 +403,8 @@
         east = jnp.where(me == 0, pair, own)
         rows += [4.0 * west + extra, 4.0 * east + extra]
     tags = jnp.concatenate(rows + rows, axis=0)
-    row_ref[...] = tags
+    row_ref[:, 0:MAIN] = tags[:, 0:MAIN]
+    row_ref[:, MAIN:] = jnp.concatenate([tags[:, MAIN:WIN]] * MY_HEADS, axis=1)
     to = lax.broadcasted_iota(jnp.int32, (WIN, WIN), 0)
     frm = lax.broadcasted_iota(jnp.int32, (WIN, WIN), 1)
     col_ref[...] = nt_dot(jnp.where(to == frm, 1.0, 0.0).astype(BF16), tags.astype(BF16))
@@ -396,13 +416,27 @@
         out_shape=(
             jax.ShapeDtypeStruct((PAIR, TALL, D), BF16),
             jax.ShapeDtypeStruct((PAIR, TALL, D), BF16),
-            jax.ShapeDtypeStruct((8, WIN), F32),
+            jax.ShapeDtypeStruct((8, MAIN + MY_HEADS * TAIL), F32),
             jax.ShapeDtypeStruct((WIN, 8), F32),
         ),
         compiler_params=vmem(16),
         cost_estimate=pl.CostEstimate(flops=10**8, bytes_accessed=2 * 10**6, transcendentals=0),
         name="enter",
     )(*mine, *other, gain)
+
+
+def give_kernel(part, *refs):
+    for k, ref in enumerate(refs[:-1]):
+        refs[-1][part * k : part * (k + 1), :] = ref[0:part, :]
+
+
+def give_call(part, pieces):
+    return pl.pallas_call(
+        functools.partial(give_kernel, part),
+        out_shape=jax.ShapeDtypeStruct((part * len(pieces), COLS), BF16),
+        compiler_params=vmem(4),
+        cost_estimate=pl.CostEstimate(flops=0, bytes_accessed=10**6, transcendentals=0),
+    )(*pieces)
 
 
 def join_kernel(b, n_fsdp, n_lat, steps, wide, own_qkv_ref, own_out_ref, *refs):
@@ -445,31 +479,63 @@
     )(qkv, out, *far, *near)
 
 
-def window_attend(q, k, v, bias_at, allowed, put):
+def window_attend(q, k, v, bias_at, tail_bias, allowed, tail_allowed, put):
     n = q.shape[0]
+    width = MY_HEADS * TAIL
     lanes = lax.broadcasted_iota(jnp.int32, (n, 128), 1)
-    owns = [(lanes >= HEAD_DIM * j) & (lanes < HEAD_DIM * (j + 1)) for j in range(GROUP)]
-    ones = jnp.ones((WIN, 128), BF16)
-    for g in range(MINE // 128):
+    owns = [lanes // HEAD_DIM == j for j in range(GROUP)]
+    blocks = [lanes // TAIL == h for h in range(MY_HEADS)]
+    row = lax.broadcasted_iota(jnp.int32, (width, MINE), 0)
+    col = lax.broadcasted_iota(jnp.int32, (width, MINE), 1)
+    same = row // TAIL == col // HEAD_DIM
+    groups = range(MINE // 128)
+
+    def spread(x):
+        x = jnp.concatenate([x[MAIN:WIN]] * MY_HEADS, axis=0)
+        return jnp.where(same, x, jnp.zeros_like(x))
+
+    tail = nt_dot(q, spread(k)) + tail_bias
+    scores = []
+    for g in groups:
         cols = slice(128 * g, 128 * (g + 1))
         q_g = q[:, cols]
-        k_g = k[:, cols]
-        v_g = jnp.concatenate([v[:, cols], ones], axis=1)
         q_all = jnp.concatenate([jnp.where(o, q_g, jnp.zeros_like(q_g)) for o in owns], axis=0)
-        scores = nt_dot(q_all, k_g)
-        probs = []
-        for j in range(GROUP):
-            s = scores[n * j : n * (j + 1)] + bias_at(GROUP * g + j)
-            if allowed is not None:
-                s = jnp.where(allowed, s, NEG)
-            peak = jnp.max(s, axis=-1, keepdims=True)
-            probs.append(jnp.exp2(s - peak).astype(BF16))
-        mixed = nn_dot(jnp.concatenate(probs, axis=0), v_g)
+        scores.append(nt_dot(q_all, k[0:MAIN, cols]))
+    yield
+    if tail_allowed is not None:
+        tail = jnp.where(tail_allowed, tail, NEG)
+    tail_peak = jnp.zeros_like(tail)
+    probs = []
+    for h in range(MY_HEADS):
+        j = h % GROUP
+        s = scores[h // GROUP][n * j : n * (j + 1)] + bias_at(h)
+        if allowed is not None:
+            s = jnp.where(allowed, s, NEG)
+        peak = jnp.max(jnp.maximum(s, jnp.where(blocks[h], tail, NEG)), axis=-1, keepdims=True)
+        tail_peak = jnp.where(blocks[h], peak, tail_peak)
+        probs.append(jnp.exp2(s - peak).astype(BF16))
+    tail = jnp.exp2(tail - tail_peak).astype(BF16)
+    yield
+    rest = nn_dot(tail, spread(v))
+    ones = jnp.where(same, 1.0, 0.0).astype(BF16)
+    rest_total = nn_dot(tail, ones)
+    for g in groups:
+        cols = slice(128 * g, 128 * (g + 1))
+        wide = jnp.concatenate([v[0:MAIN, cols], jnp.ones((MAIN, 128), BF16)], axis=1)
+        mixed = nn_dot(jnp.concatenate(probs[GROUP * g : GROUP * (g + 1)], axis=0), wide)
         value, total = mixed[0:n, 0:128], mixed[0:n, 128:256]
         for j in range(1, GROUP):
             value = jnp.where(owns[j], mixed[n * j : n * (j + 1), 0:128], value)
             total = jnp.where(owns[j], mixed[n * j : n * (j + 1), 128:256], total)
-        put(128 * g, (value / total).astype(BF16))
+        put(128 * g, ((value + rest[:, cols]) / (total + rest_total[:, cols])).astype(BF16))
+    yield
+
+
+def staggered(windows, lag):
+    for at in range(len(windows) + 2 * lag):
+        for stage in range(3):
+            if 0 <= at - stage * lag < len(windows):
+                next(windows[at - stage * lag])
 
 
 def project(n, w_ref, q_s, k_s, v_s):
@@ -479,9 +545,10 @@
     v_s[...] = both[:, 2 * MINE : 3 * MINE].astype(BF16)
 
 
-def first_kernel(n_ref, w_ref, bias_ref, wo_ref, o_ref, q_s, k_s, v_s):
+def first_kernel(n_ref, w_ref, bias_ref, tail_ref, wo_ref, o_ref, q_s, k_s, v_s):
     o_ref[PAIR * KEPT :, :] = wo_ref[...]
     project(n_ref[...].reshape(PAIR * TALL, D), w_ref, q_s, k_s, v_s)
+    windows = []
     for l in range(PAIR):
         for part, (q0, q1, o0) in enumerate(
             ((KEEP0, WIN, 0), (0, WIN, PART), (0, PART, PART + WIN))
@@ -491,17 +558,20 @@
             def put(col, value, l=l, o0=o0, q0=q0, q1=q1):
                 o_ref[KEPT * l + o0 : KEPT * l + o0 + q1 - q0, col : col + 128] = value
 
-            window_attend(
+            windows.append(window_attend(
                 q_s[t + q0 : t + q1, :],
                 k_s[t : t + WIN, :],
                 v_s[t : t + WIN, :],
                 lambda h, q0=q0, q1=q1: bias_ref[h, q0:q1, :],
+                tail_ref[q0:q1, :],
+                None,
                 None,
                 put,
-            )
-
-
-def first_call(normed, weight, bias, wo):
+            ))
+    staggered(windows, LAG)
+
+
+def first_call(normed, weight, bias, tail, wo):
     scratch = pltpu.VMEM((PAIR * TALL, MINE), BF16)
     return pl.pallas_call(
         first_kernel,
@@ -510,7 +580,7 @@
         compiler_params=vmem(24),
         cost_estimate=pl.CostEstimate(flops=2 * 10**9, bytes_accessed=4 * 10**6, transcendentals=10**6),
         name="first",
-    )(normed, weight, bias, wo)
+    )(normed, weight, bias, tail, wo)
 
 
 def pair_columns(me, ref, mine, other):
@@ -557,11 +627,12 @@
 
 
 def second_kernel(
-    win_ref, w_ref, bias_a, bias_b, row_ref, col_ref, keep_ref, send_ref, q_s, k_s, v_s, a_s, t_s
+    win_ref, w_ref, bias_a, bias_b, tail_ref, row_ref, col_ref, keep_ref, send_ref, q_s, k_s, v_s, a_s, t_s
 ):
     me = lax.axis_index("lon")
     half = MY_HEADS // 2
     project(win_ref[...], w_ref, q_s, k_s, v_s)
+    windows = []
     for w in range(4):
         q0, q1 = (KEEP0, WIN) if w < 2 else (0, PART)
         t = WIN * w
@@ -570,14 +641,17 @@
         def put(col, value, w=w):
             a_s[PART * w : PART * (w + 1), col : col + 128] = value
 
-        window_attend(
+        windows.append(window_attend(
             q_s[t + q0 : t + q1, :],
             k_s[t : t + WIN, :],
             v_s[t : t + WIN, :],
             lambda h, q0=q0, q1=q1: (bias_a, bias_b)[h // half][h % half, q0:q1, :],
-            allowed,
+            tail_ref[q0:q1, :],
+            allowed[:, 0:MAIN],
+            allowed[:, MAIN:],
             put,
-        )
+        ))
+    staggered(windows, LAG)
     tiles = nn_dot(one_hot(tile_sources(), 4 * PART), a_s[...]).astype(BF16)
     t_s[0] = tiles[0:WIN]
     t_s[1] = tiles[WIN : 2 * WIN]
@@ -585,7 +659,7 @@
     send_ref[...] = t_s[1 - me]
 
 
-def second_call(windows, weight, bias_a, bias_b, row, col):
+def second_call(windows, weight, bias_a, bias_b, tail, row, col):
     qkv = pltpu.VMEM((4 * WIN, MINE), BF16)
     half = jax.ShapeDtypeStruct((WIN, MINE), BF16)
     return pl.pallas_call(
@@ -601,7 +675,7 @@
         compiler_params=vmem(24),
         cost_estimate=pl.CostEstimate(flops=2 * 10**9, bytes_accessed=4 * 10**6, transcendentals=10**6),
         name="second",
-    )(windows, weight, bias_a, bias_b, row, col)
+    )(windows, weight, bias_a, bias_b, tail, row, col)
 
 
 def most_kernel(mid_ref, keep_ref, wo_mine_ref, wo_other_ref, sum_ref, rows_ref, wo_s):
@@ -672,24 +746,24 @@
     side = heard_from(tile, "lat", 1) if mirrored else passed_along(tile, "lat", 1)
     cross = heard_from(tile, "lat", 3) if mirrored else passed_along(tile, "lat", -1)
     far1 = spread(part1, "fsdp", range(1, n_fsdp))
-    near0 = spread(jnp.concatenate(far0, axis=0), "lat", plan[0][1])
-    near1 = spread(jnp.concatenate([f[:part] for f in far1], axis=0), "lat", plan[1][1])
+    near0 = spread(give_call(part, far0), "lat", plan[0][1])
+    near1 = spread(give_call(part, far1), "lat", plan[1][1])
     three = (side, tile, cross)
     pair = [swap(t) for t in three]
     x, normed, tag_row, tag_col = enter_call(mirrored, three, pair, norm_gain)
     table = jnp.transpose(rel_bias, (0, 2, 1))
     params = (qkv_weight, out_weight)
     w0, wo0 = join_call(0, n_lat, plan[0][1], plan[0][0], *params, far0, near0)
-    bias0, index = bias_call(bias0_kernel, MY_HEADS, True, table, bias_index)
-    o0 = first_call(normed, w0, bias0, wo0)
+    bias0, tail0, index, flip = bias_call(bias0_kernel, MY_HEADS, True, True, table, bias_index)
+    o0 = first_call(normed, w0, bias0, tail0, wo0)
     w1, wo1 = join_call(1, n_lat, plan[1][1], plan[1][0], *params, far1, near1)
     half = MY_HEADS // 2
-    bias1 = [
-        bias_call(functools.partial(bias1_kernel, half * i), half, False, table, index)
-        for i in range(2)
-    ]
+    (bias_a,) = bias_call(functools.partial(bias1_kernel, 0), half, False, False, table, index)
+    bias_b, tail1 = bias_call(
+        functools.partial(bias1_tail_kernel, half), half, True, False, table, index, flip
+    )
     mid, windows = middle_call(o0, swap(o0), x, norm_gain)
-    keep, send = second_call(windows, w1, *bias1, tag_row, tag_col)
+    keep, send = second_call(windows, w1, bias_a, bias_b, tail1, tag_row, tag_col)
     total, rows = most_call(mid, keep, wo1, swap(wo1))
     out = last_call(total, rows, swap(send))
     return jnp.transpose(out.reshape(WH, WW, WZ, D), (2, 0, 1, 3))[None]

time: 65.1 us -> 63.1 us (0.969)
  Pallas kernels: 15.8 us -> 13.6 us
    pallas_call x3 -> x5, Pallas kernels: 4.54 us -> 3.53 us  [the longest x3 3.5 us: bias_call(): pl.pallas_call(kernel, out_shape=out, scratch_shapes=[pltpu.VMEM((MY_HEAD...]
    pallas_call x1, Pallas kernels: 3.13 us -> 2.26 us  [first_call(): pl.pallas_call(first_kernel, out_shape=jax.ShapeDtypeStruct((PAIR * KEPT...]
  transfers between devices with their start and end apart: 19 -> 19, of which waited for: 9 -> 9; matrix products, arithmetic and copies ran while one was open for 0% -> 0% of each run, Pallas kernels for 14% -> 12%
where the time goes in v7:
time: 63.1 us; the launch traced here: 62.1 us
  waiting for transfers between devices  26.8 us (42%)
  starting transfers between devices  21 us (33%)
  Pallas kernels  13.6 us (22%)
    ppermute x13, waiting for transfers between devices, heard_from(): lax.ppermute(block, axis, [(partner(i, step, size), i) for i in range(siz...  26.1 us
    ppermute x13, starting transfers between devices, heard_from(): lax.ppermute(block, axis, [(partner(i, step, size), i) for i in range(siz...  19.8 us
    pallas_call x3, Pallas kernels, bias_call(): pl.pallas_call(kernel, out_shape=out, scratch_shapes=[pltpu.VMEM((MY_HEAD...  3.5 us
    pallas_call x1, Pallas kernels, first_call(): pl.pallas_call(first_kernel, out_shape=jax.ShapeDtypeStruct((PAIR * KEPT...  2.26 us
    pallas_call x1, Pallas kernels, open_call(): pl.pallas_call(functools.partial(open_kernel, wide), out_shape=(jax.Shape...  2.11 us
    pallas_call x1, Pallas kernels, second_call(): pl.pallas_call(second_kernel, out_shape=(half, half), scratch_shapes=[qkv...  2.06 us
    pallas_call x1, Pallas kernels, middle_call(): pl.pallas_call(middle_kernel, out_shape=(jax.ShapeDtypeStruct((WIN, D), B...  1.53 us
  transfers between devices with their start and end apart: 19, of which 9 were waited for; matrix products, arithmetic and copies ran while one was open for 0% of the time, Pallas kernels for 12%

profile of v7, /device:TPU:0, one launch (start us, length us, event | category | flops | bytes accessed | tf_op | source)
XLA Modules:
  0.0 62.1 jit_solution(3272251153994155769)
XLA Ops:
  0.0 2.1 %open.1 = (bf16[32,1024]{1,0:T(8,128)(2,1)}, bf16[64,1024]{1,0:T(8,128)(2,1)}, bf16[152,512]{1,0:T(8,128)(2,1)}) custom-call(bf16[72,2,512]{2,1,0:T(2,128)(2,1)} %bitcast.15, s32[6,2,12]{2,1,0:T(2,128)} %bitcast.16, bf16[2,128,1536]{2,1,0:T(8,128)(2,1)} %own_qkv_ref.3, bf16[2,128,512]{2,1,0:T(8,128)(2,1)} %own_out_ref.3), custom_call_target="tpu_custom_call" | custom-call | flops 1000000 | bytes 1000000 | tf_op jit(solution)/shard_map/open/pallas_call | solution.py:355
  2.1 3.1 %collective-permute-start.5 = (bf16[32,1024]{1,0:T(8,128)(2,1)}, bf16[32,1024]{1,0:T(8,128)(2,1)S(1)}, u32[]{:S(2)}, u32[]{:S(2)}) collective-permute-start(bf16[32,1024]{1,0:T(8,128)(2,1)} %get-tuple-element.30), channel_id=1, source_target_pairs={{1,0},{0,1},{3,2},{2,3},{5,4},{4,5},{7,6},{6,7},{9,8},{8,9},{11,10... | collective-permute-start | bytes 196616 | tf_op jit(solution)/shard_map/ppermute | solution.py:161
  5.3 2.6 %collective-permute-start.6 = (bf16[32,1024]{1,0:T(8,128)(2,1)}, bf16[32,1024]{1,0:T(8,128)(2,1)S(1)}, u32[]{:S(2)}, u32[]{:S(2)}) collective-permute-start(bf16[32,1024]{1,0:T(8,128)(2,1)} %get-tuple-element.30), channel_id=1, source_target_pairs={{2,0},{3,1},{0,2},{1,3},{6,4},{7,5},{4,6},{5,7},{10,8},{11,9},{8,1... | collective-permute-start | bytes 196616 | tf_op jit(solution)/shard_map/ppermute | solution.py:161
  7.9 4.9 %collective-permute-done.6.refs_1_ = bf16[32,1024]{1,0:T(8,128)(2,1)S(1)} collective-permute-done((bf16[32,1024]{1,0:T(8,128)(2,1)}, bf16[32,1024]{1,0:T(8,128)(2,1)S(1)}, u32[]{:S(2)}, u32[]{:S(2)}) %collective-permute-start.6) | collective-permute-done | bytes 65568 | tf_op jit(solution)/shard_map/ppermute | solution.py:161
  12.8 1.4 %collective-permute-done.7.refs_2_ = bf16[32,1024]{1,0:T(8,128)(2,1)S(1)} collective-permute-done((bf16[32,1024]{1,0:T(8,128)(2,1)}, bf16[32,1024]{1,0:T(8,128)(2,1)S(1)}, u32[]{:S(2)}, u32[]{:S(2)}) %collective-permute-start.7) | collective-permute-done | bytes 65568 | tf_op jit(solution)/shard_map/ppermute | solution.py:161
  14.2 2.5 %collective-permute-start.10 = (bf16[96,1024]{1,0:T(8,128)(2,1)S(1)}, bf16[96,1024]{1,0:T(8,128)(2,1)S(1)}, u32[]{:S(2)}, u32[]{:S(2)}) collective-permute-start(bf16[96,1024]{1,0:T(8,128)(2,1)S(1)} %shard_map.73), channel_id=1, source_target_pairs={{24,0},{16,8},{8,16},{0,24},{25,1},{17,9},{9,17},{1,25},{26,2},{18... | collective-permute-start | bytes 589832 | tf_op jit(solution)/shard_map/ppermute | solution.py:161
  16.7 0.5 collective-permute-start
  17.2 1.4 %collective-permute-start.1 = (bf16[152,512]{1,0:T(8,128)(2,1)S(1)}, bf16[152,512]{1,0:T(8,128)(2,1)S(1)}, u32[]{:S(2)}, u32[]{:S(2)}) collective-permute-start(bf16[152,512]{1,0:T(8,128)(2,1)S(1)} %copy-done.2), channel_id=1, source_target_pairs={{24,0},{16,8},{8,16},{0,24},{25,1},{17,9},{9,17},{1,25},{26,2},{18... | collective-permute-start | bytes 466952 | tf_op jit(solution)/shard_map/ppermute | solution.py:161
  18.7 0.5 collective-permute-start.8
  19.2 1.5 %collective-permute-start.9 = (bf16[96,1024]{1,0:T(8,128)(2,1)S(1)}, bf16[96,1024]{1,0:T(8,128)(2,1)S(1)}, u32[]{:S(2)}, u32[]{:S(2)}) collective-permute-start(bf16[96,1024]{1,0:T(8,128)(2,1)S(1)} %shard_map.73), channel_id=1, source_target_pairs={{16,0},{24,8},{0,16},{8,24},{17,1},{25,9},{1,17},{9,25},{18,2},{26... | collective-permute-start | bytes 589832 | tf_op jit(solution)/shard_map/ppermute | solution.py:161
  20.7 5.6 %collective-permute-done.refs_0_ = bf16[152,512]{1,0:T(8,128)(2,1)S(1)} collective-permute-done((bf16[152,512]{1,0:T(8,128)(2,1)S(1)}, bf16[152,512]{1,0:T(8,128)(2,1)S(1)}, u32[]{:S(2)}, u32[]{:S(2)}) %collective-permute-start) | collective-permute-done | bytes 155680 | tf_op jit(solution)/shard_map/ppermute | solution.py:161
  26.4 2.6 %collective-permute-done.1.refs_2_ = bf16[152,512]{1,0:T(8,128)(2,1)S(1)} collective-permute-done((bf16[152,512]{1,0:T(8,128)(2,1)S(1)}, bf16[152,512]{1,0:T(8,128)(2,1)S(1)}, u32[]{:S(2)}, u32[]{:S(2)}) %collective-permute-start.1) | collective-permute-done | bytes 155680 | tf_op jit(solution)/shard_map/ppermute | solution.py:161
  29.0 0.5 collective-permute-start.4
  29.5 1.9 %shard_map.75 = (f32[8,144,128]{2,1,0:T(8,128)S(1)}, f32[144,128]{1,0:T(8,128)S(1)}, s32[144,144]{1,0:T(8,128)S(1)}, s32[16,256]{1,0:T(8,128)S(1)}) custom-call(f32[2,16,759]{2,1,0:T(8,128)S(1)} %bitcast.12, s32[144,144]{1,0:T(8,128)S(1)} %copy-done.4), custom_call_target="tpu_custom_call" | custom-call | flops 1000000000 | bytes 1000000 | tf_op jit(solution)/shard_map/pallas_call | solution.py:287
  32.1 0.7 %enter.1 = (bf16[2,432,512]{2,1,0:T(8,128)(2,1)S(1)}, bf16[2,432,512]{2,1,0:T(8,128)(2,1)S(1)}, f32[8,256]{1,0:T(8,128)S(1)}, f32[144,8]{1,0:T(8,128)S(1)}) custom-call(bf16[152,512]{1,0:T(8,128)(2,1)S(1)} %collective-permute-done.refs_0_, bf16[152,512]{1,0:T(8,128)(2,1)S(1)} %copy-done.2, bf16[152,512]{1,0:T(8,128)(2,1)S(1)} %collective-permute-done.1.refs_2_, ...), custom_call_target="tpu_custom_call" | custom-call | flops 100000000 | bytes 2000000 | tf_op jit(solution)/shard_map/enter/pallas_call | solution.py:414
  32.8 2.3 %first.1.mine_ref = bf16[1120,256]{1,0:T(8,128)(2,1)S(1)} custom-call(bf16[2,432,512]{2,1,0:T(8,128)(2,1)S(1)} %get-tuple-element.29.n_ref, bf16[512,768]{1,0:T(8,128)(2,1)S(1)} %get-tuple-element.31.w_ref, f32[8,144,128]{2,1,0:T(8,128)S(1)} %get-tuple-element.32.bias_ref, f32[144,128]{1,0:T(8,128)S(1)} %get-tuple-element.33.tail_ref, ...), custom_call_target="tpu_custom_call" | custom-call | flops 2000000000 | bytes 4000000 | tf_op jit(solution)/shard_map/first/pallas_call | solution.py:576
  35.1 0.5 collective-permute-start.12
  35.7 1.7 %collective-permute-start.13 = (bf16[64,1024]{1,0:T(8,128)(2,1)S(1)}, bf16[64,1024]{1,0:T(8,128)(2,1)S(1)}, u32[]{:S(2)}, u32[]{:S(2)}) collective-permute-start(bf16[64,1024]{1,0:T(8,128)(2,1)S(1)} %copy-done.6), channel_id=1, source_target_pairs={{2,0},{3,1},{0,2},{1,3},{6,4},{7,5},{4,6},{5,7},{10,8},{11,9},{8,1... | collective-permute-start | bytes 393224 | tf_op jit(solution)/shard_map/ppermute | solution.py:161
  37.4 2.2 %collective-permute-start.14 = (bf16[64,1024]{1,0:T(8,128)(2,1)S(1)}, bf16[64,1024]{1,0:T(8,128)(2,1)S(1)}, u32[]{:S(2)}, u32[]{:S(2)}) collective-permute-start(bf16[64,1024]{1,0:T(8,128)(2,1)S(1)} %copy-done.6), channel_id=1, source_target_pairs={{3,0},{2,1},{1,2},{0,3},{7,4},{6,5},{5,6},{4,7},{11,8},{10,9},{9,1... | collective-permute-start | bytes 393224 | tf_op jit(solution)/shard_map/ppermute | solution.py:161
  39.6 4.1 %collective-permute-done.12.refs_0_ = bf16[64,1024]{1,0:T(8,128)(2,1)S(1)} collective-permute-done((bf16[64,1024]{1,0:T(8,128)(2,1)S(1)}, bf16[64,1024]{1,0:T(8,128)(2,1)S(1)}, u32[]{:S(2)}, u32[]{:S(2)}) %collective-permute-start.12) | collective-permute-done | bytes 131104 | tf_op jit(solution)/shard_map/ppermute | solution.py:161
  43.6 5.0 %collective-permute-done.13.refs_1_ = bf16[64,1024]{1,0:T(8,128)(2,1)S(1)} collective-permute-done((bf16[64,1024]{1,0:T(8,128)(2,1)S(1)}, bf16[64,1024]{1,0:T(8,128)(2,1)S(1)}, u32[]{:S(2)}, u32[]{:S(2)}) %collective-permute-start.13) | collective-permute-done | bytes 131104 | tf_op jit(solution)/shard_map/ppermute | solution.py:161
  48.6 1.6 %collective-permute-start.15 = (bf16[96,1024]{1,0:T(8,128)(2,1)S(1)}, bf16[96,1024]{1,0:T(8,128)(2,1)S(1)}, u32[]{:S(2)}, u32[]{:S(2)}) collective-permute-start(bf16[96,1024]{1,0:T(8,128)(2,1)S(1)} %shard_map.76), channel_id=1, source_target_pairs={{8,0},{0,8},{24,16},{16,24},{9,1},{1,9},{25,17},{17,25},{10,2},{2,... | collective-permute-start | bytes 589832 | tf_op jit(solution)/shard_map/ppermute | solution.py:161
  50.2 1.5 %collective-permute-start.16 = (bf16[96,1024]{1,0:T(8,128)(2,1)S(1)}, bf16[96,1024]{1,0:T(8,128)(2,1)S(1)}, u32[]{:S(2)}, u32[]{:S(2)}) collective-permute-start(bf16[96,1024]{1,0:T(8,128)(2,1)S(1)} %shard_map.76), channel_id=1, source_target_pairs={{16,0},{24,8},{0,16},{8,24},{17,1},{25,9},{1,17},{9,25},{18,2},{26... | collective-permute-start | bytes 589832 | tf_op jit(solution)/shard_map/ppermute | solution.py:161
  51.7 0.7 %shard_map.78.bias_a = f32[4,144,128]{2,1,0:T(8,128)S(1)} custom-call(f32[2,16,759]{2,1,0:T(8,128)S(1)} %bitcast.13, s32[144,144]{1,0:T(8,128)S(1)} %get-tuple-element.40.index_ref), custom_call_target="tpu_custom_call" | custom-call | flops 1000000000 | bytes 1000000 | tf_op jit(solution)/shard_map/pallas_call | solution.py:287
  52.4 1.0 %shard_map.79 = (f32[4,144,128]{2,1,0:T(8,128)S(1)}, f32[144,128]{1,0:T(8,128)S(1)}) custom-call(f32[2,16,759]{2,1,0:T(8,128)S(1)} %bitcast.14, s32[144,144]{1,0:T(8,128)S(1)} %get-tuple-element.40.index_ref, s32[16,256]{1,0:T(8,128)S(1)} %get-tuple-element.41.flip_ref), custom_call_target="tpu_custom_call" | custom-call | flops 1000000000 | bytes 1000000 | tf_op jit(solution)/shard_map/pallas_call | solution.py:287
  53.4 1.3 %collective-permute-done.15.refs_3_ = bf16[96,1024]{1,0:T(8,128)(2,1)S(1)} collective-permute-done((bf16[96,1024]{1,0:T(8,128)(2,1)S(1)}, bf16[96,1024]{1,0:T(8,128)(2,1)S(1)}, u32[]{:S(2)}, u32[]{:S(2)}) %collective-permute-start.15) | collective-permute-done | bytes 196640 | tf_op jit(solution)/shard_map/ppermute | solution.py:161
  54.7 1.2 %collective-permute-done.16.refs_4_ = bf16[96,1024]{1,0:T(8,128)(2,1)S(1)} collective-permute-done((bf16[96,1024]{1,0:T(8,128)(2,1)S(1)}, bf16[96,1024]{1,0:T(8,128)(2,1)S(1)}, u32[]{:S(2)}, u32[]{:S(2)}) %collective-permute-start.16) | collective-permute-done | bytes 196640 | tf_op jit(solution)/shard_map/ppermute | solution.py:161
  56.1 1.5 %middle.1 = (bf16[144,512]{1,0:T(8,128)(2,1)S(1)}, bf16[576,512]{1,0:T(8,128)(2,1)S(1)}) custom-call(bf16[1120,256]{1,0:T(8,128)(2,1)S(1)} %first.1.mine_ref, bf16[1120,256]{1,0:T(8,128)(2,1)S(1)} %collective-permute-done.11.other_ref, bf16[2,432,512]{2,1,0:T(8,128)(2,1)S(1)} %get-tuple-element.35.x_ref, f32[2,512]{1,0:T(2,128)S(1)} %copy-done.3), custom_call_target="tpu_custom_call" | custom-call | flops 1000000000 | bytes 3000000 | tf_op jit(solution)/shard_map/middle/pallas_call | solution.py:611
  57.6 2.1 %second.1 = (bf16[144,256]{1,0:T(8,128)(2,1)S(1)}, bf16[144,256]{1,0:T(8,128)(2,1)S(1)}) custom-call(bf16[576,512]{1,0:T(8,128)(2,1)S(1)} %get-tuple-element.37.win_ref, bf16[512,768]{1,0:T(8,128)(2,1)S(1)} %get-tuple-element.39.w_ref, f32[4,144,128]{2,1,0:T(8,128)S(1)} %shard_map.78.bias_a, f32[4,144,128]{2,1,0:T(8,128)S(1)} %get-tuple-element.42.bias_b, ...), custom_call_target="tpu_custom_call" | custom-call | flops 2000000000 | bytes 4000000 | tf_op jit(solution)/shard_map/second/pallas_call | solution.py:665
  59.7 0.6 collective-permute-start.18
  60.5 0.6 %collective-permute-done.18.got_ref = bf16[144,256]{1,0:T(8,128)(2,1)S(1)} collective-permute-done((bf16[144,256]{1,0:T(8,128)(2,1)S(1)}, bf16[144,256]{1,0:T(8,128)(2,1)S(1)}, u32[]{:S(2)}, u32[]{:S(2)}) %collective-permute-start.18) | collective-permute-done | bytes 73760 | tf_op jit(solution)/shard_map/ppermute | solution.py:28
  61.1 1.0 %last.1 = bf16[72,2,512]{2,1,0:T(2,128)(2,1)} custom-call(f32[144,512]{1,0:T(8,128)S(1)} %get-tuple-element.48.sum_ref, bf16[256,512]{1,0:T(8,128)(2,1)S(1)} %get-tuple-element.49.rows_ref, bf16[144,256]{1,0:T(8,128)(2,1)S(1)} %collective-permute-done.18.got_ref), custom_call_target="tpu_custom_call" | custom-call | flops 100000000 | bytes 1000000 | tf_op jit(solution)/shard_map/last/pallas_call | solution.py:706
  (34 shorter events, 1.2 us)
Async XLA Ops:
  0.0 29.5 %copy-start.5 = (f32[2,759,16]{1,2,0:T(8,128)S(1)}, f32[2,759,16]{1,2,0:T(8,128)}, u32[]{:S(2)}) copy-start(f32[2,759,16]{1,2,0:T(8,128)} %param.11) | copy-start | bytes 291460
  2.1 14.6 %copy-start.2 = (bf16[152,512]{1,0:T(8,128)(2,1)S(1)}, bf16[152,512]{1,0:T(8,128)(2,1)}, u32[]{:S(2)}) copy-start(bf16[152,512]{1,0:T(8,128)(2,1)} %get-tuple-element.28.refs_1_) | copy-start | bytes 466948
  2.1 27.4 %copy-start.4 = (s32[144,144]{1,0:T(8,128)S(1)}, s32[144,144]{1,0:T(8,128)}, u32[]{:S(2)}) copy-start(s32[144,144]{1,0:T(8,128)} %index_ref.1) | copy-start | bytes 248836
  2.1 5.7 %collective-permute-start.5 = (bf16[32,1024]{1,0:T(8,128)(2,1)}, bf16[32,1024]{1,0:T(8,128)(2,1)S(1)}, u32[]{:S(2)}, u32[]{:S(2)}) collective-permute-start(bf16[32,1024]{1,0:T(8,128)(2,1)} %get-tuple-element.30), channel_id=1, source_target_pairs={{1,0},{0,1},{3,2},{2,3},{5,4},{4,5},{7,6},{6,7},{9,8},{8,9},{11,10... | collective-permute-start | bytes 196616 | tf_op jit(solution)/shard_map/ppermute | solution.py:161
  5.3 7.5 %collective-permute-start.6 = (bf16[32,1024]{1,0:T(8,128)(2,1)}, bf16[32,1024]{1,0:T(8,128)(2,1)S(1)}, u32[]{:S(2)}, u32[]{:S(2)}) collective-permute-start(bf16[32,1024]{1,0:T(8,128)(2,1)} %get-tuple-element.30), channel_id=1, source_target_pairs={{2,0},{3,1},{0,2},{1,3},{6,4},{7,5},{4,6},{5,7},{10,8},{11,9},{8,1... | collective-permute-start | bytes 196616 | tf_op jit(solution)/shard_map/ppermute | solution.py:161
  7.9 6.3 %collective-permute-start.7 = (bf16[32,1024]{1,0:T(8,128)(2,1)}, bf16[32,1024]{1,0:T(8,128)(2,1)S(1)}, u32[]{:S(2)}, u32[]{:S(2)}) collective-permute-start(bf16[32,1024]{1,0:T(8,128)(2,1)} %get-tuple-element.30), channel_id=1, source_target_pairs={{3,0},{2,1},{1,2},{0,3},{7,4},{6,5},{5,6},{4,7},{11,8},{10,9},{9,1... | collective-permute-start | bytes 196616 | tf_op jit(solution)/shard_map/ppermute | solution.py:161
  14.2 14.8 %collective-permute-start.10 = (bf16[96,1024]{1,0:T(8,128)(2,1)S(1)}, bf16[96,1024]{1,0:T(8,128)(2,1)S(1)}, u32[]{:S(2)}, u32[]{:S(2)}) collective-permute-start(bf16[96,1024]{1,0:T(8,128)(2,1)S(1)} %shard_map.73), channel_id=1, source_target_pairs={{24,0},{16,8},{8,16},{0,24},{25,1},{17,9},{9,17},{1,25},{26,2},{18... | collective-permute-start | bytes 589832 | tf_op jit(solution)/shard_map/ppermute | solution.py:161
  16.7 9.7 %collective-permute-start = (bf16[152,512]{1,0:T(8,128)(2,1)S(1)}, bf16[152,512]{1,0:T(8,128)(2,1)S(1)}, u32[]{:S(2)}, u32[]{:S(2)}) collective-permute-start(bf16[152,512]{1,0:T(8,128)(2,1)S(1)} %copy-done.2), channel_id=1, source_target_pairs={{8,0},{0,8},{24,16},{16,24},{9,1},{1,9},{25,17},{17,25},{10,2},{2,... | collective-permute-start | bytes 466952 | tf_op jit(solution)/shard_map/ppermute | solution.py:161
  17.2 11.7 %collective-permute-start.1 = (bf16[152,512]{1,0:T(8,128)(2,1)S(1)}, bf16[152,512]{1,0:T(8,128)(2,1)S(1)}, u32[]{:S(2)}, u32[]{:S(2)}) collective-permute-start(bf16[152,512]{1,0:T(8,128)(2,1)S(1)} %copy-done.2), channel_id=1, source_target_pairs={{24,0},{16,8},{8,16},{0,24},{25,1},{17,9},{9,17},{1,25},{26,2},{18... | collective-permute-start | bytes 466952 | tf_op jit(solution)/shard_map/ppermute | solution.py:161
  18.7 12.7 %collective-permute-start.8 = (bf16[96,1024]{1,0:T(8,128)(2,1)S(1)}, bf16[96,1024]{1,0:T(8,128)(2,1)S(1)}, u32[]{:S(2)}, u32[]{:S(2)}) collective-permute-start(bf16[96,1024]{1,0:T(8,128)(2,1)S(1)} %shard_map.73), channel_id=1, source_target_pairs={{8,0},{0,8},{24,16},{16,24},{9,1},{1,9},{25,17},{17,25},{10,2},{2,... | collective-permute-start | bytes 589832 | tf_op jit(solution)/shard_map/ppermute | solution.py:161
  19.2 12.2 %collective-permute-start.9 = (bf16[96,1024]{1,0:T(8,128)(2,1)S(1)}, bf16[96,1024]{1,0:T(8,128)(2,1)S(1)}, u32[]{:S(2)}, u32[]{:S(2)}) collective-permute-start(bf16[96,1024]{1,0:T(8,128)(2,1)S(1)} %shard_map.73), channel_id=1, source_target_pairs={{16,0},{24,8},{0,16},{8,24},{17,1},{25,9},{1,17},{9,25},{18,2},{26... | collective-permute-start | bytes 589832 | tf_op jit(solution)/shard_map/ppermute | solution.py:161
  26.4 5.2 %collective-permute-start.3 = (bf16[152,512]{1,0:T(8,128)(2,1)S(1)}, bf16[152,512]{1,0:T(8,128)(2,1)S(1)}, u32[]{:S(2)}, u32[]{:S(2)}) collective-permute-start(bf16[152,512]{1,0:T(8,128)(2,1)S(1)} %copy-done.2), channel_id=1, source_target_pairs={{4,0},{0,4},{5,1},{1,5},{6,2},{2,6},{7,3},{3,7},{12,8},{8,12},{13,... | collective-permute-start | bytes 466952 | tf_op jit(solution)/shard_map/ppermute | solution.py:28
  29.0 2.6 %collective-permute-start.2 = (bf16[152,512]{1,0:T(8,128)(2,1)S(1)}, bf16[152,512]{1,0:T(8,128)(2,1)S(1)}, u32[]{:S(2)}, u32[]{:S(2)}) collective-permute-start(bf16[152,512]{1,0:T(8,128)(2,1)S(1)} %collective-permute-done.refs_0_), channel_id=1, source_target_pairs={{4,0},{0,4},{5,1},{1,5},{6,2},{2,6},{7,3},{3,7},{12,8},{8,12},{13,... | collective-permute-start | bytes 466952 | tf_op jit(solution)/shard_map/ppermute | solution.py:28
  29.0 2.6 %collective-permute-start.4 = (bf16[152,512]{1,0:T(8,128)(2,1)S(1)}, bf16[152,512]{1,0:T(8,128)(2,1)S(1)}, u32[]{:S(2)}, u32[]{:S(2)}) collective-permute-start(bf16[152,512]{1,0:T(8,128)(2,1)S(1)} %collective-permute-done.1.refs_2_), channel_id=1, source_target_pairs={{4,0},{0,4},{5,1},{1,5},{6,2},{2,6},{7,3},{3,7},{12,8},{8,12},{13,... | collective-permute-start | bytes 466952 | tf_op jit(solution)/shard_map/ppermute | solution.py:28
  29.5 1.9 %copy-start = (bf16[2,128,1536]{2,1,0:T(8,128)(2,1)S(1)}, bf16[2,128,1536]{2,1,0:T(8,128)(2,1)}, u32[]{:S(2)}) copy-start(bf16[2,128,1536]{2,1,0:T(8,128)(2,1)} %own_qkv_ref.3) | copy-start | bytes 2359300
  29.5 1.9 %copy-start.1 = (bf16[2,128,512]{2,1,0:T(8,128)(2,1)S(1)}, bf16[2,128,512]{2,1,0:T(8,128)(2,1)}, u32[]{:S(2)}) copy-start(bf16[2,128,512]{2,1,0:T(8,128)(2,1)} %own_out_ref.3) | copy-start | bytes 786436
  31.4 0.7 %copy-start.3 = (f32[2,512]{1,0:T(2,128)S(1)}, f32[2,512]{1,0:T(2,128)}, u32[]{:S(2)}) copy-start(f32[2,512]{1,0:T(2,128)} %gain_ref.1) | copy-start | bytes 12292
  32.8 2.4 %copy-start.6 = (bf16[64,1024]{1,0:T(8,128)(2,1)S(1)}, bf16[64,1024]{1,0:T(8,128)(2,1)}, u32[]{:S(2)}) copy-start(bf16[64,1024]{1,0:T(8,128)(2,1)} %get-tuple-element.38) | copy-start | bytes 393220
  35.0 21.0 %collective-permute-start.11 = (bf16[1120,256]{1,0:T(8,128)(2,1)S(1)}, bf16[1120,256]{1,0:T(8,128)(2,1)S(1)}, u32[]{:S(2)}, u32[]{:S(2)}) collective-permute-start(bf16[1120,256]{1,0:T(8,128)(2,1)S(1)} %first.1.mine_ref), channel_id=1, source_target_pairs={{4,0},{0,4},{5,1},{1,5},{6,2},{2,6},{7,3},{3,7},{12,8},{8,12},{13,... | collective-permute-start | bytes 1720328 | tf_op jit(solution)/shard_map/ppermute | solution.py:28
  35.1 8.5 %collective-permute-start.12 = (bf16[64,1024]{1,0:T(8,128)(2,1)S(1)}, bf16[64,1024]{1,0:T(8,128)(2,1)S(1)}, u32[]{:S(2)}, u32[]{:S(2)}) collective-permute-start(bf16[64,1024]{1,0:T(8,128)(2,1)S(1)} %copy-done.6), channel_id=1, source_target_pairs={{1,0},{0,1},{3,2},{2,3},{5,4},{4,5},{7,6},{6,7},{9,8},{8,9},{11,10... | collective-permute-start | bytes 393224 | tf_op jit(solution)/shard_map/ppermute | solution.py:161
  35.7 12.9 %collective-permute-start.13 = (bf16[64,1024]{1,0:T(8,128)(2,1)S(1)}, bf16[64,1024]{1,0:T(8,128)(2,1)S(1)}, u32[]{:S(2)}, u32[]{:S(2)}) collective-permute-start(bf16[64,1024]{1,0:T(8,128)(2,1)S(1)} %copy-done.6), channel_id=1, source_target_pairs={{2,0},{3,1},{0,2},{1,3},{6,4},{7,5},{4,6},{5,7},{10,8},{11,9},{8,1... | collective-permute-start | bytes 393224 | tf_op jit(solution)/shard_map/ppermute | solution.py:161
  37.4 11.3 %collective-permute-start.14 = (bf16[64,1024]{1,0:T(8,128)(2,1)S(1)}, bf16[64,1024]{1,0:T(8,128)(2,1)S(1)}, u32[]{:S(2)}, u32[]{:S(2)}) collective-permute-start(bf16[64,1024]{1,0:T(8,128)(2,1)S(1)} %copy-done.6), channel_id=1, source_target_pairs={{3,0},{2,1},{1,2},{0,3},{7,4},{6,5},{5,6},{4,7},{11,8},{10,9},{9,1... | collective-permute-start | bytes 393224 | tf_op jit(solution)/shard_map/ppermute | solution.py:161
  48.6 6.0 %collective-permute-start.15 = (bf16[96,1024]{1,0:T(8,128)(2,1)S(1)}, bf16[96,1024]{1,0:T(8,128)(2,1)S(1)}, u32[]{:S(2)}, u32[]{:S(2)}) collective-permute-start(bf16[96,1024]{1,0:T(8,128)(2,1)S(1)} %shard_map.76), channel_id=1, source_target_pairs={{8,0},{0,8},{24,16},{16,24},{9,1},{1,9},{25,17},{17,25},{10,2},{2,... | collective-permute-start | bytes 589832 | tf_op jit(solution)/shard_map/ppermute | solution.py:161
  50.2 5.7 %collective-permute-start.16 = (bf16[96,1024]{1,0:T(8,128)(2,1)S(1)}, bf16[96,1024]{1,0:T(8,128)(2,1)S(1)}, u32[]{:S(2)}, u32[]{:S(2)}) collective-permute-start(bf16[96,1024]{1,0:T(8,128)(2,1)S(1)} %shard_map.76), channel_id=1, source_target_pairs={{16,0},{24,8},{0,16},{8,24},{17,1},{25,9},{1,17},{9,25},{18,2},{26... | collective-permute-start | bytes 589832 | tf_op jit(solution)/shard_map/ppermute | solution.py:161
  56.0 4.3 %collective-permute-start.17 = (bf16[512,256]{1,0:T(8,128)(2,1)S(1)}, bf16[512,256]{1,0:T(8,128)(2,1)S(1)}, u32[]{:S(2)}, u32[]{:S(2)}) collective-permute-start(bf16[512,256]{1,0:T(8,128)(2,1)S(1)} %get-tuple-element.47.wo_mine_ref), channel_id=1, source_target_pairs={{4,0},{0,4},{5,1},{1,5},{6,2},{2,6},{7,3},{3,7},{12,8},{8,12},{13,... | collective-permute-start | bytes 786440 | tf_op jit(solution)/shard_map/ppermute | solution.py:28
  59.7 1.5 %collective-permute-start.18 = (bf16[144,256]{1,0:T(8,128)(2,1)S(1)}, bf16[144,256]{1,0:T(8,128)(2,1)S(1)}, u32[]{:S(2)}, u32[]{:S(2)}) collective-permute-start(bf16[144,256]{1,0:T(8,128)(2,1)S(1)} %get-tuple-element.50), channel_id=1, source_target_pairs={{4,0},{0,4},{5,1},{1,5},{6,2},{2,6},{7,3},{3,7},{12,8},{8,12},{13,... | collective-permute-start | bytes 221192 | tf_op jit(solution)/shard_map/ppermute | solution.py:28

commit v8 on v7

--- a/solution.py
+++ b/solution.py
@@ -166,13 +166,12 @@
 
 
 def window_sources():
-    token = lax.broadcasted_iota(jnp.int32, (8, 5 * 128), 1)
-    a, v = token // (2 * WIN), token // WIN % 2
-    dh, dw, dz = token % WIN // (WW * WZ), token % (WW * WZ) // WZ, token % WZ
-    row = dh + WH * a - WH // 2
+    token = lax.broadcasted_iota(jnp.int32, (8, 3 * 128), 1)
+    v, dh = token // WIN, token % WIN // (WW * WZ)
+    dw, dz = token % (WW * WZ) // WZ, token % WZ
     col = (WW // 2 + WW * v + dw) % (2 * WW)
     level = (dz + 1) % WZ
-    return as_column(col // WW * KEPT + (row + WH) * WW * WZ + col % WW * WZ + level - KEEP0, 4 * WIN)
+    return as_column(col // WW * WIN + dh * WW * WZ + col % WW * WZ + level, 2 * WIN)
 
 
 def tile_sources():
@@ -596,14 +595,19 @@
     tokens = PAIR * KEPT
     pair_columns(me, o_s, mine_ref[0:tokens, :], other_ref[0:tokens, :])
     pair_columns(me, wo_s, mine_ref[tokens:, :], other_ref[tokens:, :])
+    pick = one_hot(window_sources(), 2 * WIN)
     for l in range(PAIR):
         rows = slice(KEPT * l, KEPT * (l + 1))
         value = x_ref[l, KEEP0:KEEP1, :].astype(F32) + nn_dot(o_s[rows, :], wo_s[...])
         value = value.astype(BF16)
         m_s[l] = value
-        n_s[rows, :] = norm_rows(value.astype(F32), gain_ref[1:2, :])
+        normed = norm_rows(value.astype(F32), gain_ref[1:2, :])
+        for a in range(2):
+            at = HALF - KEEP0 + WIN * a
+            n_s[a, WIN * l : WIN * (l + 1), :] = normed[at : at + WIN]
     mid_ref[...] = m_s[me, PART : PART + WIN, :]
-    win_ref[...] = nn_dot(one_hot(window_sources(), tokens), n_s[...]).astype(BF16)
+    for a in range(2):
+        win_ref[2 * WIN * a : 2 * WIN * (a + 1), :] = nn_dot(pick, n_s[a]).astype(BF16)
 
 
 def middle_call(mine, other, x, gain):
@@ -618,7 +622,7 @@
             pltpu.VMEM((tokens, D), BF16),
             pltpu.VMEM((D, D), BF16),
             pltpu.VMEM((PAIR, KEPT, D), BF16),
-            pltpu.VMEM((tokens, D), BF16),
+            pltpu.VMEM((2, 2 * WIN, D), BF16),
         ],
         compiler_params=vmem(16),
         cost_estimate=pl.CostEstimate(flops=10**9, bytes_accessed=3 * 10**6, transcendentals=0),

time: 63.1 us -> 63 us (level)
  no operation moved by 1% of the time
where the time goes in v8:
time: 63 us; the launch traced here: 61.9 us
  waiting for transfers between devices  26.8 us (43%)
  starting transfers between devices  21 us (33%)
  Pallas kernels  13.5 us (21%)
    ppermute x13, waiting for transfers between devices, heard_from(): lax.ppermute(block, axis, [(partner(i, step, size), i) for i in range(siz...  26.1 us
    ppermute x13, starting transfers between devices, heard_from(): lax.ppermute(block, axis, [(partner(i, step, size), i) for i in range(siz...  19.8 us
    pallas_call x3, Pallas kernels, bias_call(): pl.pallas_call(kernel, out_shape=out, scratch_shapes=[pltpu.VMEM((MY_HEAD...  3.5 us
    pallas_call x1, Pallas kernels, first_call(): pl.pallas_call(first_kernel, out_shape=jax.ShapeDtypeStruct((PAIR * KEPT...  2.26 us
    pallas_call x1, Pallas kernels, open_call(): pl.pallas_call(functools.partial(open_kernel, wide), out_shape=(jax.Shape...  2.11 us
    pallas_call x1, Pallas kernels, second_call(): pl.pallas_call(second_kernel, out_shape=(half, half), scratch_shapes=[qkv...  2.06 us
    pallas_call x1, Pallas kernels, middle_call(): pl.pallas_call(middle_kernel, out_shape=(jax.ShapeDtypeStruct((WIN, D), B...  1.38 us
  transfers between devices with their start and end apart: 19, of which 9 were waited for; matrix products, arithmetic and copies ran while one was open for 0% of the time, Pallas kernels for 12%

profile of v8, /device:TPU:0, one launch (start us, length us, event | category | flops | bytes accessed | tf_op | source)
XLA Modules:
  0.0 61.9 jit_solution(6463227591253340998)
XLA Ops:
  0.0 2.1 %open.1 = (bf16[32,1024]{1,0:T(8,128)(2,1)}, bf16[64,1024]{1,0:T(8,128)(2,1)}, bf16[152,512]{1,0:T(8,128)(2,1)}) custom-call(bf16[72,2,512]{2,1,0:T(2,128)(2,1)} %bitcast.15, s32[6,2,12]{2,1,0:T(2,128)} %bitcast.16, bf16[2,128,1536]{2,1,0:T(8,128)(2,1)} %own_qkv_ref.3, bf16[2,128,512]{2,1,0:T(8,128)(2,1)} %own_out_ref.3), custom_call_target="tpu_custom_call" | custom-call | flops 1000000 | bytes 1000000 | tf_op jit(solution)/shard_map/open/pallas_call | solution.py:354
  2.1 3.1 %collective-permute-start.5 = (bf16[32,1024]{1,0:T(8,128)(2,1)}, bf16[32,1024]{1,0:T(8,128)(2,1)S(1)}, u32[]{:S(2)}, u32[]{:S(2)}) collective-permute-start(bf16[32,1024]{1,0:T(8,128)(2,1)} %get-tuple-element.30), channel_id=1, source_target_pairs={{1,0},{0,1},{3,2},{2,3},{5,4},{4,5},{7,6},{6,7},{9,8},{8,9},{11,10... | collective-permute-start | bytes 196616 | tf_op jit(solution)/shard_map/ppermute | solution.py:161
  5.3 2.6 %collective-permute-start.6 = (bf16[32,1024]{1,0:T(8,128)(2,1)}, bf16[32,1024]{1,0:T(8,128)(2,1)S(1)}, u32[]{:S(2)}, u32[]{:S(2)}) collective-permute-start(bf16[32,1024]{1,0:T(8,128)(2,1)} %get-tuple-element.30), channel_id=1, source_target_pairs={{2,0},{3,1},{0,2},{1,3},{6,4},{7,5},{4,6},{5,7},{10,8},{11,9},{8,1... | collective-permute-start | bytes 196616 | tf_op jit(solution)/shard_map/ppermute | solution.py:161
  7.9 4.9 %collective-permute-done.6.refs_1_ = bf16[32,1024]{1,0:T(8,128)(2,1)S(1)} collective-permute-done((bf16[32,1024]{1,0:T(8,128)(2,1)}, bf16[32,1024]{1,0:T(8,128)(2,1)S(1)}, u32[]{:S(2)}, u32[]{:S(2)}) %collective-permute-start.6) | collective-permute-done | bytes 65568 | tf_op jit(solution)/shard_map/ppermute | solution.py:161
  12.8 1.4 %collective-permute-done.7.refs_2_ = bf16[32,1024]{1,0:T(8,128)(2,1)S(1)} collective-permute-done((bf16[32,1024]{1,0:T(8,128)(2,1)}, bf16[32,1024]{1,0:T(8,128)(2,1)S(1)}, u32[]{:S(2)}, u32[]{:S(2)}) %collective-permute-start.7) | collective-permute-done | bytes 65568 | tf_op jit(solution)/shard_map/ppermute | solution.py:161
  14.2 2.5 %collective-permute-start.10 = (bf16[96,1024]{1,0:T(8,128)(2,1)S(1)}, bf16[96,1024]{1,0:T(8,128)(2,1)S(1)}, u32[]{:S(2)}, u32[]{:S(2)}) collective-permute-start(bf16[96,1024]{1,0:T(8,128)(2,1)S(1)} %shard_map.73), channel_id=1, source_target_pairs={{24,0},{16,8},{8,16},{0,24},{25,1},{17,9},{9,17},{1,25},{26,2},{18... | collective-permute-start | bytes 589832 | tf_op jit(solution)/shard_map/ppermute | solution.py:161
  16.7 0.5 collective-permute-start
  17.2 1.4 %collective-permute-start.1 = (bf16[152,512]{1,0:T(8,128)(2,1)S(1)}, bf16[152,512]{1,0:T(8,128)(2,1)S(1)}, u32[]{:S(2)}, u32[]{:S(2)}) collective-permute-start(bf16[152,512]{1,0:T(8,128)(2,1)S(1)} %copy-done.2), channel_id=1, source_target_pairs={{24,0},{16,8},{8,16},{0,24},{25,1},{17,9},{9,17},{1,25},{26,2},{18... | collective-permute-start | bytes 466952 | tf_op jit(solution)/shard_map/ppermute | solution.py:161
  18.7 0.5 collective-permute-start.8
  19.2 1.5 %collective-permute-start.9 = (bf16[96,1024]{1,0:T(8,128)(2,1)S(1)}, bf16[96,1024]{1,0:T(8,128)(2,1)S(1)}, u32[]{:S(2)}, u32[]{:S(2)}) collective-permute-start(bf16[96,1024]{1,0:T(8,128)(2,1)S(1)} %shard_map.73), channel_id=1, source_target_pairs={{16,0},{24,8},{0,16},{8,24},{17,1},{25,9},{1,17},{9,25},{18,2},{26... | collective-permute-start | bytes 589832 | tf_op jit(solution)/shard_map/ppermute | solution.py:161
  20.7 5.6 %collective-permute-done.refs_0_ = bf16[152,512]{1,0:T(8,128)(2,1)S(1)} collective-permute-done((bf16[152,512]{1,0:T(8,128)(2,1)S(1)}, bf16[152,512]{1,0:T(8,128)(2,1)S(1)}, u32[]{:S(2)}, u32[]{:S(2)}) %collective-permute-start) | collective-permute-done | bytes 155680 | tf_op jit(solution)/shard_map/ppermute | solution.py:161
  26.4 2.6 %collective-permute-done.1.refs_2_ = bf16[152,512]{1,0:T(8,128)(2,1)S(1)} collective-permute-done((bf16[152,512]{1,0:T(8,128)(2,1)S(1)}, bf16[152,512]{1,0:T(8,128)(2,1)S(1)}, u32[]{:S(2)}, u32[]{:S(2)}) %collective-permute-start.1) | collective-permute-done | bytes 155680 | tf_op jit(solution)/shard_map/ppermute | solution.py:161
  29.0 0.5 collective-permute-start.4
  29.5 1.9 %shard_map.75 = (f32[8,144,128]{2,1,0:T(8,128)S(1)}, f32[144,128]{1,0:T(8,128)S(1)}, s32[144,144]{1,0:T(8,128)S(1)}, s32[16,256]{1,0:T(8,128)S(1)}) custom-call(f32[2,16,759]{2,1,0:T(8,128)S(1)} %bitcast.12, s32[144,144]{1,0:T(8,128)S(1)} %copy-done.4), custom_call_target="tpu_custom_call" | custom-call | flops 1000000000 | bytes 1000000 | tf_op jit(solution)/shard_map/pallas_call | solution.py:286
  32.1 0.7 %enter.1 = (bf16[2,432,512]{2,1,0:T(8,128)(2,1)S(1)}, bf16[2,432,512]{2,1,0:T(8,128)(2,1)S(1)}, f32[8,256]{1,0:T(8,128)S(1)}, f32[144,8]{1,0:T(8,128)S(1)}) custom-call(bf16[152,512]{1,0:T(8,128)(2,1)S(1)} %collective-permute-done.refs_0_, bf16[152,512]{1,0:T(8,128)(2,1)S(1)} %copy-done.2, bf16[152,512]{1,0:T(8,128)(2,1)S(1)} %collective-permute-done.1.refs_2_, ...), custom_call_target="tpu_custom_call" | custom-call | flops 100000000 | bytes 2000000 | tf_op jit(solution)/shard_map/enter/pallas_call | solution.py:413
  32.8 2.3 %first.1.mine_ref = bf16[1120,256]{1,0:T(8,128)(2,1)S(1)} custom-call(bf16[2,432,512]{2,1,0:T(8,128)(2,1)S(1)} %get-tuple-element.29.n_ref, bf16[512,768]{1,0:T(8,128)(2,1)S(1)} %get-tuple-element.31.w_ref, f32[8,144,128]{2,1,0:T(8,128)S(1)} %get-tuple-element.32.bias_ref, f32[144,128]{1,0:T(8,128)S(1)} %get-tuple-element.33.tail_ref, ...), custom_call_target="tpu_custom_call" | custom-call | flops 2000000000 | bytes 4000000 | tf_op jit(solution)/shard_map/first/pallas_call | solution.py:575
  35.1 0.5 collective-permute-start.12
  35.7 1.7 %collective-permute-start.13 = (bf16[64,1024]{1,0:T(8,128)(2,1)S(1)}, bf16[64,1024]{1,0:T(8,128)(2,1)S(1)}, u32[]{:S(2)}, u32[]{:S(2)}) collective-permute-start(bf16[64,1024]{1,0:T(8,128)(2,1)S(1)} %copy-done.6), channel_id=1, source_target_pairs={{2,0},{3,1},{0,2},{1,3},{6,4},{7,5},{4,6},{5,7},{10,8},{11,9},{8,1... | collective-permute-start | bytes 393224 | tf_op jit(solution)/shard_map/ppermute | solution.py:161
  37.4 2.2 %collective-permute-start.14 = (bf16[64,1024]{1,0:T(8,128)(2,1)S(1)}, bf16[64,1024]{1,0:T(8,128)(2,1)S(1)}, u32[]{:S(2)}, u32[]{:S(2)}) collective-permute-start(bf16[64,1024]{1,0:T(8,128)(2,1)S(1)} %copy-done.6), channel_id=1, source_target_pairs={{3,0},{2,1},{1,2},{0,3},{7,4},{6,5},{5,6},{4,7},{11,8},{10,9},{9,1... | collective-permute-start | bytes 393224 | tf_op jit(solution)/shard_map/ppermute | solution.py:161
  39.6 4.1 %collective-permute-done.12.refs_0_ = bf16[64,1024]{1,0:T(8,128)(2,1)S(1)} collective-permute-done((bf16[64,1024]{1,0:T(8,128)(2,1)S(1)}, bf16[64,1024]{1,0:T(8,128)(2,1)S(1)}, u32[]{:S(2)}, u32[]{:S(2)}) %collective-permute-start.12) | collective-permute-done | bytes 131104 | tf_op jit(solution)/shard_map/ppermute | solution.py:161
  43.6 5.0 %collective-permute-done.13.refs_1_ = bf16[64,1024]{1,0:T(8,128)(2,1)S(1)} collective-permute-done((bf16[64,1024]{1,0:T(8,128)(2,1)S(1)}, bf16[64,1024]{1,0:T(8,128)(2,1)S(1)}, u32[]{:S(2)}, u32[]{:S(2)}) %collective-permute-start.13) | collective-permute-done | bytes 131104 | tf_op jit(solution)/shard_map/ppermute | solution.py:161
  48.6 1.6 %collective-permute-start.15 = (bf16[96,1024]{1,0:T(8,128)(2,1)S(1)}, bf16[96,1024]{1,0:T(8,128)(2,1)S(1)}, u32[]{:S(2)}, u32[]{:S(2)}) collective-permute-start(bf16[96,1024]{1,0:T(8,128)(2,1)S(1)} %shard_map.76), channel_id=1, source_target_pairs={{8,0},{0,8},{24,16},{16,24},{9,1},{1,9},{25,17},{17,25},{10,2},{2,... | collective-permute-start | bytes 589832 | tf_op jit(solution)/shard_map/ppermute | solution.py:161
  50.2 1.5 %collective-permute-start.16 = (bf16[96,1024]{1,0:T(8,128)(2,1)S(1)}, bf16[96,1024]{1,0:T(8,128)(2,1)S(1)}, u32[]{:S(2)}, u32[]{:S(2)}) collective-permute-start(bf16[96,1024]{1,0:T(8,128)(2,1)S(1)} %shard_map.76), channel_id=1, source_target_pairs={{16,0},{24,8},{0,16},{8,24},{17,1},{25,9},{1,17},{9,25},{18,2},{26... | collective-permute-start | bytes 589832 | tf_op jit(solution)/shard_map/ppermute | solution.py:161
  51.7 0.7 %shard_map.78.bias_a = f32[4,144,128]{2,1,0:T(8,128)S(1)} custom-call(f32[2,16,759]{2,1,0:T(8,128)S(1)} %bitcast.13, s32[144,144]{1,0:T(8,128)S(1)} %get-tuple-element.40.index_ref), custom_call_target="tpu_custom_call" | custom-call | flops 1000000000 | bytes 1000000 | tf_op jit(solution)/shard_map/pallas_call | solution.py:286
  52.4 1.0 %shard_map.79 = (f32[4,144,128]{2,1,0:T(8,128)S(1)}, f32[144,128]{1,0:T(8,128)S(1)}) custom-call(f32[2,16,759]{2,1,0:T(8,128)S(1)} %bitcast.14, s32[144,144]{1,0:T(8,128)S(1)} %get-tuple-element.40.index_ref, s32[16,256]{1,0:T(8,128)S(1)} %get-tuple-element.41.flip_ref), custom_call_target="tpu_custom_call" | custom-call | flops 1000000000 | bytes 1000000 | tf_op jit(solution)/shard_map/pallas_call | solution.py:286
  53.4 1.3 %collective-permute-done.15.refs_3_ = bf16[96,1024]{1,0:T(8,128)(2,1)S(1)} collective-permute-done((bf16[96,1024]{1,0:T(8,128)(2,1)S(1)}, bf16[96,1024]{1,0:T(8,128)(2,1)S(1)}, u32[]{:S(2)}, u32[]{:S(2)}) %collective-permute-start.15) | collective-permute-done | bytes 196640 | tf_op jit(solution)/shard_map/ppermute | solution.py:161
  54.7 1.2 %collective-permute-done.16.refs_4_ = bf16[96,1024]{1,0:T(8,128)(2,1)S(1)} collective-permute-done((bf16[96,1024]{1,0:T(8,128)(2,1)S(1)}, bf16[96,1024]{1,0:T(8,128)(2,1)S(1)}, u32[]{:S(2)}, u32[]{:S(2)}) %collective-permute-start.16) | collective-permute-done | bytes 196640 | tf_op jit(solution)/shard_map/ppermute | solution.py:161
  56.1 1.4 %middle.1 = (bf16[144,512]{1,0:T(8,128)(2,1)S(1)}, bf16[576,512]{1,0:T(8,128)(2,1)S(1)}) custom-call(bf16[1120,256]{1,0:T(8,128)(2,1)S(1)} %first.1.mine_ref, bf16[1120,256]{1,0:T(8,128)(2,1)S(1)} %collective-permute-done.11.other_ref, bf16[2,432,512]{2,1,0:T(8,128)(2,1)S(1)} %get-tuple-element.35.x_ref, f32[2,512]{1,0:T(2,128)S(1)} %copy-done.3), custom_call_target="tpu_custom_call" | custom-call | flops 1000000000 | bytes 3000000 | tf_op jit(solution)/shard_map/middle/pallas_call | solution.py:615
  57.4 2.1 %second.1 = (bf16[144,256]{1,0:T(8,128)(2,1)S(1)}, bf16[144,256]{1,0:T(8,128)(2,1)S(1)}) custom-call(bf16[576,512]{1,0:T(8,128)(2,1)S(1)} %get-tuple-element.37.win_ref, bf16[512,768]{1,0:T(8,128)(2,1)S(1)} %get-tuple-element.39.w_ref, f32[4,144,128]{2,1,0:T(8,128)S(1)} %shard_map.78.bias_a, f32[4,144,128]{2,1,0:T(8,128)S(1)} %get-tuple-element.42.bias_b, ...), custom_call_target="tpu_custom_call" | custom-call | flops 2000000000 | bytes 4000000 | tf_op jit(solution)/shard_map/second/pallas_call | solution.py:669
  59.5 0.6 collective-permute-start.18
  60.3 0.6 %collective-permute-done.18.got_ref = bf16[144,256]{1,0:T(8,128)(2,1)S(1)} collective-permute-done((bf16[144,256]{1,0:T(8,128)(2,1)S(1)}, bf16[144,256]{1,0:T(8,128)(2,1)S(1)}, u32[]{:S(2)}, u32[]{:S(2)}) %collective-permute-start.18) | collective-permute-done | bytes 73760 | tf_op jit(solution)/shard_map/ppermute | solution.py:28
  61.0 1.0 %last.1 = bf16[72,2,512]{2,1,0:T(2,128)(2,1)} custom-call(f32[144,512]{1,0:T(8,128)S(1)} %get-tuple-element.48.sum_ref, bf16[256,512]{1,0:T(8,128)(2,1)S(1)} %get-tuple-element.49.rows_ref, bf16[144,256]{1,0:T(8,128)(2,1)S(1)} %collective-permute-done.18.got_ref), custom_call_target="tpu_custom_call" | custom-call | flops 100000000 | bytes 1000000 | tf_op jit(solution)/shard_map/last/pallas_call | solution.py:710
  (34 shorter events, 1.2 us)
Async XLA Ops:
  0.0 29.5 %copy-start.5 = (f32[2,759,16]{1,2,0:T(8,128)S(1)}, f32[2,759,16]{1,2,0:T(8,128)}, u32[]{:S(2)}) copy-start(f32[2,759,16]{1,2,0:T(8,128)} %param.11) | copy-start | bytes 291460
  2.1 14.6 %copy-start.2 = (bf16[152,512]{1,0:T(8,128)(2,1)S(1)}, bf16[152,512]{1,0:T(8,128)(2,1)}, u32[]{:S(2)}) copy-start(bf16[152,512]{1,0:T(8,128)(2,1)} %get-tuple-element.28.refs_1_) | copy-start | bytes 466948
  2.1 27.4 %copy-start.4 = (s32[144,144]{1,0:T(8,128)S(1)}, s32[144,144]{1,0:T(8,128)}, u32[]{:S(2)}) copy-start(s32[144,144]{1,0:T(8,128)} %index_ref.1) | copy-start | bytes 248836
  2.1 5.7 %collective-permute-start.5 = (bf16[32,1024]{1,0:T(8,128)(2,1)}, bf16[32,1024]{1,0:T(8,128)(2,1)S(1)}, u32[]{:S(2)}, u32[]{:S(2)}) collective-permute-start(bf16[32,1024]{1,0:T(8,128)(2,1)} %get-tuple-element.30), channel_id=1, source_target_pairs={{1,0},{0,1},{3,2},{2,3},{5,4},{4,5},{7,6},{6,7},{9,8},{8,9},{11,10... | collective-permute-start | bytes 196616 | tf_op jit(solution)/shard_map/ppermute | solution.py:161
  5.3 7.5 %collective-permute-start.6 = (bf16[32,1024]{1,0:T(8,128)(2,1)}, bf16[32,1024]{1,0:T(8,128)(2,1)S(1)}, u32[]{:S(2)}, u32[]{:S(2)}) collective-permute-start(bf16[32,1024]{1,0:T(8,128)(2,1)} %get-tuple-element.30), channel_id=1, source_target_pairs={{2,0},{3,1},{0,2},{1,3},{6,4},{7,5},{4,6},{5,7},{10,8},{11,9},{8,1... | collective-permute-start | bytes 196616 | tf_op jit(solution)/shard_map/ppermute | solution.py:161
  7.9 6.3 %collective-permute-start.7 = (bf16[32,1024]{1,0:T(8,128)(2,1)}, bf16[32,1024]{1,0:T(8,128)(2,1)S(1)}, u32[]{:S(2)}, u32[]{:S(2)}) collective-permute-start(bf16[32,1024]{1,0:T(8,128)(2,1)} %get-tuple-element.30), channel_id=1, source_target_pairs={{3,0},{2,1},{1,2},{0,3},{7,4},{6,5},{5,6},{4,7},{11,8},{10,9},{9,1... | collective-permute-start | bytes 196616 | tf_op jit(solution)/shard_map/ppermute | solution.py:161
  14.2 14.8 %collective-permute-start.10 = (bf16[96,1024]{1,0:T(8,128)(2,1)S(1)}, bf16[96,1024]{1,0:T(8,128)(2,1)S(1)}, u32[]{:S(2)}, u32[]{:S(2)}) collective-permute-start(bf16[96,1024]{1,0:T(8,128)(2,1)S(1)} %shard_map.73), channel_id=1, source_target_pairs={{24,0},{16,8},{8,16},{0,24},{25,1},{17,9},{9,17},{1,25},{26,2},{18... | collective-permute-start | bytes 589832 | tf_op jit(solution)/shard_map/ppermute | solution.py:161
  16.7 9.7 %collective-permute-start = (bf16[152,512]{1,0:T(8,128)(2,1)S(1)}, bf16[152,512]{1,0:T(8,128)(2,1)S(1)}, u32[]{:S(2)}, u32[]{:S(2)}) collective-permute-start(bf16[152,512]{1,0:T(8,128)(2,1)S(1)} %copy-done.2), channel_id=1, source_target_pairs={{8,0},{0,8},{24,16},{16,24},{9,1},{1,9},{25,17},{17,25},{10,2},{2,... | collective-permute-start | bytes 466952 | tf_op jit(solution)/shard_map/ppermute | solution.py:161
  17.2 11.7 %collective-permute-start.1 = (bf16[152,512]{1,0:T(8,128)(2,1)S(1)}, bf16[152,512]{1,0:T(8,128)(2,1)S(1)}, u32[]{:S(2)}, u32[]{:S(2)}) collective-permute-start(bf16[152,512]{1,0:T(8,128)(2,1)S(1)} %copy-done.2), channel_id=1, source_target_pairs={{24,0},{16,8},{8,16},{0,24},{25,1},{17,9},{9,17},{1,25},{26,2},{18... | collective-permute-start | bytes 466952 | tf_op jit(solution)/shard_map/ppermute | solution.py:161
  18.7 12.7 %collective-permute-start.8 = (bf16[96,1024]{1,0:T(8,128)(2,1)S(1)}, bf16[96,1024]{1,0:T(8,128)(2,1)S(1)}, u32[]{:S(2)}, u32[]{:S(2)}) collective-permute-start(bf16[96,1024]{1,0:T(8,128)(2,1)S(1)} %shard_map.73), channel_id=1, source_target_pairs={{8,0},{0,8},{24,16},{16,24},{9,1},{1,9},{25,17},{17,25},{10,2},{2,... | collective-permute-start | bytes 589832 | tf_op jit(solution)/shard_map/ppermute | solution.py:161
  19.2 12.2 %collective-permute-start.9 = (bf16[96,1024]{1,0:T(8,128)(2,1)S(1)}, bf16[96,1024]{1,0:T(8,128)(2,1)S(1)}, u32[]{:S(2)}, u32[]{:S(2)}) collective-permute-start(bf16[96,1024]{1,0:T(8,128)(2,1)S(1)} %shard_map.73), channel_id=1, source_target_pairs={{16,0},{24,8},{0,16},{8,24},{17,1},{25,9},{1,17},{9,25},{18,2},{26... | collective-permute-start | bytes 589832 | tf_op jit(solution)/shard_map/ppermute | solution.py:161
  26.4 5.2 %collective-permute-start.3 = (bf16[152,512]{1,0:T(8,128)(2,1)S(1)}, bf16[152,512]{1,0:T(8,128)(2,1)S(1)}, u32[]{:S(2)}, u32[]{:S(2)}) collective-permute-start(bf16[152,512]{1,0:T(8,128)(2,1)S(1)} %copy-done.2), channel_id=1, source_target_pairs={{4,0},{0,4},{5,1},{1,5},{6,2},{2,6},{7,3},{3,7},{12,8},{8,12},{13,... | collective-permute-start | bytes 466952 | tf_op jit(solution)/shard_map/ppermute | solution.py:28
  29.0 2.6 %collective-permute-start.2 = (bf16[152,512]{1,0:T(8,128)(2,1)S(1)}, bf16[152,512]{1,0:T(8,128)(2,1)S(1)}, u32[]{:S(2)}, u32[]{:S(2)}) collective-permute-start(bf16[152,512]{1,0:T(8,128)(2,1)S(1)} %collective-permute-done.refs_0_), channel_id=1, source_target_pairs={{4,0},{0,4},{5,1},{1,5},{6,2},{2,6},{7,3},{3,7},{12,8},{8,12},{13,... | collective-permute-start | bytes 466952 | tf_op jit(solution)/shard_map/ppermute | solution.py:28
  29.0 2.6 %collective-permute-start.4 = (bf16[152,512]{1,0:T(8,128)(2,1)S(1)}, bf16[152,512]{1,0:T(8,128)(2,1)S(1)}, u32[]{:S(2)}, u32[]{:S(2)}) collective-permute-start(bf16[152,512]{1,0:T(8,128)(2,1)S(1)} %collective-permute-done.1.refs_2_), channel_id=1, source_target_pairs={{4,0},{0,4},{5,1},{1,5},{6,2},{2,6},{7,3},{3,7},{12,8},{8,12},{13,... | collective-permute-start | bytes 466952 | tf_op jit(solution)/shard_map/ppermute | solution.py:28
  29.5 1.9 %copy-start = (bf16[2,128,1536]{2,1,0:T(8,128)(2,1)S(1)}, bf16[2,128,1536]{2,1,0:T(8,128)(2,1)}, u32[]{:S(2)}) copy-start(bf16[2,128,1536]{2,1,0:T(8,128)(2,1)} %own_qkv_ref.3) | copy-start | bytes 2359300
  29.5 1.9 %copy-start.1 = (bf16[2,128,512]{2,1,0:T(8,128)(2,1)S(1)}, bf16[2,128,512]{2,1,0:T(8,128)(2,1)}, u32[]{:S(2)}) copy-start(bf16[2,128,512]{2,1,0:T(8,128)(2,1)} %own_out_ref.3) | copy-start | bytes 786436
  31.4 0.7 %copy-start.3 = (f32[2,512]{1,0:T(2,128)S(1)}, f32[2,512]{1,0:T(2,128)}, u32[]{:S(2)}) copy-start(f32[2,512]{1,0:T(2,128)} %gain_ref.1) | copy-start | bytes 12292
  32.8 2.4 %copy-start.6 = (bf16[64,1024]{1,0:T(8,128)(2,1)S(1)}, bf16[64,1024]{1,0:T(8,128)(2,1)}, u32[]{:S(2)}) copy-start(bf16[64,1024]{1,0:T(8,128)(2,1)} %get-tuple-element.38) | copy-start | bytes 393220
  35.0 21.0 %collective-permute-start.11 = (bf16[1120,256]{1,0:T(8,128)(2,1)S(1)}, bf16[1120,256]{1,0:T(8,128)(2,1)S(1)}, u32[]{:S(2)}, u32[]{:S(2)}) collective-permute-start(bf16[1120,256]{1,0:T(8,128)(2,1)S(1)} %first.1.mine_ref), channel_id=1, source_target_pairs={{4,0},{0,4},{5,1},{1,5},{6,2},{2,6},{7,3},{3,7},{12,8},{8,12},{13,... | collective-permute-start | bytes 1720328 | tf_op jit(solution)/shard_map/ppermute | solution.py:28
  35.1 8.5 %collective-permute-start.12 = (bf16[64,1024]{1,0:T(8,128)(2,1)S(1)}, bf16[64,1024]{1,0:T(8,128)(2,1)S(1)}, u32[]{:S(2)}, u32[]{:S(2)}) collective-permute-start(bf16[64,1024]{1,0:T(8,128)(2,1)S(1)} %copy-done.6), channel_id=1, source_target_pairs={{1,0},{0,1},{3,2},{2,3},{5,4},{4,5},{7,6},{6,7},{9,8},{8,9},{11,10... | collective-permute-start | bytes 393224 | tf_op jit(solution)/shard_map/ppermute | solution.py:161
  35.7 12.9 %collective-permute-start.13 = (bf16[64,1024]{1,0:T(8,128)(2,1)S(1)}, bf16[64,1024]{1,0:T(8,128)(2,1)S(1)}, u32[]{:S(2)}, u32[]{:S(2)}) collective-permute-start(bf16[64,1024]{1,0:T(8,128)(2,1)S(1)} %copy-done.6), channel_id=1, source_target_pairs={{2,0},{3,1},{0,2},{1,3},{6,4},{7,5},{4,6},{5,7},{10,8},{11,9},{8,1... | collective-permute-start | bytes 393224 | tf_op jit(solution)/shard_map/ppermute | solution.py:161
  37.4 11.3 %collective-permute-start.14 = (bf16[64,1024]{1,0:T(8,128)(2,1)S(1)}, bf16[64,1024]{1,0:T(8,128)(2,1)S(1)}, u32[]{:S(2)}, u32[]{:S(2)}) collective-permute-start(bf16[64,1024]{1,0:T(8,128)(2,1)S(1)} %copy-done.6), channel_id=1, source_target_pairs={{3,0},{2,1},{1,2},{0,3},{7,4},{6,5},{5,6},{4,7},{11,8},{10,9},{9,1... | collective-permute-start | bytes 393224 | tf_op jit(solution)/shard_map/ppermute | solution.py:161
  48.6 6.0 %collective-permute-start.15 = (bf16[96,1024]{1,0:T(8,128)(2,1)S(1)}, bf16[96,1024]{1,0:T(8,128)(2,1)S(1)}, u32[]{:S(2)}, u32[]{:S(2)}) collective-permute-start(bf16[96,1024]{1,0:T(8,128)(2,1)S(1)} %shard_map.76), channel_id=1, source_target_pairs={{8,0},{0,8},{24,16},{16,24},{9,1},{1,9},{25,17},{17,25},{10,2},{2,... | collective-permute-start | bytes 589832 | tf_op jit(solution)/shard_map/ppermute | solution.py:161
  50.2 5.7 %collective-permute-start.16 = (bf16[96,1024]{1,0:T(8,128)(2,1)S(1)}, bf16[96,1024]{1,0:T(8,128)(2,1)S(1)}, u32[]{:S(2)}, u32[]{:S(2)}) collective-permute-start(bf16[96,1024]{1,0:T(8,128)(2,1)S(1)} %shard_map.76), channel_id=1, source_target_pairs={{16,0},{24,8},{0,16},{8,24},{17,1},{25,9},{1,17},{9,25},{18,2},{26... | collective-permute-start | bytes 589832 | tf_op jit(solution)/shard_map/ppermute | solution.py:161
  56.0 4.1 %collective-permute-start.17 = (bf16[512,256]{1,0:T(8,128)(2,1)S(1)}, bf16[512,256]{1,0:T(8,128)(2,1)S(1)}, u32[]{:S(2)}, u32[]{:S(2)}) collective-permute-start(bf16[512,256]{1,0:T(8,128)(2,1)S(1)} %get-tuple-element.47.wo_mine_ref), channel_id=1, source_target_pairs={{4,0},{0,4},{5,1},{1,5},{6,2},{2,6},{7,3},{3,7},{12,8},{8,12},{13,... | collective-permute-start | bytes 786440 | tf_op jit(solution)/shard_map/ppermute | solution.py:28
  59.5 1.5 %collective-permute-start.18 = (bf16[144,256]{1,0:T(8,128)(2,1)S(1)}, bf16[144,256]{1,0:T(8,128)(2,1)S(1)}, u32[]{:S(2)}, u32[]{:S(2)}) collective-permute-start(bf16[144,256]{1,0:T(8,128)(2,1)S(1)} %get-tuple-element.50), channel_id=1, source_target_pairs={{4,0},{0,4},{5,1},{1,5},{6,2},{2,6},{7,3},{3,7},{12,8},{8,12},{13,... | collective-permute-start | bytes 221192 | tf_op jit(solution)/shard_map/ppermute | solution.py:28
